TPU v7x, 512 devices: a whole 4x8x8 slice. The times are simulated.
512 devices in a mesh: centre: 16 (over y, core), sample: 32 (over z, x).
Axes of the slice: x: 4, y: 8, z: 8, core: 2. Of those that a mesh axis runs over, the one named last changes fastest.
Arguments:
- centres: bfloat16 [1024, 32768], P(None, 'centre'), may hold values from -40 to 40
- pool: bfloat16 [1024, 32768], P('centre', 'sample'), may hold values from -40 to 40
- labels: int32 [32768], P('sample'), may hold values from 0 to 143
- picks: int32 [2, 16384], P(None, 'sample'), may hold values from 0 to 32767, as said below
- coefs: float32 [144, 32768], P(None, ('centre', 'sample')), may hold values from -192 to 1024000
Outputs:
- new_coefs: float32 [144, 32768], P(None, ('centre', 'sample'))
Inputs may be any that keep to these rules, and one draw needn't show every extreme that they name: `picks`: entry b of a step's batch is a pool column in [(b // 512) * 1024, (b // 512 + 1) * 1024); entries may repeat.
All inputs are finite; a program needn't handle non-finite values.
Results may differ from a plain program's by a relative error of at most 0.00065.
Values may be sent and summed in bfloat16 or wider, within the bound.
No kernel may reach another device: no remote copies, remote signals or barrier semaphores. Data moves between devices by JAX's collectives and lax.ppermute only.
A program may use at most 64 MiB of HBM per device.

v0:
```python
import jax
import jax.numpy as jnp
from jax import lax
from jax.sharding import PartitionSpec as P

STEPS = 2


LOGIT_GAIN = 16.0
LENGTH_SCALE = 0.5
STEP_GAIN = 2048.0
EPS = 1e-06


def from_everyone(array, axis):
    peers = lax.axis_size(axis)
    return lax.all_to_all(
        jnp.broadcast_to(array[None], (peers, *array.shape)), axis, 0, 0, tiled=True
    )


def joined_along(parts, dim):
    dims = list(parts.shape[1:])
    dims[dim] *= parts.shape[0]
    return jnp.moveaxis(parts, 0, dim).reshape(dims)


def collect(array, axis, dim):
    parts = from_everyone(array, axis)
    return joined_along(parts, dim)


def over_pieces(array, axis):
    return lax.all_gather(array, axis).sum(0)


def cut_along(array, dim, peers):
    dims = array.shape
    parts = array.reshape(*dims[:dim], peers, dims[dim] // peers, *dims[dim + 1 :])
    return jnp.moveaxis(parts, dim, 0)


def summed_on_arrival(array, axis, dim):
    peers = lax.axis_size(axis)
    parts = lax.all_to_all(cut_along(array, dim, peers), axis, 0, 0, tiled=True)
    return jnp.sum(parts, axis=0)


def laplace(cross, sample_sq, centre_sq, width):
    mean_sq = (sample_sq[:, None] + centre_sq[None, :] - 2.0 * cross) / width
    return jnp.exp(-jnp.sqrt(mean_sq + EPS) / LENGTH_SCALE).astype(jnp.bfloat16)


def on_device(centres, pool, labels, picks, coefs):
    width = centres.shape[0]
    cen_dev = centres.shape[1]
    pool_dev = pool.shape[1]
    batch_dev = picks.shape[1]
    classes = coefs.shape[0]
    total_centres = cen_dev * lax.axis_size("centre")
    total_batch = batch_dev * lax.axis_size("sample")
    rate = STEP_GAIN * LOGIT_GAIN / total_batch
    centre_sq = jnp.sum(jnp.square(centres.astype(jnp.float32)), axis=0)
    local_picks = picks - lax.axis_index("sample") * pool_dev
    current = coefs
    for step in range(STEPS):
        coef_half = collect(current.astype(jnp.bfloat16), "sample", 1)
        chosen = local_picks[step]
        feats = jnp.take(pool, chosen, axis=1)
        labs = jnp.take(labels, chosen)
        gathered = lax.all_gather(feats, "centre", axis=0, tiled=True)
        cross = lax.dot_general(
            gathered, centres, (((0,), (0,)), ((), ())), preferred_element_type=jnp.float32
        )
        sample_sq = jnp.sum(jnp.square(gathered.astype(jnp.float32)), axis=0)
        kern = laplace(cross, sample_sq, centre_sq, width)
        partial_logits = lax.dot_general(
            coef_half, kern, (((1,), (1,)), ((), ())), preferred_element_type=jnp.float32
        )
        logits = over_pieces(partial_logits, "centre") * (LOGIT_GAIN / total_centres)
        top = jnp.max(logits, axis=0, keepdims=True)
        expo = jnp.exp(logits - top)
        probs = expo / jnp.sum(expo, axis=0, keepdims=True)
        class_ids = jnp.arange(classes, dtype=jnp.int32)
        onehot = (class_ids[:, None] == labs[None, :]).astype(jnp.float32)
        resid = (probs - onehot).astype(jnp.bfloat16)
        grad_part = jnp.dot(resid, kern, preferred_element_type=jnp.float32)
        current = current - rate * summed_on_arrival(grad_part, "sample", 1)
    return current


def solution(mesh):
    placed = (
        P(None, "centre"),
        P("centre", "sample"),
        P("sample"),
        P(None, "sample"),
        P(None, ("centre", "sample")),
    )
    return jax.shard_map(
        on_device,
        mesh=mesh,
        in_specs=placed,
        out_specs=P(None, ("centre", "sample")),
        check_vma=False,
    )
```

profile of v0, /device:TPU:1, one launch (start us, length us, event | category | flops | bytes accessed | tf_op | source)
XLA Modules:
  0.0 335.6 jit_solution(12417494301291164431)
XLA Ops:
  7.3 2.3 gather_fusion.1
  14.9 13.7 %all-to-all-start = ((bf16[32,144,64]{1,2,0:T(8,128)(2,1)}), bf16[32,144,64]{1,2,0:T(8,128)(2,1)S(1)}, u32[]{:S(2)}, u32[]{:S(2)}) async-start(bf16[32,144,64]{1,2,0:T(8,128)(2,1)} %broadcast_in_dim.19), calls=%async_computation | async-start | bytes 2097152 | tf_op jit(solution)/shard_map/all_to_all | solution.py:17
  28.7 3.1 multiply_reduce_fusion
  31.8 28.1 %all-gather.7.cloned.1.call-done = bf16[1024,512]{1,0:T(8,128)(2,1)} async-done(((bf16[64,512]{1,0:T(8,128)(2,1)}), bf16[1024,512]{1,0:T(8,128)(2,1)}) %all-gather.7.cloned.1.call-update) | async-done | bytes 1048592 | tf_op jit(solution)/shard_map/all_gather | solution.py:71
  61.4 6.8 %exponential_convert_fusion.1 = bf16[512,2048]{1,0:T(8,128)(2,1)S(1)} fusion(bf16[1024,512]{1,0:T(8,128)(2,1)} %all-gather.7.cloned.1.call-done, bf16[1024,2048]{1,0:T(8,128)(2,1)} %param.9, f32[2048]{0:T(1024)S(1)} %multiply_reduce_fusion, f32[512]{0:T(512)S(1)} %multiply_reduce_fusion.2), kind=kOutput, calls=%fused_computation.6 | convolution fusion | flops 2155872256 | bytes 7350272 | tf_op jit(solution)/shard_map/dot_general | solution.py:72
  68.1 1.6 convolution_bitcast_fusion
  69.7 44.5 %all-gather.11.cloned.1.call-done = f32[2304,512]{1,0:T(8,128)} async-done(((f32[144,512]{1,0:T(8,128)}), f32[2304,512]{1,0:T(8,128)}) %all-gather.11.cloned.1.call-update) | async-done | bytes 4718608 | tf_op jit(solution)/shard_map/all_gather | solution.py:34
  114.2 2.9 reduce_sum.83
  117.2 1.6 fusion.2
  118.8 2.1 reshape.34
  120.9 2.4 copy.43
  123.3 10.0 %all-to-all-start.1 = ((f32[32,144,64]{1,2,0:T(8,128)}), f32[32,144,64]{1,2,0:T(8,128)S(1)}, u32[]{:S(2)}, u32[]{:S(2)}) async-start(f32[32,144,64]{1,2,0:T(8,128)} %copy.43), calls=%async_computation.1 | async-start | bytes 4194304 | tf_op jit(solution)/shard_map/all_to_all | solution.py:45
  133.4 2.3 gather_fusion.3
  138.0 43.7 %all-to-all-done.1 = f32[32,144,64]{1,2,0:T(8,128)S(1)} async-done(((f32[32,144,64]{1,2,0:T(8,128)}), f32[32,144,64]{1,2,0:T(8,128)S(1)}, u32[]{:S(2)}, u32[]{:S(2)}) %all-to-all-start.1) | async-done | bytes 1179680 | tf_op jit(solution)/shard_map/all_to_all | solution.py:45
  183.0 7.4 %all-to-all-start.2 = ((bf16[32,144,64]{1,2,0:T(8,128)(2,1)}), bf16[32,144,64]{1,2,0:T(8,128)(2,1)S(1)}, u32[]{:S(2)}, u32[]{:S(2)}) async-start(bf16[32,144,64]{1,2,0:T(8,128)(2,1)} %broadcast_in_dim.20), calls=%async_computation.2 | async-start | bytes 2097152 | tf_op jit(solution)/shard_map/all_to_all | solution.py:17
  190.5 1.5 multiply_reduce_fusion.1
  192.0 6.7 %exponential_convert_fusion = bf16[512,2048]{1,0:T(8,128)(2,1)S(1)} fusion(bf16[1024,512]{1,0:T(8,128)(2,1)} %all-gather.9.cloned.1.call-done, bf16[1024,2048]{1,0:T(8,128)(2,1)} %param.9, f32[512]{0:T(512)S(1)} %multiply_reduce_fusion.1, f32[2048]{0:T(1024)S(1)} %multiply_reduce_fusion), kind=kOutput, calls=%fused_computation.5 | convolution fusion | flops 2155872256 | bytes 7350272 | tf_op jit(solution)/shard_map/dot_general | solution.py:72
  198.7 17.9 %all-to-all-done.2 = bf16[32,144,64]{1,2,0:T(8,128)(2,1)S(1)} async-done(((bf16[32,144,64]{1,2,0:T(8,128)(2,1)}), bf16[32,144,64]{1,2,0:T(8,128)(2,1)S(1)}, u32[]{:S(2)}, u32[]{:S(2)}) %all-to-all-start.2) | async-done | bytes 589856 | tf_op jit(solution)/shard_map/all_to_all | solution.py:17
  216.6 1.6 fusion.16
  218.2 42.2 %all-gather.13.cloned.1.call-done = f32[2304,512]{1,0:T(8,128)} async-done(((f32[144,512]{1,0:T(8,128)}), f32[2304,512]{1,0:T(8,128)}) %all-gather.13.cloned.1.call-update) | async-done | bytes 4718608 | tf_op jit(solution)/shard_map/all_gather | solution.py:34
  260.4 2.9 reduce_sum.87
  263.4 2.1 fusion.3
  266.5 2.4 copy.49
  268.9 59.4 %all_to_all.20 = f32[32,144,64]{1,2,0:T(8,128)S(1)} all-to-all(f32[32,144,64]{1,2,0:T(8,128)} %copy.49), channel_id=1, replica_groups=mesh['centre'=16,'sample'=32] {'sample'}, dimensions={0} | all-to-all | bytes 2359296 | tf_op jit(solution)/shard_map/all_to_all | solution.py:45
  (50 shorter events, 13.2 us)
Async XLA Ops:
  6.5 0.7 copy-start
  6.5 53.3 %all-gather.7.cloned.1.call-start = ((), (), s32[]{:S(2)}) async-start(), calls=%async_computation.4 | async-start | bytes 1114112 | tf_op jit(solution)/shard_map/all_gather | solution.py:71
  14.9 53.2 %all-to-all-start = ((bf16[32,144,64]{1,2,0:T(8,128)(2,1)}), bf16[32,144,64]{1,2,0:T(8,128)(2,1)S(1)}, u32[]{:S(2)}, u32[]{:S(2)}) async-start(bf16[32,144,64]{1,2,0:T(8,128)(2,1)} %broadcast_in_dim.19), calls=%async_computation | async-start | bytes 2097152 | tf_op jit(solution)/shard_map/all_to_all | solution.py:17
  28.6 85.6 %all-gather.11.cloned.1.call-start = ((), (), s32[]{:S(2)}) async-start(), calls=%async_computation.6 | async-start | bytes 5013504 | tf_op jit(solution)/shard_map/all_gather | solution.py:34
  123.3 58.5 %copy-start.4 = (f32[144,64]{0,1:T(8,128)S(1)}, f32[144,64]{0,1:T(8,128)}, u32[]{:S(2)}) copy-start(f32[144,64]{0,1:T(8,128)} %param.13) | copy-start | bytes 110596
  123.3 58.4 %all-to-all-start.1 = ((f32[32,144,64]{1,2,0:T(8,128)}), f32[32,144,64]{1,2,0:T(8,128)S(1)}, u32[]{:S(2)}, u32[]{:S(2)}) async-start(f32[32,144,64]{1,2,0:T(8,128)} %copy.43), calls=%async_computation.1 | async-start | bytes 4194304 | tf_op jit(solution)/shard_map/all_to_all | solution.py:45
  133.3 57.1 %all-gather.9.cloned.1.call-start = ((), (), s32[]{:S(2)}) async-start(), calls=%async_computation.5 | async-start | bytes 1114112 | tf_op jit(solution)/shard_map/all_gather | solution.py:71
  181.8 8.6 %copy-start.2 = (f32[144,64]{0,1:T(8,128)}, f32[144,64]{0,1:T(8,128)S(1)}, u32[]{:S(2)}) copy-start(f32[144,64]{0,1:T(8,128)S(1)} %reduce_sum.85) | copy-start | bytes 110596
  183.0 33.6 %all-to-all-start.2 = ((bf16[32,144,64]{1,2,0:T(8,128)(2,1)}), bf16[32,144,64]{1,2,0:T(8,128)(2,1)S(1)}, u32[]{:S(2)}, u32[]{:S(2)}) async-start(bf16[32,144,64]{1,2,0:T(8,128)(2,1)} %broadcast_in_dim.20), calls=%async_computation.2 | async-start | bytes 2097152 | tf_op jit(solution)/shard_map/all_to_all | solution.py:17
  190.4 70.1 %all-gather.13.cloned.1.call-start = ((), (), s32[]{:S(2)}) async-start(), calls=%async_computation.7 | async-start | bytes 5013504 | tf_op jit(solution)/shard_map/all_gather | solution.py:34
  198.7 61.7 %copy-start.1 = (bf16[512,2048]{1,0:T(8,128)(2,1)}, bf16[512,2048]{1,0:T(8,128)(2,1)S(1)}, u32[]{:S(2)}) copy-start(bf16[512,2048]{1,0:T(8,128)(2,1)S(1)} %exponential_convert_fusion) | copy-start | bytes 6291460
  268.9 59.5 %copy-start.3 = (f32[144,64]{0,1:T(8,128)S(1)}, f32[144,64]{0,1:T(8,128)}, u32[]{:S(2)}) copy-start(f32[144,64]{0,1:T(8,128)} %copy-done.2) | copy-start | bytes 110596
  268.9 59.5 %copy-start.5 = (f32[144,64]{0,1:T(8,128)S(1)}, f32[144,64]{0,1:T(8,128)}, u32[]{:S(2)}) copy-start(f32[144,64]{0,1:T(8,128)} %param.13) | copy-start | bytes 110596
Sparse Core Ops, SparseCore 0:
  13.0 46.7 all-gather.6
  69.8 44.3 all-gather.10
  138.1 39.5 all-gather.8
  218.3 42.0 all-gather.12
where the time goes:
time: 337 us; the launch traced here: 336 us
  waiting for transfers between devices  177 us (53%)
  blocking collectives  59.4 us (18%)
  starting transfers between devices  31.3 us (9%)
  matrix products  20.3 us (6%)
  local copies, waits for them, and re-layouts  19.9 us (6%)
  other arithmetic  14.8 us (4%)
  between operations  13.4 us (4%)
    all_gather x2, waiting for transfers between devices, over_pieces(): return lax.all_gather(array, axis).sum(0)  86.8 us
    all_to_all x1, blocking collectives, summed_on_arrival(): parts = lax.all_to_all(cut_along(array, dim, peers), axis, 0, 0, tiled=True)  59.4 us
    all_to_all x1, waiting for transfers between devices, summed_on_arrival(): parts = lax.all_to_all(cut_along(array, dim, peers), axis, 0, 0, tiled=True)  43.7 us
    all_gather x2, waiting for transfers between devices, on_device(): gathered = lax.all_gather(feats, 'centre', axis=0, tiled=True)  28.1 us
    all_to_all x2, starting transfers between devices, from_everyone(): lax.all_to_all(jnp.broadcast_to(array[None], (peers, *array.shape)), axis...  21.1 us
    all_to_all x2, waiting for transfers between devices, from_everyone(): lax.all_to_all(jnp.broadcast_to(array[None], (peers, *array.shape)), axis...  17.9 us
    dot_general x2, matrix products, on_device(): lax.dot_general(gathered, centres, (((0,), (0,)), ((), ())), preferred_el...  13.5 us
    all_to_all x1, starting transfers between devices, summed_on_arrival(): parts = lax.all_to_all(cut_along(array, dim, peers), axis, 0, 0, tiled=True)  10 us
  transfers between devices with their start and end apart: 7, of which 5 were waited for; matrix products, arithmetic and copies ran while one was open for 8% of the time, Pallas kernels for 0%

commit v1 on v0

v1 whole, which is shorter than its diff:
```python
import jax
import jax.numpy as jnp
from jax import lax
from jax.sharding import Mesh, PartitionSpec as P

STEPS = 2


LOGIT_GAIN = 16.0
LENGTH_SCALE = 0.5
STEP_GAIN = 2048.0
EPS = 1e-06

CENTRE = ("y", "core")
SAMPLE = ("z", "x")


def exchange(parts, axes):
    return lax.all_to_all(parts, axes, 0, 0, tiled=True)


def spread(array, axes):
    peers = lax.axis_size(axes)
    return exchange(jnp.broadcast_to(array[None], (peers, *array.shape)), axes)


def pack(array, peers, lanes=128):
    rows, columns = array.shape
    width = columns // peers
    fold = lanes // width
    parts = array.reshape(fold, rows // fold, peers, width)
    return jnp.transpose(parts, (2, 1, 0, 3)).reshape(peers, rows // fold, lanes)


def unpack(parts, width):
    peers, height, lanes = parts.shape
    fold = lanes // width
    parts = parts.reshape(peers, height, fold, width)
    return jnp.transpose(parts, (2, 1, 0, 3)).reshape(fold * height, peers * width)


def laplace(cross, sample_sq, centre_sq, width):
    mean_sq = (sample_sq[:, None] + centre_sq[None, :] - 2.0 * cross) / width
    return jnp.exp(-jnp.sqrt(mean_sq + EPS) / LENGTH_SCALE).astype(jnp.bfloat16)


def on_device(centres, pool, labels, picks, coefs):
    width = centres.shape[0]
    cen_dev = centres.shape[1]
    pool_dev = pool.shape[1]
    batch_dev = picks.shape[1]
    classes = coefs.shape[0]
    n_centre, n_sample = lax.axis_size(CENTRE), lax.axis_size(SAMPLE)
    total_centres = cen_dev * n_centre
    total_batch = batch_dev * n_sample
    rate = STEP_GAIN * LOGIT_GAIN / total_batch
    own = batch_dev // n_centre
    cen_own = coefs.shape[1]
    me = lax.axis_index(CENTRE)
    core = lax.axis_index("core")
    local_picks = picks - lax.axis_index(SAMPLE) * pool_dev
    centre_sq = jnp.sum(jnp.square(centres.astype(jnp.float32)), axis=0)

    kerns, labs = [], []
    for step in range(STEPS):
        chosen = local_picks[step]
        feats = jnp.take(pool, chosen, axis=1, mode="clip")
        labs.append(jnp.take(labels, lax.dynamic_slice(chosen, (me * own,), (own,)), mode="clip"))
        mine = lax.all_gather(feats, "y", axis=0)
        other = lax.ppermute(mine, "core", [(0, 1), (1, 0)])
        first = jnp.where(core == 0, mine, other)
        second = jnp.where(core == 0, other, mine)
        gathered = jnp.stack([first, second], axis=1).reshape(width, batch_dev)
        cross = lax.dot_general(
            gathered, centres, (((0,), (0,)), ((), ())), preferred_element_type=jnp.float32
        )
        sample_sq = jnp.sum(jnp.square(gathered.astype(jnp.float32)), axis=0)
        kerns.append(laplace(cross, sample_sq, centre_sq, width))

    current = coefs
    for step in range(STEPS):
        coef_half = unpack(spread(pack(current.astype(jnp.bfloat16), 1)[0], SAMPLE), cen_own)
        kern = kerns[step]
        partial_logits = lax.dot_general(
            coef_half, kern, (((1,), (1,)), ((), ())), preferred_element_type=jnp.float32
        )
        arrived = exchange(pack(partial_logits.astype(jnp.bfloat16), n_centre), CENTRE)
        total = jnp.sum(arrived.astype(jnp.float32), axis=0, keepdims=True)
        logits = unpack(total, own) * (LOGIT_GAIN / total_centres)
        top = jnp.max(logits, axis=0, keepdims=True)
        expo = jnp.exp(logits - top)
        probs = expo / jnp.sum(expo, axis=0, keepdims=True)
        class_ids = jnp.arange(classes, dtype=jnp.int32)
        onehot = (class_ids[:, None] == labs[step][None, :]).astype(jnp.float32)
        resid = (probs - onehot).astype(jnp.bfloat16)
        resid = unpack(spread(pack(resid, 1)[0], CENTRE), own)
        grad_part = jnp.dot(resid, kern, preferred_element_type=jnp.float32)
        arrived = exchange(pack(grad_part.astype(jnp.bfloat16), n_sample), SAMPLE)
        grad = unpack(jnp.sum(arrived.astype(jnp.float32), axis=0, keepdims=True), cen_own)
        current = current - rate * grad
    return current


def solution(mesh):
    sizes = (mesh.shape["centre"] // 2, 2, 8, mesh.shape["sample"] // 8)
    fine = Mesh(mesh.devices.reshape(sizes), (*CENTRE, *SAMPLE))
    placed = (
        P(None, CENTRE),
        P(CENTRE, SAMPLE),
        P(SAMPLE),
        P(None, SAMPLE),
        P(None, (*CENTRE, *SAMPLE)),
    )
    return jax.shard_map(
        on_device,
        mesh=fine,
        in_specs=placed,
        out_specs=P(None, (*CENTRE, *SAMPLE)),
        check_vma=False,
    )
```

time: 337 us -> 251 us (0.74)
  waiting for transfers between devices: 177 us -> 35.1 us
  blocking collectives: 59.4 us -> 111 us
  starting transfers between devices: 31.3 us -> 48.5 us
  between operations: 13.4 us -> 0.47 us
  local copies, waits for them, and re-layouts: 19.9 us -> 30.3 us
  other arithmetic: 14.8 us -> 9.02 us
  matrix products: 20.3 us -> 15.8 us
    all_gather x4 -> x0, waiting for transfers between devices: 115 us -> none  [the longest x2 86.8 us: over_pieces(): return lax.all_gather(array, axis).sum(0)]
    all_gather x0 -> x2, blocking collectives: none -> 41.2 us  [on_device(): mine = lax.all_gather(feats, 'y', axis=0)]
    all_to_all x3 -> x4, waiting for transfers between devices: 61.6 us -> 35.1 us  [exchange(): return lax.all_to_all(parts, axes, 0, 0, tiled=True)]
    ppermute x0 -> x2, starting transfers between devices: none -> 20.4 us  [on_device(): other = lax.ppermute(mine, 'core', [(0, 1), (1, 0)])]
    reshape x2 -> x22, local copies, waits for them, and re-layouts: 3.02 us -> 15.2 us  [the longest x4 4.11 us: unpack(): jnp.transpose(parts, (2, 1, 0, 3)).reshape(fold * height, peers * width)]
    all_to_all x1 -> x4, blocking collectives: 59.4 us -> 69.6 us  [exchange(): return lax.all_to_all(parts, axes, 0, 0, tiled=True)]
    reduce_sum x4, other arithmetic: 6.01 us -> 0.25 us  [the longest x2 0.19 us: on_device(): jnp.sum(arrived.astype(jnp.float32), axis=0, keepdims=True)]
    dot_general x2, matrix products: 13.5 us -> 9.94 us  [on_device(): lax.dot_general(gathered, centres, (((0,), (0,)), ((), ())), preferred_el...]
  transfers between devices with their start and end apart: 7 -> 6, of which waited for: 5 -> 4; matrix products, arithmetic and copies ran while one was open for 8% -> 8% of each run, Pallas kernels for 0% -> 0%
where the time goes in v1:
time: 251 us; the launch traced here: 250 us
  blocking collectives  111 us (44%)
  starting transfers between devices  48.5 us (19%)
  waiting for transfers between devices  35.1 us (14%)
  local copies, waits for them, and re-layouts  30.3 us (12%)
  matrix products  15.8 us (6%)
  other arithmetic  9.02 us (4%)
    all_to_all x4, blocking collectives, exchange(): return lax.all_to_all(parts, axes, 0, 0, tiled=True)  69.6 us
    all_gather x2, blocking collectives, on_device(): mine = lax.all_gather(feats, 'y', axis=0)  41.2 us
    all_to_all x4, waiting for transfers between devices, exchange(): return lax.all_to_all(parts, axes, 0, 0, tiled=True)  35.1 us
    all_to_all x4, starting transfers between devices, exchange(): return lax.all_to_all(parts, axes, 0, 0, tiled=True)  28.1 us
    ppermute x2, starting transfers between devices, on_device(): other = lax.ppermute(mine, 'core', [(0, 1), (1, 0)])  20.4 us
    dot_general x2, matrix products, on_device(): lax.dot_general(gathered, centres, (((0,), (0,)), ((), ())), preferred_el...  9.94 us
  transfers between devices with their start and end apart: 6, of which 4 were waited for; matrix products, arithmetic and copies ran while one was open for 8% of the time, Pallas kernels for 0%

profile of v1, /device:TPU:1, one launch (start us, length us, event | category | flops | bytes accessed | tf_op | source)
XLA Modules:
  0.0 250.1 jit_solution(9616961221477925817)
XLA Ops:
  3.3 21.7 %all-gather = bf16[512,512]{1,0:T(8,128)(2,1)S(1)} all-gather(bf16[64,512]{1,0:T(8,128)(2,1)S(1)} %copy.43), channel_id=2, replica_groups=mesh['y'=8,'core'=2,'z'=8,'x'=4] {'y'}, dimensions={0}, use_global_device_ids=true | all-gather | bytes 589824 | tf_op jit(solution)/shard_map/all_gather | solution.py:69
  25.0 12.6 %collective-permute-start = (bf16[8,64,512]{2,1,0:T(8,128)(2,1)S(1)}, bf16[8,64,512]{2,1,0:T(8,128)(2,1)S(1)}, u32[]{:S(2)}, u32[]{:S(2)}) collective-permute-start(bf16[8,64,512]{2,1,0:T(8,128)(2,1)S(1)} %bitcast.90), channel_id=1, source_target_pairs={{0,32},{32,0},{1,33},{33,1},{2,34},{34,2},{3,35},{35,3},{4,36},{36... | collective-permute-start | bytes 1572872 | tf_op jit(solution)/shard_map/ppermute | solution.py:70
  39.1 19.5 %all-gather.1 = bf16[512,512]{1,0:T(8,128)(2,1)S(1)} all-gather(bf16[64,512]{1,0:T(8,128)(2,1)S(1)} %copy.56), channel_id=3, replica_groups=mesh['y'=8,'core'=2,'z'=8,'x'=4] {'y'}, dimensions={0}, use_global_device_ids=true | all-gather | bytes 589824 | tf_op jit(solution)/shard_map/all_gather | solution.py:69
  58.6 7.8 %collective-permute-start.1 = (bf16[8,64,512]{2,1,0:T(8,128)(2,1)S(1)}, bf16[8,64,512]{2,1,0:T(8,128)(2,1)}, u32[]{:S(2)}, u32[]{:S(2)}) collective-permute-start(bf16[8,64,512]{2,1,0:T(8,128)(2,1)S(1)} %bitcast.92), channel_id=1, source_target_pairs={{0,32},{32,0},{1,33},{33,1},{2,34},{34,2},{3,35},{35,3},{4,36},{36... | collective-permute-start | bytes 1572872 | tf_op jit(solution)/shard_map/ppermute | solution.py:70
  68.4 8.8 %all-to-all-start = ((bf16[32,72,128]{2,1,0:T(8,128)(2,1)}), bf16[32,72,128]{2,1,0:T(8,128)(2,1)S(1)}, u32[]{:S(2)}, u32[]{:S(2)}) async-start(bf16[32,72,128]{2,1,0:T(8,128)(2,1)} %broadcast_in_dim.56), calls=%async_computation | async-start | bytes 1179648 | tf_op jit(solution)/shard_map/all_to_all | solution.py:19
  77.2 3.1 %multiply_reduce_fusion = f32[2048]{0:T(1024)S(1)} fusion(bf16[1024,2048]{1,0:T(8,128)(2,1)} %param.5), kind=kLoop, calls=%fused_computation.4 | loop fusion | flops 6289408 | bytes 4202496 | tf_op jit(solution)/shard_map/reduce_sum | solution.py:62
  82.6 5.7 %exponential_convert_fusion.1 = bf16[512,2048]{1,0:T(8,128)(2,1)} fusion(bf16[1024,512]{1,0:T(8,128)(2,1)S(1)} %bitcast.95, bf16[1024,2048]{1,0:T(8,128)(2,1)S(1)} %copy-done.1, f32[2048]{0:T(1024)S(1)} %multiply_reduce_fusion, f32[512]{0:T(512)S(1)} %multiply_reduce_fusion.2), kind=kOutput, calls=%fused_computation.6 | convolution fusion | flops 2155872256 | bytes 7350272 | tf_op jit(solution)/shard_map/dot_general | solution.py:74
  88.3 7.0 %all-to-all-done = bf16[32,72,128]{2,1,0:T(8,128)(2,1)S(1)} async-done(((bf16[32,72,128]{2,1,0:T(8,128)(2,1)}), bf16[32,72,128]{2,1,0:T(8,128)(2,1)S(1)}, u32[]{:S(2)}, u32[]{:S(2)}) %all-to-all-start) | async-done | bytes 589856 | tf_op jit(solution)/shard_map/all_to_all | solution.py:19
  97.0 2.5 fusion
  101.3 7.6 %all-to-all-start.1 = ((bf16[16,36,128]{2,1,0:T(8,128)(2,1)}), bf16[16,36,128]{2,1,0:T(8,128)(2,1)S(1)}, u32[]{:S(2)}, u32[]{:S(2)}) async-start(bf16[16,36,128]{2,1,0:T(8,128)(2,1)} %reshape.223), calls=%async_computation.1 | async-start | bytes 327680 | tf_op jit(solution)/shard_map/all_to_all | solution.py:19
  109.7 8.9 %all-to-all-done.1 = bf16[16,36,128]{2,1,0:T(8,128)(2,1)S(1)} async-done(((bf16[16,36,128]{2,1,0:T(8,128)(2,1)}), bf16[16,36,128]{2,1,0:T(8,128)(2,1)S(1)}, u32[]{:S(2)}, u32[]{:S(2)}) %all-to-all-start.1) | async-done | bytes 147488 | tf_op jit(solution)/shard_map/all_to_all | solution.py:19
  119.1 12.3 %all_to_all.40 = bf16[16,36,128]{2,1,0:T(8,128)(2,1)S(1)} all-to-all(bf16[16,36,128]{2,1,0:T(8,128)(2,1)S(1)} %broadcast_in_dim.59), channel_id=1, replica_groups=mesh['y'=8,'core'=2,'z'=8,'x'=4] {'y','core'}, dimensions={0} | all-to-all | bytes 294912 | tf_op jit(solution)/shard_map/all_to_all | solution.py:19
  132.3 2.1 convolution_convert_fusion.1
  137.5 22.9 %all_to_all.41 = bf16[32,72,128]{2,1,0:T(8,128)(2,1)S(1)} all-to-all(bf16[32,72,128]{2,1,0:T(8,128)(2,1)S(1)} %reshape.174), channel_id=1, replica_groups=mesh['y'=8,'core'=2,'z'=8,'x'=4] {'z','x'}, dimensions={0} | all-to-all | bytes 1179648 | tf_op jit(solution)/shard_map/all_to_all | solution.py:19
  162.8 4.8 %all-to-all-start.4 = ((bf16[32,72,128]{2,1,0:T(8,128)(2,1)}), bf16[32,72,128]{2,1,0:T(8,128)(2,1)}, u32[]{:S(2)}, u32[]{:S(2)}) async-start(bf16[32,72,128]{2,1,0:T(8,128)(2,1)} %broadcast_in_dim.61), calls=%async_computation.4 | async-start | bytes 1179648 | tf_op jit(solution)/shard_map/all_to_all | solution.py:19
  168.1 1.7 copy-done.2
  169.8 4.3 %exponential_convert_fusion = bf16[512,2048]{1,0:T(8,128)(2,1)S(1)} fusion(bf16[1024,512]{1,0:T(8,128)(2,1)S(1)} %bitcast.94, bf16[1024,2048]{1,0:T(8,128)(2,1)S(1)} %copy-done.2, f32[512]{0:T(512)S(1)} %multiply_reduce_fusion.1, f32[2048]{0:T(1024)S(1)} %multiply_reduce_fusion), kind=kOutput, calls=%fused_computation.5 | convolution fusion | flops 2155872256 | bytes 7350272 | tf_op jit(solution)/shard_map/dot_general | solution.py:74
  174.1 10.0 %all-to-all-done.4 = bf16[32,72,128]{2,1,0:T(8,128)(2,1)} async-done(((bf16[32,72,128]{2,1,0:T(8,128)(2,1)}), bf16[32,72,128]{2,1,0:T(8,128)(2,1)}, u32[]{:S(2)}, u32[]{:S(2)}) %all-to-all-start.4) | async-done | bytes 589856 | tf_op jit(solution)/shard_map/all_to_all | solution.py:19
  184.1 2.6 %reshape.176 = bf16[32,72,2,64]{3,2,1,0:T(2,128)(2,1)S(1)} reshape(bf16[32,72,128]{2,1,0:T(8,128)(2,1)} %all-to-all-done.4) | data formatting | bytes 1179648 | tf_op jit(solution)/shard_map/reshape | solution.py:38
  188.0 2.2 reshape.177
  192.9 6.8 %all-to-all-start.5 = ((bf16[16,36,128]{2,1,0:T(8,128)(2,1)}), bf16[16,36,128]{2,1,0:T(8,128)(2,1)S(1)}, u32[]{:S(2)}, u32[]{:S(2)}) async-start(bf16[16,36,128]{2,1,0:T(8,128)(2,1)} %reshape.224), calls=%async_computation.5 | async-start | bytes 327680 | tf_op jit(solution)/shard_map/all_to_all | solution.py:19
  200.4 9.2 %all-to-all-done.5 = bf16[16,36,128]{2,1,0:T(8,128)(2,1)S(1)} async-done(((bf16[16,36,128]{2,1,0:T(8,128)(2,1)}), bf16[16,36,128]{2,1,0:T(8,128)(2,1)S(1)}, u32[]{:S(2)}, u32[]{:S(2)}) %all-to-all-start.5) | async-done | bytes 147488 | tf_op jit(solution)/shard_map/all_to_all | solution.py:19
  210.1 12.0 %all_to_all.42 = bf16[16,36,128]{2,1,0:T(8,128)(2,1)S(1)} all-to-all(bf16[16,36,128]{2,1,0:T(8,128)(2,1)S(1)} %broadcast_in_dim.65), channel_id=1, replica_groups=mesh['y'=8,'core'=2,'z'=8,'x'=4] {'y','core'}, dimensions={0} | all-to-all | bytes 294912 | tf_op jit(solution)/shard_map/all_to_all | solution.py:19
  226.6 22.4 %all_to_all.43 = bf16[32,72,128]{2,1,0:T(8,128)(2,1)S(1)} all-to-all(bf16[32,72,128]{2,1,0:T(8,128)(2,1)S(1)} %reshape.184), channel_id=1, replica_groups=mesh['y'=8,'core'=2,'z'=8,'x'=4] {'z','x'}, dimensions={0} | all-to-all | bytes 1179648 | tf_op jit(solution)/shard_map/all_to_all | solution.py:19
  (94 shorter events, 31.1 us)
Async XLA Ops:
  0.0 109.0 %copy-start = (s32[1024]{0:T(1024)S(1)}, s32[1024]{0:T(1024)}, u32[]{:S(2)}) copy-start(s32[1024]{0:T(1024)} %param.7) | copy-start | bytes 12292
  25.0 55.3 %collective-permute-start = (bf16[8,64,512]{2,1,0:T(8,128)(2,1)S(1)}, bf16[8,64,512]{2,1,0:T(8,128)(2,1)S(1)}, u32[]{:S(2)}, u32[]{:S(2)}) collective-permute-start(bf16[8,64,512]{2,1,0:T(8,128)(2,1)S(1)} %bitcast.90), channel_id=1, source_target_pairs={{0,32},{32,0},{1,33},{33,1},{2,34},{34,2},{3,35},{35,3},{4,36},{36... | collective-permute-start | bytes 1572872 | tf_op jit(solution)/shard_map/ppermute | solution.py:70
  58.6 21.7 %collective-permute-start.1 = (bf16[8,64,512]{2,1,0:T(8,128)(2,1)S(1)}, bf16[8,64,512]{2,1,0:T(8,128)(2,1)}, u32[]{:S(2)}, u32[]{:S(2)}) collective-permute-start(bf16[8,64,512]{2,1,0:T(8,128)(2,1)S(1)} %bitcast.92), channel_id=1, source_target_pairs={{0,32},{32,0},{1,33},{33,1},{2,34},{34,2},{3,35},{35,3},{4,36},{36... | collective-permute-start | bytes 1572872 | tf_op jit(solution)/shard_map/ppermute | solution.py:70
  68.4 26.9 %all-to-all-start = ((bf16[32,72,128]{2,1,0:T(8,128)(2,1)}), bf16[32,72,128]{2,1,0:T(8,128)(2,1)S(1)}, u32[]{:S(2)}, u32[]{:S(2)}) async-start(bf16[32,72,128]{2,1,0:T(8,128)(2,1)} %broadcast_in_dim.56), calls=%async_computation | async-start | bytes 1179648 | tf_op jit(solution)/shard_map/all_to_all | solution.py:19
  80.3 2.3 copy-start.1
  101.3 17.3 %all-to-all-start.1 = ((bf16[16,36,128]{2,1,0:T(8,128)(2,1)}), bf16[16,36,128]{2,1,0:T(8,128)(2,1)S(1)}, u32[]{:S(2)}, u32[]{:S(2)}) async-start(bf16[16,36,128]{2,1,0:T(8,128)(2,1)} %reshape.223), calls=%async_computation.1 | async-start | bytes 327680 | tf_op jit(solution)/shard_map/all_to_all | solution.py:19
  162.8 21.3 %all-to-all-start.4 = ((bf16[32,72,128]{2,1,0:T(8,128)(2,1)}), bf16[32,72,128]{2,1,0:T(8,128)(2,1)}, u32[]{:S(2)}, u32[]{:S(2)}) async-start(bf16[32,72,128]{2,1,0:T(8,128)(2,1)} %broadcast_in_dim.61), calls=%async_computation.4 | async-start | bytes 1179648 | tf_op jit(solution)/shard_map/all_to_all | solution.py:19
  167.6 2.2 copy-start.2
  192.9 16.7 %all-to-all-start.5 = ((bf16[16,36,128]{2,1,0:T(8,128)(2,1)}), bf16[16,36,128]{2,1,0:T(8,128)(2,1)S(1)}, u32[]{:S(2)}, u32[]{:S(2)}) async-start(bf16[16,36,128]{2,1,0:T(8,128)(2,1)} %reshape.224), calls=%async_computation.5 | async-start | bytes 327680 | tf_op jit(solution)/shard_map/all_to_all | solution.py:19

commit v2 on v1

v2 whole, which is shorter than its diff:
```python
import functools

import jax
import jax.numpy as jnp
from jax import lax
from jax.experimental import pallas as pl
from jax.experimental.pallas import tpu as pltpu
from jax.sharding import Mesh, PartitionSpec as P

STEPS = 2


LOGIT_GAIN = 16.0
LENGTH_SCALE = 0.5
STEP_GAIN = 2048.0
EPS = 1e-06

LANES = 128
CENTRE = ("y", "core")
SAMPLE = ("z", "x")


def exchange(parts, axes):
    return lax.all_to_all(parts, axes, 0, 0, tiled=True)


def spread(array, axes):
    peers = lax.axis_size(axes)
    return exchange(jnp.broadcast_to(array[None], (peers, *array.shape)), axes)


def call(body, out, flops, *operands, scratch=()):
    vmem = pl.BlockSpec(memory_space=pltpu.VMEM)
    many = isinstance(out, (list, tuple))
    nbytes = sum(a.size * a.dtype.itemsize for a in operands)
    return pl.pallas_call(
        body,
        out_shape=out,
        in_specs=[vmem] * len(operands),
        out_specs=[vmem] * len(out) if many else vmem,
        scratch_shapes=list(scratch),
        cost_estimate=pl.CostEstimate(flops=flops, bytes_accessed=nbytes, transcendentals=0),
        compiler_params=pltpu.CompilerParams(vmem_limit_bytes=24 << 20),
    )(*operands)


def regroup(blocks, fold):
    width = LANES // fold
    lane_block = lax.broadcasted_iota(jnp.int32, blocks[0].shape, 1) // width
    out = []
    for q in range(fold):
        merged = None
        for k in range(fold):
            shift = width * (k - q) % LANES
            moved = pltpu.roll(blocks[k], shift, 1) if shift else blocks[k]
            merged = moved if merged is None else jnp.where(lane_block == k, moved, merged)
        out.append(merged)
    return out


def logits_body(coef_ref, kern_ref, out_ref, coef, logits):
    peers, height, _ = coef_ref.shape
    for pair in range(peers // 2):
        halves = regroup([coef_ref[2 * pair + i].astype(jnp.float32) for i in range(2)], 2)
        for h in range(2):
            coef[height * h : height * (h + 1), LANES * pair : LANES * (pair + 1)] = halves[h]
    logits[...] = lax.dot_general(
        coef[...].astype(jnp.bfloat16),
        kern_ref[...],
        (((1,), (1,)), ((), ())),
        preferred_element_type=jnp.float32,
    )
    receivers, rows, _ = out_ref.shape
    fold = coef.shape[0] // rows
    for group in range(receivers // fold):
        columns = slice(LANES * group, LANES * (group + 1))
        blocks = regroup([logits[rows * q : rows * (q + 1), columns] for q in range(fold)], fold)
        for k in range(fold):
            out_ref[fold * group + k] = blocks[k].astype(out_ref.dtype)


def partial_logits(coef_parts, kern, peers):
    classes = 2 * coef_parts.shape[1]
    batch, centres = kern.shape
    rows = classes * (batch // peers) // LANES
    return call(
        logits_body,
        jax.ShapeDtypeStruct((peers, rows, LANES), jnp.bfloat16),
        2 * classes * batch * centres,
        coef_parts,
        kern,
        scratch=[pltpu.VMEM((classes, centres), jnp.float32), pltpu.VMEM((classes, batch), jnp.float32)],
    )


def fold_all(row, fold, op):
    while fold > 1:
        row = op(row, pltpu.roll(row, LANES // fold, 1))
        fold //= 2
    return row


def residual_body(gain, fold, arrived_ref, labs_ref, out_ref):
    peers, rows, _ = arrived_ref.shape
    total = arrived_ref[0].astype(jnp.float32)
    for peer in range(1, peers):
        total = total + arrived_ref[peer].astype(jnp.float32)
    logits = total * gain
    top = fold_all(jnp.max(logits, axis=0, keepdims=True), fold, jnp.maximum)
    expo = jnp.exp(logits - top)
    mass = fold_all(jnp.sum(expo, axis=0, keepdims=True), fold, jnp.add)
    probs = expo / mass
    block = lax.broadcasted_iota(jnp.int32, logits.shape, 1) // (LANES // fold)
    class_ids = block * rows + lax.broadcasted_iota(jnp.int32, logits.shape, 0)
    onehot = (class_ids == labs_ref[...]).astype(jnp.float32)
    resid = (probs - onehot).astype(out_ref.dtype)
    for peer in range(peers):
        out_ref[peer] = resid


def residual(arrived, labs, gain, fold):
    return call(
        functools.partial(residual_body, gain, fold),
        jax.ShapeDtypeStruct(arrived.shape, jnp.bfloat16),
        8 * arrived.size,
        arrived,
        jnp.tile(labs, fold)[None],
    )


def grad_body(resid_ref, kern_ref, out_ref, resid):
    peers, rows, _ = resid_ref.shape
    classes = resid.shape[0]
    fold = classes // rows
    for group in range(peers // fold):
        blocks = regroup([resid_ref[fold * group + k].astype(jnp.float32) for k in range(fold)], fold)
        for q in range(fold):
            resid[rows * q : rows * (q + 1), LANES * group : LANES * (group + 1)] = blocks[q]
    held = resid[...].astype(jnp.bfloat16)
    receivers, height, _ = out_ref.shape
    step = 4 * LANES
    for start in range(0, kern_ref.shape[1], step):
        grad = jnp.dot(held, kern_ref[:, start : start + step], preferred_element_type=jnp.float32)
        for at in range(0, step, LANES):
            halves = [grad[height * h : height * (h + 1), at : at + LANES] for h in range(2)]
            first = 2 * (start + at) // LANES
            for i, block in enumerate(regroup(halves, 2)):
                out_ref[first + i] = block.astype(out_ref.dtype)


def partial_grad(resid_parts, kern, peers):
    batch, centres = kern.shape
    classes = resid_parts.size // batch
    height = classes * (centres // peers) // LANES
    return call(
        grad_body,
        jax.ShapeDtypeStruct((peers, height, LANES), jnp.bfloat16),
        2 * classes * batch * centres,
        resid_parts,
        kern,
        scratch=[pltpu.VMEM((classes, batch), jnp.float32)],
    )


def update_body(rate, arrived_ref, current_ref, new_ref, half_ref):
    peers = arrived_ref.shape[0]
    total = arrived_ref[0].astype(jnp.float32)
    for peer in range(1, peers):
        total = total + arrived_ref[peer].astype(jnp.float32)
    new = current_ref[...] - rate * total
    new_ref[...] = new
    half = new.astype(half_ref.dtype)
    for peer in range(peers):
        half_ref[peer] = half


def updated(arrived, current, rate):
    return call(
        functools.partial(update_body, rate),
        [
            jax.ShapeDtypeStruct(current.shape, jnp.float32),
            jax.ShapeDtypeStruct(arrived.shape, jnp.bfloat16),
        ],
        2 * arrived.size,
        arrived,
        current,
    )


def last_body(rate, arrived_ref, current_ref, new_ref):
    total = arrived_ref[0].astype(jnp.float32)
    for peer in range(1, arrived_ref.shape[0]):
        total = total + arrived_ref[peer].astype(jnp.float32)
    new_ref[...] = current_ref[...] - rate * total


def last_updated(arrived, current, rate):
    return call(
        functools.partial(last_body, rate),
        jax.ShapeDtypeStruct(current.shape, jnp.float32),
        2 * arrived.size,
        arrived,
        current,
    )


def laplace(cross, sample_sq, centre_sq, width):
    mean_sq = (sample_sq[:, None] + centre_sq[None, :] - 2.0 * cross) / width
    return jnp.exp(-jnp.sqrt(mean_sq + EPS) / LENGTH_SCALE).astype(jnp.bfloat16)


def on_device(centres, pool, labels, picks, coefs):
    width = centres.shape[0]
    cen_dev = centres.shape[1]
    pool_dev = pool.shape[1]
    batch_dev = picks.shape[1]
    classes, cen_own = coefs.shape
    n_centre, n_sample = lax.axis_size(CENTRE), lax.axis_size(SAMPLE)
    total_centres = cen_dev * n_centre
    total_batch = batch_dev * n_sample
    rate = STEP_GAIN * LOGIT_GAIN / total_batch
    own = batch_dev // n_centre
    fold = LANES // own
    me = lax.axis_index(CENTRE)
    core = lax.axis_index("core")
    local_picks = picks - lax.axis_index(SAMPLE) * pool_dev
    centre_sq = jnp.sum(jnp.square(centres.astype(jnp.float32)), axis=0)

    def picked(step):
        return jnp.take(pool, local_picks[step], axis=1, mode="clip")

    def own_labels(step):
        chosen = lax.dynamic_slice(local_picks[step], (me * own,), (own,))
        return jnp.take(labels, chosen, mode="clip")

    def kernel_matrix(gathered):
        cross = lax.dot_general(
            gathered, centres, (((0,), (0,)), ((), ())), preferred_element_type=jnp.float32
        )
        sample_sq = jnp.sum(jnp.square(gathered.astype(jnp.float32)), axis=0)
        return laplace(cross, sample_sq, centre_sq, width)

    mine = spread(picked(0), "y")
    other = lax.ppermute(mine, "core", [(0, 1), (1, 0)])
    first = jnp.where(core == 0, mine, other)
    second = jnp.where(core == 0, other, mine)
    later = lax.all_gather(picked(1), CENTRE, axis=0, tiled=True)
    kerns = [
        kernel_matrix(jnp.stack([first, second], axis=1).reshape(width, batch_dev)),
        kernel_matrix(later),
    ]
    labs = [own_labels(step) for step in range(STEPS)]

    current = jnp.concatenate([coefs[: classes // 2], coefs[classes // 2 :]], axis=1)
    half = jnp.broadcast_to(current.astype(jnp.bfloat16), (n_sample, *current.shape))
    for step in range(STEPS):
        coef_parts = exchange(half, SAMPLE)
        arrived = exchange(partial_logits(coef_parts, kerns[step], n_centre), CENTRE)
        resid = residual(arrived, labs[step], LOGIT_GAIN / total_centres, fold)
        arrived = exchange(partial_grad(exchange(resid, CENTRE), kerns[step], n_sample), SAMPLE)
        if step < STEPS - 1:
            current, half = updated(arrived, current, rate)
        else:
            current = last_updated(arrived, current, rate)
    return jnp.concatenate([current[:, :cen_own], current[:, cen_own:]], axis=0)


def solution(mesh):
    sizes = (mesh.shape["centre"] // 2, 2, 8, mesh.shape["sample"] // 8)
    fine = Mesh(mesh.devices.reshape(sizes), (*CENTRE, *SAMPLE))
    placed = (
        P(None, CENTRE),
        P(CENTRE, SAMPLE),
        P(SAMPLE),
        P(None, SAMPLE),
        P(None, (*CENTRE, *SAMPLE)),
    )
    return jax.shard_map(
        on_device,
        mesh=fine,
        in_specs=placed,
        out_specs=P(None, (*CENTRE, *SAMPLE)),
        check_vma=False,
    )
```

time: 251 us -> 210 us (0.84)
  blocking collectives: 111 us -> 70.9 us
  local copies, waits for them, and re-layouts: 30.3 us -> 9.91 us
  waiting for transfers between devices: 35.1 us -> 49 us
  between operations: 0.47 us -> 13.6 us
  Pallas kernels: 0 us -> 6.53 us
  starting transfers between devices: 48.5 us -> 42.6 us
  matrix products: 15.8 us -> 11 us
  other arithmetic: 9.02 us -> 6 us
    all_gather x2 -> x0, blocking collectives: 41.2 us -> none  [on_device(): mine = lax.all_gather(feats, 'y', axis=0)]
    reshape x22 -> x0, local copies, waits for them, and re-layouts: 15.2 us -> none  [the longest x4 4.11 us: unpack(): jnp.transpose(parts, (2, 1, 0, 3)).reshape(fold * height, peers * width)]
    ppermute x2 -> x1, starting transfers between devices: 20.4 us -> 5.59 us  [on_device(): other = lax.ppermute(mine, 'core', [(0, 1), (1, 0)])]
    all_to_all x4 -> x5, waiting for transfers between devices: 35.1 us -> 48.9 us  [exchange(): return lax.all_to_all(parts, axes, 0, 0, tiled=True)]
    all_to_all x4 -> x5, starting transfers between devices: 28.1 us -> 37 us  [exchange(): return lax.all_to_all(parts, axes, 0, 0, tiled=True)]
    pallas_call x0 -> x8, Pallas kernels: none -> 6.53 us  [call(): pl.pallas_call(body, out_shape=out, in_specs=[vmem] * len(operands), out_...]
    dot_general x6 -> x2, matrix products: 15.8 us -> 11 us  [kernel_matrix(): lax.dot_general(gathered, centres, (((0,), (0,)), ((), ())), preferred_el...]
    transpose x6 -> x0, local copies, waits for them, and re-layouts: 4.21 us -> none  [the longest x2 2.43 us: pack(): jnp.transpose(parts, (2, 1, 0, 3)).reshape(peers, rows // fold, lanes)]
  transfers between devices with their start and end apart: 6 -> 7, of which waited for: 4 -> 5; matrix products, arithmetic and copies ran while one was open for 8% -> 11% of each run, Pallas kernels for 0% -> 2%
where the time goes in v2:
time: 210 us
  blocking collectives  70.9 us (34%)
  waiting for transfers between devices  49 us (23%)
  starting transfers between devices  42.6 us (20%)
  between operations  13.6 us (6%)
  matrix products  11 us (5%)
  local copies, waits for them, and re-layouts  9.91 us (5%)
  Pallas kernels  6.53 us (3%)
  other arithmetic  6 us (3%)
    all_to_all x4, blocking collectives, exchange(): return lax.all_to_all(parts, axes, 0, 0, tiled=True)  70.9 us
    all_to_all x5, waiting for transfers between devices, exchange(): return lax.all_to_all(parts, axes, 0, 0, tiled=True)  48.9 us
    all_to_all x5, starting transfers between devices, exchange(): return lax.all_to_all(parts, axes, 0, 0, tiled=True)  37 us
    dot_general x2, matrix products, kernel_matrix(): lax.dot_general(gathered, centres, (((0,), (0,)), ((), ())), preferred_el...  11 us
    pallas_call x8, Pallas kernels, call(): pl.pallas_call(body, out_shape=out, in_specs=[vmem] * len(operands), out_...  6.53 us
    ppermute x1, starting transfers between devices, on_device(): other = lax.ppermute(mine, 'core', [(0, 1), (1, 0)])  5.59 us
  transfers between devices with their start and end apart: 7, of which 5 were waited for; matrix products, arithmetic and copies ran while one was open for 11% of the time, Pallas kernels for 2%

profile of v2, /device:TPU:1, one launch (start us, length us, event | category | flops | bytes accessed | tf_op | source)
XLA Modules:
  0.0 209.6 jit_solution(4093153343212152221)
XLA Ops:
  7.3 1.1 copy.21
  8.3 1.3 gather_fusion
  10.6 7.7 %all-to-all-start.1 = ((bf16[8,64,512]{2,1,0:T(8,128)(2,1)}), bf16[8,64,512]{2,1,0:T(8,128)(2,1)S(1)}, u32[]{:S(2)}, u32[]{:S(2)}) async-start(bf16[8,64,512]{2,1,0:T(8,128)(2,1)} %broadcast_in_dim.29), calls=%async_computation.1 | async-start | bytes 1048576 | tf_op jit(solution)/shard_map/all_to_all | solution.py:24
  19.4 13.6 %all-to-all-done.1 = bf16[8,64,512]{2,1,0:T(8,128)(2,1)S(1)} async-done(((bf16[8,64,512]{2,1,0:T(8,128)(2,1)}), bf16[8,64,512]{2,1,0:T(8,128)(2,1)S(1)}, u32[]{:S(2)}, u32[]{:S(2)}) %all-to-all-start.1) | async-done | bytes 524320 | tf_op jit(solution)/shard_map/all_to_all | solution.py:24
  33.0 5.6 %collective-permute-start = (bf16[8,64,512]{2,1,0:T(8,128)(2,1)S(1)}, bf16[8,64,512]{2,1,0:T(8,128)(2,1)S(1)}, u32[]{:S(2)}, u32[]{:S(2)}) collective-permute-start(bf16[8,64,512]{2,1,0:T(8,128)(2,1)S(1)} %all-to-all-done.1), channel_id=1, source_target_pairs={{0,32},{32,0},{1,33},{33,1},{2,34},{34,2},{3,35},{35,3},{4,36},{36... | collective-permute-start | bytes 1572872 | tf_op jit(solution)/shard_map/ppermute | solution.py:244
  39.7 12.9 %all-to-all-start = ((bf16[32,72,128]{2,1,0:T(8,128)(2,1)}), bf16[32,72,128]{2,1,0:T(8,128)(2,1)S(1)}, u32[]{:S(2)}, u32[]{:S(2)}) async-start(bf16[32,72,128]{2,1,0:T(8,128)(2,1)} %broadcast_in_dim.27), calls=%async_computation | async-start | bytes 1179648 | tf_op jit(solution)/shard_map/all_to_all | solution.py:24
  52.6 1.3 gather_fusion.2
  54.7 3.2 %multiply_reduce_fusion = f32[2048]{0:T(1024)S(1)} fusion(bf16[1024,2048]{1,0:T(8,128)(2,1)} %param.5), kind=kLoop, calls=%fused_computation.4 | loop fusion | flops 6289408 | bytes 4202496 | tf_op jit(solution)/shard_map/reduce_sum | solution.py:227
  58.4 4.3 %exponential_convert_fusion.1.kern_ref = bf16[512,2048]{1,0:T(8,128)(2,1)S(1)} fusion(bf16[1024,512]{1,0:T(8,128)(2,1)S(1)} %bitcast.19, bf16[1024,2048]{1,0:T(8,128)(2,1)S(1)} %copy-done.1, f32[2048]{0:T(1024)S(1)} %multiply_reduce_fusion, f32[512]{0:T(512)S(1)} %multiply_reduce_fusion.2), kind=kOutput, calls=%fused_computation.6 | convolution fusion | flops 2155872256 | bytes 7350272 | tf_op jit(solution)/shard_map/dot_general | solution.py:237
  62.7 7.9 %all-to-all-done.coef_ref = bf16[32,72,128]{2,1,0:T(8,128)(2,1)S(1)} async-done(((bf16[32,72,128]{2,1,0:T(8,128)(2,1)}), bf16[32,72,128]{2,1,0:T(8,128)(2,1)S(1)}, u32[]{:S(2)}, u32[]{:S(2)}) %all-to-all-start) | async-done | bytes 589856 | tf_op jit(solution)/shard_map/all_to_all | solution.py:24
  70.7 1.7 shard_map.55
  72.3 5.1 %all-to-all-start.2 = ((bf16[16,36,128]{2,1,0:T(8,128)(2,1)}), bf16[16,36,128]{2,1,0:T(8,128)(2,1)S(1)}, u32[]{:S(2)}, u32[]{:S(2)}) async-start(bf16[16,36,128]{2,1,0:T(8,128)(2,1)} %shard_map.55), calls=%async_computation.2 | async-start | bytes 327680 | tf_op jit(solution)/shard_map/all_to_all | solution.py:24
  78.3 9.8 %all-to-all-done.2.arrived_ref = bf16[16,36,128]{2,1,0:T(8,128)(2,1)S(1)} async-done(((bf16[16,36,128]{2,1,0:T(8,128)(2,1)}), bf16[16,36,128]{2,1,0:T(8,128)(2,1)S(1)}, u32[]{:S(2)}, u32[]{:S(2)}) %all-to-all-start.2) | async-done | bytes 147488 | tf_op jit(solution)/shard_map/all_to_all | solution.py:24
  88.4 12.2 %all_to_all.45.resid_ref = bf16[16,36,128]{2,1,0:T(8,128)(2,1)S(1)} all-to-all(bf16[16,36,128]{2,1,0:T(8,128)(2,1)S(1)} %shard_map.56), channel_id=1, replica_groups=mesh['y'=8,'core'=2,'z'=8,'x'=4] {'y','core'}, dimensions={0} | all-to-all | bytes 294912 | tf_op jit(solution)/shard_map/all_to_all | solution.py:24
  101.4 23.8 %all_to_all.46.arrived_ref = bf16[32,72,128]{2,1,0:T(8,128)(2,1)S(1)} all-to-all(bf16[32,72,128]{2,1,0:T(8,128)(2,1)S(1)} %shard_map.57), channel_id=1, replica_groups=mesh['y'=8,'core'=2,'z'=8,'x'=4] {'z','x'}, dimensions={0} | all-to-all | bytes 1179648 | tf_op jit(solution)/shard_map/all_to_all | solution.py:24
  126.1 5.1 %all-to-all-start.5 = ((bf16[32,72,128]{2,1,0:T(8,128)(2,1)}), bf16[32,72,128]{2,1,0:T(8,128)(2,1)S(1)}, u32[]{:S(2)}, u32[]{:S(2)}) async-start(bf16[32,72,128]{2,1,0:T(8,128)(2,1)} %get-tuple-element.7), calls=%async_computation.5 | async-start | bytes 1179648 | tf_op jit(solution)/shard_map/all_to_all | solution.py:24
  131.3 1.5 multiply_reduce_fusion.1
  132.8 6.7 %exponential_convert_fusion.kern_ref = bf16[512,2048]{1,0:T(8,128)(2,1)S(1)} fusion(bf16[1024,512]{1,0:T(8,128)(2,1)} %all-gather.3.cloned.1.call-done, bf16[1024,2048]{1,0:T(8,128)(2,1)} %param.5, f32[512]{0:T(512)S(1)} %multiply_reduce_fusion.1, f32[2048]{0:T(1024)S(1)} %multiply_reduce_fusion), kind=kOutput, calls=%fused_computation.5 | convolution fusion | flops 2155872256 | bytes 7350272 | tf_op jit(solution)/shard_map/dot_general | solution.py:237
  139.5 8.5 %all-to-all-done.5.coef_ref = bf16[32,72,128]{2,1,0:T(8,128)(2,1)S(1)} async-done(((bf16[32,72,128]{2,1,0:T(8,128)(2,1)}), bf16[32,72,128]{2,1,0:T(8,128)(2,1)S(1)}, u32[]{:S(2)}, u32[]{:S(2)}) %all-to-all-start.5) | async-done | bytes 589856 | tf_op jit(solution)/shard_map/all_to_all | solution.py:24
  148.0 1.7 shard_map.59
  149.7 6.3 %all-to-all-start.6 = ((bf16[16,36,128]{2,1,0:T(8,128)(2,1)}), bf16[16,36,128]{2,1,0:T(8,128)(2,1)S(1)}, u32[]{:S(2)}, u32[]{:S(2)}) async-start(bf16[16,36,128]{2,1,0:T(8,128)(2,1)} %shard_map.59), calls=%async_computation.6 | async-start | bytes 327680 | tf_op jit(solution)/shard_map/all_to_all | solution.py:24
  156.7 9.1 %all-to-all-done.6.arrived_ref = bf16[16,36,128]{2,1,0:T(8,128)(2,1)S(1)} async-done(((bf16[16,36,128]{2,1,0:T(8,128)(2,1)}), bf16[16,36,128]{2,1,0:T(8,128)(2,1)S(1)}, u32[]{:S(2)}, u32[]{:S(2)}) %all-to-all-start.6) | async-done | bytes 147488 | tf_op jit(solution)/shard_map/all_to_all | solution.py:24
  166.2 12.1 %all_to_all.47.resid_ref = bf16[16,36,128]{2,1,0:T(8,128)(2,1)S(1)} all-to-all(bf16[16,36,128]{2,1,0:T(8,128)(2,1)S(1)} %shard_map.60), channel_id=1, replica_groups=mesh['y'=8,'core'=2,'z'=8,'x'=4] {'y','core'}, dimensions={0} | all-to-all | bytes 294912 | tf_op jit(solution)/shard_map/all_to_all | solution.py:24
  179.0 22.8 %all_to_all.48.arrived_ref = bf16[32,72,128]{2,1,0:T(8,128)(2,1)S(1)} all-to-all(bf16[32,72,128]{2,1,0:T(8,128)(2,1)S(1)} %shard_map.61), channel_id=1, replica_groups=mesh['y'=8,'core'=2,'z'=8,'x'=4] {'z','x'}, dimensions={0} | all-to-all | bytes 1179648 | tf_op jit(solution)/shard_map/all_to_all | solution.py:24
  (41 shorter events, 10.7 us)
Async XLA Ops:
  6.5 71.0 %copy-start = (s32[1024]{0:T(1024)S(1)}, s32[1024]{0:T(1024)}, u32[]{:S(2)}) copy-start(s32[1024]{0:T(1024)} %param.7) | copy-start | bytes 12292
  10.6 22.4 %all-to-all-start.1 = ((bf16[8,64,512]{2,1,0:T(8,128)(2,1)}), bf16[8,64,512]{2,1,0:T(8,128)(2,1)S(1)}, u32[]{:S(2)}, u32[]{:S(2)}) async-start(bf16[8,64,512]{2,1,0:T(8,128)(2,1)} %broadcast_in_dim.29), calls=%async_computation.1 | async-start | bytes 1048576 | tf_op jit(solution)/shard_map/all_to_all | solution.py:24
  33.0 24.9 %collective-permute-start = (bf16[8,64,512]{2,1,0:T(8,128)(2,1)S(1)}, bf16[8,64,512]{2,1,0:T(8,128)(2,1)S(1)}, u32[]{:S(2)}, u32[]{:S(2)}) collective-permute-start(bf16[8,64,512]{2,1,0:T(8,128)(2,1)S(1)} %all-to-all-done.1), channel_id=1, source_target_pairs={{0,32},{32,0},{1,33},{33,1},{2,34},{34,2},{3,35},{35,3},{4,36},{36... | collective-permute-start | bytes 1572872 | tf_op jit(solution)/shard_map/ppermute | solution.py:244
  39.7 31.0 %all-to-all-start = ((bf16[32,72,128]{2,1,0:T(8,128)(2,1)}), bf16[32,72,128]{2,1,0:T(8,128)(2,1)S(1)}, u32[]{:S(2)}, u32[]{:S(2)}) async-start(bf16[32,72,128]{2,1,0:T(8,128)(2,1)} %broadcast_in_dim.27), calls=%async_computation | async-start | bytes 1179648 | tf_op jit(solution)/shard_map/all_to_all | solution.py:24
  52.6 78.7 %all-gather.3.cloned.1.call-start = ((), (), s32[]{:S(2)}) async-start(), calls=%async_computation.9 | async-start | bytes 1114112 | tf_op jit(solution)/shard_map/all_gather | solution.py:247
  54.7 3.7 %copy-start.1 = (bf16[1024,2048]{1,0:T(8,128)(2,1)S(1)}, bf16[1024,2048]{1,0:T(8,128)(2,1)}, u32[]{:S(2)}) copy-start(bf16[1024,2048]{1,0:T(8,128)(2,1)} %param.5) | copy-start | bytes 12582916
  72.3 15.7 %all-to-all-start.2 = ((bf16[16,36,128]{2,1,0:T(8,128)(2,1)}), bf16[16,36,128]{2,1,0:T(8,128)(2,1)S(1)}, u32[]{:S(2)}, u32[]{:S(2)}) async-start(bf16[16,36,128]{2,1,0:T(8,128)(2,1)} %shard_map.55), calls=%async_computation.2 | async-start | bytes 327680 | tf_op jit(solution)/shard_map/all_to_all | solution.py:24
  126.1 21.9 %all-to-all-start.5 = ((bf16[32,72,128]{2,1,0:T(8,128)(2,1)}), bf16[32,72,128]{2,1,0:T(8,128)(2,1)S(1)}, u32[]{:S(2)}, u32[]{:S(2)}) async-start(bf16[32,72,128]{2,1,0:T(8,128)(2,1)} %get-tuple-element.7), calls=%async_computation.5 | async-start | bytes 1179648 | tf_op jit(solution)/shard_map/all_to_all | solution.py:24
  149.7 16.2 %all-to-all-start.6 = ((bf16[16,36,128]{2,1,0:T(8,128)(2,1)}), bf16[16,36,128]{2,1,0:T(8,128)(2,1)S(1)}, u32[]{:S(2)}, u32[]{:S(2)}) async-start(bf16[16,36,128]{2,1,0:T(8,128)(2,1)} %shard_map.59), calls=%async_computation.6 | async-start | bytes 327680 | tf_op jit(solution)/shard_map/all_to_all | solution.py:24
Sparse Core Ops, SparseCore 0:
  55.5 37.2 all-gather.2

commit v3 on v2

--- a/solution.py
+++ b/solution.py
@@ -59,9 +59,10 @@
 
 
 def logits_body(coef_ref, kern_ref, out_ref, coef, logits):
-    peers, height, _ = coef_ref.shape
-    for pair in range(peers // 2):
-        halves = regroup([coef_ref[2 * pair + i].astype(jnp.float32) for i in range(2)], 2)
+    over_x, over_z, height, _ = coef_ref.shape
+    for pair in range(over_x * over_z // 2):
+        at = [divmod(2 * pair + i, over_x) for i in range(2)]
+        halves = regroup([coef_ref[x, z].astype(jnp.float32) for z, x in at], 2)
         for h in range(2):
             coef[height * h : height * (h + 1), LANES * pair : LANES * (pair + 1)] = halves[h]
     logits[...] = lax.dot_general(
@@ -80,7 +81,7 @@
 
 
 def partial_logits(coef_parts, kern, peers):
-    classes = 2 * coef_parts.shape[1]
+    classes = 2 * coef_parts.shape[2]
     batch, centres = kern.shape
     rows = classes * (batch // peers) // LANES
     return call(
@@ -137,7 +138,7 @@
         for q in range(fold):
             resid[rows * q : rows * (q + 1), LANES * group : LANES * (group + 1)] = blocks[q]
     held = resid[...].astype(jnp.bfloat16)
-    receivers, height, _ = out_ref.shape
+    over_x, _, height, _ = out_ref.shape
     step = 4 * LANES
     for start in range(0, kern_ref.shape[1], step):
         grad = jnp.dot(held, kern_ref[:, start : start + step], preferred_element_type=jnp.float32)
@@ -145,21 +146,77 @@
             halves = [grad[height * h : height * (h + 1), at : at + LANES] for h in range(2)]
             first = 2 * (start + at) // LANES
             for i, block in enumerate(regroup(halves, 2)):
-                out_ref[first + i] = block.astype(out_ref.dtype)
-
-
-def partial_grad(resid_parts, kern, peers):
+                z, x = divmod(first + i, over_x)
+                out_ref[x, z] = block.astype(out_ref.dtype)
+
+
+def partial_grad(resid_parts, kern, over_x, over_z):
     batch, centres = kern.shape
     classes = resid_parts.size // batch
-    height = classes * (centres // peers) // LANES
+    height = classes * (centres // (over_x * over_z)) // LANES
     return call(
         grad_body,
-        jax.ShapeDtypeStruct((peers, height, LANES), jnp.bfloat16),
+        jax.ShapeDtypeStruct((over_x, over_z, height, LANES), jnp.bfloat16),
         2 * classes * batch * centres,
         resid_parts,
         kern,
         scratch=[pltpu.VMEM((classes, batch), jnp.float32)],
     )
+
+
+def merged_body(arrived_ref, out_ref):
+    for z in range(arrived_ref.shape[1]):
+        total = arrived_ref[0, z].astype(jnp.float32)
+        for peer in range(1, arrived_ref.shape[0]):
+            total = total + arrived_ref[peer, z].astype(jnp.float32)
+        out_ref[z] = total.astype(out_ref.dtype)
+
+
+def merged(arrived):
+    out = jax.ShapeDtypeStruct(arrived.shape[1:], jnp.bfloat16)
+    return call(merged_body, out, arrived.size, arrived)
+
+
+def assemble_body(offsets, mine_ref, other_ref, out_ref, square_ref):
+    y, core = lax.axis_index("y"), lax.axis_index("core")
+    total = None
+    for i in range(mine_ref.shape[0]):
+        at = i if offsets is None else lax.bitwise_xor(y, offsets[i])
+        for which, ref in ((core, mine_ref), (1 - core, other_ref)):
+            block = ref[i]
+            out_ref[at, which] = block
+            wide = block.astype(jnp.float32)
+            square = jnp.sum(wide * wide, axis=0, keepdims=True)
+            total = square if total is None else total + square
+    square_ref[...] = total
+
+
+def assembled(mine, other, offsets=None):
+    blocks, rows, batch = mine.shape
+    feats, squares = call(
+        functools.partial(assemble_body, offsets),
+        [
+            jax.ShapeDtypeStruct((blocks, 2, rows, batch), mine.dtype),
+            jax.ShapeDtypeStruct((1, batch), jnp.float32),
+        ],
+        4 * mine.size,
+        mine,
+        other,
+    )
+    return feats.reshape(blocks * 2 * rows, batch), squares[0]
+
+
+def gathered_by_swaps(block):
+    held, offsets = block[None], [0]
+    peers = lax.axis_size("y")
+    hop = peers // 2
+    while hop:
+        moved = lax.ppermute(held, "y", [(i, i ^ hop) for i in range(peers)])
+        held = jnp.concatenate([held, moved])
+        offsets = offsets + [o ^ hop for o in offsets]
+        hop //= 2
+    other = lax.ppermute(held, "core", [(0, 1), (1, 0)])
+    return assembled(held, other, offsets)
 
 
 def update_body(rate, arrived_ref, current_ref, new_ref, half_ref):
@@ -222,7 +279,7 @@
     own = batch_dev // n_centre
     fold = LANES // own
     me = lax.axis_index(CENTRE)
-    core = lax.axis_index("core")
+    over_z, over_x = lax.axis_size("z"), lax.axis_size("x")
     local_picks = picks - lax.axis_index(SAMPLE) * pool_dev
     centre_sq = jnp.sum(jnp.square(centres.astype(jnp.float32)), axis=0)
 
@@ -233,31 +290,28 @@
         chosen = lax.dynamic_slice(local_picks[step], (me * own,), (own,))
         return jnp.take(labels, chosen, mode="clip")
 
-    def kernel_matrix(gathered):
+    def kernel_matrix(gathered, sample_sq):
         cross = lax.dot_general(
             gathered, centres, (((0,), (0,)), ((), ())), preferred_element_type=jnp.float32
         )
-        sample_sq = jnp.sum(jnp.square(gathered.astype(jnp.float32)), axis=0)
         return laplace(cross, sample_sq, centre_sq, width)
 
     mine = spread(picked(0), "y")
     other = lax.ppermute(mine, "core", [(0, 1), (1, 0)])
-    first = jnp.where(core == 0, mine, other)
-    second = jnp.where(core == 0, other, mine)
-    later = lax.all_gather(picked(1), CENTRE, axis=0, tiled=True)
     kerns = [
-        kernel_matrix(jnp.stack([first, second], axis=1).reshape(width, batch_dev)),
-        kernel_matrix(later),
+        kernel_matrix(*assembled(mine, other)),
+        kernel_matrix(*gathered_by_swaps(picked(1))),
     ]
     labs = [own_labels(step) for step in range(STEPS)]
 
     current = jnp.concatenate([coefs[: classes // 2], coefs[classes // 2 :]], axis=1)
-    half = jnp.broadcast_to(current.astype(jnp.bfloat16), (n_sample, *current.shape))
+    half = jnp.broadcast_to(current.astype(jnp.bfloat16), (over_z, *current.shape))
     for step in range(STEPS):
-        coef_parts = exchange(half, SAMPLE)
+        coef_parts = spread(exchange(half, "z"), "x").reshape(over_x, over_z, *current.shape)
         arrived = exchange(partial_logits(coef_parts, kerns[step], n_centre), CENTRE)
         resid = residual(arrived, labs[step], LOGIT_GAIN / total_centres, fold)
-        arrived = exchange(partial_grad(exchange(resid, CENTRE), kerns[step], n_sample), SAMPLE)
+        grads = partial_grad(exchange(resid, CENTRE), kerns[step], over_x, over_z)
+        arrived = exchange(merged(exchange(grads, "x")), "z")
         if step < STEPS - 1:
             current, half = updated(arrived, current, rate)
         else:

time: 210 us -> 210 us (level)
  starting transfers between devices: 42.6 us -> 64.5 us
  between operations: 13.6 us -> 0.26 us
  waiting for transfers between devices: 49 us -> 38.4 us
  matrix products: 11 us -> 13.2 us
  blocking collectives: 70.9 us -> 68.8 us
    all_to_all x5 -> x8, waiting for transfers between devices: 48.9 us -> 30.4 us  [exchange(): return lax.all_to_all(parts, axes, 0, 0, tiled=True)]
    ppermute x0 -> x4, starting transfers between devices: none -> 15.5 us  [the longest x3 13.4 us: gathered_by_swaps(): moved = lax.ppermute(held, 'y', [(i, i ^ hop) for i in range(peers)])]
    ppermute x0 -> x4, waiting for transfers between devices: none -> 8.09 us  [the longest x3 8.08 us: gathered_by_swaps(): moved = lax.ppermute(held, 'y', [(i, i ^ hop) for i in range(peers)])]
    all_to_all x5 -> x8, starting transfers between devices: 37 us -> 43.5 us  [exchange(): return lax.all_to_all(parts, axes, 0, 0, tiled=True)]
    all_to_all x4 -> x5, blocking collectives: 70.9 us -> 68.8 us  [exchange(): return lax.all_to_all(parts, axes, 0, 0, tiled=True)]
    dot_general x2, matrix products: 11 us -> 13.2 us  [kernel_matrix(): lax.dot_general(gathered, centres, (((0,), (0,)), ((), ())), preferred_el...]
    pallas_call x8 -> x12, Pallas kernels: 6.53 us -> 8.24 us  [call(): pl.pallas_call(body, out_shape=out, in_specs=[vmem] * len(operands), out_...]
  transfers between devices with their start and end apart: 7 -> 13, of which waited for: 5 -> 8; matrix products, arithmetic and copies ran while one was open for 11% -> 11% of each run, Pallas kernels for 2% -> 2%
where the time goes in v3:
time: 210 us; the launch traced here: 209 us
  blocking collectives  68.8 us (33%)
  starting transfers between devices  64.5 us (31%)
  waiting for transfers between devices  38.4 us (18%)
  matrix products  13.2 us (6%)
  local copies, waits for them, and re-layouts  11.1 us (5%)
  Pallas kernels  8.24 us (4%)
  other arithmetic  3.98 us (2%)
    all_to_all x5, blocking collectives, exchange(): return lax.all_to_all(parts, axes, 0, 0, tiled=True)  68.8 us
    all_to_all x8, starting transfers between devices, exchange(): return lax.all_to_all(parts, axes, 0, 0, tiled=True)  43.5 us
    all_to_all x8, waiting for transfers between devices, exchange(): return lax.all_to_all(parts, axes, 0, 0, tiled=True)  30.4 us
    ppermute x3, starting transfers between devices, gathered_by_swaps(): moved = lax.ppermute(held, 'y', [(i, i ^ hop) for i in range(peers)])  13.4 us
    dot_general x2, matrix products, kernel_matrix(): lax.dot_general(gathered, centres, (((0,), (0,)), ((), ())), preferred_el...  13.2 us
    pallas_call x12, Pallas kernels, call(): pl.pallas_call(body, out_shape=out, in_specs=[vmem] * len(operands), out_...  8.24 us
    ppermute x3, waiting for transfers between devices, gathered_by_swaps(): moved = lax.ppermute(held, 'y', [(i, i ^ hop) for i in range(peers)])  8.08 us
    ppermute x1, starting transfers between devices, on_device(): other = lax.ppermute(mine, 'core', [(0, 1), (1, 0)])  5.6 us
  transfers between devices with their start and end apart: 13, of which 8 were waited for; matrix products, arithmetic and copies ran while one was open for 11% of the time, Pallas kernels for 2%

profile of v3, /device:TPU:1, one launch (start us, length us, event | category | flops | bytes accessed | tf_op | source)
XLA Modules:
  0.0 208.5 jit_solution(18013354327123389074)
XLA Ops:
  3.3 22.2 %all_to_all.65.mine_ref = bf16[8,64,512]{2,1,0:T(8,128)(2,1)S(1)} all-to-all(bf16[8,64,512]{2,1,0:T(8,128)(2,1)S(1)} %broadcast_in_dim.43), channel_id=1, replica_groups=mesh['y'=8,'core'=2,'z'=8,'x'=4] {'y'}, dimensions={0} | all-to-all | bytes 1048576 | tf_op jit(solution)/shard_map/all_to_all | solution.py:24
  25.5 5.6 %collective-permute-start = (bf16[8,64,512]{2,1,0:T(8,128)(2,1)S(1)}, bf16[8,64,512]{2,1,0:T(8,128)(2,1)S(1)}, u32[]{:S(2)}, u32[]{:S(2)}) collective-permute-start(bf16[8,64,512]{2,1,0:T(8,128)(2,1)S(1)} %all_to_all.65.mine_ref), channel_id=1, source_target_pairs={{0,32},{32,0},{1,33},{33,1},{2,34},{34,2},{3,35},{35,3},{4,36},{36... | collective-permute-start | bytes 1572872 | tf_op jit(solution)/shard_map/ppermute | solution.py:300
  33.1 10.0 %all-to-all-start = ((bf16[8,72,128]{2,1,0:T(8,128)(2,1)}), bf16[8,72,128]{2,1,0:T(8,128)(2,1)S(1)}, u32[]{:S(2)}, u32[]{:S(2)}) async-start(bf16[8,72,128]{2,1,0:T(8,128)(2,1)} %broadcast_in_dim.40), calls=%async_computation | async-start | bytes 294912 | tf_op jit(solution)/shard_map/all_to_all | solution.py:24
  43.1 3.1 %multiply_reduce_fusion = f32[2048]{0:T(1024)S(1)} fusion(bf16[1024,2048]{1,0:T(8,128)(2,1)} %param.5), kind=kLoop, calls=%fused_computation.4 | loop fusion | flops 6289408 | bytes 4202496 | tf_op jit(solution)/shard_map/reduce_sum | solution.py:284
  46.2 5.8 %all-to-all-done = bf16[8,72,128]{2,1,0:T(8,128)(2,1)S(1)} async-done(((bf16[8,72,128]{2,1,0:T(8,128)(2,1)}), bf16[8,72,128]{2,1,0:T(8,128)(2,1)S(1)}, u32[]{:S(2)}, u32[]{:S(2)}) %all-to-all-start) | async-done | bytes 147488 | tf_op jit(solution)/shard_map/all_to_all | solution.py:24
  52.9 4.0 %all-to-all-start.1 = ((bf16[4,8,72,128]{3,2,1,0:T(8,128)(2,1)}), bf16[4,8,72,128]{3,2,1,0:T(8,128)(2,1)S(1)}, u32[]{:S(2)}, u32[]{:S(2)}) async-start(bf16[4,8,72,128]{3,2,1,0:T(8,128)(2,1)} %broadcast_in_dim.41), calls=%async_computation.1 | async-start | bytes 1179648 | tf_op jit(solution)/shard_map/all_to_all | solution.py:24
  57.1 6.5 %exponential_convert_fusion.1.kern_ref = bf16[512,2048]{1,0:T(8,128)(2,1)S(1)} fusion(bf16[1024,512]{1,0:T(8,128)(2,1)S(1)} %bitcast.19, bf16[1024,2048]{1,0:T(8,128)(2,1)} %param.5, f32[2048]{0:T(1024)S(1)} %multiply_reduce_fusion, f32[512]{0:T(512)S(1)} %bitcast.21), kind=kOutput, calls=%fused_computation.6 | convolution fusion | flops 2155872256 | bytes 7350272 | tf_op jit(solution)/shard_map/dot_general | solution.py:294
  66.7 6.3 %all-to-all-start.3 = ((bf16[16,36,128]{2,1,0:T(8,128)(2,1)}), bf16[16,36,128]{2,1,0:T(8,128)(2,1)S(1)}, u32[]{:S(2)}, u32[]{:S(2)}) async-start(bf16[16,36,128]{2,1,0:T(8,128)(2,1)} %shard_map.56), calls=%async_computation.3 | async-start | bytes 327680 | tf_op jit(solution)/shard_map/all_to_all | solution.py:24
  74.5 7.2 %collective-permute-start.1 = (bf16[1,64,512]{2,1,0:T(8,128)(2,1)S(1)}, bf16[1,64,512]{2,1,0:T(8,128)(2,1)S(1)}, u32[]{:S(2)}, u32[]{:S(2)}) collective-permute-start(bf16[1,64,512]{2,1,0:T(8,128)(2,1)S(1)} %bitcast.22), channel_id=1, source_target_pairs={{0,256},{64,320},{128,384},{192,448},{256,0},{320,64},{384,128},{4... | collective-permute-start | bytes 196616 | tf_op jit(solution)/shard_map/ppermute | solution.py:214
  84.0 3.6 %all-to-all-start.4 = ((bf16[16,36,128]{2,1,0:T(8,128)(2,1)}), bf16[16,36,128]{2,1,0:T(8,128)(2,1)S(1)}, u32[]{:S(2)}, u32[]{:S(2)}) async-start(bf16[16,36,128]{2,1,0:T(8,128)(2,1)} %shard_map.57), calls=%async_computation.4 | async-start | bytes 327680 | tf_op jit(solution)/shard_map/all_to_all | solution.py:24
  87.6 4.2 %collective-permute-start.2 = (bf16[2,64,512]{2,1,0:T(8,128)(2,1)S(1)}, bf16[2,64,512]{2,1,0:T(8,128)(2,1)S(1)}, u32[]{:S(2)}, u32[]{:S(2)}) collective-permute-start(bf16[2,64,512]{2,1,0:T(8,128)(2,1)S(1)} %pad_maximum_fusion.2), channel_id=1, source_target_pairs={{0,128},{64,192},{128,0},{192,64},{256,384},{320,448},{384,256},{4... | collective-permute-start | bytes 393224 | tf_op jit(solution)/shard_map/ppermute | solution.py:214
  91.8 5.8 %all-to-all-done.4.resid_ref = bf16[16,36,128]{2,1,0:T(8,128)(2,1)S(1)} async-done(((bf16[16,36,128]{2,1,0:T(8,128)(2,1)}), bf16[16,36,128]{2,1,0:T(8,128)(2,1)S(1)}, u32[]{:S(2)}, u32[]{:S(2)}) %all-to-all-start.4) | async-done | bytes 147488 | tf_op jit(solution)/shard_map/all_to_all | solution.py:24
  99.2 3.5 %all-to-all-start.5 = ((bf16[4,8,72,128]{3,2,1,0:T(8,128)(2,1)}), bf16[4,8,72,128]{3,2,1,0:T(8,128)(2,1)S(1)}, u32[]{:S(2)}, u32[]{:S(2)}) async-start(bf16[4,8,72,128]{3,2,1,0:T(8,128)(2,1)} %shard_map.58), calls=%async_computation.5 | async-start | bytes 1179648 | tf_op jit(solution)/shard_map/all_to_all | solution.py:24
  104.7 8.1 %collective-permute-done.3 = bf16[4,64,512]{2,1,0:T(8,128)(2,1)S(1)} collective-permute-done((bf16[4,64,512]{2,1,0:T(8,128)(2,1)S(1)}, bf16[4,64,512]{2,1,0:T(8,128)(2,1)S(1)}, u32[]{:S(2)}, u32[]{:S(2)}) %collective-permute-start.3) | collective-permute-done | bytes 262176 | tf_op jit(solution)/shard_map/ppermute | solution.py:214
  115.0 11.2 %all_to_all.66.arrived_ref = bf16[8,72,128]{2,1,0:T(8,128)(2,1)S(1)} all-to-all(bf16[8,72,128]{2,1,0:T(8,128)(2,1)S(1)} %shard_map.59), channel_id=1, replica_groups=mesh['y'=8,'core'=2,'z'=8,'x'=4] {'z'}, dimensions={0} | all-to-all | bytes 294912 | tf_op jit(solution)/shard_map/all_to_all | solution.py:24
  126.9 3.4 %all-to-all-start.7 = ((bf16[8,72,128]{2,1,0:T(8,128)(2,1)}), bf16[8,72,128]{2,1,0:T(8,128)(2,1)S(1)}, u32[]{:S(2)}, u32[]{:S(2)}) async-start(bf16[8,72,128]{2,1,0:T(8,128)(2,1)} %get-tuple-element.13), calls=%async_computation.7 | async-start | bytes 294912 | tf_op jit(solution)/shard_map/all_to_all | solution.py:24
  131.5 6.9 %all-to-all-done.7 = bf16[8,72,128]{2,1,0:T(8,128)(2,1)S(1)} async-done(((bf16[8,72,128]{2,1,0:T(8,128)(2,1)}), bf16[8,72,128]{2,1,0:T(8,128)(2,1)S(1)}, u32[]{:S(2)}, u32[]{:S(2)}) %all-to-all-start.7) | async-done | bytes 147488 | tf_op jit(solution)/shard_map/all_to_all | solution.py:24
  139.3 5.9 %all-to-all-start.8 = ((bf16[4,8,72,128]{3,2,1,0:T(8,128)(2,1)}), bf16[4,8,72,128]{3,2,1,0:T(8,128)(2,1)S(1)}, u32[]{:S(2)}, u32[]{:S(2)}) async-start(bf16[4,8,72,128]{3,2,1,0:T(8,128)(2,1)} %broadcast_in_dim.45), calls=%async_computation.8 | async-start | bytes 1179648 | tf_op jit(solution)/shard_map/all_to_all | solution.py:24
  145.2 6.8 %exponential_convert_fusion.kern_ref = bf16[512,2048]{1,0:T(8,128)(2,1)S(1)} fusion(bf16[1024,512]{1,0:T(8,128)(2,1)} %bitcast.18, bf16[1024,2048]{1,0:T(8,128)(2,1)} %param.5, f32[512]{0:T(512)S(1)} %bitcast.20, f32[2048]{0:T(1024)S(1)} %multiply_reduce_fusion), kind=kOutput, calls=%fused_computation.5 | convolution fusion | flops 2155872256 | bytes 7350272 | tf_op jit(solution)/shard_map/dot_general | solution.py:294
  154.5 6.8 %all-to-all-start.9 = ((bf16[16,36,128]{2,1,0:T(8,128)(2,1)}), bf16[16,36,128]{2,1,0:T(8,128)(2,1)S(1)}, u32[]{:S(2)}, u32[]{:S(2)}) async-start(bf16[16,36,128]{2,1,0:T(8,128)(2,1)} %shard_map.62), calls=%async_computation.9 | async-start | bytes 327680 | tf_op jit(solution)/shard_map/all_to_all | solution.py:24
  162.0 9.1 %all-to-all-done.9.arrived_ref = bf16[16,36,128]{2,1,0:T(8,128)(2,1)S(1)} async-done(((bf16[16,36,128]{2,1,0:T(8,128)(2,1)}), bf16[16,36,128]{2,1,0:T(8,128)(2,1)S(1)}, u32[]{:S(2)}, u32[]{:S(2)}) %all-to-all-start.9) | async-done | bytes 147488 | tf_op jit(solution)/shard_map/all_to_all | solution.py:24
  171.5 12.1 %all_to_all.67.resid_ref = bf16[16,36,128]{2,1,0:T(8,128)(2,1)S(1)} all-to-all(bf16[16,36,128]{2,1,0:T(8,128)(2,1)S(1)} %shard_map.63), channel_id=1, replica_groups=mesh['y'=8,'core'=2,'z'=8,'x'=4] {'y','core'}, dimensions={0} | all-to-all | bytes 294912 | tf_op jit(solution)/shard_map/all_to_all | solution.py:24
  184.3 12.7 %all_to_all.68.arrived_ref = bf16[4,8,72,128]{3,2,1,0:T(8,128)(2,1)S(1)} all-to-all(bf16[4,8,72,128]{3,2,1,0:T(8,128)(2,1)S(1)} %shard_map.64), channel_id=1, replica_groups=mesh['y'=8,'core'=2,'z'=8,'x'=4] {'x'}, dimensions={0} | all-to-all | bytes 1179648 | tf_op jit(solution)/shard_map/all_to_all | solution.py:24
  197.1 10.6 %all_to_all.69.arrived_ref = bf16[8,72,128]{2,1,0:T(8,128)(2,1)S(1)} all-to-all(bf16[8,72,128]{2,1,0:T(8,128)(2,1)S(1)} %shard_map.65), channel_id=1, replica_groups=mesh['y'=8,'core'=2,'z'=8,'x'=4] {'z'}, dimensions={0} | all-to-all | bytes 294912 | tf_op jit(solution)/shard_map/all_to_all | solution.py:24
  (58 shorter events, 27.0 us)
Async XLA Ops:
  0.0 81.9 %copy-start = (s32[1024]{0:T(1024)S(1)}, s32[1024]{0:T(1024)}, u32[]{:S(2)}) copy-start(s32[1024]{0:T(1024)} %param.7) | copy-start | bytes 12292
  25.5 31.4 %collective-permute-start = (bf16[8,64,512]{2,1,0:T(8,128)(2,1)S(1)}, bf16[8,64,512]{2,1,0:T(8,128)(2,1)S(1)}, u32[]{:S(2)}, u32[]{:S(2)}) collective-permute-start(bf16[8,64,512]{2,1,0:T(8,128)(2,1)S(1)} %all_to_all.65.mine_ref), channel_id=1, source_target_pairs={{0,32},{32,0},{1,33},{33,1},{2,34},{34,2},{3,35},{35,3},{4,36},{36... | collective-permute-start | bytes 1572872 | tf_op jit(solution)/shard_map/ppermute | solution.py:300
  33.1 18.9 %all-to-all-start = ((bf16[8,72,128]{2,1,0:T(8,128)(2,1)}), bf16[8,72,128]{2,1,0:T(8,128)(2,1)S(1)}, u32[]{:S(2)}, u32[]{:S(2)}) async-start(bf16[8,72,128]{2,1,0:T(8,128)(2,1)} %broadcast_in_dim.40), calls=%async_computation | async-start | bytes 294912 | tf_op jit(solution)/shard_map/all_to_all | solution.py:24
  52.9 12.2 %all-to-all-start.1 = ((bf16[4,8,72,128]{3,2,1,0:T(8,128)(2,1)}), bf16[4,8,72,128]{3,2,1,0:T(8,128)(2,1)S(1)}, u32[]{:S(2)}, u32[]{:S(2)}) async-start(bf16[4,8,72,128]{3,2,1,0:T(8,128)(2,1)} %broadcast_in_dim.41), calls=%async_computation.1 | async-start | bytes 1179648 | tf_op jit(solution)/shard_map/all_to_all | solution.py:24
  66.7 16.2 %all-to-all-start.3 = ((bf16[16,36,128]{2,1,0:T(8,128)(2,1)}), bf16[16,36,128]{2,1,0:T(8,128)(2,1)S(1)}, u32[]{:S(2)}, u32[]{:S(2)}) async-start(bf16[16,36,128]{2,1,0:T(8,128)(2,1)} %shard_map.56), calls=%async_computation.3 | async-start | bytes 327680 | tf_op jit(solution)/shard_map/all_to_all | solution.py:24
  74.5 13.1 %collective-permute-start.1 = (bf16[1,64,512]{2,1,0:T(8,128)(2,1)S(1)}, bf16[1,64,512]{2,1,0:T(8,128)(2,1)S(1)}, u32[]{:S(2)}, u32[]{:S(2)}) collective-permute-start(bf16[1,64,512]{2,1,0:T(8,128)(2,1)S(1)} %bitcast.22), channel_id=1, source_target_pairs={{0,256},{64,320},{128,384},{192,448},{256,0},{320,64},{384,128},{4... | collective-permute-start | bytes 196616 | tf_op jit(solution)/shard_map/ppermute | solution.py:214
  84.0 13.7 %all-to-all-start.4 = ((bf16[16,36,128]{2,1,0:T(8,128)(2,1)}), bf16[16,36,128]{2,1,0:T(8,128)(2,1)S(1)}, u32[]{:S(2)}, u32[]{:S(2)}) async-start(bf16[16,36,128]{2,1,0:T(8,128)(2,1)} %shard_map.57), calls=%async_computation.4 | async-start | bytes 327680 | tf_op jit(solution)/shard_map/all_to_all | solution.py:24
  87.6 15.1 %collective-permute-start.2 = (bf16[2,64,512]{2,1,0:T(8,128)(2,1)S(1)}, bf16[2,64,512]{2,1,0:T(8,128)(2,1)S(1)}, u32[]{:S(2)}, u32[]{:S(2)}) collective-permute-start(bf16[2,64,512]{2,1,0:T(8,128)(2,1)S(1)} %pad_maximum_fusion.2), channel_id=1, source_target_pairs={{0,128},{64,192},{128,0},{192,64},{256,384},{320,448},{384,256},{4... | collective-permute-start | bytes 393224 | tf_op jit(solution)/shard_map/ppermute | solution.py:214
  99.2 15.7 %all-to-all-start.5 = ((bf16[4,8,72,128]{3,2,1,0:T(8,128)(2,1)}), bf16[4,8,72,128]{3,2,1,0:T(8,128)(2,1)S(1)}, u32[]{:S(2)}, u32[]{:S(2)}) async-start(bf16[4,8,72,128]{3,2,1,0:T(8,128)(2,1)} %shard_map.58), calls=%async_computation.5 | async-start | bytes 1179648 | tf_op jit(solution)/shard_map/all_to_all | solution.py:24
  102.8 10.0 %collective-permute-start.3 = (bf16[4,64,512]{2,1,0:T(8,128)(2,1)S(1)}, bf16[4,64,512]{2,1,0:T(8,128)(2,1)S(1)}, u32[]{:S(2)}, u32[]{:S(2)}) collective-permute-start(bf16[4,64,512]{2,1,0:T(8,128)(2,1)S(1)} %pad_maximum_fusion.1), channel_id=1, source_target_pairs={{0,64},{64,0},{128,192},{192,128},{256,320},{320,256},{384,448},{4... | collective-permute-start | bytes 786440 | tf_op jit(solution)/shard_map/ppermute | solution.py:214
  112.8 17.5 %collective-permute-start.4 = (bf16[8,64,512]{2,1,0:T(8,128)(2,1)S(1)}, bf16[8,64,512]{2,1,0:T(8,128)(2,1)S(1)}, u32[]{:S(2)}, u32[]{:S(2)}) collective-permute-start(bf16[8,64,512]{2,1,0:T(8,128)(2,1)S(1)} %pad_maximum_fusion.mine_ref), channel_id=1, source_target_pairs={{0,32},{32,0},{1,33},{33,1},{2,34},{34,2},{3,35},{35,3},{4,36},{36... | collective-permute-start | bytes 1572872 | tf_op jit(solution)/shard_map/ppermute | solution.py:218
  126.9 11.5 %all-to-all-start.7 = ((bf16[8,72,128]{2,1,0:T(8,128)(2,1)}), bf16[8,72,128]{2,1,0:T(8,128)(2,1)S(1)}, u32[]{:S(2)}, u32[]{:S(2)}) async-start(bf16[8,72,128]{2,1,0:T(8,128)(2,1)} %get-tuple-element.13), calls=%async_computation.7 | async-start | bytes 294912 | tf_op jit(solution)/shard_map/all_to_all | solution.py:24
  130.5 1.0 copy-start.1
  139.3 13.5 %all-to-all-start.8 = ((bf16[4,8,72,128]{3,2,1,0:T(8,128)(2,1)}), bf16[4,8,72,128]{3,2,1,0:T(8,128)(2,1)S(1)}, u32[]{:S(2)}, u32[]{:S(2)}) async-start(bf16[4,8,72,128]{3,2,1,0:T(8,128)(2,1)} %broadcast_in_dim.45), calls=%async_computation.8 | async-start | bytes 1179648 | tf_op jit(solution)/shard_map/all_to_all | solution.py:24
  154.5 16.6 %all-to-all-start.9 = ((bf16[16,36,128]{2,1,0:T(8,128)(2,1)}), bf16[16,36,128]{2,1,0:T(8,128)(2,1)S(1)}, u32[]{:S(2)}, u32[]{:S(2)}) async-start(bf16[16,36,128]{2,1,0:T(8,128)(2,1)} %shard_map.62), calls=%async_computation.9 | async-start | bytes 327680 | tf_op jit(solution)/shard_map/all_to_all | solution.py:24

commit v4 on v3

--- a/solution.py
+++ b/solution.py
@@ -58,13 +58,22 @@
     return out
 
 
-def logits_body(coef_ref, kern_ref, out_ref, coef, logits):
-    over_x, over_z, height, _ = coef_ref.shape
-    for pair in range(over_x * over_z // 2):
-        at = [divmod(2 * pair + i, over_x) for i in range(2)]
-        halves = regroup([coef_ref[x, z].astype(jnp.float32) for z, x in at], 2)
-        for h in range(2):
-            coef[height * h : height * (h + 1), LANES * pair : LANES * (pair + 1)] = halves[h]
+def logits_body(offsets, coef_ref, kern_ref, out_ref, coef, logits):
+    over_z, over_x, height, _ = coef_ref.shape
+    if offsets is not None:
+        over_z, over_x = over_x, over_z
+    for i in range(over_z):
+        for p in range(over_x // 2):
+            if offsets is None:
+                pair = coef_ref[i, 2 * p], coef_ref[i, 2 * p + 1]
+                at = LANES * (i * over_x // 2 + p)
+            else:
+                pair = coef_ref[2 * p, i], coef_ref[2 * p + 1, i]
+                at = LANES * (lax.bitwise_xor(lax.axis_index("z"), offsets[i]) * (over_x // 2) + p)
+                at = pl.multiple_of(at, LANES)
+            halves = regroup([block.astype(jnp.float32) for block in pair], 2)
+            for h in range(2):
+                coef[height * h : height * (h + 1), pl.ds(at, LANES)] = halves[h]
     logits[...] = lax.dot_general(
         coef[...].astype(jnp.bfloat16),
         kern_ref[...],
@@ -80,12 +89,12 @@
             out_ref[fold * group + k] = blocks[k].astype(out_ref.dtype)
 
 
-def partial_logits(coef_parts, kern, peers):
+def partial_logits(coef_parts, kern, peers, offsets=None):
     classes = 2 * coef_parts.shape[2]
     batch, centres = kern.shape
     rows = classes * (batch // peers) // LANES
     return call(
-        logits_body,
+        functools.partial(logits_body, offsets),
         jax.ShapeDtypeStruct((peers, rows, LANES), jnp.bfloat16),
         2 * classes * batch * centres,
         coef_parts,
@@ -138,7 +147,7 @@
         for q in range(fold):
             resid[rows * q : rows * (q + 1), LANES * group : LANES * (group + 1)] = blocks[q]
     held = resid[...].astype(jnp.bfloat16)
-    over_x, _, height, _ = out_ref.shape
+    _, height, _ = out_ref.shape
     step = 4 * LANES
     for start in range(0, kern_ref.shape[1], step):
         grad = jnp.dot(held, kern_ref[:, start : start + step], preferred_element_type=jnp.float32)
@@ -146,35 +155,21 @@
             halves = [grad[height * h : height * (h + 1), at : at + LANES] for h in range(2)]
             first = 2 * (start + at) // LANES
             for i, block in enumerate(regroup(halves, 2)):
-                z, x = divmod(first + i, over_x)
-                out_ref[x, z] = block.astype(out_ref.dtype)
-
-
-def partial_grad(resid_parts, kern, over_x, over_z):
+                out_ref[first + i] = block.astype(out_ref.dtype)
+
+
+def partial_grad(resid_parts, kern, peers):
     batch, centres = kern.shape
     classes = resid_parts.size // batch
-    height = classes * (centres // (over_x * over_z)) // LANES
+    height = classes * (centres // peers) // LANES
     return call(
         grad_body,
-        jax.ShapeDtypeStruct((over_x, over_z, height, LANES), jnp.bfloat16),
+        jax.ShapeDtypeStruct((peers, height, LANES), jnp.bfloat16),
         2 * classes * batch * centres,
         resid_parts,
         kern,
         scratch=[pltpu.VMEM((classes, batch), jnp.float32)],
     )
-
-
-def merged_body(arrived_ref, out_ref):
-    for z in range(arrived_ref.shape[1]):
-        total = arrived_ref[0, z].astype(jnp.float32)
-        for peer in range(1, arrived_ref.shape[0]):
-            total = total + arrived_ref[peer, z].astype(jnp.float32)
-        out_ref[z] = total.astype(out_ref.dtype)
-
-
-def merged(arrived):
-    out = jax.ShapeDtypeStruct(arrived.shape[1:], jnp.bfloat16)
-    return call(merged_body, out, arrived.size, arrived)
 
 
 def assemble_body(offsets, mine_ref, other_ref, out_ref, square_ref):
@@ -206,17 +201,42 @@
     return feats.reshape(blocks * 2 * rows, batch), squares[0]
 
 
-def gathered_by_swaps(block):
+def doubled(block, axis):
     held, offsets = block[None], [0]
-    peers = lax.axis_size("y")
+    peers = lax.axis_size(axis)
     hop = peers // 2
     while hop:
-        moved = lax.ppermute(held, "y", [(i, i ^ hop) for i in range(peers)])
+        moved = lax.ppermute(held, axis, [(i, i ^ hop) for i in range(peers)])
         held = jnp.concatenate([held, moved])
         offsets = offsets + [o ^ hop for o in offsets]
         hop //= 2
-    other = lax.ppermute(held, "core", [(0, 1), (1, 0)])
-    return assembled(held, other, offsets)
+    return held, offsets
+
+
+def swapped_cores(array):
+    return lax.ppermute(array, "core", [(0, 1), (1, 0)])
+
+
+def pick_body(step, pool_ref, picks_ref, out_ref):
+    pool_dev = pool_ref.shape[1]
+    first = (lax.axis_index("z") * lax.axis_size("x") + lax.axis_index("x")) * pool_dev
+    chosen = picks_ref[step : step + 1, :] - first
+    rows = lax.broadcasted_iota(jnp.int32, (pool_dev, chosen.shape[1]), 0)
+    onehot = (rows == chosen).astype(jnp.float32).astype(jnp.bfloat16)
+    feats = jnp.dot(pool_ref[...], onehot, preferred_element_type=jnp.float32).astype(out_ref.dtype)
+    for peer in range(out_ref.shape[0]):
+        out_ref[peer] = feats
+
+
+def picked(pool, picks, step, copies):
+    feats, batch = pool.shape[0], picks.shape[1]
+    return call(
+        functools.partial(pick_body, step),
+        jax.ShapeDtypeStruct((copies, feats, batch), pool.dtype),
+        2 * pool.size * batch,
+        pool,
+        picks,
+    )
 
 
 def update_body(rate, arrived_ref, current_ref, new_ref, half_ref):
@@ -283,9 +303,6 @@
     local_picks = picks - lax.axis_index(SAMPLE) * pool_dev
     centre_sq = jnp.sum(jnp.square(centres.astype(jnp.float32)), axis=0)
 
-    def picked(step):
-        return jnp.take(pool, local_picks[step], axis=1, mode="clip")
-
     def own_labels(step):
         chosen = lax.dynamic_slice(local_picks[step], (me * own,), (own,))
         return jnp.take(labels, chosen, mode="clip")
@@ -296,22 +313,24 @@
         )
         return laplace(cross, sample_sq, centre_sq, width)
 
-    mine = spread(picked(0), "y")
-    other = lax.ppermute(mine, "core", [(0, 1), (1, 0)])
+    mine = exchange(picked(pool, picks, 0, lax.axis_size("y")), "y")
+    later, offsets = doubled(picked(pool, picks, 1, 1)[0], "y")
     kerns = [
-        kernel_matrix(*assembled(mine, other)),
-        kernel_matrix(*gathered_by_swaps(picked(1))),
+        kernel_matrix(*assembled(mine, swapped_cores(mine))),
+        kernel_matrix(*assembled(later, swapped_cores(later), offsets)),
     ]
     labs = [own_labels(step) for step in range(STEPS)]
 
     current = jnp.concatenate([coefs[: classes // 2], coefs[classes // 2 :]], axis=1)
-    half = jnp.broadcast_to(current.astype(jnp.bfloat16), (over_z, *current.shape))
+    held, offsets = doubled(current.astype(jnp.bfloat16), "z")
+    coef_parts = spread(held, "x")
     for step in range(STEPS):
-        coef_parts = spread(exchange(half, "z"), "x").reshape(over_x, over_z, *current.shape)
-        arrived = exchange(partial_logits(coef_parts, kerns[step], n_centre), CENTRE)
+        if step > 0:
+            coef_parts = exchange(half, SAMPLE).reshape(over_z, over_x, *current.shape)
+            offsets = None
+        arrived = exchange(partial_logits(coef_parts, kerns[step], n_centre, offsets), CENTRE)
         resid = residual(arrived, labs[step], LOGIT_GAIN / total_centres, fold)
-        grads = partial_grad(exchange(resid, CENTRE), kerns[step], over_x, over_z)
-        arrived = exchange(merged(exchange(grads, "x")), "z")
+        arrived = exchange(partial_grad(exchange(resid, CENTRE), kerns[step], n_sample), SAMPLE)
         if step < STEPS - 1:
             current, half = updated(arrived, current, rate)
         else:

time: 210 us -> 214 us (1.019)
  blocking collectives: 68.8 us -> 47.2 us
  waiting for transfers between devices: 38.4 us -> 56.3 us
  starting transfers between devices: 64.5 us -> 76.9 us
  local copies, waits for them, and re-layouts: 11.1 us -> 6.06 us
    all_to_all x5 -> x3, blocking collectives: 68.8 us -> 47.2 us  [exchange(): return lax.all_to_all(parts, axes, 0, 0, tiled=True)]
    ppermute x5 -> x8, waiting for transfers between devices: 8.09 us -> 24.9 us  [the longest x6 24.9 us: doubled(): moved = lax.ppermute(held, axis, [(i, i ^ hop) for i in range(peers)])]
    ppermute x5 -> x8, starting transfers between devices: 21.1 us -> 32.6 us  [the longest x6 24.4 us: doubled(): moved = lax.ppermute(held, axis, [(i, i ^ hop) for i in range(peers)])]
    gather x4 -> x0, local copies, waits for them, and re-layouts: 2.88 us -> none  [picked(): return jnp.take(pool, local_picks[step], axis=1, mode='clip')]
    all_to_all x8 -> x6, waiting for transfers between devices: 30.4 us -> 31.4 us  [exchange(): return lax.all_to_all(parts, axes, 0, 0, tiled=True)]
    all_to_all x8 -> x6, starting transfers between devices: 43.5 us -> 44.3 us  [exchange(): return lax.all_to_all(parts, axes, 0, 0, tiled=True)]
  transfers between devices with their start and end apart: 13 -> 14, of which waited for: 8 -> 9; matrix products, arithmetic and copies ran while one was open for 11% -> 9% of each run, Pallas kernels for 2% -> 1%
where the time goes in v4:
time: 214 us; the launch traced here: 213 us
  starting transfers between devices  76.9 us (36%)
  waiting for transfers between devices  56.3 us (26%)
  blocking collectives  47.2 us (22%)
  matrix products  12.9 us (6%)
  Pallas kernels  9.41 us (4%)
  local copies, waits for them, and re-layouts  6.06 us (3%)
  other arithmetic  3.62 us (2%)
    all_to_all x3, blocking collectives, exchange(): return lax.all_to_all(parts, axes, 0, 0, tiled=True)  47.2 us
    all_to_all x6, starting transfers between devices, exchange(): return lax.all_to_all(parts, axes, 0, 0, tiled=True)  44.3 us
    all_to_all x6, waiting for transfers between devices, exchange(): return lax.all_to_all(parts, axes, 0, 0, tiled=True)  31.4 us
    ppermute x6, waiting for transfers between devices, doubled(): moved = lax.ppermute(held, axis, [(i, i ^ hop) for i in range(peers)])  24.9 us
    ppermute x6, starting transfers between devices, doubled(): moved = lax.ppermute(held, axis, [(i, i ^ hop) for i in range(peers)])  24.4 us
    dot_general x2, matrix products, kernel_matrix(): lax.dot_general(gathered, centres, (((0,), (0,)), ((), ())), preferred_el...  12.9 us
    pallas_call x12, Pallas kernels, call(): pl.pallas_call(body, out_shape=out, in_specs=[vmem] * len(operands), out_...  9.41 us
    ppermute x2, starting transfers between devices, swapped_cores(): return lax.ppermute(array, 'core', [(0, 1), (1, 0)])  8.12 us
  transfers between devices with their start and end apart: 14, of which 9 were waited for; matrix products, arithmetic and copies ran while one was open for 9% of the time, Pallas kernels for 1%

profile of v4, /device:TPU:1, one launch (start us, length us, event | category | flops | bytes accessed | tf_op | source)
XLA Modules:
  0.0 212.6 jit_solution(17746922206441847120)
XLA Ops:
  2.8 7.7 %all-to-all-start.1 = ((bf16[8,64,512]{2,1,0:T(8,128)(2,1)}), bf16[8,64,512]{2,1,0:T(8,128)(2,1)S(1)}, u32[]{:S(2)}, u32[]{:S(2)}) async-start(bf16[8,64,512]{2,1,0:T(8,128)(2,1)} %shard_map.55), calls=%async_computation.1 | async-start | bytes 1048576 | tf_op jit(solution)/shard_map/all_to_all | solution.py:24
  11.7 10.6 %collective-permute-start = (bf16[1,72,128]{2,1,0:T(8,128)(2,1)S(1)}, bf16[1,72,128]{2,1,0:T(8,128)(2,1)S(1)}, u32[]{:S(2)}, u32[]{:S(2)}) collective-permute-start(bf16[1,72,128]{2,1,0:T(8,128)(2,1)S(1)} %pad_maximum_fusion.8), channel_id=1, source_target_pairs={{0,16},{4,20},{8,24},{12,28},{16,0},{20,4},{24,8},{28,12},{1,17},{... | collective-permute-start | bytes 55304 | tf_op jit(solution)/shard_map/ppermute | solution.py:209
  23.5 4.2 %collective-permute-start.1 = (bf16[2,72,128]{2,1,0:T(8,128)(2,1)S(1)}, bf16[2,72,128]{2,1,0:T(8,128)(2,1)S(1)}, u32[]{:S(2)}, u32[]{:S(2)}) collective-permute-start(bf16[2,72,128]{2,1,0:T(8,128)(2,1)S(1)} %pad_maximum_fusion.6), channel_id=1, source_target_pairs={{0,8},{4,12},{8,0},{12,4},{16,24},{20,28},{24,16},{28,20},{1,9},{5... | collective-permute-start | bytes 110600 | tf_op jit(solution)/shard_map/ppermute | solution.py:209
  27.7 4.0 %collective-permute-start.3 = (bf16[8,64,512]{2,1,0:T(8,128)(2,1)S(1)}, bf16[8,64,512]{2,1,0:T(8,128)(2,1)S(1)}, u32[]{:S(2)}, u32[]{:S(2)}) collective-permute-start(bf16[8,64,512]{2,1,0:T(8,128)(2,1)S(1)} %all-to-all-done.1.mine_ref), channel_id=1, source_target_pairs={{0,32},{32,0},{1,33},{33,1},{2,34},{34,2},{3,35},{35,3},{4,36},{36... | collective-permute-start | bytes 1572872 | tf_op jit(solution)/shard_map/ppermute | solution.py:217
  31.7 3.1 %multiply_reduce_fusion = f32[2048]{0:T(1024)S(1)} fusion(bf16[1024,2048]{1,0:T(8,128)(2,1)} %param.5), kind=kLoop, calls=%fused_computation.2 | loop fusion | flops 6289408 | bytes 4202496 | tf_op jit(solution)/shard_map/reduce_sum | solution.py:304
  34.9 3.0 %collective-permute-start.2 = (bf16[4,72,128]{2,1,0:T(8,128)(2,1)S(1)}, bf16[4,72,128]{2,1,0:T(8,128)(2,1)S(1)}, u32[]{:S(2)}, u32[]{:S(2)}) collective-permute-start(bf16[4,72,128]{2,1,0:T(8,128)(2,1)S(1)} %pad_maximum_fusion.4), channel_id=1, source_target_pairs={{0,4},{4,0},{8,12},{12,8},{16,20},{20,16},{24,28},{28,24},{1,5},{5... | collective-permute-start | bytes 221192 | tf_op jit(solution)/shard_map/ppermute | solution.py:209
  41.7 4.0 %all-to-all-start = ((bf16[4,8,72,128]{3,2,1,0:T(8,128)(2,1)}), bf16[4,8,72,128]{3,2,1,0:T(8,128)(2,1)S(1)}, u32[]{:S(2)}, u32[]{:S(2)}) async-start(bf16[4,8,72,128]{3,2,1,0:T(8,128)(2,1)} %broadcast_in_dim.16), calls=%async_computation | async-start | bytes 1179648 | tf_op jit(solution)/shard_map/all_to_all | solution.py:24
  45.9 6.4 %exponential_convert_fusion.1.kern_ref = bf16[512,2048]{1,0:T(8,128)(2,1)S(1)} fusion(bf16[1024,512]{1,0:T(8,128)(2,1)S(1)} %bitcast.19, bf16[1024,2048]{1,0:T(8,128)(2,1)} %param.5, f32[2048]{0:T(1024)S(1)} %multiply_reduce_fusion, f32[512]{0:T(512)S(1)} %bitcast.21), kind=kOutput, calls=%fused_computation.4 | convolution fusion | flops 2155872256 | bytes 7350272 | tf_op jit(solution)/shard_map/dot_general | solution.py:311
  56.4 9.5 %all-to-all-start.2 = ((bf16[16,36,128]{2,1,0:T(8,128)(2,1)}), bf16[16,36,128]{2,1,0:T(8,128)(2,1)S(1)}, u32[]{:S(2)}, u32[]{:S(2)}) async-start(bf16[16,36,128]{2,1,0:T(8,128)(2,1)} %shard_map.57), calls=%async_computation.2 | async-start | bytes 327680 | tf_op jit(solution)/shard_map/all_to_all | solution.py:24
  66.8 8.8 %all-to-all-done.2.arrived_ref = bf16[16,36,128]{2,1,0:T(8,128)(2,1)S(1)} async-done(((bf16[16,36,128]{2,1,0:T(8,128)(2,1)}), bf16[16,36,128]{2,1,0:T(8,128)(2,1)S(1)}, u32[]{:S(2)}, u32[]{:S(2)}) %all-to-all-start.2) | async-done | bytes 147488 | tf_op jit(solution)/shard_map/all_to_all | solution.py:24
  75.9 12.3 %all_to_all.45.resid_ref = bf16[16,36,128]{2,1,0:T(8,128)(2,1)S(1)} all-to-all(bf16[16,36,128]{2,1,0:T(8,128)(2,1)S(1)} %shard_map.58), channel_id=1, replica_groups=mesh['y'=8,'core'=2,'z'=8,'x'=4] {'y','core'}, dimensions={0} | all-to-all | bytes 294912 | tf_op jit(solution)/shard_map/all_to_all | solution.py:24
  89.8 7.9 %all-to-all-start.4 = ((bf16[32,72,128]{2,1,0:T(8,128)(2,1)}), bf16[32,72,128]{2,1,0:T(8,128)(2,1)S(1)}, u32[]{:S(2)}, u32[]{:S(2)}) async-start(bf16[32,72,128]{2,1,0:T(8,128)(2,1)} %shard_map.59), calls=%async_computation.4 | async-start | bytes 1179648 | tf_op jit(solution)/shard_map/all_to_all | solution.py:24
  98.0 2.8 %collective-permute-start.4 = (bf16[1,64,512]{2,1,0:T(8,128)(2,1)S(1)}, bf16[1,64,512]{2,1,0:T(8,128)(2,1)S(1)}, u32[]{:S(2)}, u32[]{:S(2)}) collective-permute-start(bf16[1,64,512]{2,1,0:T(8,128)(2,1)S(1)} %shard_map.61), channel_id=1, source_target_pairs={{0,256},{64,320},{128,384},{192,448},{256,0},{320,64},{384,128},{4... | collective-permute-start | bytes 196616 | tf_op jit(solution)/shard_map/ppermute | solution.py:209
  100.8 7.6 %collective-permute-done.4 = bf16[1,64,512]{2,1,0:T(8,128)(2,1)S(1)} collective-permute-done((bf16[1,64,512]{2,1,0:T(8,128)(2,1)S(1)}, bf16[1,64,512]{2,1,0:T(8,128)(2,1)S(1)}, u32[]{:S(2)}, u32[]{:S(2)}) %collective-permute-start.4) | collective-permute-done | bytes 65568 | tf_op jit(solution)/shard_map/ppermute | solution.py:209
  110.4 6.9 %collective-permute-done.5 = bf16[2,64,512]{2,1,0:T(8,128)(2,1)S(1)} collective-permute-done((bf16[2,64,512]{2,1,0:T(8,128)(2,1)S(1)}, bf16[2,64,512]{2,1,0:T(8,128)(2,1)S(1)}, u32[]{:S(2)}, u32[]{:S(2)}) %collective-permute-start.5) | collective-permute-done | bytes 131104 | tf_op jit(solution)/shard_map/ppermute | solution.py:209
  119.2 6.5 %collective-permute-done.6 = bf16[4,64,512]{2,1,0:T(8,128)(2,1)S(1)} collective-permute-done((bf16[4,64,512]{2,1,0:T(8,128)(2,1)S(1)}, bf16[4,64,512]{2,1,0:T(8,128)(2,1)S(1)}, u32[]{:S(2)}, u32[]{:S(2)}) %collective-permute-start.6) | collective-permute-done | bytes 262176 | tf_op jit(solution)/shard_map/ppermute | solution.py:209
  125.8 4.1 %collective-permute-start.7 = (bf16[8,64,512]{2,1,0:T(8,128)(2,1)S(1)}, bf16[8,64,512]{2,1,0:T(8,128)(2,1)S(1)}, u32[]{:S(2)}, u32[]{:S(2)}) collective-permute-start(bf16[8,64,512]{2,1,0:T(8,128)(2,1)S(1)} %pad_maximum_fusion.mine_ref), channel_id=1, source_target_pairs={{0,32},{32,0},{1,33},{33,1},{2,34},{34,2},{3,35},{35,3},{4,36},{36... | collective-permute-start | bytes 1572872 | tf_op jit(solution)/shard_map/ppermute | solution.py:217
  130.9 10.1 %all-to-all-start.5 = ((bf16[32,72,128]{2,1,0:T(8,128)(2,1)}), bf16[32,72,128]{2,1,0:T(8,128)(2,1)S(1)}, u32[]{:S(2)}, u32[]{:S(2)}) async-start(bf16[32,72,128]{2,1,0:T(8,128)(2,1)} %get-tuple-element.13), calls=%async_computation.5 | async-start | bytes 1179648 | tf_op jit(solution)/shard_map/all_to_all | solution.py:24
  141.3 6.4 %exponential_convert_fusion.kern_ref = bf16[512,2048]{1,0:T(8,128)(2,1)S(1)} fusion(bf16[1024,512]{1,0:T(8,128)(2,1)S(1)} %bitcast.18, bf16[1024,2048]{1,0:T(8,128)(2,1)} %param.5, f32[512]{0:T(512)S(1)} %bitcast.20, f32[2048]{0:T(1024)S(1)} %multiply_reduce_fusion), kind=kOutput, calls=%fused_computation.3 | convolution fusion | flops 2155872256 | bytes 7350272 | tf_op jit(solution)/shard_map/dot_general | solution.py:311
  147.7 11.3 %all-to-all-done.5 = bf16[32,72,128]{2,1,0:T(8,128)(2,1)S(1)} async-done(((bf16[32,72,128]{2,1,0:T(8,128)(2,1)}), bf16[32,72,128]{2,1,0:T(8,128)(2,1)S(1)}, u32[]{:S(2)}, u32[]{:S(2)}) %all-to-all-start.5) | async-done | bytes 589856 | tf_op jit(solution)/shard_map/all_to_all | solution.py:24
  160.7 5.1 %all-to-all-start.6 = ((bf16[16,36,128]{2,1,0:T(8,128)(2,1)}), bf16[16,36,128]{2,1,0:T(8,128)(2,1)S(1)}, u32[]{:S(2)}, u32[]{:S(2)}) async-start(bf16[16,36,128]{2,1,0:T(8,128)(2,1)} %shard_map.63), calls=%async_computation.6 | async-start | bytes 327680 | tf_op jit(solution)/shard_map/all_to_all | solution.py:24
  166.5 9.1 %all-to-all-done.6.arrived_ref = bf16[16,36,128]{2,1,0:T(8,128)(2,1)S(1)} async-done(((bf16[16,36,128]{2,1,0:T(8,128)(2,1)}), bf16[16,36,128]{2,1,0:T(8,128)(2,1)S(1)}, u32[]{:S(2)}, u32[]{:S(2)}) %all-to-all-start.6) | async-done | bytes 147488 | tf_op jit(solution)/shard_map/all_to_all | solution.py:24
  176.0 12.1 %all_to_all.46.resid_ref = bf16[16,36,128]{2,1,0:T(8,128)(2,1)S(1)} all-to-all(bf16[16,36,128]{2,1,0:T(8,128)(2,1)S(1)} %shard_map.64), channel_id=1, replica_groups=mesh['y'=8,'core'=2,'z'=8,'x'=4] {'y','core'}, dimensions={0} | all-to-all | bytes 294912 | tf_op jit(solution)/shard_map/all_to_all | solution.py:24
  188.8 22.9 %all_to_all.47.arrived_ref = bf16[32,72,128]{2,1,0:T(8,128)(2,1)S(1)} all-to-all(bf16[32,72,128]{2,1,0:T(8,128)(2,1)S(1)} %shard_map.65), channel_id=1, replica_groups=mesh['y'=8,'core'=2,'z'=8,'x'=4] {'z','x'}, dimensions={0} | all-to-all | bytes 1179648 | tf_op jit(solution)/shard_map/all_to_all | solution.py:24
  (59 shorter events, 25.9 us)
Async XLA Ops:
  0.0 66.0 %copy-start = (s32[1024]{0:T(1024)S(1)}, s32[1024]{0:T(1024)}, u32[]{:S(2)}) copy-start(s32[1024]{0:T(1024)} %param.7) | copy-start | bytes 12292
  0.0 0.9 copy-start.1
  0.9 0.7 copy-start.3
  1.6 36.3 %copy-start.4 = (s32[2,512]{1,0:T(2,128)S(1)}, s32[2,512]{1,0:T(2,128)}, u32[]{:S(2)}) copy-start(s32[2,512]{1,0:T(2,128)} %picks_ref.3) | copy-start | bytes 12292
  2.8 25.0 %all-to-all-start.1 = ((bf16[8,64,512]{2,1,0:T(8,128)(2,1)}), bf16[8,64,512]{2,1,0:T(8,128)(2,1)S(1)}, u32[]{:S(2)}, u32[]{:S(2)}) async-start(bf16[8,64,512]{2,1,0:T(8,128)(2,1)} %shard_map.55), calls=%async_computation.1 | async-start | bytes 1048576 | tf_op jit(solution)/shard_map/all_to_all | solution.py:24
  11.7 11.8 %collective-permute-start = (bf16[1,72,128]{2,1,0:T(8,128)(2,1)S(1)}, bf16[1,72,128]{2,1,0:T(8,128)(2,1)S(1)}, u32[]{:S(2)}, u32[]{:S(2)}) collective-permute-start(bf16[1,72,128]{2,1,0:T(8,128)(2,1)S(1)} %pad_maximum_fusion.8), channel_id=1, source_target_pairs={{0,16},{4,20},{8,24},{12,28},{16,0},{20,4},{24,8},{28,12},{1,17},{... | collective-permute-start | bytes 55304 | tf_op jit(solution)/shard_map/ppermute | solution.py:209
  23.5 11.3 %collective-permute-start.1 = (bf16[2,72,128]{2,1,0:T(8,128)(2,1)S(1)}, bf16[2,72,128]{2,1,0:T(8,128)(2,1)S(1)}, u32[]{:S(2)}, u32[]{:S(2)}) collective-permute-start(bf16[2,72,128]{2,1,0:T(8,128)(2,1)S(1)} %pad_maximum_fusion.6), channel_id=1, source_target_pairs={{0,8},{4,12},{8,0},{12,4},{16,24},{20,28},{24,16},{28,20},{1,9},{5... | collective-permute-start | bytes 110600 | tf_op jit(solution)/shard_map/ppermute | solution.py:209
  27.7 17.9 %collective-permute-start.3 = (bf16[8,64,512]{2,1,0:T(8,128)(2,1)S(1)}, bf16[8,64,512]{2,1,0:T(8,128)(2,1)S(1)}, u32[]{:S(2)}, u32[]{:S(2)}) collective-permute-start(bf16[8,64,512]{2,1,0:T(8,128)(2,1)S(1)} %all-to-all-done.1.mine_ref), channel_id=1, source_target_pairs={{0,32},{32,0},{1,33},{33,1},{2,34},{34,2},{3,35},{35,3},{4,36},{36... | collective-permute-start | bytes 1572872 | tf_op jit(solution)/shard_map/ppermute | solution.py:217
  34.9 5.8 %collective-permute-start.2 = (bf16[4,72,128]{2,1,0:T(8,128)(2,1)S(1)}, bf16[4,72,128]{2,1,0:T(8,128)(2,1)S(1)}, u32[]{:S(2)}, u32[]{:S(2)}) collective-permute-start(bf16[4,72,128]{2,1,0:T(8,128)(2,1)S(1)} %pad_maximum_fusion.4), channel_id=1, source_target_pairs={{0,4},{4,0},{8,12},{12,8},{16,20},{20,16},{24,28},{28,24},{1,5},{5... | collective-permute-start | bytes 221192 | tf_op jit(solution)/shard_map/ppermute | solution.py:209
  41.7 12.9 %all-to-all-start = ((bf16[4,8,72,128]{3,2,1,0:T(8,128)(2,1)}), bf16[4,8,72,128]{3,2,1,0:T(8,128)(2,1)S(1)}, u32[]{:S(2)}, u32[]{:S(2)}) async-start(bf16[4,8,72,128]{3,2,1,0:T(8,128)(2,1)} %broadcast_in_dim.16), calls=%async_computation | async-start | bytes 1179648 | tf_op jit(solution)/shard_map/all_to_all | solution.py:24
  52.3 45.4 %copy-start.2 = (bf16[64,1024]{1,0:T(8,128)(2,1)S(1)}, bf16[64,1024]{1,0:T(8,128)(2,1)}, u32[]{:S(2)}) copy-start(bf16[64,1024]{1,0:T(8,128)(2,1)} %pool_ref.3) | copy-start | bytes 393220
  56.4 19.2 %all-to-all-start.2 = ((bf16[16,36,128]{2,1,0:T(8,128)(2,1)}), bf16[16,36,128]{2,1,0:T(8,128)(2,1)S(1)}, u32[]{:S(2)}, u32[]{:S(2)}) async-start(bf16[16,36,128]{2,1,0:T(8,128)(2,1)} %shard_map.57), calls=%async_computation.2 | async-start | bytes 327680 | tf_op jit(solution)/shard_map/all_to_all | solution.py:24
  89.8 40.2 %all-to-all-start.4 = ((bf16[32,72,128]{2,1,0:T(8,128)(2,1)}), bf16[32,72,128]{2,1,0:T(8,128)(2,1)S(1)}, u32[]{:S(2)}, u32[]{:S(2)}) async-start(bf16[32,72,128]{2,1,0:T(8,128)(2,1)} %shard_map.59), calls=%async_computation.4 | async-start | bytes 1179648 | tf_op jit(solution)/shard_map/all_to_all | solution.py:24
  98.0 10.4 %collective-permute-start.4 = (bf16[1,64,512]{2,1,0:T(8,128)(2,1)S(1)}, bf16[1,64,512]{2,1,0:T(8,128)(2,1)S(1)}, u32[]{:S(2)}, u32[]{:S(2)}) collective-permute-start(bf16[1,64,512]{2,1,0:T(8,128)(2,1)S(1)} %shard_map.61), channel_id=1, source_target_pairs={{0,256},{64,320},{128,384},{192,448},{256,0},{320,64},{384,128},{4... | collective-permute-start | bytes 196616 | tf_op jit(solution)/shard_map/ppermute | solution.py:209
  108.5 8.8 %collective-permute-start.5 = (bf16[2,64,512]{2,1,0:T(8,128)(2,1)S(1)}, bf16[2,64,512]{2,1,0:T(8,128)(2,1)S(1)}, u32[]{:S(2)}, u32[]{:S(2)}) collective-permute-start(bf16[2,64,512]{2,1,0:T(8,128)(2,1)S(1)} %pad_maximum_fusion.3), channel_id=1, source_target_pairs={{0,128},{64,192},{128,0},{192,64},{256,384},{320,448},{384,256},{4... | collective-permute-start | bytes 393224 | tf_op jit(solution)/shard_map/ppermute | solution.py:209
  117.3 8.4 %collective-permute-start.6 = (bf16[4,64,512]{2,1,0:T(8,128)(2,1)S(1)}, bf16[4,64,512]{2,1,0:T(8,128)(2,1)S(1)}, u32[]{:S(2)}, u32[]{:S(2)}) collective-permute-start(bf16[4,64,512]{2,1,0:T(8,128)(2,1)S(1)} %pad_maximum_fusion.1), channel_id=1, source_target_pairs={{0,64},{64,0},{128,192},{192,128},{256,320},{320,256},{384,448},{4... | collective-permute-start | bytes 786440 | tf_op jit(solution)/shard_map/ppermute | solution.py:209
  125.8 15.3 %collective-permute-start.7 = (bf16[8,64,512]{2,1,0:T(8,128)(2,1)S(1)}, bf16[8,64,512]{2,1,0:T(8,128)(2,1)S(1)}, u32[]{:S(2)}, u32[]{:S(2)}) collective-permute-start(bf16[8,64,512]{2,1,0:T(8,128)(2,1)S(1)} %pad_maximum_fusion.mine_ref), channel_id=1, source_target_pairs={{0,32},{32,0},{1,33},{33,1},{2,34},{34,2},{3,35},{35,3},{4,36},{36... | collective-permute-start | bytes 1572872 | tf_op jit(solution)/shard_map/ppermute | solution.py:217
  130.9 28.1 %all-to-all-start.5 = ((bf16[32,72,128]{2,1,0:T(8,128)(2,1)}), bf16[32,72,128]{2,1,0:T(8,128)(2,1)S(1)}, u32[]{:S(2)}, u32[]{:S(2)}) async-start(bf16[32,72,128]{2,1,0:T(8,128)(2,1)} %get-tuple-element.13), calls=%async_computation.5 | async-start | bytes 1179648 | tf_op jit(solution)/shard_map/all_to_all | solution.py:24
  160.7 15.0 %all-to-all-start.6 = ((bf16[16,36,128]{2,1,0:T(8,128)(2,1)}), bf16[16,36,128]{2,1,0:T(8,128)(2,1)S(1)}, u32[]{:S(2)}, u32[]{:S(2)}) async-start(bf16[16,36,128]{2,1,0:T(8,128)(2,1)} %shard_map.63), calls=%async_computation.6 | async-start | bytes 327680 | tf_op jit(solution)/shard_map/all_to_all | solution.py:24

commit v5 on v4

--- a/solution.py
+++ b/solution.py
@@ -201,16 +201,23 @@
     return feats.reshape(blocks * 2 * rows, batch), squares[0]
 
 
-def doubled(block, axis):
-    held, offsets = block[None], [0]
-    peers = lax.axis_size(axis)
-    hop = peers // 2
-    while hop:
-        moved = lax.ppermute(held, axis, [(i, i ^ hop) for i in range(peers)])
-        held = jnp.concatenate([held, moved])
+def swap_hops(axis):
+    hops = [lax.axis_size(axis) // 2]
+    while hops[-1] > 1:
+        hops.append(hops[-1] // 2)
+    return hops
+
+
+def swap_offsets(axis):
+    offsets = [0]
+    for hop in swap_hops(axis):
         offsets = offsets + [o ^ hop for o in offsets]
-        hop //= 2
-    return held, offsets
+    return offsets
+
+
+def doubled(held, axis, hop):
+    pairs = [(i, i ^ hop) for i in range(lax.axis_size(axis))]
+    return jnp.concatenate([held, lax.ppermute(held, axis, pairs)])
 
 
 def swapped_cores(array):
@@ -307,34 +314,56 @@
         chosen = lax.dynamic_slice(local_picks[step], (me * own,), (own,))
         return jnp.take(labels, chosen, mode="clip")
 
+    packed = jnp.concatenate([coefs[: classes // 2], coefs[classes // 2 :]], axis=1)
+
     def kernel_matrix(gathered, sample_sq):
         cross = lax.dot_general(
             gathered, centres, (((0,), (0,)), ((), ())), preferred_element_type=jnp.float32
         )
         return laplace(cross, sample_sq, centre_sq, width)
 
-    mine = exchange(picked(pool, picks, 0, lax.axis_size("y")), "y")
-    later, offsets = doubled(picked(pool, picks, 1, 1)[0], "y")
-    kerns = [
-        kernel_matrix(*assembled(mine, swapped_cores(mine))),
-        kernel_matrix(*assembled(later, swapped_cores(later), offsets)),
-    ]
+    held = packed.astype(jnp.bfloat16)[None]
+    held, first_picks = lax.optimization_barrier((held, picks))
+    mine = exchange(picked(pool, first_picks, 0, lax.axis_size("y")), "y")
+    *far, near = swap_hops("z")
+    for hop in far:
+        held = doubled(held, "z", hop)
+    mine, held, centre_sq = lax.optimization_barrier((mine, held, centre_sq))
+    other = swapped_cores(mine)
+    held = doubled(held, "z", near)
+    kern = kernel_matrix(*assembled(mine, other))
     labs = [own_labels(step) for step in range(STEPS)]
 
-    current = jnp.concatenate([coefs[: classes // 2], coefs[classes // 2 :]], axis=1)
-    held, offsets = doubled(current.astype(jnp.bfloat16), "z")
-    coef_parts = spread(held, "x")
-    for step in range(STEPS):
-        if step > 0:
-            coef_parts = exchange(half, SAMPLE).reshape(over_z, over_x, *current.shape)
-            offsets = None
-        arrived = exchange(partial_logits(coef_parts, kerns[step], n_centre, offsets), CENTRE)
-        resid = residual(arrived, labs[step], LOGIT_GAIN / total_centres, fold)
-        arrived = exchange(partial_grad(exchange(resid, CENTRE), kerns[step], n_sample), SAMPLE)
-        if step < STEPS - 1:
-            current, half = updated(arrived, current, rate)
-        else:
-            current = last_updated(arrived, current, rate)
+    logits = partial_logits(spread(held, "x"), kern, n_centre, swap_offsets("z"))
+
+    later = picked(pool, picks, 1, 1)
+    hops = swap_hops("y")
+    gain = LOGIT_GAIN / total_centres
+
+    logits, later = lax.optimization_barrier((logits, later))
+    arrived = exchange(logits, CENTRE)
+    later = doubled(later, "y", hops[0])
+    arrived, later = lax.optimization_barrier((arrived, later))
+    resid = residual(arrived, labs[0], gain, fold)
+    resid, later = lax.optimization_barrier((resid, later))
+    resid = exchange(resid, CENTRE)
+    later = doubled(later, "y", hops[1])
+    resid, later = lax.optimization_barrier((resid, later))
+    grads = partial_grad(resid, kern, n_sample)
+    grads, later = lax.optimization_barrier((grads, later))
+    arrived = exchange(grads, SAMPLE)
+    for hop in hops[2:]:
+        later = doubled(later, "y", hop)
+    other = swapped_cores(later)
+    arrived, later, other = lax.optimization_barrier((arrived, later, other))
+    current, half = updated(arrived, packed, rate)
+
+    kern = kernel_matrix(*assembled(later, other, swap_offsets("y")))
+    coef_parts = exchange(half, SAMPLE).reshape(over_z, over_x, *current.shape)
+    arrived = exchange(partial_logits(coef_parts, kern, n_centre), CENTRE)
+    resid = exchange(residual(arrived, labs[1], gain, fold), CENTRE)
+    arrived = exchange(partial_grad(resid, kern, n_sample), SAMPLE)
+    current = last_updated(arrived, current, rate)
     return jnp.concatenate([current[:, :cen_own], current[:, cen_own:]], axis=0)
 
 

time: 214 us -> 206 us (0.963)
  starting transfers between devices: 76.9 us -> 89.7 us
  blocking collectives: 47.2 us -> 35 us
  waiting for transfers between devices: 56.3 us -> 47.8 us
    all_to_all x3 -> x2, blocking collectives: 47.2 us -> 35 us  [exchange(): return lax.all_to_all(parts, axes, 0, 0, tiled=True)]
    all_to_all x6 -> x7, waiting for transfers between devices: 31.4 us -> 24.3 us  [exchange(): return lax.all_to_all(parts, axes, 0, 0, tiled=True)]
    all_to_all x6 -> x7, starting transfers between devices: 44.3 us -> 50.9 us  [exchange(): return lax.all_to_all(parts, axes, 0, 0, tiled=True)]
    ppermute x6, starting transfers between devices: 24.4 us -> 31 us  [doubled(): return jnp.concatenate([held, lax.ppermute(held, axis, pairs)])]
    ppermute x6, waiting for transfers between devices: 24.9 us -> 22.1 us  [doubled(): return jnp.concatenate([held, lax.ppermute(held, axis, pairs)])]
  transfers between devices with their start and end apart: 14 -> 15, of which waited for: 9 -> 10; matrix products, arithmetic and copies ran while one was open for 9% -> 9% of each run, Pallas kernels for 1% -> 0%
where the time goes in v5:
time: 206 us; the launch traced here: 205 us
  starting transfers between devices  89.7 us (44%)
  waiting for transfers between devices  47.8 us (23%)
  blocking collectives  35 us (17%)
  matrix products  12.9 us (6%)
  Pallas kernels  10 us (5%)
  local copies, waits for them, and re-layouts  6.08 us (3%)
  other arithmetic  3.35 us (2%)
    all_to_all x7, starting transfers between devices, exchange(): return lax.all_to_all(parts, axes, 0, 0, tiled=True)  50.9 us
    all_to_all x2, blocking collectives, exchange(): return lax.all_to_all(parts, axes, 0, 0, tiled=True)  35 us
    ppermute x6, starting transfers between devices, doubled(): return jnp.concatenate([held, lax.ppermute(held, axis, pairs)])  31 us
    all_to_all x7, waiting for transfers between devices, exchange(): return lax.all_to_all(parts, axes, 0, 0, tiled=True)  24.3 us
    ppermute x6, waiting for transfers between devices, doubled(): return jnp.concatenate([held, lax.ppermute(held, axis, pairs)])  22.1 us
    dot_general x2, matrix products, kernel_matrix(): lax.dot_general(gathered, centres, (((0,), (0,)), ((), ())), preferred_el...  12.9 us
    pallas_call x12, Pallas kernels, call(): pl.pallas_call(body, out_shape=out, in_specs=[vmem] * len(operands), out_...  10 us
    ppermute x2, starting transfers between devices, swapped_cores(): return lax.ppermute(array, 'core', [(0, 1), (1, 0)])  7.77 us
  transfers between devices with their start and end apart: 15, of which 10 were waited for; matrix products, arithmetic and copies ran while one was open for 9% of the time, Pallas kernels for 0%

profile of v5, /device:TPU:1, one launch (start us, length us, event | category | flops | bytes accessed | tf_op | source)
XLA Modules:
  0.0 205.3 jit_solution(12680832610362354863)
XLA Ops:
  4.0 7.7 %all-to-all-start = ((bf16[8,64,512]{2,1,0:T(8,128)(2,1)}), bf16[8,64,512]{2,1,0:T(8,128)(2,1)S(1)}, u32[]{:S(2)}, u32[]{:S(2)}) async-start(bf16[8,64,512]{2,1,0:T(8,128)(2,1)} %shard_map.55), calls=%async_computation | async-start | bytes 1048576 | tf_op jit(solution)/shard_map/all_to_all | solution.py:24
  11.7 10.6 %collective-permute-start = (bf16[1,72,128]{2,1,0:T(8,128)(2,1)S(1)}, bf16[1,72,128]{2,1,0:T(8,128)(2,1)S(1)}, u32[]{:S(2)}, u32[]{:S(2)}) collective-permute-start(bf16[1,72,128]{2,1,0:T(8,128)(2,1)S(1)} %pad_maximum_fusion.7), channel_id=1, source_target_pairs={{0,16},{4,20},{8,24},{12,28},{16,0},{20,4},{24,8},{28,12},{1,17},{... | collective-permute-start | bytes 55304 | tf_op jit(solution)/shard_map/ppermute | solution.py:220
  23.5 4.2 %collective-permute-start.1 = (bf16[2,72,128]{2,1,0:T(8,128)(2,1)S(1)}, bf16[2,72,128]{2,1,0:T(8,128)(2,1)S(1)}, u32[]{:S(2)}, u32[]{:S(2)}) collective-permute-start(bf16[2,72,128]{2,1,0:T(8,128)(2,1)S(1)} %pad_maximum_fusion.5), channel_id=1, source_target_pairs={{0,8},{4,12},{8,0},{12,4},{16,24},{20,28},{24,16},{28,20},{1,9},{5... | collective-permute-start | bytes 110600 | tf_op jit(solution)/shard_map/ppermute | solution.py:220
  27.6 3.1 %multiply_reduce_fusion = f32[2048]{0:T(1024)S(1)} fusion(bf16[1024,2048]{1,0:T(8,128)(2,1)} %param.5), kind=kLoop, calls=%fused_computation.2 | loop fusion | flops 6289408 | bytes 4202496 | tf_op jit(solution)/shard_map/reduce_sum | solution.py:311
  30.7 4.0 %collective-permute-start.3 = (bf16[8,64,512]{2,1,0:T(8,128)(2,1)S(1)}, bf16[8,64,512]{2,1,0:T(8,128)(2,1)S(1)}, u32[]{:S(2)}, u32[]{:S(2)}) collective-permute-start(bf16[8,64,512]{2,1,0:T(8,128)(2,1)S(1)} %all-to-all-done.mine_ref), channel_id=1, source_target_pairs={{0,32},{32,0},{1,33},{33,1},{2,34},{34,2},{3,35},{35,3},{4,36},{36... | collective-permute-start | bytes 1572872 | tf_op jit(solution)/shard_map/ppermute | solution.py:224
  41.5 4.0 %all-to-all-start.1 = ((bf16[4,8,72,128]{3,2,1,0:T(8,128)(2,1)}), bf16[4,8,72,128]{3,2,1,0:T(8,128)(2,1)S(1)}, u32[]{:S(2)}, u32[]{:S(2)}) async-start(bf16[4,8,72,128]{3,2,1,0:T(8,128)(2,1)} %broadcast_in_dim.16), calls=%async_computation.1 | async-start | bytes 1179648 | tf_op jit(solution)/shard_map/all_to_all | solution.py:24
  45.7 6.5 %exponential_convert_fusion.1.kern_ref = bf16[512,2048]{1,0:T(8,128)(2,1)S(1)} fusion(bf16[1024,512]{1,0:T(8,128)(2,1)S(1)} %bitcast.19, bf16[1024,2048]{1,0:T(8,128)(2,1)} %param.5, f32[2048]{0:T(1024)S(1)} %multiply_reduce_fusion, f32[512]{0:T(512)S(1)} %bitcast.21), kind=kOutput, calls=%fused_computation.4 | convolution fusion | flops 2155872256 | bytes 7350272 | tf_op jit(solution)/shard_map/dot_general | solution.py:320
  56.2 9.5 %all-to-all-start.2 = ((bf16[16,36,128]{2,1,0:T(8,128)(2,1)}), bf16[16,36,128]{2,1,0:T(8,128)(2,1)S(1)}, u32[]{:S(2)}, u32[]{:S(2)}) async-start(bf16[16,36,128]{2,1,0:T(8,128)(2,1)} %shard_map.57), calls=%async_computation.2 | async-start | bytes 327680 | tf_op jit(solution)/shard_map/all_to_all | solution.py:24
  65.8 7.2 %collective-permute-start.4 = (bf16[1,64,512]{2,1,0:T(8,128)(2,1)S(1)}, bf16[1,64,512]{2,1,0:T(8,128)(2,1)S(1)}, u32[]{:S(2)}, u32[]{:S(2)}) collective-permute-start(bf16[1,64,512]{2,1,0:T(8,128)(2,1)S(1)} %shard_map.58), channel_id=1, source_target_pairs={{0,256},{64,320},{128,384},{192,448},{256,0},{320,64},{384,128},{4... | collective-permute-start | bytes 196616 | tf_op jit(solution)/shard_map/ppermute | solution.py:220
  73.8 3.3 %collective-permute-done.4 = bf16[1,64,512]{2,1,0:T(8,128)(2,1)S(1)} collective-permute-done((bf16[1,64,512]{2,1,0:T(8,128)(2,1)S(1)}, bf16[1,64,512]{2,1,0:T(8,128)(2,1)S(1)}, u32[]{:S(2)}, u32[]{:S(2)}) %collective-permute-start.4) | collective-permute-done | bytes 65568 | tf_op jit(solution)/shard_map/ppermute | solution.py:220
  78.1 7.1 %all-to-all-start.3 = ((bf16[16,36,128]{2,1,0:T(8,128)(2,1)}), bf16[16,36,128]{2,1,0:T(8,128)(2,1)S(1)}, u32[]{:S(2)}, u32[]{:S(2)}) async-start(bf16[16,36,128]{2,1,0:T(8,128)(2,1)} %shard_map.59), calls=%async_computation.3 | async-start | bytes 327680 | tf_op jit(solution)/shard_map/all_to_all | solution.py:24
  85.2 4.2 %collective-permute-start.5 = (bf16[2,64,512]{2,1,0:T(8,128)(2,1)S(1)}, bf16[2,64,512]{2,1,0:T(8,128)(2,1)S(1)}, u32[]{:S(2)}, u32[]{:S(2)}) collective-permute-start(bf16[2,64,512]{2,1,0:T(8,128)(2,1)S(1)} %pad_maximum_fusion.2), channel_id=1, source_target_pairs={{0,128},{64,192},{128,0},{192,64},{256,384},{320,448},{384,256},{4... | collective-permute-start | bytes 393224 | tf_op jit(solution)/shard_map/ppermute | solution.py:220
  89.4 8.4 %collective-permute-done.5 = bf16[2,64,512]{2,1,0:T(8,128)(2,1)S(1)} collective-permute-done((bf16[2,64,512]{2,1,0:T(8,128)(2,1)S(1)}, bf16[2,64,512]{2,1,0:T(8,128)(2,1)S(1)}, u32[]{:S(2)}, u32[]{:S(2)}) %collective-permute-start.5) | collective-permute-done | bytes 131104 | tf_op jit(solution)/shard_map/ppermute | solution.py:220
  99.4 7.9 %all-to-all-start.4 = ((bf16[32,72,128]{2,1,0:T(8,128)(2,1)}), bf16[32,72,128]{2,1,0:T(8,128)(2,1)S(1)}, u32[]{:S(2)}, u32[]{:S(2)}) async-start(bf16[32,72,128]{2,1,0:T(8,128)(2,1)} %shard_map.60), calls=%async_computation.4 | async-start | bytes 1179648 | tf_op jit(solution)/shard_map/all_to_all | solution.py:24
  109.2 6.8 %collective-permute-done.6 = bf16[4,64,512]{2,1,0:T(8,128)(2,1)S(1)} collective-permute-done((bf16[4,64,512]{2,1,0:T(8,128)(2,1)S(1)}, bf16[4,64,512]{2,1,0:T(8,128)(2,1)S(1)}, u32[]{:S(2)}, u32[]{:S(2)}) %collective-permute-start.6) | collective-permute-done | bytes 262176 | tf_op jit(solution)/shard_map/ppermute | solution.py:220
  116.1 3.8 %collective-permute-start.7 = (bf16[8,64,512]{2,1,0:T(8,128)(2,1)S(1)}, bf16[8,64,512]{2,1,0:T(8,128)(2,1)S(1)}, u32[]{:S(2)}, u32[]{:S(2)}) collective-permute-start(bf16[8,64,512]{2,1,0:T(8,128)(2,1)S(1)} %constant_dynamic-update-slice_fusion.mine_ref), channel_id=1, source_target_pairs={{0,32},{32,0},{1,33},{33,1},{2,34},{34,2},{3,35},{35,3},{4,36},{36... | collective-permute-start | bytes 1572872 | tf_op jit(solution)/shard_map/ppermute | solution.py:224
  121.4 3.4 %all-to-all-done.4.arrived_ref = bf16[32,72,128]{2,1,0:T(8,128)(2,1)S(1)} async-done(((bf16[32,72,128]{2,1,0:T(8,128)(2,1)}), bf16[32,72,128]{2,1,0:T(8,128)(2,1)S(1)}, u32[]{:S(2)}, u32[]{:S(2)}) %all-to-all-start.4) | async-done | bytes 589856 | tf_op jit(solution)/shard_map/all_to_all | solution.py:24
  125.7 6.0 %all-to-all-start.5 = ((bf16[32,72,128]{2,1,0:T(8,128)(2,1)}), bf16[32,72,128]{2,1,0:T(8,128)(2,1)S(1)}, u32[]{:S(2)}, u32[]{:S(2)}) async-start(bf16[32,72,128]{2,1,0:T(8,128)(2,1)} %get-tuple-element.47), calls=%async_computation.5 | async-start | bytes 1179648 | tf_op jit(solution)/shard_map/all_to_all | solution.py:24
  131.9 6.5 %exponential_convert_fusion.kern_ref = bf16[512,2048]{1,0:T(8,128)(2,1)S(1)} fusion(bf16[1024,512]{1,0:T(8,128)(2,1)S(1)} %bitcast.18, bf16[1024,2048]{1,0:T(8,128)(2,1)} %param.5, f32[512]{0:T(512)S(1)} %bitcast.20, f32[2048]{0:T(1024)S(1)} %multiply_reduce_fusion), kind=kOutput, calls=%fused_computation.3 | convolution fusion | flops 2155872256 | bytes 7350272 | tf_op jit(solution)/shard_map/dot_general | solution.py:320
  138.4 9.8 %all-to-all-done.5 = bf16[32,72,128]{2,1,0:T(8,128)(2,1)S(1)} async-done(((bf16[32,72,128]{2,1,0:T(8,128)(2,1)}), bf16[32,72,128]{2,1,0:T(8,128)(2,1)S(1)}, u32[]{:S(2)}, u32[]{:S(2)}) %all-to-all-start.5) | async-done | bytes 589856 | tf_op jit(solution)/shard_map/all_to_all | solution.py:24
  149.8 8.7 %all-to-all-start.6 = ((bf16[16,36,128]{2,1,0:T(8,128)(2,1)}), bf16[16,36,128]{2,1,0:T(8,128)(2,1)S(1)}, u32[]{:S(2)}, u32[]{:S(2)}) async-start(bf16[16,36,128]{2,1,0:T(8,128)(2,1)} %shard_map.63), calls=%async_computation.6 | async-start | bytes 327680 | tf_op jit(solution)/shard_map/all_to_all | solution.py:24
  159.3 8.9 %all-to-all-done.6.arrived_ref = bf16[16,36,128]{2,1,0:T(8,128)(2,1)S(1)} async-done(((bf16[16,36,128]{2,1,0:T(8,128)(2,1)}), bf16[16,36,128]{2,1,0:T(8,128)(2,1)S(1)}, u32[]{:S(2)}, u32[]{:S(2)}) %all-to-all-start.6) | async-done | bytes 147488 | tf_op jit(solution)/shard_map/all_to_all | solution.py:24
  168.6 12.3 %all_to_all.45.resid_ref = bf16[16,36,128]{2,1,0:T(8,128)(2,1)S(1)} all-to-all(bf16[16,36,128]{2,1,0:T(8,128)(2,1)S(1)} %shard_map.64), channel_id=1, replica_groups=mesh['y'=8,'core'=2,'z'=8,'x'=4] {'y','core'}, dimensions={0} | all-to-all | bytes 294912 | tf_op jit(solution)/shard_map/all_to_all | solution.py:24
  181.6 22.8 %all_to_all.46.arrived_ref = bf16[32,72,128]{2,1,0:T(8,128)(2,1)S(1)} all-to-all(bf16[32,72,128]{2,1,0:T(8,128)(2,1)S(1)} %shard_map.65), channel_id=1, replica_groups=mesh['y'=8,'core'=2,'z'=8,'x'=4] {'z','x'}, dimensions={0} | all-to-all | bytes 1179648 | tf_op jit(solution)/shard_map/all_to_all | solution.py:24
  (61 shorter events, 28.5 us)
Async XLA Ops:
  0.0 73.0 %copy-start = (s32[1024]{0:T(1024)S(1)}, s32[1024]{0:T(1024)}, u32[]{:S(2)}) copy-start(s32[1024]{0:T(1024)} %param.7) | copy-start | bytes 12292
  0.0 34.7 %copy-start.4 = (s32[2,512]{1,0:T(2,128)S(1)}, s32[2,512]{1,0:T(2,128)}, u32[]{:S(2)}) copy-start(s32[2,512]{1,0:T(2,128)} %picks_ref.2) | copy-start | bytes 12292
  0.0 37.7 %copy-start.2 = (bf16[64,1024]{1,0:T(8,128)(2,1)S(1)}, bf16[64,1024]{1,0:T(8,128)(2,1)}, u32[]{:S(2)}) copy-start(bf16[64,1024]{1,0:T(8,128)(2,1)} %pool_ref.3) | copy-start | bytes 393220
  1.3 0.9 copy-start.1
  2.2 0.7 copy-start.3
  4.0 26.7 %all-to-all-start = ((bf16[8,64,512]{2,1,0:T(8,128)(2,1)}), bf16[8,64,512]{2,1,0:T(8,128)(2,1)S(1)}, u32[]{:S(2)}, u32[]{:S(2)}) async-start(bf16[8,64,512]{2,1,0:T(8,128)(2,1)} %shard_map.55), calls=%async_computation | async-start | bytes 1048576 | tf_op jit(solution)/shard_map/all_to_all | solution.py:24
  11.7 11.8 %collective-permute-start = (bf16[1,72,128]{2,1,0:T(8,128)(2,1)S(1)}, bf16[1,72,128]{2,1,0:T(8,128)(2,1)S(1)}, u32[]{:S(2)}, u32[]{:S(2)}) collective-permute-start(bf16[1,72,128]{2,1,0:T(8,128)(2,1)S(1)} %pad_maximum_fusion.7), channel_id=1, source_target_pairs={{0,16},{4,20},{8,24},{12,28},{16,0},{20,4},{24,8},{28,12},{1,17},{... | collective-permute-start | bytes 55304 | tf_op jit(solution)/shard_map/ppermute | solution.py:220
  23.5 7.3 %collective-permute-start.1 = (bf16[2,72,128]{2,1,0:T(8,128)(2,1)S(1)}, bf16[2,72,128]{2,1,0:T(8,128)(2,1)S(1)}, u32[]{:S(2)}, u32[]{:S(2)}) collective-permute-start(bf16[2,72,128]{2,1,0:T(8,128)(2,1)S(1)} %pad_maximum_fusion.5), channel_id=1, source_target_pairs={{0,8},{4,12},{8,0},{12,4},{16,24},{20,28},{24,16},{28,20},{1,9},{5... | collective-permute-start | bytes 110600 | tf_op jit(solution)/shard_map/ppermute | solution.py:220
  30.7 14.8 %collective-permute-start.3 = (bf16[8,64,512]{2,1,0:T(8,128)(2,1)S(1)}, bf16[8,64,512]{2,1,0:T(8,128)(2,1)S(1)}, u32[]{:S(2)}, u32[]{:S(2)}) collective-permute-start(bf16[8,64,512]{2,1,0:T(8,128)(2,1)S(1)} %all-to-all-done.mine_ref), channel_id=1, source_target_pairs={{0,32},{32,0},{1,33},{33,1},{2,34},{34,2},{3,35},{35,3},{4,36},{36... | collective-permute-start | bytes 1572872 | tf_op jit(solution)/shard_map/ppermute | solution.py:224
  34.8 5.8 %collective-permute-start.2 = (bf16[4,72,128]{2,1,0:T(8,128)(2,1)S(1)}, bf16[4,72,128]{2,1,0:T(8,128)(2,1)S(1)}, u32[]{:S(2)}, u32[]{:S(2)}) collective-permute-start(bf16[4,72,128]{2,1,0:T(8,128)(2,1)S(1)} %pad_maximum_fusion.3), channel_id=1, source_target_pairs={{0,4},{4,0},{8,12},{12,8},{16,20},{20,16},{24,28},{28,24},{1,5},{5... | collective-permute-start | bytes 221192 | tf_op jit(solution)/shard_map/ppermute | solution.py:220
  41.5 12.9 %all-to-all-start.1 = ((bf16[4,8,72,128]{3,2,1,0:T(8,128)(2,1)}), bf16[4,8,72,128]{3,2,1,0:T(8,128)(2,1)S(1)}, u32[]{:S(2)}, u32[]{:S(2)}) async-start(bf16[4,8,72,128]{3,2,1,0:T(8,128)(2,1)} %broadcast_in_dim.16), calls=%async_computation.1 | async-start | bytes 1179648 | tf_op jit(solution)/shard_map/all_to_all | solution.py:24
  56.2 20.9 %all-to-all-start.2 = ((bf16[16,36,128]{2,1,0:T(8,128)(2,1)}), bf16[16,36,128]{2,1,0:T(8,128)(2,1)S(1)}, u32[]{:S(2)}, u32[]{:S(2)}) async-start(bf16[16,36,128]{2,1,0:T(8,128)(2,1)} %shard_map.57), calls=%async_computation.2 | async-start | bytes 327680 | tf_op jit(solution)/shard_map/all_to_all | solution.py:24
  65.8 11.3 %collective-permute-start.4 = (bf16[1,64,512]{2,1,0:T(8,128)(2,1)S(1)}, bf16[1,64,512]{2,1,0:T(8,128)(2,1)S(1)}, u32[]{:S(2)}, u32[]{:S(2)}) collective-permute-start(bf16[1,64,512]{2,1,0:T(8,128)(2,1)S(1)} %shard_map.58), channel_id=1, source_target_pairs={{0,256},{64,320},{128,384},{192,448},{256,0},{320,64},{384,128},{4... | collective-permute-start | bytes 196616 | tf_op jit(solution)/shard_map/ppermute | solution.py:220
  78.1 19.7 %all-to-all-start.3 = ((bf16[16,36,128]{2,1,0:T(8,128)(2,1)}), bf16[16,36,128]{2,1,0:T(8,128)(2,1)S(1)}, u32[]{:S(2)}, u32[]{:S(2)}) async-start(bf16[16,36,128]{2,1,0:T(8,128)(2,1)} %shard_map.59), calls=%async_computation.3 | async-start | bytes 327680 | tf_op jit(solution)/shard_map/all_to_all | solution.py:24
  85.2 12.6 %collective-permute-start.5 = (bf16[2,64,512]{2,1,0:T(8,128)(2,1)S(1)}, bf16[2,64,512]{2,1,0:T(8,128)(2,1)S(1)}, u32[]{:S(2)}, u32[]{:S(2)}) collective-permute-start(bf16[2,64,512]{2,1,0:T(8,128)(2,1)S(1)} %pad_maximum_fusion.2), channel_id=1, source_target_pairs={{0,128},{64,192},{128,0},{192,64},{256,384},{320,448},{384,256},{4... | collective-permute-start | bytes 393224 | tf_op jit(solution)/shard_map/ppermute | solution.py:220
  99.4 25.4 %all-to-all-start.4 = ((bf16[32,72,128]{2,1,0:T(8,128)(2,1)}), bf16[32,72,128]{2,1,0:T(8,128)(2,1)S(1)}, u32[]{:S(2)}, u32[]{:S(2)}) async-start(bf16[32,72,128]{2,1,0:T(8,128)(2,1)} %shard_map.60), calls=%async_computation.4 | async-start | bytes 1179648 | tf_op jit(solution)/shard_map/all_to_all | solution.py:24
  107.3 8.8 %collective-permute-start.6 = (bf16[4,64,512]{2,1,0:T(8,128)(2,1)S(1)}, bf16[4,64,512]{2,1,0:T(8,128)(2,1)S(1)}, u32[]{:S(2)}, u32[]{:S(2)}) collective-permute-start(bf16[4,64,512]{2,1,0:T(8,128)(2,1)S(1)} %pad_maximum_fusion), channel_id=1, source_target_pairs={{0,64},{64,0},{128,192},{192,128},{256,320},{320,256},{384,448},{4... | collective-permute-start | bytes 786440 | tf_op jit(solution)/shard_map/ppermute | solution.py:220
  116.1 5.3 %collective-permute-start.7 = (bf16[8,64,512]{2,1,0:T(8,128)(2,1)S(1)}, bf16[8,64,512]{2,1,0:T(8,128)(2,1)S(1)}, u32[]{:S(2)}, u32[]{:S(2)}) collective-permute-start(bf16[8,64,512]{2,1,0:T(8,128)(2,1)S(1)} %constant_dynamic-update-slice_fusion.mine_ref), channel_id=1, source_target_pairs={{0,32},{32,0},{1,33},{33,1},{2,34},{34,2},{3,35},{35,3},{4,36},{36... | collective-permute-start | bytes 1572872 | tf_op jit(solution)/shard_map/ppermute | solution.py:224
  125.7 22.4 %all-to-all-start.5 = ((bf16[32,72,128]{2,1,0:T(8,128)(2,1)}), bf16[32,72,128]{2,1,0:T(8,128)(2,1)S(1)}, u32[]{:S(2)}, u32[]{:S(2)}) async-start(bf16[32,72,128]{2,1,0:T(8,128)(2,1)} %get-tuple-element.47), calls=%async_computation.5 | async-start | bytes 1179648 | tf_op jit(solution)/shard_map/all_to_all | solution.py:24
  149.8 18.4 %all-to-all-start.6 = ((bf16[16,36,128]{2,1,0:T(8,128)(2,1)}), bf16[16,36,128]{2,1,0:T(8,128)(2,1)S(1)}, u32[]{:S(2)}, u32[]{:S(2)}) async-start(bf16[16,36,128]{2,1,0:T(8,128)(2,1)} %shard_map.63), calls=%async_computation.6 | async-start | bytes 327680 | tf_op jit(solution)/shard_map/all_to_all | solution.py:24

commit v6 on v5

--- a/solution.py
+++ b/solution.py
@@ -201,16 +201,9 @@
     return feats.reshape(blocks * 2 * rows, batch), squares[0]
 
 
-def swap_hops(axis):
-    hops = [lax.axis_size(axis) // 2]
-    while hops[-1] > 1:
-        hops.append(hops[-1] // 2)
-    return hops
-
-
-def swap_offsets(axis):
+def swap_offsets(hops):
     offsets = [0]
-    for hop in swap_hops(axis):
+    for hop in hops:
         offsets = offsets + [o ^ hop for o in offsets]
     return offsets
 
@@ -322,43 +315,32 @@
         )
         return laplace(cross, sample_sq, centre_sq, width)
 
-    held = packed.astype(jnp.bfloat16)[None]
-    held, first_picks = lax.optimization_barrier((held, picks))
-    mine = exchange(picked(pool, first_picks, 0, lax.axis_size("y")), "y")
-    *far, near = swap_hops("z")
-    for hop in far:
+    z_hops = [1 << i for i in range(over_z.bit_length() - 1)]
+    y_hops = [1 << i for i in reversed(range(lax.axis_size("y").bit_length() - 1))]
+    held = doubled(packed.astype(jnp.bfloat16)[None], "z", z_hops[0])
+    mine = picked(pool, picks, 0, lax.axis_size("y"))
+    mine, held = lax.optimization_barrier((mine, held))
+    mine = exchange(mine, "y")
+    for hop in z_hops[1:]:
         held = doubled(held, "z", hop)
-    mine, held, centre_sq = lax.optimization_barrier((mine, held, centre_sq))
-    other = swapped_cores(mine)
-    held = doubled(held, "z", near)
-    kern = kernel_matrix(*assembled(mine, other))
+    later = doubled(picked(pool, picks, 1, 1), "y", y_hops[0])
+    mine, held, later, centre_sq = lax.optimization_barrier((mine, held, later, centre_sq))
+    coef_parts = spread(held, "x")
+    kern = kernel_matrix(*assembled(mine, swapped_cores(mine)))
     labs = [own_labels(step) for step in range(STEPS)]
 
-    logits = partial_logits(spread(held, "x"), kern, n_centre, swap_offsets("z"))
-
-    later = picked(pool, picks, 1, 1)
-    hops = swap_hops("y")
     gain = LOGIT_GAIN / total_centres
-
-    logits, later = lax.optimization_barrier((logits, later))
-    arrived = exchange(logits, CENTRE)
-    later = doubled(later, "y", hops[0])
-    arrived, later = lax.optimization_barrier((arrived, later))
-    resid = residual(arrived, labs[0], gain, fold)
-    resid, later = lax.optimization_barrier((resid, later))
-    resid = exchange(resid, CENTRE)
-    later = doubled(later, "y", hops[1])
-    resid, later = lax.optimization_barrier((resid, later))
+    logits = partial_logits(coef_parts, kern, n_centre, swap_offsets(z_hops))
+    resid = exchange(residual(exchange(logits, CENTRE), labs[0], gain, fold), CENTRE)
     grads = partial_grad(resid, kern, n_sample)
     grads, later = lax.optimization_barrier((grads, later))
     arrived = exchange(grads, SAMPLE)
-    for hop in hops[2:]:
+    for hop in y_hops[1:]:
         later = doubled(later, "y", hop)
-    other = swapped_cores(later)
-    arrived, later, other = lax.optimization_barrier((arrived, later, other))
+    arrived, later = lax.optimization_barrier((arrived, later))
     current, half = updated(arrived, packed, rate)
 
-    kern = kernel_matrix(*assembled(later, other, swap_offsets("y")))
+    kern = kernel_matrix(*assembled(later, swapped_cores(later), swap_offsets(y_hops)))
     coef_parts = exchange(half, SAMPLE).reshape(over_z, over_x, *current.shape)
     arrived = exchange(partial_logits(coef_parts, kern, n_centre), CENTRE)
     resid = exchange(residual(arrived, labs[1], gain, fold), CENTRE)

time: 206 us -> 208 us (level)
  starting transfers between devices: 89.7 us -> 75.9 us
  blocking collectives: 35 us -> 47.1 us
  waiting for transfers between devices: 47.8 us -> 50.4 us
    all_to_all x7 -> x6, starting transfers between devices: 50.9 us -> 37.7 us  [exchange(): return lax.all_to_all(parts, axes, 0, 0, tiled=True)]
    all_to_all x2 -> x3, blocking collectives: 35 us -> 47.1 us  [exchange(): return lax.all_to_all(parts, axes, 0, 0, tiled=True)]
    all_to_all x7 -> x6, waiting for transfers between devices: 24.3 us -> 32.8 us  [exchange(): return lax.all_to_all(parts, axes, 0, 0, tiled=True)]
    ppermute x6, waiting for transfers between devices: 22.1 us -> 17.7 us  [doubled(): return jnp.concatenate([held, lax.ppermute(held, axis, pairs)])]
  transfers between devices with their start and end apart: 15 -> 14, of which waited for: 10 -> 7; matrix products, arithmetic and copies ran while one was open for 9% -> 9% of each run, Pallas kernels for 0% -> 1%
where the time goes in v6:
time: 208 us; the launch traced here: 207 us
  starting transfers between devices  75.9 us (36%)
  waiting for transfers between devices  50.4 us (24%)
  blocking collectives  47.1 us (23%)
  matrix products  12.9 us (6%)
  Pallas kernels  9.34 us (4%)
  local copies, waits for them, and re-layouts  7.61 us (4%)
  other arithmetic  3.48 us (2%)
    all_to_all x3, blocking collectives, exchange(): return lax.all_to_all(parts, axes, 0, 0, tiled=True)  47.1 us
    all_to_all x6, starting transfers between devices, exchange(): return lax.all_to_all(parts, axes, 0, 0, tiled=True)  37.7 us
    all_to_all x6, waiting for transfers between devices, exchange(): return lax.all_to_all(parts, axes, 0, 0, tiled=True)  32.8 us
    ppermute x6, starting transfers between devices, doubled(): return jnp.concatenate([held, lax.ppermute(held, axis, pairs)])  30 us
    ppermute x6, waiting for transfers between devices, doubled(): return jnp.concatenate([held, lax.ppermute(held, axis, pairs)])  17.7 us
    dot_general x2, matrix products, kernel_matrix(): lax.dot_general(gathered, centres, (((0,), (0,)), ((), ())), preferred_el...  12.9 us
    pallas_call x12, Pallas kernels, call(): pl.pallas_call(body, out_shape=out, in_specs=[vmem] * len(operands), out_...  9.34 us
    ppermute x2, starting transfers between devices, swapped_cores(): return lax.ppermute(array, 'core', [(0, 1), (1, 0)])  8.14 us
  transfers between devices with their start and end apart: 14, of which 7 were waited for; matrix products, arithmetic and copies ran while one was open for 9% of the time, Pallas kernels for 1%

profile of v6, /device:TPU:1, one launch (start us, length us, event | category | flops | bytes accessed | tf_op | source)
XLA Modules:
  0.0 207.0 jit_solution(16756406925000513744)
XLA Ops:
  1.3 4.8 %collective-permute-start = (bf16[1,72,128]{2,1,0:T(8,128)(2,1)S(1)}, bf16[1,72,128]{2,1,0:T(8,128)(2,1)S(1)}, u32[]{:S(2)}, u32[]{:S(2)}) collective-permute-start(bf16[1,72,128]{2,1,0:T(8,128)(2,1)S(1)} %pad_maximum_fusion.8), channel_id=1, source_target_pairs={{0,4},{4,0},{8,12},{12,8},{16,20},{20,16},{24,28},{28,24},{1,5},{5... | collective-permute-start | bytes 55304 | tf_op jit(solution)/shard_map/ppermute | solution.py:213
  8.9 6.8 %all-to-all-start = ((bf16[8,64,512]{2,1,0:T(8,128)(2,1)}), bf16[8,64,512]{2,1,0:T(8,128)(2,1)S(1)}, u32[]{:S(2)}, u32[]{:S(2)}) async-start(bf16[8,64,512]{2,1,0:T(8,128)(2,1)} %shard_map.55), calls=%async_computation | async-start | bytes 1048576 | tf_op jit(solution)/shard_map/all_to_all | solution.py:24
  17.6 7.3 %collective-permute-start.3 = (bf16[1,64,512]{2,1,0:T(8,128)(2,1)S(1)}, bf16[1,64,512]{2,1,0:T(8,128)(2,1)S(1)}, u32[]{:S(2)}, u32[]{:S(2)}) collective-permute-start(bf16[1,64,512]{2,1,0:T(8,128)(2,1)S(1)} %shard_map.56), channel_id=1, source_target_pairs={{0,256},{64,320},{128,384},{192,448},{256,0},{320,64},{384,128},{4... | collective-permute-start | bytes 196616 | tf_op jit(solution)/shard_map/ppermute | solution.py:213
  24.9 5.8 %collective-permute-start.1 = (bf16[2,72,128]{2,1,0:T(8,128)(2,1)S(1)}, bf16[2,72,128]{2,1,0:T(8,128)(2,1)S(1)}, u32[]{:S(2)}, u32[]{:S(2)}) collective-permute-start(bf16[2,72,128]{2,1,0:T(8,128)(2,1)S(1)} %pad_maximum_fusion.6), channel_id=1, source_target_pairs={{0,8},{4,12},{8,0},{12,4},{16,24},{20,28},{24,16},{28,20},{1,9},{5... | collective-permute-start | bytes 110600 | tf_op jit(solution)/shard_map/ppermute | solution.py:213
  30.7 3.1 %multiply_reduce_fusion = f32[2048]{0:T(1024)S(1)} fusion(bf16[1024,2048]{1,0:T(8,128)(2,1)} %param.5), kind=kLoop, calls=%fused_computation.2 | loop fusion | flops 6289408 | bytes 4202496 | tf_op jit(solution)/shard_map/reduce_sum | solution.py:304
  33.8 7.9 %collective-permute-start.2 = (bf16[4,72,128]{2,1,0:T(8,128)(2,1)S(1)}, bf16[4,72,128]{2,1,0:T(8,128)(2,1)S(1)}, u32[]{:S(2)}, u32[]{:S(2)}) collective-permute-start(bf16[4,72,128]{2,1,0:T(8,128)(2,1)S(1)} %pad_maximum_fusion.4), channel_id=1, source_target_pairs={{0,16},{4,20},{8,24},{12,28},{16,0},{20,4},{24,8},{28,12},{1,17},{... | collective-permute-start | bytes 221192 | tf_op jit(solution)/shard_map/ppermute | solution.py:213
  43.5 5.0 %collective-permute-start.4 = (bf16[8,64,512]{2,1,0:T(8,128)(2,1)S(1)}, bf16[8,64,512]{2,1,0:T(8,128)(2,1)S(1)}, u32[]{:S(2)}, u32[]{:S(2)}) collective-permute-start(bf16[8,64,512]{2,1,0:T(8,128)(2,1)S(1)} %all-to-all-done.mine_ref), channel_id=1, source_target_pairs={{0,32},{32,0},{1,33},{33,1},{2,34},{34,2},{3,35},{35,3},{4,36},{36... | collective-permute-start | bytes 1572872 | tf_op jit(solution)/shard_map/ppermute | solution.py:217
  49.4 4.0 %all-to-all-start.1 = ((bf16[4,8,72,128]{3,2,1,0:T(8,128)(2,1)}), bf16[4,8,72,128]{3,2,1,0:T(8,128)(2,1)S(1)}, u32[]{:S(2)}, u32[]{:S(2)}) async-start(bf16[4,8,72,128]{3,2,1,0:T(8,128)(2,1)} %broadcast_in_dim.16), calls=%async_computation.1 | async-start | bytes 1179648 | tf_op jit(solution)/shard_map/all_to_all | solution.py:24
  53.6 6.5 %exponential_convert_fusion.1.kern_ref = bf16[512,2048]{1,0:T(8,128)(2,1)S(1)} fusion(bf16[1024,512]{1,0:T(8,128)(2,1)S(1)} %bitcast.19, bf16[1024,2048]{1,0:T(8,128)(2,1)} %param.5, f32[2048]{0:T(1024)S(1)} %multiply_reduce_fusion, f32[512]{0:T(512)S(1)} %bitcast.21), kind=kOutput, calls=%fused_computation.4 | convolution fusion | flops 2155872256 | bytes 7350272 | tf_op jit(solution)/shard_map/dot_general | solution.py:313
  60.1 3.4 %all-to-all-done.1.coef_ref = bf16[4,8,72,128]{3,2,1,0:T(8,128)(2,1)S(1)} async-done(((bf16[4,8,72,128]{3,2,1,0:T(8,128)(2,1)}), bf16[4,8,72,128]{3,2,1,0:T(8,128)(2,1)S(1)}, u32[]{:S(2)}, u32[]{:S(2)}) %all-to-all-start.1) | async-done | bytes 589856 | tf_op jit(solution)/shard_map/all_to_all | solution.py:24
  65.4 4.4 %all-to-all-start.2 = ((bf16[16,36,128]{2,1,0:T(8,128)(2,1)}), bf16[16,36,128]{2,1,0:T(8,128)(2,1)S(1)}, u32[]{:S(2)}, u32[]{:S(2)}) async-start(bf16[16,36,128]{2,1,0:T(8,128)(2,1)} %shard_map.58), calls=%async_computation.2 | async-start | bytes 327680 | tf_op jit(solution)/shard_map/all_to_all | solution.py:24
  70.6 9.0 %all-to-all-done.2.arrived_ref = bf16[16,36,128]{2,1,0:T(8,128)(2,1)S(1)} async-done(((bf16[16,36,128]{2,1,0:T(8,128)(2,1)}), bf16[16,36,128]{2,1,0:T(8,128)(2,1)S(1)}, u32[]{:S(2)}, u32[]{:S(2)}) %all-to-all-start.2) | async-done | bytes 147488 | tf_op jit(solution)/shard_map/all_to_all | solution.py:24
  80.0 12.1 %all_to_all.45.resid_ref = bf16[16,36,128]{2,1,0:T(8,128)(2,1)S(1)} all-to-all(bf16[16,36,128]{2,1,0:T(8,128)(2,1)S(1)} %shard_map.59), channel_id=1, replica_groups=mesh['y'=8,'core'=2,'z'=8,'x'=4] {'y','core'}, dimensions={0} | all-to-all | bytes 294912 | tf_op jit(solution)/shard_map/all_to_all | solution.py:24
  93.6 8.0 %all-to-all-start.4 = ((bf16[32,72,128]{2,1,0:T(8,128)(2,1)}), bf16[32,72,128]{2,1,0:T(8,128)(2,1)S(1)}, u32[]{:S(2)}, u32[]{:S(2)}) async-start(bf16[32,72,128]{2,1,0:T(8,128)(2,1)} %shard_map.60), calls=%async_computation.4 | async-start | bytes 1179648 | tf_op jit(solution)/shard_map/all_to_all | solution.py:24
  103.9 8.5 %collective-permute-done.5 = bf16[2,64,512]{2,1,0:T(8,128)(2,1)S(1)} collective-permute-done((bf16[2,64,512]{2,1,0:T(8,128)(2,1)S(1)}, bf16[2,64,512]{2,1,0:T(8,128)(2,1)S(1)}, u32[]{:S(2)}, u32[]{:S(2)}) %collective-permute-start.5) | collective-permute-done | bytes 131104 | tf_op jit(solution)/shard_map/ppermute | solution.py:213
  114.4 7.4 %collective-permute-done.6 = bf16[4,64,512]{2,1,0:T(8,128)(2,1)S(1)} collective-permute-done((bf16[4,64,512]{2,1,0:T(8,128)(2,1)S(1)}, bf16[4,64,512]{2,1,0:T(8,128)(2,1)S(1)}, u32[]{:S(2)}, u32[]{:S(2)}) %collective-permute-start.6) | collective-permute-done | bytes 262176 | tf_op jit(solution)/shard_map/ppermute | solution.py:213
  121.9 3.2 %collective-permute-start.7 = (bf16[8,64,512]{2,1,0:T(8,128)(2,1)S(1)}, bf16[8,64,512]{2,1,0:T(8,128)(2,1)S(1)}, u32[]{:S(2)}, u32[]{:S(2)}) collective-permute-start(bf16[8,64,512]{2,1,0:T(8,128)(2,1)S(1)} %pad_maximum_fusion.mine_ref), channel_id=1, source_target_pairs={{0,32},{32,0},{1,33},{33,1},{2,34},{34,2},{3,35},{35,3},{4,36},{36... | collective-permute-start | bytes 1572872 | tf_op jit(solution)/shard_map/ppermute | solution.py:217
  126.1 9.4 %all-to-all-start.5 = ((bf16[32,72,128]{2,1,0:T(8,128)(2,1)}), bf16[32,72,128]{2,1,0:T(8,128)(2,1)S(1)}, u32[]{:S(2)}, u32[]{:S(2)}) async-start(bf16[32,72,128]{2,1,0:T(8,128)(2,1)} %get-tuple-element.32), calls=%async_computation.5 | async-start | bytes 1179648 | tf_op jit(solution)/shard_map/all_to_all | solution.py:24
  135.7 6.5 %exponential_convert_fusion.kern_ref = bf16[512,2048]{1,0:T(8,128)(2,1)S(1)} fusion(bf16[1024,512]{1,0:T(8,128)(2,1)S(1)} %bitcast.18, bf16[1024,2048]{1,0:T(8,128)(2,1)} %param.5, f32[512]{0:T(512)S(1)} %bitcast.20, f32[2048]{0:T(1024)S(1)} %multiply_reduce_fusion), kind=kOutput, calls=%fused_computation.3 | convolution fusion | flops 2155872256 | bytes 7350272 | tf_op jit(solution)/shard_map/dot_general | solution.py:313
  142.1 11.3 %all-to-all-done.5 = bf16[32,72,128]{2,1,0:T(8,128)(2,1)S(1)} async-done(((bf16[32,72,128]{2,1,0:T(8,128)(2,1)}), bf16[32,72,128]{2,1,0:T(8,128)(2,1)S(1)}, u32[]{:S(2)}, u32[]{:S(2)}) %all-to-all-start.5) | async-done | bytes 589856 | tf_op jit(solution)/shard_map/all_to_all | solution.py:24
  155.1 5.1 %all-to-all-start.6 = ((bf16[16,36,128]{2,1,0:T(8,128)(2,1)}), bf16[16,36,128]{2,1,0:T(8,128)(2,1)S(1)}, u32[]{:S(2)}, u32[]{:S(2)}) async-start(bf16[16,36,128]{2,1,0:T(8,128)(2,1)} %shard_map.63), calls=%async_computation.6 | async-start | bytes 327680 | tf_op jit(solution)/shard_map/all_to_all | solution.py:24
  160.9 9.1 %all-to-all-done.6.arrived_ref = bf16[16,36,128]{2,1,0:T(8,128)(2,1)S(1)} async-done(((bf16[16,36,128]{2,1,0:T(8,128)(2,1)}), bf16[16,36,128]{2,1,0:T(8,128)(2,1)S(1)}, u32[]{:S(2)}, u32[]{:S(2)}) %all-to-all-start.6) | async-done | bytes 147488 | tf_op jit(solution)/shard_map/all_to_all | solution.py:24
  170.4 12.1 %all_to_all.46.resid_ref = bf16[16,36,128]{2,1,0:T(8,128)(2,1)S(1)} all-to-all(bf16[16,36,128]{2,1,0:T(8,128)(2,1)S(1)} %shard_map.64), channel_id=1, replica_groups=mesh['y'=8,'core'=2,'z'=8,'x'=4] {'y','core'}, dimensions={0} | all-to-all | bytes 294912 | tf_op jit(solution)/shard_map/all_to_all | solution.py:24
  183.2 22.9 %all_to_all.47.arrived_ref = bf16[32,72,128]{2,1,0:T(8,128)(2,1)S(1)} all-to-all(bf16[32,72,128]{2,1,0:T(8,128)(2,1)S(1)} %shard_map.65), channel_id=1, replica_groups=mesh['y'=8,'core'=2,'z'=8,'x'=4] {'z','x'}, dimensions={0} | all-to-all | bytes 1179648 | tf_op jit(solution)/shard_map/all_to_all | solution.py:24
  (61 shorter events, 23.3 us)
Async XLA Ops:
  0.0 69.9 %copy-start = (s32[1024]{0:T(1024)S(1)}, s32[1024]{0:T(1024)}, u32[]{:S(2)}) copy-start(s32[1024]{0:T(1024)} %param.7) | copy-start | bytes 12292
  0.0 48.5 %copy-start.5 = (s32[2,512]{1,0:T(2,128)S(1)}, s32[2,512]{1,0:T(2,128)}, u32[]{:S(2)}) copy-start(s32[2,512]{1,0:T(2,128)} %picks_ref.3) | copy-start | bytes 12292
  1.3 7.6 %collective-permute-start = (bf16[1,72,128]{2,1,0:T(8,128)(2,1)S(1)}, bf16[1,72,128]{2,1,0:T(8,128)(2,1)S(1)}, u32[]{:S(2)}, u32[]{:S(2)}) collective-permute-start(bf16[1,72,128]{2,1,0:T(8,128)(2,1)S(1)} %pad_maximum_fusion.8), channel_id=1, source_target_pairs={{0,4},{4,0},{8,12},{12,8},{16,20},{20,16},{24,28},{28,24},{1,5},{5... | collective-permute-start | bytes 55304 | tf_op jit(solution)/shard_map/ppermute | solution.py:213
  6.1 0.9 copy-start.1
  7.0 0.7 copy-start.3
  8.9 34.6 %all-to-all-start = ((bf16[8,64,512]{2,1,0:T(8,128)(2,1)}), bf16[8,64,512]{2,1,0:T(8,128)(2,1)S(1)}, u32[]{:S(2)}, u32[]{:S(2)}) async-start(bf16[8,64,512]{2,1,0:T(8,128)(2,1)} %shard_map.55), calls=%async_computation | async-start | bytes 1048576 | tf_op jit(solution)/shard_map/all_to_all | solution.py:24
  15.7 0.9 copy-start.2
  16.6 0.7 copy-start.4
  17.6 24.1 %collective-permute-start.3 = (bf16[1,64,512]{2,1,0:T(8,128)(2,1)S(1)}, bf16[1,64,512]{2,1,0:T(8,128)(2,1)S(1)}, u32[]{:S(2)}, u32[]{:S(2)}) collective-permute-start(bf16[1,64,512]{2,1,0:T(8,128)(2,1)S(1)} %shard_map.56), channel_id=1, source_target_pairs={{0,256},{64,320},{128,384},{192,448},{256,0},{320,64},{384,128},{4... | collective-permute-start | bytes 196616 | tf_op jit(solution)/shard_map/ppermute | solution.py:213
  24.9 8.9 %collective-permute-start.1 = (bf16[2,72,128]{2,1,0:T(8,128)(2,1)S(1)}, bf16[2,72,128]{2,1,0:T(8,128)(2,1)S(1)}, u32[]{:S(2)}, u32[]{:S(2)}) collective-permute-start(bf16[2,72,128]{2,1,0:T(8,128)(2,1)S(1)} %pad_maximum_fusion.6), channel_id=1, source_target_pairs={{0,8},{4,12},{8,0},{12,4},{16,24},{20,28},{24,16},{28,20},{1,9},{5... | collective-permute-start | bytes 110600 | tf_op jit(solution)/shard_map/ppermute | solution.py:213
  33.8 9.7 %collective-permute-start.2 = (bf16[4,72,128]{2,1,0:T(8,128)(2,1)S(1)}, bf16[4,72,128]{2,1,0:T(8,128)(2,1)S(1)}, u32[]{:S(2)}, u32[]{:S(2)}) collective-permute-start(bf16[4,72,128]{2,1,0:T(8,128)(2,1)S(1)} %pad_maximum_fusion.4), channel_id=1, source_target_pairs={{0,16},{4,20},{8,24},{12,28},{16,0},{20,4},{24,8},{28,12},{1,17},{... | collective-permute-start | bytes 221192 | tf_op jit(solution)/shard_map/ppermute | solution.py:213
  43.5 9.9 %collective-permute-start.4 = (bf16[8,64,512]{2,1,0:T(8,128)(2,1)S(1)}, bf16[8,64,512]{2,1,0:T(8,128)(2,1)S(1)}, u32[]{:S(2)}, u32[]{:S(2)}) collective-permute-start(bf16[8,64,512]{2,1,0:T(8,128)(2,1)S(1)} %all-to-all-done.mine_ref), channel_id=1, source_target_pairs={{0,32},{32,0},{1,33},{33,1},{2,34},{34,2},{3,35},{35,3},{4,36},{36... | collective-permute-start | bytes 1572872 | tf_op jit(solution)/shard_map/ppermute | solution.py:217
  49.4 14.0 %all-to-all-start.1 = ((bf16[4,8,72,128]{3,2,1,0:T(8,128)(2,1)}), bf16[4,8,72,128]{3,2,1,0:T(8,128)(2,1)S(1)}, u32[]{:S(2)}, u32[]{:S(2)}) async-start(bf16[4,8,72,128]{3,2,1,0:T(8,128)(2,1)} %broadcast_in_dim.16), calls=%async_computation.1 | async-start | bytes 1179648 | tf_op jit(solution)/shard_map/all_to_all | solution.py:24
  65.4 14.3 %all-to-all-start.2 = ((bf16[16,36,128]{2,1,0:T(8,128)(2,1)}), bf16[16,36,128]{2,1,0:T(8,128)(2,1)S(1)}, u32[]{:S(2)}, u32[]{:S(2)}) async-start(bf16[16,36,128]{2,1,0:T(8,128)(2,1)} %shard_map.58), calls=%async_computation.2 | async-start | bytes 327680 | tf_op jit(solution)/shard_map/all_to_all | solution.py:24
  93.6 28.3 %all-to-all-start.4 = ((bf16[32,72,128]{2,1,0:T(8,128)(2,1)}), bf16[32,72,128]{2,1,0:T(8,128)(2,1)S(1)}, u32[]{:S(2)}, u32[]{:S(2)}) async-start(bf16[32,72,128]{2,1,0:T(8,128)(2,1)} %shard_map.60), calls=%async_computation.4 | async-start | bytes 1179648 | tf_op jit(solution)/shard_map/all_to_all | solution.py:24
  101.6 10.8 %collective-permute-start.5 = (bf16[2,64,512]{2,1,0:T(8,128)(2,1)S(1)}, bf16[2,64,512]{2,1,0:T(8,128)(2,1)S(1)}, u32[]{:S(2)}, u32[]{:S(2)}) collective-permute-start(bf16[2,64,512]{2,1,0:T(8,128)(2,1)S(1)} %pad_maximum_fusion.3), channel_id=1, source_target_pairs={{0,128},{64,192},{128,0},{192,64},{256,384},{320,448},{384,256},{4... | collective-permute-start | bytes 393224 | tf_op jit(solution)/shard_map/ppermute | solution.py:213
  112.5 9.3 %collective-permute-start.6 = (bf16[4,64,512]{2,1,0:T(8,128)(2,1)S(1)}, bf16[4,64,512]{2,1,0:T(8,128)(2,1)S(1)}, u32[]{:S(2)}, u32[]{:S(2)}) collective-permute-start(bf16[4,64,512]{2,1,0:T(8,128)(2,1)S(1)} %pad_maximum_fusion.1), channel_id=1, source_target_pairs={{0,64},{64,0},{128,192},{192,128},{256,320},{320,256},{384,448},{4... | collective-permute-start | bytes 786440 | tf_op jit(solution)/shard_map/ppermute | solution.py:213
  121.9 13.6 %collective-permute-start.7 = (bf16[8,64,512]{2,1,0:T(8,128)(2,1)S(1)}, bf16[8,64,512]{2,1,0:T(8,128)(2,1)S(1)}, u32[]{:S(2)}, u32[]{:S(2)}) collective-permute-start(bf16[8,64,512]{2,1,0:T(8,128)(2,1)S(1)} %pad_maximum_fusion.mine_ref), channel_id=1, source_target_pairs={{0,32},{32,0},{1,33},{33,1},{2,34},{34,2},{3,35},{35,3},{4,36},{36... | collective-permute-start | bytes 1572872 | tf_op jit(solution)/shard_map/ppermute | solution.py:217
  126.1 27.3 %all-to-all-start.5 = ((bf16[32,72,128]{2,1,0:T(8,128)(2,1)}), bf16[32,72,128]{2,1,0:T(8,128)(2,1)S(1)}, u32[]{:S(2)}, u32[]{:S(2)}) async-start(bf16[32,72,128]{2,1,0:T(8,128)(2,1)} %get-tuple-element.32), calls=%async_computation.5 | async-start | bytes 1179648 | tf_op jit(solution)/shard_map/all_to_all | solution.py:24
  155.1 15.0 %all-to-all-start.6 = ((bf16[16,36,128]{2,1,0:T(8,128)(2,1)}), bf16[16,36,128]{2,1,0:T(8,128)(2,1)S(1)}, u32[]{:S(2)}, u32[]{:S(2)}) async-start(bf16[16,36,128]{2,1,0:T(8,128)(2,1)} %shard_map.63), calls=%async_computation.6 | async-start | bytes 327680 | tf_op jit(solution)/shard_map/all_to_all | solution.py:24

commit v7 on v6

--- a/solution.py
+++ b/solution.py
@@ -172,33 +172,28 @@
     )
 
 
-def assemble_body(offsets, mine_ref, other_ref, out_ref, square_ref):
-    y, core = lax.axis_index("y"), lax.axis_index("core")
-    total = None
-    for i in range(mine_ref.shape[0]):
-        at = i if offsets is None else lax.bitwise_xor(y, offsets[i])
-        for which, ref in ((core, mine_ref), (1 - core, other_ref)):
-            block = ref[i]
-            out_ref[at, which] = block
-            wide = block.astype(jnp.float32)
-            square = jnp.sum(wide * wide, axis=0, keepdims=True)
-            total = square if total is None else total + square
-    square_ref[...] = total
-
-
-def assembled(mine, other, offsets=None):
-    blocks, rows, batch = mine.shape
-    feats, squares = call(
-        functools.partial(assemble_body, offsets),
-        [
-            jax.ShapeDtypeStruct((blocks, 2, rows, batch), mine.dtype),
-            jax.ShapeDtypeStruct((1, batch), jnp.float32),
-        ],
-        4 * mine.size,
-        mine,
-        other,
-    )
-    return feats.reshape(blocks * 2 * rows, batch), squares[0]
+def assemble_body(mine_ref, other_ref, *out_refs):
+    core = lax.axis_index("core")
+    steps = mine_ref.shape[1]
+    for step in range(steps):
+        feats_ref, square_ref = out_refs[step], out_refs[steps + step]
+        total = None
+        for i in range(mine_ref.shape[0]):
+            for which, ref in ((core, mine_ref), (1 - core, other_ref)):
+                block = ref[i, step]
+                feats_ref[i, which] = block
+                wide = block.astype(jnp.float32)
+                square = jnp.sum(wide * wide, axis=0, keepdims=True)
+                total = square if total is None else total + square
+        square_ref[...] = total
+
+
+def assembled(mine, other):
+    blocks, steps, rows, batch = mine.shape
+    feats = jax.ShapeDtypeStruct((blocks, 2, rows, batch), mine.dtype)
+    squares = jax.ShapeDtypeStruct((1, batch), jnp.float32)
+    out = call(assemble_body, [feats] * steps + [squares] * steps, 4 * mine.size, mine, other)
+    return [(out[step].reshape(blocks * 2 * rows, batch), out[steps + step][0]) for step in range(steps)]
 
 
 def swap_offsets(hops):
@@ -217,23 +212,25 @@
     return lax.ppermute(array, "core", [(0, 1), (1, 0)])
 
 
-def pick_body(step, pool_ref, picks_ref, out_ref):
+def pick_body(pool_ref, picks_ref, out_ref):
     pool_dev = pool_ref.shape[1]
+    copies, steps, _, batch = out_ref.shape
     first = (lax.axis_index("z") * lax.axis_size("x") + lax.axis_index("x")) * pool_dev
-    chosen = picks_ref[step : step + 1, :] - first
-    rows = lax.broadcasted_iota(jnp.int32, (pool_dev, chosen.shape[1]), 0)
-    onehot = (rows == chosen).astype(jnp.float32).astype(jnp.bfloat16)
-    feats = jnp.dot(pool_ref[...], onehot, preferred_element_type=jnp.float32).astype(out_ref.dtype)
-    for peer in range(out_ref.shape[0]):
-        out_ref[peer] = feats
-
-
-def picked(pool, picks, step, copies):
-    feats, batch = pool.shape[0], picks.shape[1]
-    return call(
-        functools.partial(pick_body, step),
-        jax.ShapeDtypeStruct((copies, feats, batch), pool.dtype),
-        2 * pool.size * batch,
+    rows = lax.broadcasted_iota(jnp.int32, (pool_dev, batch), 0)
+    for step in range(steps):
+        chosen = picks_ref[step : step + 1, :] - first
+        onehot = (rows == chosen).astype(jnp.float32).astype(jnp.bfloat16)
+        feats = jnp.dot(pool_ref[...], onehot, preferred_element_type=jnp.float32).astype(out_ref.dtype)
+        for peer in range(copies):
+            out_ref[peer, step] = feats
+
+
+def picked(pool, picks, copies):
+    steps, batch = picks.shape
+    return call(
+        pick_body,
+        jax.ShapeDtypeStruct((copies, steps, pool.shape[0], batch), pool.dtype),
+        2 * pool.size * batch * steps,
         pool,
         picks,
     )
@@ -315,32 +312,24 @@
         )
         return laplace(cross, sample_sq, centre_sq, width)
 
-    z_hops = [1 << i for i in range(over_z.bit_length() - 1)]
-    y_hops = [1 << i for i in reversed(range(lax.axis_size("y").bit_length() - 1))]
-    held = doubled(packed.astype(jnp.bfloat16)[None], "z", z_hops[0])
-    mine = picked(pool, picks, 0, lax.axis_size("y"))
-    mine, held = lax.optimization_barrier((mine, held))
-    mine = exchange(mine, "y")
-    for hop in z_hops[1:]:
+    z_hops = [1 << i for i in reversed(range(over_z.bit_length() - 1))]
+    held = packed.astype(jnp.bfloat16)[None]
+    for hop in z_hops:
         held = doubled(held, "z", hop)
-    later = doubled(picked(pool, picks, 1, 1), "y", y_hops[0])
-    mine, held, later, centre_sq = lax.optimization_barrier((mine, held, later, centre_sq))
+    mine = exchange(picked(pool, picks, lax.axis_size("y")), "y")
+    mine, held, centre_sq = lax.optimization_barrier((mine, held, centre_sq))
     coef_parts = spread(held, "x")
-    kern = kernel_matrix(*assembled(mine, swapped_cores(mine)))
+    gathered = assembled(mine, swapped_cores(mine))
+    kern = kernel_matrix(*gathered[0])
     labs = [own_labels(step) for step in range(STEPS)]
 
     gain = LOGIT_GAIN / total_centres
     logits = partial_logits(coef_parts, kern, n_centre, swap_offsets(z_hops))
     resid = exchange(residual(exchange(logits, CENTRE), labs[0], gain, fold), CENTRE)
-    grads = partial_grad(resid, kern, n_sample)
-    grads, later = lax.optimization_barrier((grads, later))
-    arrived = exchange(grads, SAMPLE)
-    for hop in y_hops[1:]:
-        later = doubled(later, "y", hop)
-    arrived, later = lax.optimization_barrier((arrived, later))
+    arrived = exchange(partial_grad(resid, kern, n_sample), SAMPLE)
     current, half = updated(arrived, packed, rate)
 
-    kern = kernel_matrix(*assembled(later, swapped_cores(later), swap_offsets(y_hops)))
+    kern = kernel_matrix(*gathered[1])
     coef_parts = exchange(half, SAMPLE).reshape(over_z, over_x, *current.shape)
     arrived = exchange(partial_logits(coef_parts, kern, n_centre), CENTRE)
     resid = exchange(residual(arrived, labs[1], gain, fold), CENTRE)

time: 208 us -> 195 us (0.938)
  starting transfers between devices: 75.9 us -> 61.1 us
  waiting for transfers between devices: 50.4 us -> 52.8 us
    all_to_all x6, waiting for transfers between devices: 32.8 us -> 50 us  [exchange(): return lax.all_to_all(parts, axes, 0, 0, tiled=True)]
    ppermute x6 -> x3, waiting for transfers between devices: 17.7 us -> 2.86 us  [doubled(): return jnp.concatenate([held, lax.ppermute(held, axis, pairs)])]
    ppermute x6 -> x3, starting transfers between devices: 30 us -> 17.9 us  [doubled(): return jnp.concatenate([held, lax.ppermute(held, axis, pairs)])]
    ppermute x2 -> x1, starting transfers between devices: 8.14 us -> 4.4 us  [swapped_cores(): return lax.ppermute(array, 'core', [(0, 1), (1, 0)])]
    pallas_call x12 -> x10, Pallas kernels: 9.34 us -> 9.46 us  [call(): pl.pallas_call(body, out_shape=out, in_specs=[vmem] * len(operands), out_...]
  transfers between devices with their start and end apart: 14 -> 10, of which waited for: 7 -> 8; matrix products, arithmetic and copies ran while one was open for 9% -> 10% of each run, Pallas kernels for 1% -> 0%
where the time goes in v7:
time: 195 us; the launch traced here: 194 us
  starting transfers between devices  61.1 us (31%)
  waiting for transfers between devices  52.8 us (27%)
  blocking collectives  47.2 us (24%)
  matrix products  13.2 us (7%)
  Pallas kernels  9.46 us (5%)
  local copies, waits for them, and re-layouts  7.07 us (4%)
  other arithmetic  3.52 us (2%)
    all_to_all x6, waiting for transfers between devices, exchange(): return lax.all_to_all(parts, axes, 0, 0, tiled=True)  50 us
    all_to_all x3, blocking collectives, exchange(): return lax.all_to_all(parts, axes, 0, 0, tiled=True)  47.2 us
    all_to_all x6, starting transfers between devices, exchange(): return lax.all_to_all(parts, axes, 0, 0, tiled=True)  38.8 us
    ppermute x3, starting transfers between devices, doubled(): return jnp.concatenate([held, lax.ppermute(held, axis, pairs)])  17.9 us
    dot_general x2, matrix products, kernel_matrix(): lax.dot_general(gathered, centres, (((0,), (0,)), ((), ())), preferred_el...  13.2 us
    pallas_call x10, Pallas kernels, call(): pl.pallas_call(body, out_shape=out, in_specs=[vmem] * len(operands), out_...  9.46 us
    ppermute x1, starting transfers between devices, swapped_cores(): return lax.ppermute(array, 'core', [(0, 1), (1, 0)])  4.4 us
  transfers between devices with their start and end apart: 10, of which 8 were waited for; matrix products, arithmetic and copies ran while one was open for 10% of the time, Pallas kernels for 0%

profile of v7, /device:TPU:1, one launch (start us, length us, event | category | flops | bytes accessed | tf_op | source)
XLA Modules:
  0.0 194.5 jit_solution(13456563926116787425)
XLA Ops:
  3.2 7.7 %all-to-all-start = ((bf16[8,2,64,512]{3,2,1,0:T(8,128)(2,1)}), bf16[8,2,64,512]{3,2,1,0:T(8,128)(2,1)S(1)}, u32[]{:S(2)}, u32[]{:S(2)}) async-start(bf16[8,2,64,512]{3,2,1,0:T(8,128)(2,1)} %shard_map.55), calls=%async_computation | async-start | bytes 2097152 | tf_op jit(solution)/shard_map/all_to_all | solution.py:24
  12.1 10.6 %collective-permute-start = (bf16[1,72,128]{2,1,0:T(8,128)(2,1)S(1)}, bf16[1,72,128]{2,1,0:T(8,128)(2,1)S(1)}, u32[]{:S(2)}, u32[]{:S(2)}) collective-permute-start(bf16[1,72,128]{2,1,0:T(8,128)(2,1)S(1)} %pad_maximum_fusion.5), channel_id=1, source_target_pairs={{0,16},{4,20},{8,24},{12,28},{16,0},{20,4},{24,8},{28,12},{1,17},{... | collective-permute-start | bytes 55304 | tf_op jit(solution)/shard_map/ppermute | solution.py:208
  23.9 4.2 %collective-permute-start.1 = (bf16[2,72,128]{2,1,0:T(8,128)(2,1)S(1)}, bf16[2,72,128]{2,1,0:T(8,128)(2,1)S(1)}, u32[]{:S(2)}, u32[]{:S(2)}) collective-permute-start(bf16[2,72,128]{2,1,0:T(8,128)(2,1)S(1)} %pad_maximum_fusion.3), channel_id=1, source_target_pairs={{0,8},{4,12},{8,0},{12,4},{16,24},{20,28},{24,16},{28,20},{1,9},{5... | collective-permute-start | bytes 110600 | tf_op jit(solution)/shard_map/ppermute | solution.py:208
  28.1 1.7 collective-permute-done.1
  29.9 3.1 %collective-permute-start.2 = (bf16[4,72,128]{2,1,0:T(8,128)(2,1)S(1)}, bf16[4,72,128]{2,1,0:T(8,128)(2,1)S(1)}, u32[]{:S(2)}, u32[]{:S(2)}) collective-permute-start(bf16[4,72,128]{2,1,0:T(8,128)(2,1)S(1)} %pad_maximum_fusion.1), channel_id=1, source_target_pairs={{0,4},{4,0},{8,12},{12,8},{16,20},{20,16},{24,28},{28,24},{1,5},{5... | collective-permute-start | bytes 221192 | tf_op jit(solution)/shard_map/ppermute | solution.py:208
  33.0 3.1 %multiply_reduce_fusion = f32[2048]{0:T(1024)S(1)} fusion(bf16[1024,2048]{1,0:T(8,128)(2,1)} %param.5), kind=kLoop, calls=%fused_computation.2 | loop fusion | flops 6289408 | bytes 4202496 | tf_op jit(solution)/shard_map/reduce_sum | solution.py:301
  36.2 1.8 all-to-all-done.mine_ref
  38.0 4.4 %collective-permute-start.3 = (bf16[8,2,64,512]{3,2,1,0:T(8,128)(2,1)S(1)}, bf16[8,2,64,512]{3,2,1,0:T(8,128)(2,1)S(1)}, u32[]{:S(2)}, u32[]{:S(2)}) collective-permute-start(bf16[8,2,64,512]{3,2,1,0:T(8,128)(2,1)S(1)} %all-to-all-done.mine_ref), channel_id=1, source_target_pairs={{0,32},{32,0},{1,33},{33,1},{2,34},{34,2},{3,35},{35,3},{4,36},{36... | collective-permute-start | bytes 3145736 | tf_op jit(solution)/shard_map/ppermute | solution.py:212
  43.4 4.0 %all-to-all-start.1 = ((bf16[4,8,72,128]{3,2,1,0:T(8,128)(2,1)}), bf16[4,8,72,128]{3,2,1,0:T(8,128)(2,1)S(1)}, u32[]{:S(2)}, u32[]{:S(2)}) async-start(bf16[4,8,72,128]{3,2,1,0:T(8,128)(2,1)} %broadcast_in_dim.16), calls=%async_computation.1 | async-start | bytes 1179648 | tf_op jit(solution)/shard_map/all_to_all | solution.py:24
  48.7 6.5 %exponential_convert_fusion.1.kern_ref = bf16[512,2048]{1,0:T(8,128)(2,1)S(1)} fusion(bf16[1024,512]{1,0:T(8,128)(2,1)S(1)} %bitcast.19, bf16[1024,2048]{1,0:T(8,128)(2,1)} %param.5, f32[2048]{0:T(1024)S(1)} %multiply_reduce_fusion, f32[512]{0:T(512)S(1)} %bitcast.21), kind=kOutput, calls=%fused_computation.4 | convolution fusion | flops 2155872256 | bytes 7350272 | tf_op jit(solution)/shard_map/dot_general | solution.py:310
  55.2 2.2 %all-to-all-done.1.coef_ref = bf16[4,8,72,128]{3,2,1,0:T(8,128)(2,1)S(1)} async-done(((bf16[4,8,72,128]{3,2,1,0:T(8,128)(2,1)}), bf16[4,8,72,128]{3,2,1,0:T(8,128)(2,1)S(1)}, u32[]{:S(2)}, u32[]{:S(2)}) %all-to-all-start.1) | async-done | bytes 589856 | tf_op jit(solution)/shard_map/all_to_all | solution.py:24
  57.4 1.9 shard_map.57
  59.3 7.0 %all-to-all-start.2 = ((bf16[16,36,128]{2,1,0:T(8,128)(2,1)}), bf16[16,36,128]{2,1,0:T(8,128)(2,1)S(1)}, u32[]{:S(2)}, u32[]{:S(2)}) async-start(bf16[16,36,128]{2,1,0:T(8,128)(2,1)} %shard_map.57), calls=%async_computation.2 | async-start | bytes 327680 | tf_op jit(solution)/shard_map/all_to_all | solution.py:24
  67.1 8.8 %all-to-all-done.2.arrived_ref = bf16[16,36,128]{2,1,0:T(8,128)(2,1)S(1)} async-done(((bf16[16,36,128]{2,1,0:T(8,128)(2,1)}), bf16[16,36,128]{2,1,0:T(8,128)(2,1)S(1)}, u32[]{:S(2)}, u32[]{:S(2)}) %all-to-all-start.2) | async-done | bytes 147488 | tf_op jit(solution)/shard_map/all_to_all | solution.py:24
  76.2 12.3 %all_to_all.45.resid_ref = bf16[16,36,128]{2,1,0:T(8,128)(2,1)S(1)} all-to-all(bf16[16,36,128]{2,1,0:T(8,128)(2,1)S(1)} %shard_map.58), channel_id=1, replica_groups=mesh['y'=8,'core'=2,'z'=8,'x'=4] {'y','core'}, dimensions={0} | all-to-all | bytes 294912 | tf_op jit(solution)/shard_map/all_to_all | solution.py:24
  90.1 8.5 %all-to-all-start.4 = ((bf16[32,72,128]{2,1,0:T(8,128)(2,1)}), bf16[32,72,128]{2,1,0:T(8,128)(2,1)S(1)}, u32[]{:S(2)}, u32[]{:S(2)}) async-start(bf16[32,72,128]{2,1,0:T(8,128)(2,1)} %shard_map.59), calls=%async_computation.4 | async-start | bytes 1179648 | tf_op jit(solution)/shard_map/all_to_all | solution.py:24
  98.7 18.4 %all-to-all-done.4.arrived_ref = bf16[32,72,128]{2,1,0:T(8,128)(2,1)S(1)} async-done(((bf16[32,72,128]{2,1,0:T(8,128)(2,1)}), bf16[32,72,128]{2,1,0:T(8,128)(2,1)S(1)}, u32[]{:S(2)}, u32[]{:S(2)}) %all-to-all-start.4) | async-done | bytes 589856 | tf_op jit(solution)/shard_map/all_to_all | solution.py:24
  118.1 4.9 %all-to-all-start.5 = ((bf16[32,72,128]{2,1,0:T(8,128)(2,1)}), bf16[32,72,128]{2,1,0:T(8,128)(2,1)S(1)}, u32[]{:S(2)}, u32[]{:S(2)}) async-start(bf16[32,72,128]{2,1,0:T(8,128)(2,1)} %get-tuple-element.19), calls=%async_computation.5 | async-start | bytes 1179648 | tf_op jit(solution)/shard_map/all_to_all | solution.py:24
  123.0 6.8 %exponential_convert_fusion.kern_ref = bf16[512,2048]{1,0:T(8,128)(2,1)S(1)} fusion(bf16[1024,512]{1,0:T(8,128)(2,1)} %bitcast.18, bf16[1024,2048]{1,0:T(8,128)(2,1)} %param.5, f32[512]{0:T(512)S(1)} %bitcast.20, f32[2048]{0:T(1024)S(1)} %multiply_reduce_fusion), kind=kOutput, calls=%fused_computation.3 | convolution fusion | flops 2155872256 | bytes 7350272 | tf_op jit(solution)/shard_map/dot_general | solution.py:310
  129.7 9.6 %all-to-all-done.5 = bf16[32,72,128]{2,1,0:T(8,128)(2,1)S(1)} async-done(((bf16[32,72,128]{2,1,0:T(8,128)(2,1)}), bf16[32,72,128]{2,1,0:T(8,128)(2,1)S(1)}, u32[]{:S(2)}, u32[]{:S(2)}) %all-to-all-start.5) | async-done | bytes 589856 | tf_op jit(solution)/shard_map/all_to_all | solution.py:24
  141.0 6.7 %all-to-all-start.6 = ((bf16[16,36,128]{2,1,0:T(8,128)(2,1)}), bf16[16,36,128]{2,1,0:T(8,128)(2,1)S(1)}, u32[]{:S(2)}, u32[]{:S(2)}) async-start(bf16[16,36,128]{2,1,0:T(8,128)(2,1)} %shard_map.61), calls=%async_computation.6 | async-start | bytes 327680 | tf_op jit(solution)/shard_map/all_to_all | solution.py:24
  148.5 9.1 %all-to-all-done.6.arrived_ref = bf16[16,36,128]{2,1,0:T(8,128)(2,1)S(1)} async-done(((bf16[16,36,128]{2,1,0:T(8,128)(2,1)}), bf16[16,36,128]{2,1,0:T(8,128)(2,1)S(1)}, u32[]{:S(2)}, u32[]{:S(2)}) %all-to-all-start.6) | async-done | bytes 147488 | tf_op jit(solution)/shard_map/all_to_all | solution.py:24
  158.0 12.1 %all_to_all.46.resid_ref = bf16[16,36,128]{2,1,0:T(8,128)(2,1)S(1)} all-to-all(bf16[16,36,128]{2,1,0:T(8,128)(2,1)S(1)} %shard_map.62), channel_id=1, replica_groups=mesh['y'=8,'core'=2,'z'=8,'x'=4] {'y','core'}, dimensions={0} | all-to-all | bytes 294912 | tf_op jit(solution)/shard_map/all_to_all | solution.py:24
  170.8 22.8 %all_to_all.47.arrived_ref = bf16[32,72,128]{2,1,0:T(8,128)(2,1)S(1)} all-to-all(bf16[32,72,128]{2,1,0:T(8,128)(2,1)S(1)} %shard_map.63), channel_id=1, replica_groups=mesh['y'=8,'core'=2,'z'=8,'x'=4] {'z','x'}, dimensions={0} | all-to-all | bytes 1179648 | tf_op jit(solution)/shard_map/all_to_all | solution.py:24
  (46 shorter events, 16.3 us)
Async XLA Ops:
  0.0 66.3 %copy-start = (s32[1024]{0:T(1024)S(1)}, s32[1024]{0:T(1024)}, u32[]{:S(2)}) copy-start(s32[1024]{0:T(1024)} %param.7) | copy-start | bytes 12292
  0.0 0.9 copy-start.1
  0.9 0.7 copy-start.2
  1.6 40.8 %copy-start.3 = (s32[2,512]{1,0:T(2,128)S(1)}, s32[2,512]{1,0:T(2,128)}, u32[]{:S(2)}) copy-start(s32[2,512]{1,0:T(2,128)} %picks_ref.1) | copy-start | bytes 12292
  3.2 34.8 %all-to-all-start = ((bf16[8,2,64,512]{3,2,1,0:T(8,128)(2,1)}), bf16[8,2,64,512]{3,2,1,0:T(8,128)(2,1)S(1)}, u32[]{:S(2)}, u32[]{:S(2)}) async-start(bf16[8,2,64,512]{3,2,1,0:T(8,128)(2,1)} %shard_map.55), calls=%async_computation | async-start | bytes 2097152 | tf_op jit(solution)/shard_map/all_to_all | solution.py:24
  12.1 11.8 %collective-permute-start = (bf16[1,72,128]{2,1,0:T(8,128)(2,1)S(1)}, bf16[1,72,128]{2,1,0:T(8,128)(2,1)S(1)}, u32[]{:S(2)}, u32[]{:S(2)}) collective-permute-start(bf16[1,72,128]{2,1,0:T(8,128)(2,1)S(1)} %pad_maximum_fusion.5), channel_id=1, source_target_pairs={{0,16},{4,20},{8,24},{12,28},{16,0},{20,4},{24,8},{28,12},{1,17},{... | collective-permute-start | bytes 55304 | tf_op jit(solution)/shard_map/ppermute | solution.py:208
  23.9 5.9 %collective-permute-start.1 = (bf16[2,72,128]{2,1,0:T(8,128)(2,1)S(1)}, bf16[2,72,128]{2,1,0:T(8,128)(2,1)S(1)}, u32[]{:S(2)}, u32[]{:S(2)}) collective-permute-start(bf16[2,72,128]{2,1,0:T(8,128)(2,1)S(1)} %pad_maximum_fusion.3), channel_id=1, source_target_pairs={{0,8},{4,12},{8,0},{12,4},{16,24},{20,28},{24,16},{28,20},{1,9},{5... | collective-permute-start | bytes 110600 | tf_op jit(solution)/shard_map/ppermute | solution.py:208
  29.9 6.2 %collective-permute-start.2 = (bf16[4,72,128]{2,1,0:T(8,128)(2,1)S(1)}, bf16[4,72,128]{2,1,0:T(8,128)(2,1)S(1)}, u32[]{:S(2)}, u32[]{:S(2)}) collective-permute-start(bf16[4,72,128]{2,1,0:T(8,128)(2,1)S(1)} %pad_maximum_fusion.1), channel_id=1, source_target_pairs={{0,4},{4,0},{8,12},{12,8},{16,20},{20,16},{24,28},{28,24},{1,5},{5... | collective-permute-start | bytes 221192 | tf_op jit(solution)/shard_map/ppermute | solution.py:208
  38.0 9.4 %collective-permute-start.3 = (bf16[8,2,64,512]{3,2,1,0:T(8,128)(2,1)S(1)}, bf16[8,2,64,512]{3,2,1,0:T(8,128)(2,1)S(1)}, u32[]{:S(2)}, u32[]{:S(2)}) collective-permute-start(bf16[8,2,64,512]{3,2,1,0:T(8,128)(2,1)S(1)} %all-to-all-done.mine_ref), channel_id=1, source_target_pairs={{0,32},{32,0},{1,33},{33,1},{2,34},{34,2},{3,35},{35,3},{4,36},{36... | collective-permute-start | bytes 3145736 | tf_op jit(solution)/shard_map/ppermute | solution.py:212
  43.4 14.0 %all-to-all-start.1 = ((bf16[4,8,72,128]{3,2,1,0:T(8,128)(2,1)}), bf16[4,8,72,128]{3,2,1,0:T(8,128)(2,1)S(1)}, u32[]{:S(2)}, u32[]{:S(2)}) async-start(bf16[4,8,72,128]{3,2,1,0:T(8,128)(2,1)} %broadcast_in_dim.16), calls=%async_computation.1 | async-start | bytes 1179648 | tf_op jit(solution)/shard_map/all_to_all | solution.py:24
  47.7 1.0 copy-start.4
  59.3 16.6 %all-to-all-start.2 = ((bf16[16,36,128]{2,1,0:T(8,128)(2,1)}), bf16[16,36,128]{2,1,0:T(8,128)(2,1)S(1)}, u32[]{:S(2)}, u32[]{:S(2)}) async-start(bf16[16,36,128]{2,1,0:T(8,128)(2,1)} %shard_map.57), calls=%async_computation.2 | async-start | bytes 327680 | tf_op jit(solution)/shard_map/all_to_all | solution.py:24
  90.1 27.0 %all-to-all-start.4 = ((bf16[32,72,128]{2,1,0:T(8,128)(2,1)}), bf16[32,72,128]{2,1,0:T(8,128)(2,1)S(1)}, u32[]{:S(2)}, u32[]{:S(2)}) async-start(bf16[32,72,128]{2,1,0:T(8,128)(2,1)} %shard_map.59), calls=%async_computation.4 | async-start | bytes 1179648 | tf_op jit(solution)/shard_map/all_to_all | solution.py:24
  118.1 21.3 %all-to-all-start.5 = ((bf16[32,72,128]{2,1,0:T(8,128)(2,1)}), bf16[32,72,128]{2,1,0:T(8,128)(2,1)S(1)}, u32[]{:S(2)}, u32[]{:S(2)}) async-start(bf16[32,72,128]{2,1,0:T(8,128)(2,1)} %get-tuple-element.19), calls=%async_computation.5 | async-start | bytes 1179648 | tf_op jit(solution)/shard_map/all_to_all | solution.py:24
  141.0 16.6 %all-to-all-start.6 = ((bf16[16,36,128]{2,1,0:T(8,128)(2,1)}), bf16[16,36,128]{2,1,0:T(8,128)(2,1)S(1)}, u32[]{:S(2)}, u32[]{:S(2)}) async-start(bf16[16,36,128]{2,1,0:T(8,128)(2,1)} %shard_map.61), calls=%async_computation.6 | async-start | bytes 327680 | tf_op jit(solution)/shard_map/all_to_all | solution.py:24

commit v8 on v7

--- a/solution.py
+++ b/solution.py
@@ -16,6 +16,7 @@
 EPS = 1e-06
 
 LANES = 128
+KERN_VMEM = 48
 CENTRE = ("y", "core")
 SAMPLE = ("z", "x")
 
@@ -172,28 +173,73 @@
     )
 
 
-def assemble_body(mine_ref, other_ref, *out_refs):
+def laplace_body(feats, centres_ref, held, sems, centre_sq_ref, out_ref, arrivals, kept):
+    blocks, _, rows, batch = feats.shape
+    width, centres = held.shape
+    columns = 2 * LANES
+    parts = [slice(start, start + columns) for start in range(0, centres, columns)]
+    staged = [
+        pltpu.make_async_copy(centres_ref.at[:, part], held.at[:, part], sems.at[i])
+        for i, part in enumerate(parts)
+    ]
+    for copy in arrivals + staged + kept:
+        copy.start()
+    for copy in arrivals:
+        copy.wait()
+    together = feats[...].reshape(width, batch)
+    squares = jnp.sum(jnp.square(together.astype(jnp.float32)), axis=0, keepdims=True)
+    sample_sq = jnp.transpose(jnp.broadcast_to(squares, (LANES, batch)))[:, :1]
+    samples = jnp.transpose(together)
+    for part, copy in zip(parts, staged):
+        copy.wait()
+        cross = jnp.dot(samples, held[:, part], preferred_element_type=jnp.float32)
+        mean_sq = (sample_sq + centre_sq_ref[:, part] - 2.0 * cross) * (1.0 / width) + EPS
+        mean_sq = jnp.maximum(mean_sq, 1e-37)
+        root = mean_sq * lax.rsqrt(mean_sq)
+        out_ref[:, part] = jnp.exp(root * (-1.0 / LENGTH_SCALE)).astype(out_ref.dtype)
+    for copy in kept:
+        copy.wait()
+
+
+def first_laplace_body(mine_ref, other_ref, centres_ref, centre_sq_ref, out_ref, later_ref, feats, held, sems, more):
     core = lax.axis_index("core")
-    steps = mine_ref.shape[1]
-    for step in range(steps):
-        feats_ref, square_ref = out_refs[step], out_refs[steps + step]
-        total = None
-        for i in range(mine_ref.shape[0]):
-            for which, ref in ((core, mine_ref), (1 - core, other_ref)):
-                block = ref[i, step]
-                feats_ref[i, which] = block
-                wide = block.astype(jnp.float32)
-                square = jnp.sum(wide * wide, axis=0, keepdims=True)
-                total = square if total is None else total + square
-        square_ref[...] = total
-
-
-def assembled(mine, other):
-    blocks, steps, rows, batch = mine.shape
-    feats = jax.ShapeDtypeStruct((blocks, 2, rows, batch), mine.dtype)
-    squares = jax.ShapeDtypeStruct((1, batch), jnp.float32)
-    out = call(assemble_body, [feats] * steps + [squares] * steps, 4 * mine.size, mine, other)
-    return [(out[step].reshape(blocks * 2 * rows, batch), out[steps + step][0]) for step in range(steps)]
+    sides = ((mine_ref, core), (other_ref, 1 - core))
+    arrivals, kept = [
+        [
+            pltpu.make_async_copy(ref.at[:, step], into.at[:, which], more.at[2 * step + i])
+            for i, (ref, which) in enumerate(sides)
+        ]
+        for step, into in enumerate((feats, later_ref))
+    ]
+    laplace_body(feats, centres_ref, held, sems, centre_sq_ref, out_ref, arrivals, kept)
+
+
+def later_laplace_body(feats_ref, centres_ref, centre_sq_ref, out_ref, held, sems):
+    laplace_body(feats_ref, centres_ref, held, sems, centre_sq_ref, out_ref, [], [])
+
+
+def kernel_matrix(body, feats, centres, centre_sq, batch, later=None):
+    width, columns = centres.shape
+    vmem, anywhere = pl.BlockSpec(memory_space=pltpu.VMEM), pl.BlockSpec(memory_space=pl.ANY)
+    out = [jax.ShapeDtypeStruct((batch, columns), jnp.bfloat16)]
+    scratch = [
+        pltpu.VMEM(centres.shape, jnp.bfloat16),
+        pltpu.SemaphoreType.DMA((columns // (2 * LANES),)),
+    ]
+    if later is not None:
+        out.append(later)
+        scratch = [pltpu.VMEM(later.shape, later.dtype), *scratch, pltpu.SemaphoreType.DMA((4,))]
+    return pl.pallas_call(
+        body,
+        out_shape=out,
+        in_specs=[vmem if later is None else anywhere] * len(feats) + [anywhere, vmem],
+        out_specs=[vmem] * len(out),
+        scratch_shapes=scratch,
+        cost_estimate=pl.CostEstimate(
+            flops=2 * centres.size * batch, bytes_accessed=2 * centres.size, transcendentals=0
+        ),
+        compiler_params=pltpu.CompilerParams(vmem_limit_bytes=KERN_VMEM << 20),
+    )(*feats, centres, centre_sq)
 
 
 def swap_offsets(hops):
@@ -278,13 +324,7 @@
     )
 
 
-def laplace(cross, sample_sq, centre_sq, width):
-    mean_sq = (sample_sq[:, None] + centre_sq[None, :] - 2.0 * cross) / width
-    return jnp.exp(-jnp.sqrt(mean_sq + EPS) / LENGTH_SCALE).astype(jnp.bfloat16)
-
-
 def on_device(centres, pool, labels, picks, coefs):
-    width = centres.shape[0]
     cen_dev = centres.shape[1]
     pool_dev = pool.shape[1]
     batch_dev = picks.shape[1]
@@ -298,29 +338,24 @@
     me = lax.axis_index(CENTRE)
     over_z, over_x = lax.axis_size("z"), lax.axis_size("x")
     local_picks = picks - lax.axis_index(SAMPLE) * pool_dev
-    centre_sq = jnp.sum(jnp.square(centres.astype(jnp.float32)), axis=0)
+    centre_sq = jnp.sum(jnp.square(centres.astype(jnp.float32)), axis=0, keepdims=True)
 
     def own_labels(step):
         chosen = lax.dynamic_slice(local_picks[step], (me * own,), (own,))
         return jnp.take(labels, chosen, mode="clip")
 
     packed = jnp.concatenate([coefs[: classes // 2], coefs[classes // 2 :]], axis=1)
-
-    def kernel_matrix(gathered, sample_sq):
-        cross = lax.dot_general(
-            gathered, centres, (((0,), (0,)), ((), ())), preferred_element_type=jnp.float32
-        )
-        return laplace(cross, sample_sq, centre_sq, width)
 
     z_hops = [1 << i for i in reversed(range(over_z.bit_length() - 1))]
     held = packed.astype(jnp.bfloat16)[None]
     for hop in z_hops:
         held = doubled(held, "z", hop)
     mine = exchange(picked(pool, picks, lax.axis_size("y")), "y")
-    mine, held, centre_sq = lax.optimization_barrier((mine, held, centre_sq))
+    mine, held, centre_sq, packed = lax.optimization_barrier((mine, held, centre_sq, packed))
     coef_parts = spread(held, "x")
-    gathered = assembled(mine, swapped_cores(mine))
-    kern = kernel_matrix(*gathered[0])
+    other = swapped_cores(mine)
+    later = jax.ShapeDtypeStruct((mine.shape[0], 2, *mine.shape[2:]), mine.dtype)
+    kern, later = kernel_matrix(first_laplace_body, (mine, other), centres, centre_sq, batch_dev, later)
     labs = [own_labels(step) for step in range(STEPS)]
 
     gain = LOGIT_GAIN / total_centres
@@ -329,7 +364,7 @@
     arrived = exchange(partial_grad(resid, kern, n_sample), SAMPLE)
     current, half = updated(arrived, packed, rate)
 
-    kern = kernel_matrix(*gathered[1])
+    (kern,) = kernel_matrix(later_laplace_body, (later,), centres, centre_sq, batch_dev)
     coef_parts = exchange(half, SAMPLE).reshape(over_z, over_x, *current.shape)
     arrived = exchange(partial_logits(coef_parts, kern, n_centre), CENTRE)
     resid = exchange(residual(arrived, labs[1], gain, fold), CENTRE)

time: 195 us -> 197 us (1.010)
  blocking collectives: 47.2 us -> 75.8 us
  waiting for transfers between devices: 52.8 us -> 30.5 us
  Pallas kernels: 9.46 us -> 24.6 us
  matrix products: 13.2 us -> 0 us
  starting transfers between devices: 61.1 us -> 52.2 us
  local copies, waits for them, and re-layouts: 7.07 us -> 9.52 us
    all_to_all x3 -> x4, blocking collectives: 47.2 us -> 75.8 us  [exchange(): return lax.all_to_all(parts, axes, 0, 0, tiled=True)]
    all_to_all x6 -> x5, waiting for transfers between devices: 50 us -> 27 us  [exchange(): return lax.all_to_all(parts, axes, 0, 0, tiled=True)]
    pallas_call x0 -> x2, Pallas kernels: none -> 16.3 us  [kernel_matrix(): pl.pallas_call(body, out_shape=out, in_specs=[vmem if later is None else...]
    dot_general x2 -> x0, matrix products: 13.2 us -> none  [kernel_matrix(): lax.dot_general(gathered, centres, (((0,), (0,)), ((), ())), preferred_el...]
    all_to_all x6 -> x5, starting transfers between devices: 38.8 us -> 30.1 us  [exchange(): return lax.all_to_all(parts, axes, 0, 0, tiled=True)]
    unnamed x12 -> x18, local copies, waits for them, and re-layouts: 2.76 us -> 5.22 us
    pallas_call x10 -> x9, Pallas kernels: 9.46 us -> 8.29 us  [call(): pl.pallas_call(body, out_shape=out, in_specs=[vmem] * len(operands), out_...]
  transfers between devices with their start and end apart: 10 -> 9, of which waited for: 8 -> 6; matrix products, arithmetic and copies ran while one was open for 10% -> 4% of each run, Pallas kernels for 0% -> 8%
where the time goes in v8:
time: 197 us; the launch traced here: 196 us
  blocking collectives  75.8 us (38%)
  starting transfers between devices  52.2 us (26%)
  waiting for transfers between devices  30.5 us (15%)
  Pallas kernels  24.6 us (12%)
  local copies, waits for them, and re-layouts  9.52 us (5%)
  other arithmetic  3.52 us (2%)
    all_to_all x4, blocking collectives, exchange(): return lax.all_to_all(parts, axes, 0, 0, tiled=True)  75.8 us
    all_to_all x5, starting transfers between devices, exchange(): return lax.all_to_all(parts, axes, 0, 0, tiled=True)  30.1 us
    all_to_all x5, waiting for transfers between devices, exchange(): return lax.all_to_all(parts, axes, 0, 0, tiled=True)  27 us
    ppermute x3, starting transfers between devices, doubled(): return jnp.concatenate([held, lax.ppermute(held, axis, pairs)])  17.7 us
    pallas_call x2, Pallas kernels, kernel_matrix(): pl.pallas_call(body, out_shape=out, in_specs=[vmem if later is None else...  16.3 us
    pallas_call x9, Pallas kernels, call(): pl.pallas_call(body, out_shape=out, in_specs=[vmem] * len(operands), out_...  8.29 us
    unnamed x18, local copies, waits for them, and re-layouts  5.22 us
    ppermute x1, starting transfers between devices, swapped_cores(): return lax.ppermute(array, 'core', [(0, 1), (1, 0)])  4.4 us
  transfers between devices with their start and end apart: 9, of which 6 were waited for; matrix products, arithmetic and copies ran while one was open for 4% of the time, Pallas kernels for 8%

profile of v8, /device:TPU:1, one launch (start us, length us, event | category | flops | bytes accessed | tf_op | source)
XLA Modules:
  0.0 196.3 jit_solution(15722334991026108959)
XLA Ops:
  1.6 1.6 shard_map.55
  3.2 7.8 %all-to-all-start = ((bf16[8,2,64,512]{3,2,1,0:T(8,128)(2,1)}), bf16[8,2,64,512]{3,2,1,0:T(8,128)(2,1)S(1)}, u32[]{:S(2)}, u32[]{:S(2)}) async-start(bf16[8,2,64,512]{3,2,1,0:T(8,128)(2,1)} %shard_map.55), calls=%async_computation | async-start | bytes 2097152 | tf_op jit(solution)/shard_map/all_to_all | solution.py:25
  12.2 10.6 %collective-permute-start = (bf16[1,72,128]{2,1,0:T(8,128)(2,1)S(1)}, bf16[1,72,128]{2,1,0:T(8,128)(2,1)S(1)}, u32[]{:S(2)}, u32[]{:S(2)}) collective-permute-start(bf16[1,72,128]{2,1,0:T(8,128)(2,1)S(1)} %pad_maximum_fusion.5), channel_id=1, source_target_pairs={{0,16},{4,20},{8,24},{12,28},{16,0},{20,4},{24,8},{28,12},{1,17},{... | collective-permute-start | bytes 55304 | tf_op jit(solution)/shard_map/ppermute | solution.py:254
  24.1 4.2 %collective-permute-start.1 = (bf16[2,72,128]{2,1,0:T(8,128)(2,1)S(1)}, bf16[2,72,128]{2,1,0:T(8,128)(2,1)S(1)}, u32[]{:S(2)}, u32[]{:S(2)}) collective-permute-start(bf16[2,72,128]{2,1,0:T(8,128)(2,1)S(1)} %pad_maximum_fusion.3), channel_id=1, source_target_pairs={{0,8},{4,12},{8,0},{12,4},{16,24},{20,28},{24,16},{28,20},{1,9},{5... | collective-permute-start | bytes 110600 | tf_op jit(solution)/shard_map/ppermute | solution.py:254
  28.3 3.1 %multiply_reduce_fusion = f32[2048]{0:T(1024)S(1)} fusion(bf16[1024,2048]{1,0:T(8,128)(2,1)} %centres_ref.3), kind=kLoop, calls=%fused_computation.2 | loop fusion | flops 6289408 | bytes 4202496 | tf_op jit(solution)/shard_map/reduce_sum | solution.py:341
  31.4 2.9 %collective-permute-start.2 = (bf16[4,72,128]{2,1,0:T(8,128)(2,1)S(1)}, bf16[4,72,128]{2,1,0:T(8,128)(2,1)S(1)}, u32[]{:S(2)}, u32[]{:S(2)}) collective-permute-start(bf16[4,72,128]{2,1,0:T(8,128)(2,1)S(1)} %pad_maximum_fusion.1), channel_id=1, source_target_pairs={{0,4},{4,0},{8,12},{12,8},{16,20},{20,16},{24,28},{28,24},{1,5},{5... | collective-permute-start | bytes 221192 | tf_op jit(solution)/shard_map/ppermute | solution.py:254
  34.4 2.4 %collective-permute-done.2 = bf16[4,72,128]{2,1,0:T(8,128)(2,1)S(1)} collective-permute-done((bf16[4,72,128]{2,1,0:T(8,128)(2,1)S(1)}, bf16[4,72,128]{2,1,0:T(8,128)(2,1)S(1)}, u32[]{:S(2)}, u32[]{:S(2)}) %collective-permute-start.2) | collective-permute-done | bytes 73760 | tf_op jit(solution)/shard_map/ppermute | solution.py:254
  36.9 1.3 all-to-all-done.mine_ref
  38.2 4.4 %collective-permute-start.3 = (bf16[8,2,64,512]{3,2,1,0:T(8,128)(2,1)S(1)}, bf16[8,2,64,512]{3,2,1,0:T(8,128)(2,1)}, u32[]{:S(2)}, u32[]{:S(2)}) collective-permute-start(bf16[8,2,64,512]{3,2,1,0:T(8,128)(2,1)S(1)} %all-to-all-done.mine_ref), channel_id=1, source_target_pairs={{0,32},{32,0},{1,33},{33,1},{2,34},{34,2},{3,35},{35,3},{4,36},{36... | collective-permute-start | bytes 3145736 | tf_op jit(solution)/shard_map/ppermute | solution.py:258
  43.5 4.0 %all-to-all-start.1 = ((bf16[4,8,72,128]{3,2,1,0:T(8,128)(2,1)}), bf16[4,8,72,128]{3,2,1,0:T(8,128)(2,1)S(1)}, u32[]{:S(2)}, u32[]{:S(2)}) async-start(bf16[4,8,72,128]{3,2,1,0:T(8,128)(2,1)} %broadcast_in_dim.18), calls=%async_computation.1 | async-start | bytes 1179648 | tf_op jit(solution)/shard_map/all_to_all | solution.py:25
  48.7 9.0 %shard_map.56 = (bf16[512,2048]{1,0:T(8,128)(2,1)S(1)}, bf16[8,2,64,512]{3,2,1,0:T(8,128)(2,1)S(1)}) custom-call(bf16[8,2,64,512]{3,2,1,0:T(8,128)(2,1)S(1)} %copy-done.2, bf16[8,2,64,512]{3,2,1,0:T(8,128)(2,1)} %collective-permute-done.3.other_ref, bf16[1024,2048]{1,0:T(8,128)(2,1)} %centres_ref.3, f32[1,2048]{1,0:T(1,128)S(1)} %bitcast.11), custom_call_target="tpu_custom_call" | custom-call | flops 2147483648 | bytes 4194304 | tf_op jit(solution)/shard_map/pallas_call | solution.py:232
  58.7 1.9 shard_map.57
  60.6 6.7 %all-to-all-start.2 = ((bf16[16,36,128]{2,1,0:T(8,128)(2,1)}), bf16[16,36,128]{2,1,0:T(8,128)(2,1)S(1)}, u32[]{:S(2)}, u32[]{:S(2)}) async-start(bf16[16,36,128]{2,1,0:T(8,128)(2,1)} %shard_map.57), calls=%async_computation.2 | async-start | bytes 327680 | tf_op jit(solution)/shard_map/all_to_all | solution.py:25
  68.2 8.8 %all-to-all-done.2.arrived_ref = bf16[16,36,128]{2,1,0:T(8,128)(2,1)S(1)} async-done(((bf16[16,36,128]{2,1,0:T(8,128)(2,1)}), bf16[16,36,128]{2,1,0:T(8,128)(2,1)S(1)}, u32[]{:S(2)}, u32[]{:S(2)}) %all-to-all-start.2) | async-done | bytes 147488 | tf_op jit(solution)/shard_map/all_to_all | solution.py:25
  77.3 12.3 %all_to_all.45.resid_ref = bf16[16,36,128]{2,1,0:T(8,128)(2,1)S(1)} all-to-all(bf16[16,36,128]{2,1,0:T(8,128)(2,1)S(1)} %shard_map.58), channel_id=1, replica_groups=mesh['y'=8,'core'=2,'z'=8,'x'=4] {'y','core'}, dimensions={0} | all-to-all | bytes 294912 | tf_op jit(solution)/shard_map/all_to_all | solution.py:25
  90.3 28.6 %all_to_all.46.arrived_ref = bf16[32,72,128]{2,1,0:T(8,128)(2,1)S(1)} all-to-all(bf16[32,72,128]{2,1,0:T(8,128)(2,1)S(1)} %shard_map.59), channel_id=1, replica_groups=mesh['y'=8,'core'=2,'z'=8,'x'=4] {'z','x'}, dimensions={0} | all-to-all | bytes 1179648 | tf_op jit(solution)/shard_map/all_to_all | solution.py:25
  119.9 4.9 %all-to-all-start.5 = ((bf16[32,72,128]{2,1,0:T(8,128)(2,1)}), bf16[32,72,128]{2,1,0:T(8,128)(2,1)S(1)}, u32[]{:S(2)}, u32[]{:S(2)}) async-start(bf16[32,72,128]{2,1,0:T(8,128)(2,1)} %get-tuple-element.18), calls=%async_computation.5 | async-start | bytes 1179648 | tf_op jit(solution)/shard_map/all_to_all | solution.py:25
  126.0 7.3 %shard_map.61.kern_ref = bf16[512,2048]{1,0:T(8,128)(2,1)S(1)} custom-call(bf16[8,2,64,512]{3,2,1,0:T(8,128)(2,1)S(1)} %copy-done.7, bf16[1024,2048]{1,0:T(8,128)(2,1)} %centres_ref.3, f32[1,2048]{1,0:T(1,128)S(1)} %bitcast.12), custom_call_target="tpu_custom_call" | custom-call | flops 2147483648 | bytes 4194304 | tf_op jit(solution)/shard_map/pallas_call | solution.py:232
  133.4 7.8 %all-to-all-done.5 = bf16[32,72,128]{2,1,0:T(8,128)(2,1)S(1)} async-done(((bf16[32,72,128]{2,1,0:T(8,128)(2,1)}), bf16[32,72,128]{2,1,0:T(8,128)(2,1)S(1)}, u32[]{:S(2)}, u32[]{:S(2)}) %all-to-all-start.5) | async-done | bytes 589856 | tf_op jit(solution)/shard_map/all_to_all | solution.py:25
  141.2 1.7 shard_map.62
  142.9 6.7 %all-to-all-start.6 = ((bf16[16,36,128]{2,1,0:T(8,128)(2,1)}), bf16[16,36,128]{2,1,0:T(8,128)(2,1)S(1)}, u32[]{:S(2)}, u32[]{:S(2)}) async-start(bf16[16,36,128]{2,1,0:T(8,128)(2,1)} %shard_map.62), calls=%async_computation.6 | async-start | bytes 327680 | tf_op jit(solution)/shard_map/all_to_all | solution.py:25
  150.4 9.1 %all-to-all-done.6.arrived_ref = bf16[16,36,128]{2,1,0:T(8,128)(2,1)S(1)} async-done(((bf16[16,36,128]{2,1,0:T(8,128)(2,1)}), bf16[16,36,128]{2,1,0:T(8,128)(2,1)S(1)}, u32[]{:S(2)}, u32[]{:S(2)}) %all-to-all-start.6) | async-done | bytes 147488 | tf_op jit(solution)/shard_map/all_to_all | solution.py:25
  159.9 12.1 %all_to_all.47.resid_ref = bf16[16,36,128]{2,1,0:T(8,128)(2,1)S(1)} all-to-all(bf16[16,36,128]{2,1,0:T(8,128)(2,1)S(1)} %shard_map.63), channel_id=1, replica_groups=mesh['y'=8,'core'=2,'z'=8,'x'=4] {'y','core'}, dimensions={0} | all-to-all | bytes 294912 | tf_op jit(solution)/shard_map/all_to_all | solution.py:25
  172.7 22.8 %all_to_all.48.arrived_ref = bf16[32,72,128]{2,1,0:T(8,128)(2,1)S(1)} all-to-all(bf16[32,72,128]{2,1,0:T(8,128)(2,1)S(1)} %shard_map.64), channel_id=1, replica_groups=mesh['y'=8,'core'=2,'z'=8,'x'=4] {'z','x'}, dimensions={0} | all-to-all | bytes 1179648 | tf_op jit(solution)/shard_map/all_to_all | solution.py:25
  (50 shorter events, 14.3 us)
Async XLA Ops:
  0.0 67.4 %copy-start = (s32[1024]{0:T(1024)S(1)}, s32[1024]{0:T(1024)}, u32[]{:S(2)}) copy-start(s32[1024]{0:T(1024)} %param.7) | copy-start | bytes 12292
  0.0 0.9 copy-start.3
  0.9 0.7 copy-start.4
  3.2 44.3 %copy-start.5 = (s32[2,512]{1,0:T(2,128)S(1)}, s32[2,512]{1,0:T(2,128)}, u32[]{:S(2)}) copy-start(s32[2,512]{1,0:T(2,128)} %picks_ref.1) | copy-start | bytes 12292
  3.2 35.0 %all-to-all-start = ((bf16[8,2,64,512]{3,2,1,0:T(8,128)(2,1)}), bf16[8,2,64,512]{3,2,1,0:T(8,128)(2,1)S(1)}, u32[]{:S(2)}, u32[]{:S(2)}) async-start(bf16[8,2,64,512]{3,2,1,0:T(8,128)(2,1)} %shard_map.55), calls=%async_computation | async-start | bytes 2097152 | tf_op jit(solution)/shard_map/all_to_all | solution.py:25
  12.2 11.8 %collective-permute-start = (bf16[1,72,128]{2,1,0:T(8,128)(2,1)S(1)}, bf16[1,72,128]{2,1,0:T(8,128)(2,1)S(1)}, u32[]{:S(2)}, u32[]{:S(2)}) collective-permute-start(bf16[1,72,128]{2,1,0:T(8,128)(2,1)S(1)} %pad_maximum_fusion.5), channel_id=1, source_target_pairs={{0,16},{4,20},{8,24},{12,28},{16,0},{20,4},{24,8},{28,12},{1,17},{... | collective-permute-start | bytes 55304 | tf_op jit(solution)/shard_map/ppermute | solution.py:254
  24.1 7.3 %collective-permute-start.1 = (bf16[2,72,128]{2,1,0:T(8,128)(2,1)S(1)}, bf16[2,72,128]{2,1,0:T(8,128)(2,1)S(1)}, u32[]{:S(2)}, u32[]{:S(2)}) collective-permute-start(bf16[2,72,128]{2,1,0:T(8,128)(2,1)S(1)} %pad_maximum_fusion.3), channel_id=1, source_target_pairs={{0,8},{4,12},{8,0},{12,4},{16,24},{20,28},{24,16},{28,20},{1,9},{5... | collective-permute-start | bytes 110600 | tf_op jit(solution)/shard_map/ppermute | solution.py:254
  31.4 5.4 %collective-permute-start.2 = (bf16[4,72,128]{2,1,0:T(8,128)(2,1)S(1)}, bf16[4,72,128]{2,1,0:T(8,128)(2,1)S(1)}, u32[]{:S(2)}, u32[]{:S(2)}) collective-permute-start(bf16[4,72,128]{2,1,0:T(8,128)(2,1)S(1)} %pad_maximum_fusion.1), channel_id=1, source_target_pairs={{0,4},{4,0},{8,12},{12,8},{16,20},{20,16},{24,28},{28,24},{1,5},{5... | collective-permute-start | bytes 221192 | tf_op jit(solution)/shard_map/ppermute | solution.py:254
  38.1 9.4 %copy-start.1 = (bf16[8,2,64,512]{3,2,1,0:T(8,128)(2,1)}, bf16[8,2,64,512]{3,2,1,0:T(8,128)(2,1)S(1)}, u32[]{:S(2)}) copy-start(bf16[8,2,64,512]{3,2,1,0:T(8,128)(2,1)S(1)} %all-to-all-done.mine_ref) | copy-start | bytes 3145732
  38.2 9.4 %collective-permute-start.3 = (bf16[8,2,64,512]{3,2,1,0:T(8,128)(2,1)S(1)}, bf16[8,2,64,512]{3,2,1,0:T(8,128)(2,1)}, u32[]{:S(2)}, u32[]{:S(2)}) collective-permute-start(bf16[8,2,64,512]{3,2,1,0:T(8,128)(2,1)S(1)} %all-to-all-done.mine_ref), channel_id=1, source_target_pairs={{0,32},{32,0},{1,33},{33,1},{2,34},{34,2},{3,35},{35,3},{4,36},{36... | collective-permute-start | bytes 3145736 | tf_op jit(solution)/shard_map/ppermute | solution.py:258
  43.5 15.3 %all-to-all-start.1 = ((bf16[4,8,72,128]{3,2,1,0:T(8,128)(2,1)}), bf16[4,8,72,128]{3,2,1,0:T(8,128)(2,1)S(1)}, u32[]{:S(2)}, u32[]{:S(2)}) async-start(bf16[4,8,72,128]{3,2,1,0:T(8,128)(2,1)} %broadcast_in_dim.18), calls=%async_computation.1 | async-start | bytes 1179648 | tf_op jit(solution)/shard_map/all_to_all | solution.py:25
  47.5 1.2 copy-start.2
  57.7 1.0 copy-start.6
  60.6 16.4 %all-to-all-start.2 = ((bf16[16,36,128]{2,1,0:T(8,128)(2,1)}), bf16[16,36,128]{2,1,0:T(8,128)(2,1)S(1)}, u32[]{:S(2)}, u32[]{:S(2)}) async-start(bf16[16,36,128]{2,1,0:T(8,128)(2,1)} %shard_map.57), calls=%async_computation.2 | async-start | bytes 327680 | tf_op jit(solution)/shard_map/all_to_all | solution.py:25
  119.9 21.2 %all-to-all-start.5 = ((bf16[32,72,128]{2,1,0:T(8,128)(2,1)}), bf16[32,72,128]{2,1,0:T(8,128)(2,1)S(1)}, u32[]{:S(2)}, u32[]{:S(2)}) async-start(bf16[32,72,128]{2,1,0:T(8,128)(2,1)} %get-tuple-element.18), calls=%async_computation.5 | async-start | bytes 1179648 | tf_op jit(solution)/shard_map/all_to_all | solution.py:25
  124.8 1.2 copy-start.7
  142.9 16.6 %all-to-all-start.6 = ((bf16[16,36,128]{2,1,0:T(8,128)(2,1)}), bf16[16,36,128]{2,1,0:T(8,128)(2,1)S(1)}, u32[]{:S(2)}, u32[]{:S(2)}) async-start(bf16[16,36,128]{2,1,0:T(8,128)(2,1)} %shard_map.62), calls=%async_computation.6 | async-start | bytes 327680 | tf_op jit(solution)/shard_map/all_to_all | solution.py:25

commit v9 on v7

--- a/solution.py
+++ b/solution.py
@@ -16,6 +16,7 @@
 EPS = 1e-06
 
 LANES = 128
+KERN_VMEM = 48
 CENTRE = ("y", "core")
 SAMPLE = ("z", "x")
 
@@ -134,7 +135,7 @@
         jax.ShapeDtypeStruct(arrived.shape, jnp.bfloat16),
         8 * arrived.size,
         arrived,
-        jnp.tile(labs, fold)[None],
+        labs,
     )
 
 
@@ -176,24 +177,59 @@
     core = lax.axis_index("core")
     steps = mine_ref.shape[1]
     for step in range(steps):
-        feats_ref, square_ref = out_refs[step], out_refs[steps + step]
-        total = None
         for i in range(mine_ref.shape[0]):
             for which, ref in ((core, mine_ref), (1 - core, other_ref)):
-                block = ref[i, step]
-                feats_ref[i, which] = block
-                wide = block.astype(jnp.float32)
-                square = jnp.sum(wide * wide, axis=0, keepdims=True)
-                total = square if total is None else total + square
-        square_ref[...] = total
+                out_refs[step][i, which] = ref[i, step]
 
 
 def assembled(mine, other):
     blocks, steps, rows, batch = mine.shape
     feats = jax.ShapeDtypeStruct((blocks, 2, rows, batch), mine.dtype)
-    squares = jax.ShapeDtypeStruct((1, batch), jnp.float32)
-    out = call(assemble_body, [feats] * steps + [squares] * steps, 4 * mine.size, mine, other)
-    return [(out[step].reshape(blocks * 2 * rows, batch), out[steps + step][0]) for step in range(steps)]
+    return call(assemble_body, [feats] * steps, mine.size, mine, other)
+
+
+def laplace_body(feats_ref, centres_ref, centre_sq_ref, out_ref, held, sems):
+    width, centres = held.shape
+    batch = feats_ref.shape[-1]
+    rows = width // sems.shape[0]
+    columns = 2 * LANES
+    staged = [
+        pltpu.make_async_copy(
+            centres_ref.at[pl.ds(rows * i, rows)], held.at[pl.ds(rows * i, rows)], sems.at[i]
+        )
+        for i in range(sems.shape[0])
+    ]
+    for copy in staged:
+        copy.start()
+    feats = feats_ref[...].reshape(width, batch)
+    squares = jnp.sum(jnp.square(feats.astype(jnp.float32)), axis=0, keepdims=True)
+    sample_sq = jnp.transpose(jnp.broadcast_to(squares, (LANES, batch)))[:, :1]
+    samples = jnp.transpose(feats)
+    for copy in staged:
+        copy.wait()
+    for start in range(0, centres, columns):
+        part = slice(start, start + columns)
+        cross = jnp.dot(samples, held[:, part], preferred_element_type=jnp.float32)
+        mean_sq = (sample_sq + centre_sq_ref[:, part] - 2.0 * cross) * (1.0 / width) + EPS
+        mean_sq = jnp.maximum(mean_sq, 1e-37)
+        root = mean_sq * lax.rsqrt(mean_sq)
+        out_ref[:, part] = jnp.exp(root * (-1.0 / LENGTH_SCALE)).astype(out_ref.dtype)
+
+
+def kernel_matrix(feats, centres, centre_sq):
+    columns, batch = centres.shape[1], feats.shape[-1]
+    vmem, anywhere = pl.BlockSpec(memory_space=pltpu.VMEM), pl.BlockSpec(memory_space=pl.ANY)
+    return pl.pallas_call(
+        laplace_body,
+        out_shape=jax.ShapeDtypeStruct((batch, columns), jnp.bfloat16),
+        in_specs=[vmem, anywhere, vmem],
+        out_specs=vmem,
+        scratch_shapes=[pltpu.VMEM(centres.shape, jnp.bfloat16), pltpu.SemaphoreType.DMA((4,))],
+        cost_estimate=pl.CostEstimate(
+            flops=2 * centres.size * batch, bytes_accessed=2 * centres.size, transcendentals=0
+        ),
+        compiler_params=pltpu.CompilerParams(vmem_limit_bytes=KERN_VMEM << 20),
+    )(feats, centres, centre_sq)
 
 
 def swap_offsets(hops):
@@ -265,26 +301,23 @@
     total = arrived_ref[0].astype(jnp.float32)
     for peer in range(1, arrived_ref.shape[0]):
         total = total + arrived_ref[peer].astype(jnp.float32)
-    new_ref[...] = current_ref[...] - rate * total
-
-
-def last_updated(arrived, current, rate):
+    turned = jnp.transpose(current_ref[...] - rate * total)
+    own, height = new_ref.shape[0], total.shape[0]
+    for h in range(LANES // own):
+        new_ref[:, height * h : height * (h + 1)] = turned[own * h : own * (h + 1)]
+
+
+def last_updated(arrived, current, rate, own):
     return call(
         functools.partial(last_body, rate),
-        jax.ShapeDtypeStruct(current.shape, jnp.float32),
+        jax.ShapeDtypeStruct((own, current.size // own), jnp.float32),
         2 * arrived.size,
         arrived,
         current,
     )
 
 
-def laplace(cross, sample_sq, centre_sq, width):
-    mean_sq = (sample_sq[:, None] + centre_sq[None, :] - 2.0 * cross) / width
-    return jnp.exp(-jnp.sqrt(mean_sq + EPS) / LENGTH_SCALE).astype(jnp.bfloat16)
-
-
 def on_device(centres, pool, labels, picks, coefs):
-    width = centres.shape[0]
     cen_dev = centres.shape[1]
     pool_dev = pool.shape[1]
     batch_dev = picks.shape[1]
@@ -298,30 +331,26 @@
     me = lax.axis_index(CENTRE)
     over_z, over_x = lax.axis_size("z"), lax.axis_size("x")
     local_picks = picks - lax.axis_index(SAMPLE) * pool_dev
-    centre_sq = jnp.sum(jnp.square(centres.astype(jnp.float32)), axis=0)
+    centre_sq = jnp.sum(jnp.square(centres.astype(jnp.float32)), axis=0, keepdims=True)
 
     def own_labels(step):
         chosen = lax.dynamic_slice(local_picks[step], (me * own,), (own,))
-        return jnp.take(labels, chosen, mode="clip")
+        return jnp.tile(jnp.take(labels, chosen, mode="clip"), fold)[None]
 
     packed = jnp.concatenate([coefs[: classes // 2], coefs[classes // 2 :]], axis=1)
-
-    def kernel_matrix(gathered, sample_sq):
-        cross = lax.dot_general(
-            gathered, centres, (((0,), (0,)), ((), ())), preferred_element_type=jnp.float32
-        )
-        return laplace(cross, sample_sq, centre_sq, width)
 
     z_hops = [1 << i for i in reversed(range(over_z.bit_length() - 1))]
     held = packed.astype(jnp.bfloat16)[None]
     for hop in z_hops:
         held = doubled(held, "z", hop)
     mine = exchange(picked(pool, picks, lax.axis_size("y")), "y")
-    mine, held, centre_sq = lax.optimization_barrier((mine, held, centre_sq))
+    labs = [own_labels(step) for step in range(STEPS)]
+    mine, held, centre_sq, packed, labs = lax.optimization_barrier(
+        (mine, held, centre_sq, packed, labs)
+    )
     coef_parts = spread(held, "x")
-    gathered = assembled(mine, swapped_cores(mine))
-    kern = kernel_matrix(*gathered[0])
-    labs = [own_labels(step) for step in range(STEPS)]
+    first, later = assembled(mine, swapped_cores(mine))
+    kern = kernel_matrix(first, centres, centre_sq)
 
     gain = LOGIT_GAIN / total_centres
     logits = partial_logits(coef_parts, kern, n_centre, swap_offsets(z_hops))
@@ -329,13 +358,12 @@
     arrived = exchange(partial_grad(resid, kern, n_sample), SAMPLE)
     current, half = updated(arrived, packed, rate)
 
-    kern = kernel_matrix(*gathered[1])
+    kern = kernel_matrix(later, centres, centre_sq)
     coef_parts = exchange(half, SAMPLE).reshape(over_z, over_x, *current.shape)
     arrived = exchange(partial_logits(coef_parts, kern, n_centre), CENTRE)
     resid = exchange(residual(arrived, labs[1], gain, fold), CENTRE)
     arrived = exchange(partial_grad(resid, kern, n_sample), SAMPLE)
-    current = last_updated(arrived, current, rate)
-    return jnp.concatenate([current[:, :cen_own], current[:, cen_own:]], axis=0)
+    return last_updated(arrived, current, rate, cen_own).T
 
 
 def solution(mesh):

time: 195 us -> 191 us (0.979)
  blocking collectives: 47.2 us -> 105 us
  waiting for transfers between devices: 52.8 us -> 15.2 us
  starting transfers between devices: 61.1 us -> 39.1 us
  matrix products: 13.2 us -> 0 us
  Pallas kernels: 9.46 us -> 19.2 us
    all_to_all x3 -> x6, blocking collectives: 47.2 us -> 105 us  [exchange(): return lax.all_to_all(parts, axes, 0, 0, tiled=True)]
    all_to_all x6 -> x3, waiting for transfers between devices: 50 us -> 12.7 us  [exchange(): return lax.all_to_all(parts, axes, 0, 0, tiled=True)]
    all_to_all x6 -> x3, starting transfers between devices: 38.8 us -> 16.5 us  [exchange(): return lax.all_to_all(parts, axes, 0, 0, tiled=True)]
    dot_general x2 -> x0, matrix products: 13.2 us -> none  [kernel_matrix(): lax.dot_general(gathered, centres, (((0,), (0,)), ((), ())), preferred_el...]
    pallas_call x0 -> x2, Pallas kernels: none -> 11.3 us  [kernel_matrix(): pl.pallas_call(laplace_body, out_shape=jax.ShapeDtypeStruct((batch, colum...]
  transfers between devices with their start and end apart: 10 -> 7, of which waited for: 8 -> 4; matrix products, arithmetic and copies ran while one was open for 10% -> 4% of each run, Pallas kernels for 0% -> 6%
where the time goes in v9:
time: 191 us
  blocking collectives  105 us (55%)
  starting transfers between devices  39.1 us (20%)
  Pallas kernels  19.2 us (10%)
  waiting for transfers between devices  15.2 us (8%)
  local copies, waits for them, and re-layouts  7.47 us (4%)
  other arithmetic  4.19 us (2%)
    all_to_all x6, blocking collectives, exchange(): return lax.all_to_all(parts, axes, 0, 0, tiled=True)  105 us
    ppermute x3, starting transfers between devices, doubled(): return jnp.concatenate([held, lax.ppermute(held, axis, pairs)])  17.7 us
    all_to_all x3, starting transfers between devices, exchange(): return lax.all_to_all(parts, axes, 0, 0, tiled=True)  16.5 us
    all_to_all x3, waiting for transfers between devices, exchange(): return lax.all_to_all(parts, axes, 0, 0, tiled=True)  12.7 us
    pallas_call x2, Pallas kernels, kernel_matrix(): pl.pallas_call(laplace_body, out_shape=jax.ShapeDtypeStruct((batch, colum...  11.3 us
    pallas_call x10, Pallas kernels, call(): pl.pallas_call(body, out_shape=out, in_specs=[vmem] * len(operands), out_...  7.85 us
    ppermute x1, starting transfers between devices, swapped_cores(): return lax.ppermute(array, 'core', [(0, 1), (1, 0)])  4.85 us
    unnamed x12, local copies, waits for them, and re-layouts  3.96 us
  transfers between devices with their start and end apart: 7, of which 4 were waited for; matrix products, arithmetic and copies ran while one was open for 4% of the time, Pallas kernels for 6%

profile of v9, /device:TPU:1, one launch (start us, length us, event | category | flops | bytes accessed | tf_op | source)
XLA Modules:
  0.0 190.5 jit_solution(4936534080111774562)
XLA Ops:
  1.6 1.5 shard_map.55
  3.1 7.7 %all-to-all-start = ((bf16[8,2,64,512]{3,2,1,0:T(8,128)(2,1)}), bf16[8,2,64,512]{3,2,1,0:T(8,128)(2,1)S(1)}, u32[]{:S(2)}, u32[]{:S(2)}) async-start(bf16[8,2,64,512]{3,2,1,0:T(8,128)(2,1)} %shard_map.55), calls=%async_computation | async-start | bytes 2097152 | tf_op jit(solution)/shard_map/all_to_all | solution.py:25
  10.8 1.0 fusion
  12.1 10.6 %collective-permute-start = (bf16[1,72,128]{2,1,0:T(8,128)(2,1)S(1)}, bf16[1,72,128]{2,1,0:T(8,128)(2,1)S(1)}, u32[]{:S(2)}, u32[]{:S(2)}) collective-permute-start(bf16[1,72,128]{2,1,0:T(8,128)(2,1)S(1)} %pad_maximum_fusion.4), channel_id=1, source_target_pairs={{0,16},{4,20},{8,24},{12,28},{16,0},{20,4},{24,8},{28,12},{1,17},{... | collective-permute-start | bytes 55304 | tf_op jit(solution)/shard_map/ppermute | solution.py:244
  23.5 3.1 %multiply_reduce_fusion = f32[2048]{0:T(1024)S(1)} fusion(bf16[1024,2048]{1,0:T(8,128)(2,1)} %centres_ref.3), kind=kLoop, calls=%fused_computation.2 | loop fusion | flops 6289408 | bytes 4202496 | tf_op jit(solution)/shard_map/reduce_sum | solution.py:334
  26.6 4.0 %collective-permute-start.1 = (bf16[2,72,128]{2,1,0:T(8,128)(2,1)S(1)}, bf16[2,72,128]{2,1,0:T(8,128)(2,1)S(1)}, u32[]{:S(2)}, u32[]{:S(2)}) collective-permute-start(bf16[2,72,128]{2,1,0:T(8,128)(2,1)S(1)} %pad_maximum_fusion.2), channel_id=1, source_target_pairs={{0,8},{4,12},{8,0},{12,4},{16,24},{20,28},{24,16},{28,20},{1,9},{5... | collective-permute-start | bytes 110600 | tf_op jit(solution)/shard_map/ppermute | solution.py:244
  32.6 3.1 %collective-permute-start.2 = (bf16[4,72,128]{2,1,0:T(8,128)(2,1)S(1)}, bf16[4,72,128]{2,1,0:T(8,128)(2,1)S(1)}, u32[]{:S(2)}, u32[]{:S(2)}) collective-permute-start(bf16[4,72,128]{2,1,0:T(8,128)(2,1)S(1)} %pad_maximum_fusion.1), channel_id=1, source_target_pairs={{0,4},{4,0},{8,12},{12,8},{16,20},{20,16},{24,28},{28,24},{1,5},{5... | collective-permute-start | bytes 221192 | tf_op jit(solution)/shard_map/ppermute | solution.py:244
  35.8 2.2 %collective-permute-done.2 = bf16[4,72,128]{2,1,0:T(8,128)(2,1)S(1)} collective-permute-done((bf16[4,72,128]{2,1,0:T(8,128)(2,1)S(1)}, bf16[4,72,128]{2,1,0:T(8,128)(2,1)S(1)}, u32[]{:S(2)}, u32[]{:S(2)}) %collective-permute-start.2) | collective-permute-done | bytes 73760 | tf_op jit(solution)/shard_map/ppermute | solution.py:244
  38.1 4.9 %collective-permute-start.3 = (bf16[8,2,64,512]{3,2,1,0:T(8,128)(2,1)S(1)}, bf16[8,2,64,512]{3,2,1,0:T(8,128)(2,1)S(1)}, u32[]{:S(2)}, u32[]{:S(2)}) collective-permute-start(bf16[8,2,64,512]{3,2,1,0:T(8,128)(2,1)S(1)} %all-to-all-done.mine_ref), channel_id=1, source_target_pairs={{0,32},{32,0},{1,33},{33,1},{2,34},{34,2},{3,35},{35,3},{4,36},{36... | collective-permute-start | bytes 3145736 | tf_op jit(solution)/shard_map/ppermute | solution.py:248
  43.9 4.0 %all-to-all-start.1 = ((bf16[4,8,72,128]{3,2,1,0:T(8,128)(2,1)}), bf16[4,8,72,128]{3,2,1,0:T(8,128)(2,1)S(1)}, u32[]{:S(2)}, u32[]{:S(2)}) async-start(bf16[4,8,72,128]{3,2,1,0:T(8,128)(2,1)} %broadcast_in_dim.20), calls=%async_computation.1 | async-start | bytes 1179648 | tf_op jit(solution)/shard_map/all_to_all | solution.py:25
  49.0 5.7 %shard_map.57.kern_ref = bf16[512,2048]{1,0:T(8,128)(2,1)S(1)} custom-call(bf16[8,2,64,512]{3,2,1,0:T(8,128)(2,1)S(1)} %get-tuple-element.17.feats_ref, bf16[1024,2048]{1,0:T(8,128)(2,1)} %centres_ref.3, f32[1,2048]{1,0:T(1,128)S(1)} %bitcast.12), custom_call_target="tpu_custom_call" | custom-call | flops 2147483648 | bytes 4194304 | tf_op jit(solution)/shard_map/pallas_call | solution.py:222
  54.7 3.2 %all-to-all-done.1.coef_ref = bf16[4,8,72,128]{3,2,1,0:T(8,128)(2,1)S(1)} async-done(((bf16[4,8,72,128]{3,2,1,0:T(8,128)(2,1)}), bf16[4,8,72,128]{3,2,1,0:T(8,128)(2,1)S(1)}, u32[]{:S(2)}, u32[]{:S(2)}) %all-to-all-start.1) | async-done | bytes 589856 | tf_op jit(solution)/shard_map/all_to_all | solution.py:25
  57.9 1.2 shard_map.58
  59.1 17.8 %all_to_all.45.arrived_ref = bf16[16,36,128]{2,1,0:T(8,128)(2,1)S(1)} all-to-all(bf16[16,36,128]{2,1,0:T(8,128)(2,1)S(1)} %shard_map.58), channel_id=1, replica_groups=mesh['y'=8,'core'=2,'z'=8,'x'=4] {'y','core'}, dimensions={0} | all-to-all | bytes 294912 | tf_op jit(solution)/shard_map/all_to_all | solution.py:25
  77.2 12.3 %all_to_all.46.resid_ref = bf16[16,36,128]{2,1,0:T(8,128)(2,1)S(1)} all-to-all(bf16[16,36,128]{2,1,0:T(8,128)(2,1)S(1)} %shard_map.59), channel_id=1, replica_groups=mesh['y'=8,'core'=2,'z'=8,'x'=4] {'y','core'}, dimensions={0} | all-to-all | bytes 294912 | tf_op jit(solution)/shard_map/all_to_all | solution.py:25
  90.2 24.5 %all_to_all.47.arrived_ref = bf16[32,72,128]{2,1,0:T(8,128)(2,1)S(1)} all-to-all(bf16[32,72,128]{2,1,0:T(8,128)(2,1)S(1)} %shard_map.60), channel_id=1, replica_groups=mesh['y'=8,'core'=2,'z'=8,'x'=4] {'z','x'}, dimensions={0} | all-to-all | bytes 1179648 | tf_op jit(solution)/shard_map/all_to_all | solution.py:25
  115.7 4.9 %all-to-all-start.5 = ((bf16[32,72,128]{2,1,0:T(8,128)(2,1)}), bf16[32,72,128]{2,1,0:T(8,128)(2,1)S(1)}, u32[]{:S(2)}, u32[]{:S(2)}) async-start(bf16[32,72,128]{2,1,0:T(8,128)(2,1)} %get-tuple-element.21), calls=%async_computation.5 | async-start | bytes 1179648 | tf_op jit(solution)/shard_map/all_to_all | solution.py:25
  120.6 1.2 copy-done.4
  121.8 5.7 %shard_map.62.kern_ref = bf16[512,2048]{1,0:T(8,128)(2,1)S(1)} custom-call(bf16[8,2,64,512]{3,2,1,0:T(8,128)(2,1)S(1)} %copy-done.4, bf16[1024,2048]{1,0:T(8,128)(2,1)} %centres_ref.3, f32[1,2048]{1,0:T(1,128)S(1)} %bitcast.13), custom_call_target="tpu_custom_call" | custom-call | flops 2147483648 | bytes 4194304 | tf_op jit(solution)/shard_map/pallas_call | solution.py:222
  127.5 9.5 %all-to-all-done.5 = bf16[32,72,128]{2,1,0:T(8,128)(2,1)S(1)} async-done(((bf16[32,72,128]{2,1,0:T(8,128)(2,1)}), bf16[32,72,128]{2,1,0:T(8,128)(2,1)S(1)}, u32[]{:S(2)}, u32[]{:S(2)}) %all-to-all-start.5) | async-done | bytes 589856 | tf_op jit(solution)/shard_map/all_to_all | solution.py:25
  136.9 1.0 shard_map.63
  138.0 15.7 %all_to_all.48.arrived_ref = bf16[16,36,128]{2,1,0:T(8,128)(2,1)S(1)} all-to-all(bf16[16,36,128]{2,1,0:T(8,128)(2,1)S(1)} %shard_map.63), channel_id=1, replica_groups=mesh['y'=8,'core'=2,'z'=8,'x'=4] {'y','core'}, dimensions={0} | all-to-all | bytes 294912 | tf_op jit(solution)/shard_map/all_to_all | solution.py:25
  154.1 12.1 %all_to_all.49.resid_ref = bf16[16,36,128]{2,1,0:T(8,128)(2,1)S(1)} all-to-all(bf16[16,36,128]{2,1,0:T(8,128)(2,1)S(1)} %shard_map.64), channel_id=1, replica_groups=mesh['y'=8,'core'=2,'z'=8,'x'=4] {'y','core'}, dimensions={0} | all-to-all | bytes 294912 | tf_op jit(solution)/shard_map/all_to_all | solution.py:25
  166.9 22.8 %all_to_all.50.arrived_ref = bf16[32,72,128]{2,1,0:T(8,128)(2,1)S(1)} all-to-all(bf16[32,72,128]{2,1,0:T(8,128)(2,1)S(1)} %shard_map.65), channel_id=1, replica_groups=mesh['y'=8,'core'=2,'z'=8,'x'=4] {'z','x'}, dimensions={0} | all-to-all | bytes 1179648 | tf_op jit(solution)/shard_map/all_to_all | solution.py:25
  (40 shorter events, 10.8 us)
Async XLA Ops:
  0.0 30.7 %copy-start = (s32[1024]{0:T(1024)S(1)}, s32[1024]{0:T(1024)}, u32[]{:S(2)}) copy-start(s32[1024]{0:T(1024)} %param.7) | copy-start | bytes 12292
  0.0 0.9 copy-start.1
  0.9 0.7 copy-start.2
  3.1 34.9 %all-to-all-start = ((bf16[8,2,64,512]{3,2,1,0:T(8,128)(2,1)}), bf16[8,2,64,512]{3,2,1,0:T(8,128)(2,1)S(1)}, u32[]{:S(2)}, u32[]{:S(2)}) async-start(bf16[8,2,64,512]{3,2,1,0:T(8,128)(2,1)} %shard_map.55), calls=%async_computation | async-start | bytes 2097152 | tf_op jit(solution)/shard_map/all_to_all | solution.py:25
  12.1 14.5 %collective-permute-start = (bf16[1,72,128]{2,1,0:T(8,128)(2,1)S(1)}, bf16[1,72,128]{2,1,0:T(8,128)(2,1)S(1)}, u32[]{:S(2)}, u32[]{:S(2)}) collective-permute-start(bf16[1,72,128]{2,1,0:T(8,128)(2,1)S(1)} %pad_maximum_fusion.4), channel_id=1, source_target_pairs={{0,16},{4,20},{8,24},{12,28},{16,0},{20,4},{24,8},{28,12},{1,17},{... | collective-permute-start | bytes 55304 | tf_op jit(solution)/shard_map/ppermute | solution.py:244
  26.6 5.9 %collective-permute-start.1 = (bf16[2,72,128]{2,1,0:T(8,128)(2,1)S(1)}, bf16[2,72,128]{2,1,0:T(8,128)(2,1)S(1)}, u32[]{:S(2)}, u32[]{:S(2)}) collective-permute-start(bf16[2,72,128]{2,1,0:T(8,128)(2,1)S(1)} %pad_maximum_fusion.2), channel_id=1, source_target_pairs={{0,8},{4,12},{8,0},{12,4},{16,24},{20,28},{24,16},{28,20},{1,9},{5... | collective-permute-start | bytes 110600 | tf_op jit(solution)/shard_map/ppermute | solution.py:244
  32.6 5.4 %collective-permute-start.2 = (bf16[4,72,128]{2,1,0:T(8,128)(2,1)S(1)}, bf16[4,72,128]{2,1,0:T(8,128)(2,1)S(1)}, u32[]{:S(2)}, u32[]{:S(2)}) collective-permute-start(bf16[4,72,128]{2,1,0:T(8,128)(2,1)S(1)} %pad_maximum_fusion.1), channel_id=1, source_target_pairs={{0,4},{4,0},{8,12},{12,8},{16,20},{20,16},{24,28},{28,24},{1,5},{5... | collective-permute-start | bytes 221192 | tf_op jit(solution)/shard_map/ppermute | solution.py:244
  38.1 9.8 %collective-permute-start.3 = (bf16[8,2,64,512]{3,2,1,0:T(8,128)(2,1)S(1)}, bf16[8,2,64,512]{3,2,1,0:T(8,128)(2,1)S(1)}, u32[]{:S(2)}, u32[]{:S(2)}) collective-permute-start(bf16[8,2,64,512]{3,2,1,0:T(8,128)(2,1)S(1)} %all-to-all-done.mine_ref), channel_id=1, source_target_pairs={{0,32},{32,0},{1,33},{33,1},{2,34},{34,2},{3,35},{35,3},{4,36},{36... | collective-permute-start | bytes 3145736 | tf_op jit(solution)/shard_map/ppermute | solution.py:248
  43.9 14.0 %all-to-all-start.1 = ((bf16[4,8,72,128]{3,2,1,0:T(8,128)(2,1)}), bf16[4,8,72,128]{3,2,1,0:T(8,128)(2,1)S(1)}, u32[]{:S(2)}, u32[]{:S(2)}) async-start(bf16[4,8,72,128]{3,2,1,0:T(8,128)(2,1)} %broadcast_in_dim.20), calls=%async_computation.1 | async-start | bytes 1179648 | tf_op jit(solution)/shard_map/all_to_all | solution.py:25
  48.0 1.0 copy-start.3
  115.7 21.3 %all-to-all-start.5 = ((bf16[32,72,128]{2,1,0:T(8,128)(2,1)}), bf16[32,72,128]{2,1,0:T(8,128)(2,1)S(1)}, u32[]{:S(2)}, u32[]{:S(2)}) async-start(bf16[32,72,128]{2,1,0:T(8,128)(2,1)} %get-tuple-element.21), calls=%async_computation.5 | async-start | bytes 1179648 | tf_op jit(solution)/shard_map/all_to_all | solution.py:25
  120.6 1.2 copy-start.4

commit v10 on v9

--- a/solution.py
+++ b/solution.py
@@ -17,6 +17,8 @@
 
 LANES = 128
 KERN_VMEM = 48
+PICK_VMEM = 60
+COPIES_COST = 4_000_000_000
 CENTRE = ("y", "core")
 SAMPLE = ("z", "x")
 
@@ -244,32 +246,62 @@
     return jnp.concatenate([held, lax.ppermute(held, axis, pairs)])
 
 
+def copies_body(held_ref, moved_ref, out_ref):
+    near = held_ref.shape[0]
+    for copy in range(out_ref.shape[0]):
+        out_ref[copy, :near] = held_ref[...]
+        out_ref[copy, near:] = moved_ref[...]
+
+
+def last_doubled(held, axis, hop, copies):
+    pairs = [(i, i ^ hop) for i in range(lax.axis_size(axis))]
+    moved = lax.ppermute(held, axis, pairs)
+    out = jax.ShapeDtypeStruct((copies, 2 * held.shape[0], *held.shape[1:]), held.dtype)
+    return call(copies_body, out, COPIES_COST, held, moved)
+
+
 def swapped_cores(array):
     return lax.ppermute(array, "core", [(0, 1), (1, 0)])
 
 
-def pick_body(pool_ref, picks_ref, out_ref):
-    pool_dev = pool_ref.shape[1]
+def pick_body(pool_ref, picks_ref, out_ref, pool, picks, sems):
+    fetches = [
+        pltpu.make_async_copy(ref, into, sems.at[i])
+        for i, (ref, into) in enumerate(((picks_ref, picks), (pool_ref, pool)))
+    ]
+    for copy in fetches:
+        copy.start()
+    for copy in fetches:
+        copy.wait()
+    pool_dev = pool.shape[1]
     copies, steps, _, batch = out_ref.shape
     first = (lax.axis_index("z") * lax.axis_size("x") + lax.axis_index("x")) * pool_dev
     rows = lax.broadcasted_iota(jnp.int32, (pool_dev, batch), 0)
     for step in range(steps):
-        chosen = picks_ref[step : step + 1, :] - first
+        chosen = picks[step : step + 1, :] - first
         onehot = (rows == chosen).astype(jnp.float32).astype(jnp.bfloat16)
-        feats = jnp.dot(pool_ref[...], onehot, preferred_element_type=jnp.float32).astype(out_ref.dtype)
+        feats = jnp.dot(pool[...], onehot, preferred_element_type=jnp.float32).astype(out_ref.dtype)
         for peer in range(copies):
             out_ref[peer, step] = feats
 
 
 def picked(pool, picks, copies):
     steps, batch = picks.shape
-    return call(
+    return pl.pallas_call(
         pick_body,
-        jax.ShapeDtypeStruct((copies, steps, pool.shape[0], batch), pool.dtype),
-        2 * pool.size * batch * steps,
-        pool,
-        picks,
-    )
+        out_shape=jax.ShapeDtypeStruct((copies, steps, pool.shape[0], batch), pool.dtype),
+        in_specs=[pl.BlockSpec(memory_space=pl.ANY)] * 2,
+        out_specs=pl.BlockSpec(memory_space=pltpu.VMEM),
+        scratch_shapes=[
+            pltpu.VMEM(pool.shape, pool.dtype),
+            pltpu.VMEM(picks.shape, picks.dtype),
+            pltpu.SemaphoreType.DMA((2,)),
+        ],
+        cost_estimate=pl.CostEstimate(
+            flops=2 * pool.size * batch * steps, bytes_accessed=2 * pool.size, transcendentals=0
+        ),
+        compiler_params=pltpu.CompilerParams(vmem_limit_bytes=PICK_VMEM << 20),
+    )(pool, picks)
 
 
 def update_body(rate, arrived_ref, current_ref, new_ref, half_ref):
@@ -341,14 +373,15 @@
 
     z_hops = [1 << i for i in reversed(range(over_z.bit_length() - 1))]
     held = packed.astype(jnp.bfloat16)[None]
-    for hop in z_hops:
+    for hop in z_hops[:-1]:
         held = doubled(held, "z", hop)
     mine = exchange(picked(pool, picks, lax.axis_size("y")), "y")
     labs = [own_labels(step) for step in range(STEPS)]
-    mine, held, centre_sq, packed, labs = lax.optimization_barrier(
-        (mine, held, centre_sq, packed, labs)
-    )
-    coef_parts = spread(held, "x")
+    spread_out = last_doubled(held, "z", z_hops[-1], over_x)
+    mine, spread_out, centre_sq, packed, labs = lax.optimization_barrier(
+        (mine, spread_out, centre_sq, packed, labs)
+    )
+    coef_parts = exchange(spread_out, "x")
     first, later = assembled(mine, swapped_cores(mine))
     kern = kernel_matrix(first, centres, centre_sq)
 

time: 191 us -> 196 us (1.026)
  waiting for transfers between devices: 15.2 us -> 28.2 us
  blocking collectives: 105 us -> 99.7 us
  local copies, waits for them, and re-layouts: 7.47 us -> 4.95 us
  starting transfers between devices: 39.1 us -> 36.7 us
    all_to_all x3, waiting for transfers between devices: 12.7 us -> 25.6 us  [exchange(): return lax.all_to_all(parts, axes, 0, 0, tiled=True)]
    all_to_all x6, blocking collectives: 105 us -> 99.7 us  [exchange(): return lax.all_to_all(parts, axes, 0, 0, tiled=True)]
    ppermute x0 -> x1, starting transfers between devices: none -> 3.09 us  [last_doubled(): moved = lax.ppermute(held, axis, pairs)]
    pallas_call x0 -> x1, Pallas kernels: none -> 2.47 us  [picked(): pl.pallas_call(pick_body, out_shape=jax.ShapeDtypeStruct((copies, steps,...]
    ppermute x1, starting transfers between devices: 4.85 us -> 2.39 us  [swapped_cores(): return lax.ppermute(array, 'core', [(0, 1), (1, 0)])]
    ppermute x3 -> x2, starting transfers between devices: 17.7 us -> 15.5 us  [doubled(): return jnp.concatenate([held, lax.ppermute(held, axis, pairs)])]
    ppermute x0 -> x1, waiting for transfers between devices: none -> 2.2 us  [last_doubled(): moved = lax.ppermute(held, axis, pairs)]
    ppermute x3 -> x2, waiting for transfers between devices: 2.52 us -> 0.32 us  [doubled(): return jnp.concatenate([held, lax.ppermute(held, axis, pairs)])]
  transfers between devices with their start and end apart: 7 -> 7, of which waited for: 4 -> 5; matrix products, arithmetic and copies ran while one was open for 4% -> 3% of each run, Pallas kernels for 6% -> 8%
where the time goes in v10:
time: 196 us; the launch traced here: 195 us
  blocking collectives  99.7 us (51%)
  starting transfers between devices  36.7 us (19%)
  waiting for transfers between devices  28.2 us (14%)
  Pallas kernels  21.1 us (11%)
  local copies, waits for them, and re-layouts  4.95 us (3%)
  other arithmetic  4.11 us (2%)
    all_to_all x6, blocking collectives, exchange(): return lax.all_to_all(parts, axes, 0, 0, tiled=True)  99.7 us
    all_to_all x3, waiting for transfers between devices, exchange(): return lax.all_to_all(parts, axes, 0, 0, tiled=True)  25.6 us
    all_to_all x3, starting transfers between devices, exchange(): return lax.all_to_all(parts, axes, 0, 0, tiled=True)  15.7 us
    ppermute x2, starting transfers between devices, doubled(): return jnp.concatenate([held, lax.ppermute(held, axis, pairs)])  15.5 us
    pallas_call x2, Pallas kernels, kernel_matrix(): pl.pallas_call(laplace_body, out_shape=jax.ShapeDtypeStruct((batch, colum...  11.3 us
    pallas_call x10, Pallas kernels, call(): pl.pallas_call(body, out_shape=out, in_specs=[vmem] * len(operands), out_...  7.24 us
  transfers between devices with their start and end apart: 7, of which 5 were waited for; matrix products, arithmetic and copies ran while one was open for 3% of the time, Pallas kernels for 8%

profile of v10, /device:TPU:1, one launch (start us, length us, event | category | flops | bytes accessed | tf_op | source)
XLA Modules:
  0.0 194.9 jit_solution(14020137923290616952)
XLA Ops:
  1.3 11.5 %collective-permute-start = (bf16[1,72,128]{2,1,0:T(8,128)(2,1)S(1)}, bf16[1,72,128]{2,1,0:T(8,128)(2,1)S(1)}, u32[]{:S(2)}, u32[]{:S(2)}) collective-permute-start(bf16[1,72,128]{2,1,0:T(8,128)(2,1)S(1)} %pad_maximum_fusion.3), channel_id=1, source_target_pairs={{0,16},{4,20},{8,24},{12,28},{16,0},{20,4},{24,8},{28,12},{1,17},{... | collective-permute-start | bytes 55304 | tf_op jit(solution)/shard_map/ppermute | solution.py:246
  12.7 2.5 %shard_map.55 = bf16[8,2,64,512]{3,2,1,0:T(8,128)(2,1)} custom-call(bf16[64,1024]{1,0:T(8,128)(2,1)} %pool_ref.1, s32[2,512]{1,0:T(2,128)} %picks_ref.1), custom_call_target="tpu_custom_call" | custom-call | flops 134217728 | bytes 131072 | tf_op jit(solution)/shard_map/pallas_call | solution.py:290
  15.2 6.8 %all-to-all-start = ((bf16[8,2,64,512]{3,2,1,0:T(8,128)(2,1)}), bf16[8,2,64,512]{3,2,1,0:T(8,128)(2,1)S(1)}, u32[]{:S(2)}, u32[]{:S(2)}) async-start(bf16[8,2,64,512]{3,2,1,0:T(8,128)(2,1)} %shard_map.55), calls=%async_computation | async-start | bytes 2097152 | tf_op jit(solution)/shard_map/all_to_all | solution.py:27
  22.8 3.1 %multiply_reduce_fusion = f32[2048]{0:T(1024)S(1)} fusion(bf16[1024,2048]{1,0:T(8,128)(2,1)} %centres_ref.3), kind=kLoop, calls=%fused_computation.2 | loop fusion | flops 6289408 | bytes 4202496 | tf_op jit(solution)/shard_map/reduce_sum | solution.py:366
  26.0 4.0 %collective-permute-start.1 = (bf16[2,72,128]{2,1,0:T(8,128)(2,1)S(1)}, bf16[2,72,128]{2,1,0:T(8,128)(2,1)S(1)}, u32[]{:S(2)}, u32[]{:S(2)}) collective-permute-start(bf16[2,72,128]{2,1,0:T(8,128)(2,1)S(1)} %pad_maximum_fusion.1), channel_id=1, source_target_pairs={{0,8},{4,12},{8,0},{12,4},{16,24},{20,28},{24,16},{28,20},{1,9},{5... | collective-permute-start | bytes 110600 | tf_op jit(solution)/shard_map/ppermute | solution.py:246
  31.9 3.1 %collective-permute-start.2 = (bf16[4,72,128]{2,1,0:T(8,128)(2,1)S(1)}, bf16[4,72,128]{2,1,0:T(8,128)(2,1)S(1)}, u32[]{:S(2)}, u32[]{:S(2)}) collective-permute-start(bf16[4,72,128]{2,1,0:T(8,128)(2,1)S(1)} %pad_maximum_fusion.held_ref), channel_id=1, source_target_pairs={{0,4},{4,0},{8,12},{12,8},{16,20},{20,16},{24,28},{28,24},{1,5},{5... | collective-permute-start | bytes 221192 | tf_op jit(solution)/shard_map/ppermute | solution.py:258
  35.1 2.2 %collective-permute-done.2.moved_ref = bf16[4,72,128]{2,1,0:T(8,128)(2,1)S(1)} collective-permute-done((bf16[4,72,128]{2,1,0:T(8,128)(2,1)S(1)}, bf16[4,72,128]{2,1,0:T(8,128)(2,1)S(1)}, u32[]{:S(2)}, u32[]{:S(2)}) %collective-permute-start.2) | collective-permute-done | bytes 73760 | tf_op jit(solution)/shard_map/ppermute | solution.py:258
  38.2 13.0 %all-to-all-done.mine_ref = bf16[8,2,64,512]{3,2,1,0:T(8,128)(2,1)S(1)} async-done(((bf16[8,2,64,512]{3,2,1,0:T(8,128)(2,1)}), bf16[8,2,64,512]{3,2,1,0:T(8,128)(2,1)S(1)}, u32[]{:S(2)}, u32[]{:S(2)}) %all-to-all-start) | async-done | bytes 1048608 | tf_op jit(solution)/shard_map/all_to_all | solution.py:27
  51.2 2.4 %collective-permute-start.3 = (bf16[8,2,64,512]{3,2,1,0:T(8,128)(2,1)S(1)}, bf16[8,2,64,512]{3,2,1,0:T(8,128)(2,1)S(1)}, u32[]{:S(2)}, u32[]{:S(2)}) collective-permute-start(bf16[8,2,64,512]{3,2,1,0:T(8,128)(2,1)S(1)} %all-to-all-done.mine_ref), channel_id=1, source_target_pairs={{0,32},{32,0},{1,33},{33,1},{2,34},{34,2},{3,35},{35,3},{4,36},{36... | collective-permute-start | bytes 3145736 | tf_op jit(solution)/shard_map/ppermute | solution.py:264
  53.6 4.0 %all-to-all-start.1 = ((bf16[4,8,72,128]{3,2,1,0:T(8,128)(2,1)}), bf16[4,8,72,128]{3,2,1,0:T(8,128)(2,1)S(1)}, u32[]{:S(2)}, u32[]{:S(2)}) async-start(bf16[4,8,72,128]{3,2,1,0:T(8,128)(2,1)} %shard_map.56), calls=%async_computation.1 | async-start | bytes 1179648 | tf_op jit(solution)/shard_map/all_to_all | solution.py:27
  58.8 5.7 %shard_map.58.kern_ref = bf16[512,2048]{1,0:T(8,128)(2,1)S(1)} custom-call(bf16[8,2,64,512]{3,2,1,0:T(8,128)(2,1)S(1)} %get-tuple-element.17.feats_ref, bf16[1024,2048]{1,0:T(8,128)(2,1)} %centres_ref.3, f32[1,2048]{1,0:T(1,128)S(1)} %bitcast.12), custom_call_target="tpu_custom_call" | custom-call | flops 2147483648 | bytes 4194304 | tf_op jit(solution)/shard_map/pallas_call | solution.py:224
  64.5 3.2 %all-to-all-done.1.coef_ref = bf16[4,8,72,128]{3,2,1,0:T(8,128)(2,1)S(1)} async-done(((bf16[4,8,72,128]{3,2,1,0:T(8,128)(2,1)}), bf16[4,8,72,128]{3,2,1,0:T(8,128)(2,1)S(1)}, u32[]{:S(2)}, u32[]{:S(2)}) %all-to-all-start.1) | async-done | bytes 589856 | tf_op jit(solution)/shard_map/all_to_all | solution.py:27
  67.7 1.2 shard_map.59
  68.9 13.4 %all_to_all.45.arrived_ref = bf16[16,36,128]{2,1,0:T(8,128)(2,1)S(1)} all-to-all(bf16[16,36,128]{2,1,0:T(8,128)(2,1)S(1)} %shard_map.59), channel_id=1, replica_groups=mesh['y'=8,'core'=2,'z'=8,'x'=4] {'y','core'}, dimensions={0} | all-to-all | bytes 294912 | tf_op jit(solution)/shard_map/all_to_all | solution.py:27
  82.7 12.1 %all_to_all.46.resid_ref = bf16[16,36,128]{2,1,0:T(8,128)(2,1)S(1)} all-to-all(bf16[16,36,128]{2,1,0:T(8,128)(2,1)S(1)} %shard_map.60), channel_id=1, replica_groups=mesh['y'=8,'core'=2,'z'=8,'x'=4] {'y','core'}, dimensions={0} | all-to-all | bytes 294912 | tf_op jit(solution)/shard_map/all_to_all | solution.py:27
  95.5 23.6 %all_to_all.47.arrived_ref = bf16[32,72,128]{2,1,0:T(8,128)(2,1)S(1)} all-to-all(bf16[32,72,128]{2,1,0:T(8,128)(2,1)S(1)} %shard_map.61), channel_id=1, replica_groups=mesh['y'=8,'core'=2,'z'=8,'x'=4] {'z','x'}, dimensions={0} | all-to-all | bytes 1179648 | tf_op jit(solution)/shard_map/all_to_all | solution.py:27
  120.0 4.9 %all-to-all-start.5 = ((bf16[32,72,128]{2,1,0:T(8,128)(2,1)}), bf16[32,72,128]{2,1,0:T(8,128)(2,1)S(1)}, u32[]{:S(2)}, u32[]{:S(2)}) async-start(bf16[32,72,128]{2,1,0:T(8,128)(2,1)} %get-tuple-element.21), calls=%async_computation.5 | async-start | bytes 1179648 | tf_op jit(solution)/shard_map/all_to_all | solution.py:27
  124.9 1.2 copy-done.2
  126.1 5.7 %shard_map.63.kern_ref = bf16[512,2048]{1,0:T(8,128)(2,1)S(1)} custom-call(bf16[8,2,64,512]{3,2,1,0:T(8,128)(2,1)S(1)} %copy-done.2, bf16[1024,2048]{1,0:T(8,128)(2,1)} %centres_ref.3, f32[1,2048]{1,0:T(1,128)S(1)} %bitcast.13), custom_call_target="tpu_custom_call" | custom-call | flops 2147483648 | bytes 4194304 | tf_op jit(solution)/shard_map/pallas_call | solution.py:224
  131.8 9.5 %all-to-all-done.5 = bf16[32,72,128]{2,1,0:T(8,128)(2,1)S(1)} async-done(((bf16[32,72,128]{2,1,0:T(8,128)(2,1)}), bf16[32,72,128]{2,1,0:T(8,128)(2,1)S(1)}, u32[]{:S(2)}, u32[]{:S(2)}) %all-to-all-start.5) | async-done | bytes 589856 | tf_op jit(solution)/shard_map/all_to_all | solution.py:27
  141.3 1.0 shard_map.64
  142.3 15.7 %all_to_all.48.arrived_ref = bf16[16,36,128]{2,1,0:T(8,128)(2,1)S(1)} all-to-all(bf16[16,36,128]{2,1,0:T(8,128)(2,1)S(1)} %shard_map.64), channel_id=1, replica_groups=mesh['y'=8,'core'=2,'z'=8,'x'=4] {'y','core'}, dimensions={0} | all-to-all | bytes 294912 | tf_op jit(solution)/shard_map/all_to_all | solution.py:27
  158.4 12.1 %all_to_all.49.resid_ref = bf16[16,36,128]{2,1,0:T(8,128)(2,1)S(1)} all-to-all(bf16[16,36,128]{2,1,0:T(8,128)(2,1)S(1)} %shard_map.65), channel_id=1, replica_groups=mesh['y'=8,'core'=2,'z'=8,'x'=4] {'y','core'}, dimensions={0} | all-to-all | bytes 294912 | tf_op jit(solution)/shard_map/all_to_all | solution.py:27
  171.2 22.8 %all_to_all.50.arrived_ref = bf16[32,72,128]{2,1,0:T(8,128)(2,1)S(1)} all-to-all(bf16[32,72,128]{2,1,0:T(8,128)(2,1)S(1)} %shard_map.66), channel_id=1, replica_groups=mesh['y'=8,'core'=2,'z'=8,'x'=4] {'z','x'}, dimensions={0} | all-to-all | bytes 1179648 | tf_op jit(solution)/shard_map/all_to_all | solution.py:27
  (35 shorter events, 10.1 us)
Async XLA Ops:
  0.0 30.0 %copy-start = (s32[1024]{0:T(1024)S(1)}, s32[1024]{0:T(1024)}, u32[]{:S(2)}) copy-start(s32[1024]{0:T(1024)} %param.7) | copy-start | bytes 12292
  1.3 24.6 %collective-permute-start = (bf16[1,72,128]{2,1,0:T(8,128)(2,1)S(1)}, bf16[1,72,128]{2,1,0:T(8,128)(2,1)S(1)}, u32[]{:S(2)}, u32[]{:S(2)}) collective-permute-start(bf16[1,72,128]{2,1,0:T(8,128)(2,1)S(1)} %pad_maximum_fusion.3), channel_id=1, source_target_pairs={{0,16},{4,20},{8,24},{12,28},{16,0},{20,4},{24,8},{28,12},{1,17},{... | collective-permute-start | bytes 55304 | tf_op jit(solution)/shard_map/ppermute | solution.py:246
  15.2 36.0 %all-to-all-start = ((bf16[8,2,64,512]{3,2,1,0:T(8,128)(2,1)}), bf16[8,2,64,512]{3,2,1,0:T(8,128)(2,1)S(1)}, u32[]{:S(2)}, u32[]{:S(2)}) async-start(bf16[8,2,64,512]{3,2,1,0:T(8,128)(2,1)} %shard_map.55), calls=%async_computation | async-start | bytes 2097152 | tf_op jit(solution)/shard_map/all_to_all | solution.py:27
  26.0 5.9 %collective-permute-start.1 = (bf16[2,72,128]{2,1,0:T(8,128)(2,1)S(1)}, bf16[2,72,128]{2,1,0:T(8,128)(2,1)S(1)}, u32[]{:S(2)}, u32[]{:S(2)}) collective-permute-start(bf16[2,72,128]{2,1,0:T(8,128)(2,1)S(1)} %pad_maximum_fusion.1), channel_id=1, source_target_pairs={{0,8},{4,12},{8,0},{12,4},{16,24},{20,28},{24,16},{28,20},{1,9},{5... | collective-permute-start | bytes 110600 | tf_op jit(solution)/shard_map/ppermute | solution.py:246
  31.9 5.4 %collective-permute-start.2 = (bf16[4,72,128]{2,1,0:T(8,128)(2,1)S(1)}, bf16[4,72,128]{2,1,0:T(8,128)(2,1)S(1)}, u32[]{:S(2)}, u32[]{:S(2)}) collective-permute-start(bf16[4,72,128]{2,1,0:T(8,128)(2,1)S(1)} %pad_maximum_fusion.held_ref), channel_id=1, source_target_pairs={{0,4},{4,0},{8,12},{12,8},{16,20},{20,16},{24,28},{28,24},{1,5},{5... | collective-permute-start | bytes 221192 | tf_op jit(solution)/shard_map/ppermute | solution.py:258
  51.2 6.4 %collective-permute-start.3 = (bf16[8,2,64,512]{3,2,1,0:T(8,128)(2,1)S(1)}, bf16[8,2,64,512]{3,2,1,0:T(8,128)(2,1)S(1)}, u32[]{:S(2)}, u32[]{:S(2)}) collective-permute-start(bf16[8,2,64,512]{3,2,1,0:T(8,128)(2,1)S(1)} %all-to-all-done.mine_ref), channel_id=1, source_target_pairs={{0,32},{32,0},{1,33},{33,1},{2,34},{34,2},{3,35},{35,3},{4,36},{36... | collective-permute-start | bytes 3145736 | tf_op jit(solution)/shard_map/ppermute | solution.py:264
  53.6 14.0 %all-to-all-start.1 = ((bf16[4,8,72,128]{3,2,1,0:T(8,128)(2,1)}), bf16[4,8,72,128]{3,2,1,0:T(8,128)(2,1)S(1)}, u32[]{:S(2)}, u32[]{:S(2)}) async-start(bf16[4,8,72,128]{3,2,1,0:T(8,128)(2,1)} %shard_map.56), calls=%async_computation.1 | async-start | bytes 1179648 | tf_op jit(solution)/shard_map/all_to_all | solution.py:27
  57.8 1.0 copy-start.1
  120.0 21.3 %all-to-all-start.5 = ((bf16[32,72,128]{2,1,0:T(8,128)(2,1)}), bf16[32,72,128]{2,1,0:T(8,128)(2,1)S(1)}, u32[]{:S(2)}, u32[]{:S(2)}) async-start(bf16[32,72,128]{2,1,0:T(8,128)(2,1)} %get-tuple-element.21), calls=%async_computation.5 | async-start | bytes 1179648 | tf_op jit(solution)/shard_map/all_to_all | solution.py:27
  124.9 1.2 copy-start.2

commit v11 on v10

--- a/solution.py
+++ b/solution.py
@@ -18,7 +18,7 @@
 LANES = 128
 KERN_VMEM = 48
 PICK_VMEM = 60
-COPIES_COST = 4_000_000_000
+COPIES_COST = 1000
 CENTRE = ("y", "core")
 SAMPLE = ("z", "x")
 

time: 196 us -> 191 us (0.974)
  waiting for transfers between devices: 28.2 us -> 15.2 us
  blocking collectives: 99.7 us -> 105 us
  starting transfers between devices: 36.7 us -> 39.1 us
    all_to_all x3, waiting for transfers between devices: 25.6 us -> 12.7 us  [exchange(): return lax.all_to_all(parts, axes, 0, 0, tiled=True)]
    all_to_all x6, blocking collectives: 99.7 us -> 105 us  [exchange(): return lax.all_to_all(parts, axes, 0, 0, tiled=True)]
    ppermute x1, starting transfers between devices: 2.39 us -> 4.84 us  [swapped_cores(): return lax.ppermute(array, 'core', [(0, 1), (1, 0)])]
  transfers between devices with their start and end apart: 7 -> 7, of which waited for: 5 -> 4; matrix products, arithmetic and copies ran while one was open for 3% -> 4% of each run, Pallas kernels for 8% -> 7%
where the time goes in v11:
time: 191 us; the launch traced here: 190 us
  blocking collectives  105 us (55%)
  starting transfers between devices  39.1 us (20%)
  Pallas kernels  21.1 us (11%)
  waiting for transfers between devices  15.2 us (8%)
  local copies, waits for them, and re-layouts  4.95 us (3%)
  other arithmetic  4.11 us (2%)
    all_to_all x6, blocking collectives, exchange(): return lax.all_to_all(parts, axes, 0, 0, tiled=True)  105 us
    all_to_all x3, starting transfers between devices, exchange(): return lax.all_to_all(parts, axes, 0, 0, tiled=True)  16.6 us
    ppermute x2, starting transfers between devices, doubled(): return jnp.concatenate([held, lax.ppermute(held, axis, pairs)])  14.6 us
    all_to_all x3, waiting for transfers between devices, exchange(): return lax.all_to_all(parts, axes, 0, 0, tiled=True)  12.7 us
    pallas_call x2, Pallas kernels, kernel_matrix(): pl.pallas_call(laplace_body, out_shape=jax.ShapeDtypeStruct((batch, colum...  11.3 us
    pallas_call x10, Pallas kernels, call(): pl.pallas_call(body, out_shape=out, in_specs=[vmem] * len(operands), out_...  7.25 us
    ppermute x1, starting transfers between devices, swapped_cores(): return lax.ppermute(array, 'core', [(0, 1), (1, 0)])  4.84 us
  transfers between devices with their start and end apart: 7, of which 4 were waited for; matrix products, arithmetic and copies ran while one was open for 4% of the time, Pallas kernels for 7%

profile of v11, /device:TPU:1, one launch (start us, length us, event | category | flops | bytes accessed | tf_op | source)
XLA Modules:
  0.0 189.8 jit_solution(15696957871705712261)
XLA Ops:
  0.0 2.5 %shard_map.55 = bf16[8,2,64,512]{3,2,1,0:T(8,128)(2,1)} custom-call(bf16[64,1024]{1,0:T(8,128)(2,1)} %pool_ref.1, s32[2,512]{1,0:T(2,128)} %picks_ref.1), custom_call_target="tpu_custom_call" | custom-call | flops 134217728 | bytes 131072 | tf_op jit(solution)/shard_map/pallas_call | solution.py:290
  2.5 7.7 %all-to-all-start = ((bf16[8,2,64,512]{3,2,1,0:T(8,128)(2,1)}), bf16[8,2,64,512]{3,2,1,0:T(8,128)(2,1)S(1)}, u32[]{:S(2)}, u32[]{:S(2)}) async-start(bf16[8,2,64,512]{3,2,1,0:T(8,128)(2,1)} %shard_map.55), calls=%async_computation | async-start | bytes 2097152 | tf_op jit(solution)/shard_map/all_to_all | solution.py:27
  10.1 1.0 fusion
  11.4 10.6 %collective-permute-start = (bf16[1,72,128]{2,1,0:T(8,128)(2,1)S(1)}, bf16[1,72,128]{2,1,0:T(8,128)(2,1)S(1)}, u32[]{:S(2)}, u32[]{:S(2)}) collective-permute-start(bf16[1,72,128]{2,1,0:T(8,128)(2,1)S(1)} %pad_maximum_fusion.3), channel_id=1, source_target_pairs={{0,16},{4,20},{8,24},{12,28},{16,0},{20,4},{24,8},{28,12},{1,17},{... | collective-permute-start | bytes 55304 | tf_op jit(solution)/shard_map/ppermute | solution.py:246
  22.8 3.1 %multiply_reduce_fusion = f32[2048]{0:T(1024)S(1)} fusion(bf16[1024,2048]{1,0:T(8,128)(2,1)} %centres_ref.3), kind=kLoop, calls=%fused_computation.2 | loop fusion | flops 6289408 | bytes 4202496 | tf_op jit(solution)/shard_map/reduce_sum | solution.py:366
  26.0 4.0 %collective-permute-start.1 = (bf16[2,72,128]{2,1,0:T(8,128)(2,1)S(1)}, bf16[2,72,128]{2,1,0:T(8,128)(2,1)S(1)}, u32[]{:S(2)}, u32[]{:S(2)}) collective-permute-start(bf16[2,72,128]{2,1,0:T(8,128)(2,1)S(1)} %pad_maximum_fusion.1), channel_id=1, source_target_pairs={{0,8},{4,12},{8,0},{12,4},{16,24},{20,28},{24,16},{28,20},{1,9},{5... | collective-permute-start | bytes 110600 | tf_op jit(solution)/shard_map/ppermute | solution.py:246
  32.0 3.1 %collective-permute-start.2 = (bf16[4,72,128]{2,1,0:T(8,128)(2,1)S(1)}, bf16[4,72,128]{2,1,0:T(8,128)(2,1)S(1)}, u32[]{:S(2)}, u32[]{:S(2)}) collective-permute-start(bf16[4,72,128]{2,1,0:T(8,128)(2,1)S(1)} %pad_maximum_fusion.held_ref), channel_id=1, source_target_pairs={{0,4},{4,0},{8,12},{12,8},{16,20},{20,16},{24,28},{28,24},{1,5},{5... | collective-permute-start | bytes 221192 | tf_op jit(solution)/shard_map/ppermute | solution.py:258
  35.1 2.2 %collective-permute-done.2.moved_ref = bf16[4,72,128]{2,1,0:T(8,128)(2,1)S(1)} collective-permute-done((bf16[4,72,128]{2,1,0:T(8,128)(2,1)S(1)}, bf16[4,72,128]{2,1,0:T(8,128)(2,1)S(1)}, u32[]{:S(2)}, u32[]{:S(2)}) %collective-permute-start.2) | collective-permute-done | bytes 73760 | tf_op jit(solution)/shard_map/ppermute | solution.py:258
  38.3 4.8 %collective-permute-start.3 = (bf16[8,2,64,512]{3,2,1,0:T(8,128)(2,1)S(1)}, bf16[8,2,64,512]{3,2,1,0:T(8,128)(2,1)S(1)}, u32[]{:S(2)}, u32[]{:S(2)}) collective-permute-start(bf16[8,2,64,512]{3,2,1,0:T(8,128)(2,1)S(1)} %all-to-all-done.mine_ref), channel_id=1, source_target_pairs={{0,32},{32,0},{1,33},{33,1},{2,34},{34,2},{3,35},{35,3},{4,36},{36... | collective-permute-start | bytes 3145736 | tf_op jit(solution)/shard_map/ppermute | solution.py:264
  43.1 4.0 %all-to-all-start.1 = ((bf16[4,8,72,128]{3,2,1,0:T(8,128)(2,1)}), bf16[4,8,72,128]{3,2,1,0:T(8,128)(2,1)S(1)}, u32[]{:S(2)}, u32[]{:S(2)}) async-start(bf16[4,8,72,128]{3,2,1,0:T(8,128)(2,1)} %shard_map.56), calls=%async_computation.1 | async-start | bytes 1179648 | tf_op jit(solution)/shard_map/all_to_all | solution.py:27
  48.3 5.7 %shard_map.58.kern_ref = bf16[512,2048]{1,0:T(8,128)(2,1)S(1)} custom-call(bf16[8,2,64,512]{3,2,1,0:T(8,128)(2,1)S(1)} %get-tuple-element.17.feats_ref, bf16[1024,2048]{1,0:T(8,128)(2,1)} %centres_ref.3, f32[1,2048]{1,0:T(1,128)S(1)} %bitcast.12), custom_call_target="tpu_custom_call" | custom-call | flops 2147483648 | bytes 4194304 | tf_op jit(solution)/shard_map/pallas_call | solution.py:224
  53.9 3.2 %all-to-all-done.1.coef_ref = bf16[4,8,72,128]{3,2,1,0:T(8,128)(2,1)S(1)} async-done(((bf16[4,8,72,128]{3,2,1,0:T(8,128)(2,1)}), bf16[4,8,72,128]{3,2,1,0:T(8,128)(2,1)S(1)}, u32[]{:S(2)}, u32[]{:S(2)}) %all-to-all-start.1) | async-done | bytes 589856 | tf_op jit(solution)/shard_map/all_to_all | solution.py:27
  57.2 1.2 shard_map.59
  58.4 17.8 %all_to_all.45.arrived_ref = bf16[16,36,128]{2,1,0:T(8,128)(2,1)S(1)} all-to-all(bf16[16,36,128]{2,1,0:T(8,128)(2,1)S(1)} %shard_map.59), channel_id=1, replica_groups=mesh['y'=8,'core'=2,'z'=8,'x'=4] {'y','core'}, dimensions={0} | all-to-all | bytes 294912 | tf_op jit(solution)/shard_map/all_to_all | solution.py:27
  76.5 12.3 %all_to_all.46.resid_ref = bf16[16,36,128]{2,1,0:T(8,128)(2,1)S(1)} all-to-all(bf16[16,36,128]{2,1,0:T(8,128)(2,1)S(1)} %shard_map.60), channel_id=1, replica_groups=mesh['y'=8,'core'=2,'z'=8,'x'=4] {'y','core'}, dimensions={0} | all-to-all | bytes 294912 | tf_op jit(solution)/shard_map/all_to_all | solution.py:27
  89.5 24.5 %all_to_all.47.arrived_ref = bf16[32,72,128]{2,1,0:T(8,128)(2,1)S(1)} all-to-all(bf16[32,72,128]{2,1,0:T(8,128)(2,1)S(1)} %shard_map.61), channel_id=1, replica_groups=mesh['y'=8,'core'=2,'z'=8,'x'=4] {'z','x'}, dimensions={0} | all-to-all | bytes 1179648 | tf_op jit(solution)/shard_map/all_to_all | solution.py:27
  115.0 4.9 %all-to-all-start.5 = ((bf16[32,72,128]{2,1,0:T(8,128)(2,1)}), bf16[32,72,128]{2,1,0:T(8,128)(2,1)S(1)}, u32[]{:S(2)}, u32[]{:S(2)}) async-start(bf16[32,72,128]{2,1,0:T(8,128)(2,1)} %get-tuple-element.21), calls=%async_computation.5 | async-start | bytes 1179648 | tf_op jit(solution)/shard_map/all_to_all | solution.py:27
  119.9 1.2 copy-done.2
  121.1 5.7 %shard_map.63.kern_ref = bf16[512,2048]{1,0:T(8,128)(2,1)S(1)} custom-call(bf16[8,2,64,512]{3,2,1,0:T(8,128)(2,1)S(1)} %copy-done.2, bf16[1024,2048]{1,0:T(8,128)(2,1)} %centres_ref.3, f32[1,2048]{1,0:T(1,128)S(1)} %bitcast.13), custom_call_target="tpu_custom_call" | custom-call | flops 2147483648 | bytes 4194304 | tf_op jit(solution)/shard_map/pallas_call | solution.py:224
  126.8 9.5 %all-to-all-done.5 = bf16[32,72,128]{2,1,0:T(8,128)(2,1)S(1)} async-done(((bf16[32,72,128]{2,1,0:T(8,128)(2,1)}), bf16[32,72,128]{2,1,0:T(8,128)(2,1)S(1)}, u32[]{:S(2)}, u32[]{:S(2)}) %all-to-all-start.5) | async-done | bytes 589856 | tf_op jit(solution)/shard_map/all_to_all | solution.py:27
  136.2 1.0 shard_map.64
  137.2 15.7 %all_to_all.48.arrived_ref = bf16[16,36,128]{2,1,0:T(8,128)(2,1)S(1)} all-to-all(bf16[16,36,128]{2,1,0:T(8,128)(2,1)S(1)} %shard_map.64), channel_id=1, replica_groups=mesh['y'=8,'core'=2,'z'=8,'x'=4] {'y','core'}, dimensions={0} | all-to-all | bytes 294912 | tf_op jit(solution)/shard_map/all_to_all | solution.py:27
  153.3 12.1 %all_to_all.49.resid_ref = bf16[16,36,128]{2,1,0:T(8,128)(2,1)S(1)} all-to-all(bf16[16,36,128]{2,1,0:T(8,128)(2,1)S(1)} %shard_map.65), channel_id=1, replica_groups=mesh['y'=8,'core'=2,'z'=8,'x'=4] {'y','core'}, dimensions={0} | all-to-all | bytes 294912 | tf_op jit(solution)/shard_map/all_to_all | solution.py:27
  166.2 22.8 %all_to_all.50.arrived_ref = bf16[32,72,128]{2,1,0:T(8,128)(2,1)S(1)} all-to-all(bf16[32,72,128]{2,1,0:T(8,128)(2,1)S(1)} %shard_map.66), channel_id=1, replica_groups=mesh['y'=8,'core'=2,'z'=8,'x'=4] {'z','x'}, dimensions={0} | all-to-all | bytes 1179648 | tf_op jit(solution)/shard_map/all_to_all | solution.py:27
  (35 shorter events, 9.1 us)
Async XLA Ops:
  0.0 30.0 %copy-start = (s32[1024]{0:T(1024)S(1)}, s32[1024]{0:T(1024)}, u32[]{:S(2)}) copy-start(s32[1024]{0:T(1024)} %param.7) | copy-start | bytes 12292
  2.5 35.8 %all-to-all-start = ((bf16[8,2,64,512]{3,2,1,0:T(8,128)(2,1)}), bf16[8,2,64,512]{3,2,1,0:T(8,128)(2,1)S(1)}, u32[]{:S(2)}, u32[]{:S(2)}) async-start(bf16[8,2,64,512]{3,2,1,0:T(8,128)(2,1)} %shard_map.55), calls=%async_computation | async-start | bytes 2097152 | tf_op jit(solution)/shard_map/all_to_all | solution.py:27
  11.4 14.5 %collective-permute-start = (bf16[1,72,128]{2,1,0:T(8,128)(2,1)S(1)}, bf16[1,72,128]{2,1,0:T(8,128)(2,1)S(1)}, u32[]{:S(2)}, u32[]{:S(2)}) collective-permute-start(bf16[1,72,128]{2,1,0:T(8,128)(2,1)S(1)} %pad_maximum_fusion.3), channel_id=1, source_target_pairs={{0,16},{4,20},{8,24},{12,28},{16,0},{20,4},{24,8},{28,12},{1,17},{... | collective-permute-start | bytes 55304 | tf_op jit(solution)/shard_map/ppermute | solution.py:246
  26.0 5.9 %collective-permute-start.1 = (bf16[2,72,128]{2,1,0:T(8,128)(2,1)S(1)}, bf16[2,72,128]{2,1,0:T(8,128)(2,1)S(1)}, u32[]{:S(2)}, u32[]{:S(2)}) collective-permute-start(bf16[2,72,128]{2,1,0:T(8,128)(2,1)S(1)} %pad_maximum_fusion.1), channel_id=1, source_target_pairs={{0,8},{4,12},{8,0},{12,4},{16,24},{20,28},{24,16},{28,20},{1,9},{5... | collective-permute-start | bytes 110600 | tf_op jit(solution)/shard_map/ppermute | solution.py:246
  32.0 5.4 %collective-permute-start.2 = (bf16[4,72,128]{2,1,0:T(8,128)(2,1)S(1)}, bf16[4,72,128]{2,1,0:T(8,128)(2,1)S(1)}, u32[]{:S(2)}, u32[]{:S(2)}) collective-permute-start(bf16[4,72,128]{2,1,0:T(8,128)(2,1)S(1)} %pad_maximum_fusion.held_ref), channel_id=1, source_target_pairs={{0,4},{4,0},{8,12},{12,8},{16,20},{20,16},{24,28},{28,24},{1,5},{5... | collective-permute-start | bytes 221192 | tf_op jit(solution)/shard_map/ppermute | solution.py:258
  38.3 8.9 %collective-permute-start.3 = (bf16[8,2,64,512]{3,2,1,0:T(8,128)(2,1)S(1)}, bf16[8,2,64,512]{3,2,1,0:T(8,128)(2,1)S(1)}, u32[]{:S(2)}, u32[]{:S(2)}) collective-permute-start(bf16[8,2,64,512]{3,2,1,0:T(8,128)(2,1)S(1)} %all-to-all-done.mine_ref), channel_id=1, source_target_pairs={{0,32},{32,0},{1,33},{33,1},{2,34},{34,2},{3,35},{35,3},{4,36},{36... | collective-permute-start | bytes 3145736 | tf_op jit(solution)/shard_map/ppermute | solution.py:264
  43.1 14.0 %all-to-all-start.1 = ((bf16[4,8,72,128]{3,2,1,0:T(8,128)(2,1)}), bf16[4,8,72,128]{3,2,1,0:T(8,128)(2,1)S(1)}, u32[]{:S(2)}, u32[]{:S(2)}) async-start(bf16[4,8,72,128]{3,2,1,0:T(8,128)(2,1)} %shard_map.56), calls=%async_computation.1 | async-start | bytes 1179648 | tf_op jit(solution)/shard_map/all_to_all | solution.py:27
  47.3 1.0 copy-start.1
  115.0 21.3 %all-to-all-start.5 = ((bf16[32,72,128]{2,1,0:T(8,128)(2,1)}), bf16[32,72,128]{2,1,0:T(8,128)(2,1)S(1)}, u32[]{:S(2)}, u32[]{:S(2)}) async-start(bf16[32,72,128]{2,1,0:T(8,128)(2,1)} %get-tuple-element.21), calls=%async_computation.5 | async-start | bytes 1179648 | tf_op jit(solution)/shard_map/all_to_all | solution.py:27
  119.9 1.2 copy-start.2

commit v12 on v11

--- a/solution.py
+++ b/solution.py
@@ -18,7 +18,6 @@
 LANES = 128
 KERN_VMEM = 48
 PICK_VMEM = 60
-COPIES_COST = 1000
 CENTRE = ("y", "core")
 SAMPLE = ("z", "x")
 
@@ -61,22 +60,30 @@
     return out
 
 
-def logits_body(offsets, coef_ref, kern_ref, out_ref, coef, logits):
-    over_z, over_x, height, _ = coef_ref.shape
-    if offsets is not None:
-        over_z, over_x = over_x, over_z
-    for i in range(over_z):
-        for p in range(over_x // 2):
-            if offsets is None:
-                pair = coef_ref[i, 2 * p], coef_ref[i, 2 * p + 1]
-                at = LANES * (i * over_x // 2 + p)
-            else:
-                pair = coef_ref[2 * p, i], coef_ref[2 * p + 1, i]
-                at = LANES * (lax.bitwise_xor(lax.axis_index("z"), offsets[i]) * (over_x // 2) + p)
-                at = pl.multiple_of(at, LANES)
-            halves = regroup([block.astype(jnp.float32) for block in pair], 2)
-            for h in range(2):
-                coef[height * h : height * (h + 1), pl.ds(at, LANES)] = halves[h]
+def first_coefs(offsets, part_refs):
+    z, x = lax.axis_index("z"), lax.axis_index("x")
+    odd = lax.rem(x, 2) == 1
+    for i, offset in enumerate(offsets):
+        for k in range(0, len(part_refs), 2):
+            near, far = [part_refs[k + j][i].astype(jnp.float32) for j in range(2)]
+            pair = jnp.where(odd, far, near), jnp.where(odd, near, far)
+            row = lax.bitwise_xor(z, offset) * (len(part_refs) // 2)
+            yield pair, pl.multiple_of(LANES * (row + lax.bitwise_xor(x // 2, k // 2)), LANES)
+
+
+def later_coefs(coef_ref):
+    for p in range(coef_ref.shape[0] // 2):
+        yield [coef_ref[2 * p + j].astype(jnp.float32) for j in range(2)], LANES * p
+
+
+def logits_body(offsets, *refs):
+    *part_refs, kern_ref, out_ref, coef, logits = refs
+    height = part_refs[0].shape[1]
+    pairs = later_coefs(*part_refs) if offsets is None else first_coefs(offsets, part_refs)
+    for pair, at in pairs:
+        halves = regroup(pair, 2)
+        for h in range(2):
+            coef[height * h : height * (h + 1), pl.ds(at, LANES)] = halves[h]
     logits[...] = lax.dot_general(
         coef[...].astype(jnp.bfloat16),
         kern_ref[...],
@@ -93,14 +100,14 @@
 
 
 def partial_logits(coef_parts, kern, peers, offsets=None):
-    classes = 2 * coef_parts.shape[2]
+    classes = 2 * coef_parts[0].shape[1]
     batch, centres = kern.shape
     rows = classes * (batch // peers) // LANES
     return call(
         functools.partial(logits_body, offsets),
         jax.ShapeDtypeStruct((peers, rows, LANES), jnp.bfloat16),
         2 * classes * batch * centres,
-        coef_parts,
+        *coef_parts,
         kern,
         scratch=[pltpu.VMEM((classes, centres), jnp.float32), pltpu.VMEM((classes, batch), jnp.float32)],
     )
@@ -246,20 +253,6 @@
     return jnp.concatenate([held, lax.ppermute(held, axis, pairs)])
 
 
-def copies_body(held_ref, moved_ref, out_ref):
-    near = held_ref.shape[0]
-    for copy in range(out_ref.shape[0]):
-        out_ref[copy, :near] = held_ref[...]
-        out_ref[copy, near:] = moved_ref[...]
-
-
-def last_doubled(held, axis, hop, copies):
-    pairs = [(i, i ^ hop) for i in range(lax.axis_size(axis))]
-    moved = lax.ppermute(held, axis, pairs)
-    out = jax.ShapeDtypeStruct((copies, 2 * held.shape[0], *held.shape[1:]), held.dtype)
-    return call(copies_body, out, COPIES_COST, held, moved)
-
-
 def swapped_cores(array):
     return lax.ppermute(array, "core", [(0, 1), (1, 0)])
 
@@ -373,15 +366,16 @@
 
     z_hops = [1 << i for i in reversed(range(over_z.bit_length() - 1))]
     held = packed.astype(jnp.bfloat16)[None]
-    for hop in z_hops[:-1]:
+    for hop in z_hops:
         held = doubled(held, "z", hop)
+    coef_parts = [held] + [
+        lax.ppermute(held, "x", [(i, i ^ k) for i in range(over_x)]) for k in range(1, over_x)
+    ]
     mine = exchange(picked(pool, picks, lax.axis_size("y")), "y")
     labs = [own_labels(step) for step in range(STEPS)]
-    spread_out = last_doubled(held, "z", z_hops[-1], over_x)
-    mine, spread_out, centre_sq, packed, labs = lax.optimization_barrier(
-        (mine, spread_out, centre_sq, packed, labs)
-    )
-    coef_parts = exchange(spread_out, "x")
+    mine, held, centre_sq, packed, labs = lax.optimization_barrier(
+        (mine, held, centre_sq, packed, labs)
+    )
     first, later = assembled(mine, swapped_cores(mine))
     kern = kernel_matrix(first, centres, centre_sq)
 
@@ -392,7 +386,7 @@
     current, half = updated(arrived, packed, rate)
 
     kern = kernel_matrix(later, centres, centre_sq)
-    coef_parts = exchange(half, SAMPLE).reshape(over_z, over_x, *current.shape)
+    coef_parts = [exchange(half, SAMPLE)]
     arrived = exchange(partial_logits(coef_parts, kern, n_centre), CENTRE)
     resid = exchange(residual(arrived, labs[1], gain, fold), CENTRE)
     arrived = exchange(partial_grad(resid, kern, n_sample), SAMPLE)

time: 191 us -> 193 us (1.010)
  starting transfers between devices: 39.1 us -> 44.1 us
  waiting for transfers between devices: 15.2 us -> 12 us
  blocking collectives: 105 us -> 107 us
    ppermute x1 -> x3, starting transfers between devices: 3.09 us -> 8.98 us  [on_device(): lax.ppermute(held, 'x', [(i, i ^ k) for i in range(over_x)])]
    all_to_all x3 -> x2, starting transfers between devices: 16.6 us -> 12.5 us  [exchange(): return lax.all_to_all(parts, axes, 0, 0, tiled=True)]
    all_to_all x3 -> x2, waiting for transfers between devices: 12.7 us -> 9.46 us  [exchange(): return lax.all_to_all(parts, axes, 0, 0, tiled=True)]
    ppermute x2 -> x3, starting transfers between devices: 14.6 us -> 17.7 us  [doubled(): return jnp.concatenate([held, lax.ppermute(held, axis, pairs)])]
    ppermute x2 -> x3, waiting for transfers between devices: 0.32 us -> 2.53 us  [doubled(): return jnp.concatenate([held, lax.ppermute(held, axis, pairs)])]
    ppermute x1 -> x3, waiting for transfers between devices: 2.2 us -> 0.01 us  [on_device(): lax.ppermute(held, 'x', [(i, i ^ k) for i in range(over_x)])]
    pallas_call x10 -> x9, Pallas kernels: 7.25 us -> 6.32 us  [call(): pl.pallas_call(body, out_shape=out, in_specs=[vmem] * len(operands), out_...]
  transfers between devices with their start and end apart: 7 -> 9, of which waited for: 4 -> 3; matrix products, arithmetic and copies ran while one was open for 4% -> 4% of each run, Pallas kernels for 7% -> 6%
where the time goes in v12:
time: 193 us; the launch traced here: 192 us
  blocking collectives  107 us (55%)
  starting transfers between devices  44.1 us (23%)
  Pallas kernels  20.2 us (10%)
  waiting for transfers between devices  12 us (6%)
  local copies, waits for them, and re-layouts  4.96 us (3%)
  other arithmetic  4.19 us (2%)
    all_to_all x6, blocking collectives, exchange(): return lax.all_to_all(parts, axes, 0, 0, tiled=True)  107 us
    ppermute x3, starting transfers between devices, doubled(): return jnp.concatenate([held, lax.ppermute(held, axis, pairs)])  17.7 us
    all_to_all x2, starting transfers between devices, exchange(): return lax.all_to_all(parts, axes, 0, 0, tiled=True)  12.5 us
    pallas_call x2, Pallas kernels, kernel_matrix(): pl.pallas_call(laplace_body, out_shape=jax.ShapeDtypeStruct((batch, colum...  11.4 us
    all_to_all x2, waiting for transfers between devices, exchange(): return lax.all_to_all(parts, axes, 0, 0, tiled=True)  9.46 us
    ppermute x3, starting transfers between devices, on_device(): lax.ppermute(held, 'x', [(i, i ^ k) for i in range(over_x)])  8.98 us
    pallas_call x9, Pallas kernels, call(): pl.pallas_call(body, out_shape=out, in_specs=[vmem] * len(operands), out_...  6.32 us
    ppermute x1, starting transfers between devices, swapped_cores(): return lax.ppermute(array, 'core', [(0, 1), (1, 0)])  4.85 us
  transfers between devices with their start and end apart: 9, of which 3 were waited for; matrix products, arithmetic and copies ran while one was open for 4% of the time, Pallas kernels for 6%

profile of v12, /device:TPU:1, one launch (start us, length us, event | category | flops | bytes accessed | tf_op | source)
XLA Modules:
  0.0 192.4 jit_solution(12894658652216726832)
XLA Ops:
  0.0 2.5 %shard_map.55 = bf16[8,2,64,512]{3,2,1,0:T(8,128)(2,1)} custom-call(bf16[64,1024]{1,0:T(8,128)(2,1)} %pool_ref.1, s32[2,512]{1,0:T(2,128)} %picks_ref.1), custom_call_target="tpu_custom_call" | custom-call | flops 134217728 | bytes 131072 | tf_op jit(solution)/shard_map/pallas_call | solution.py:283
  2.5 7.7 %all-to-all-start = ((bf16[8,2,64,512]{3,2,1,0:T(8,128)(2,1)}), bf16[8,2,64,512]{3,2,1,0:T(8,128)(2,1)S(1)}, u32[]{:S(2)}, u32[]{:S(2)}) async-start(bf16[8,2,64,512]{3,2,1,0:T(8,128)(2,1)} %shard_map.55), calls=%async_computation | async-start | bytes 2097152 | tf_op jit(solution)/shard_map/all_to_all | solution.py:26
  11.4 10.6 %collective-permute-start = (bf16[1,72,128]{2,1,0:T(8,128)(2,1)S(1)}, bf16[1,72,128]{2,1,0:T(8,128)(2,1)S(1)}, u32[]{:S(2)}, u32[]{:S(2)}) collective-permute-start(bf16[1,72,128]{2,1,0:T(8,128)(2,1)S(1)} %pad_maximum_fusion.4), channel_id=1, source_target_pairs={{0,16},{4,20},{8,24},{12,28},{16,0},{20,4},{24,8},{28,12},{1,17},{... | collective-permute-start | bytes 55304 | tf_op jit(solution)/shard_map/ppermute | solution.py:253
  22.8 3.1 %multiply_reduce_fusion = f32[2048]{0:T(1024)S(1)} fusion(bf16[1024,2048]{1,0:T(8,128)(2,1)} %centres_ref.3), kind=kLoop, calls=%fused_computation.2 | loop fusion | flops 6289408 | bytes 4202496 | tf_op jit(solution)/shard_map/reduce_sum | solution.py:359
  26.0 4.0 %collective-permute-start.1 = (bf16[2,72,128]{2,1,0:T(8,128)(2,1)S(1)}, bf16[2,72,128]{2,1,0:T(8,128)(2,1)S(1)}, u32[]{:S(2)}, u32[]{:S(2)}) collective-permute-start(bf16[2,72,128]{2,1,0:T(8,128)(2,1)S(1)} %pad_maximum_fusion.2), channel_id=1, source_target_pairs={{0,8},{4,12},{8,0},{12,4},{16,24},{20,28},{24,16},{28,20},{1,9},{5... | collective-permute-start | bytes 110600 | tf_op jit(solution)/shard_map/ppermute | solution.py:253
  32.0 3.1 %collective-permute-start.2 = (bf16[4,72,128]{2,1,0:T(8,128)(2,1)S(1)}, bf16[4,72,128]{2,1,0:T(8,128)(2,1)S(1)}, u32[]{:S(2)}, u32[]{:S(2)}) collective-permute-start(bf16[4,72,128]{2,1,0:T(8,128)(2,1)S(1)} %pad_maximum_fusion.1), channel_id=1, source_target_pairs={{0,4},{4,0},{8,12},{12,8},{16,20},{20,16},{24,28},{28,24},{1,5},{5... | collective-permute-start | bytes 221192 | tf_op jit(solution)/shard_map/ppermute | solution.py:253
  35.2 2.2 %collective-permute-done.2 = bf16[4,72,128]{2,1,0:T(8,128)(2,1)S(1)} collective-permute-done((bf16[4,72,128]{2,1,0:T(8,128)(2,1)S(1)}, bf16[4,72,128]{2,1,0:T(8,128)(2,1)S(1)}, u32[]{:S(2)}, u32[]{:S(2)}) %collective-permute-start.2) | collective-permute-done | bytes 73760 | tf_op jit(solution)/shard_map/ppermute | solution.py:253
  37.4 4.9 %collective-permute-start.6 = (bf16[8,2,64,512]{3,2,1,0:T(8,128)(2,1)S(1)}, bf16[8,2,64,512]{3,2,1,0:T(8,128)(2,1)S(1)}, u32[]{:S(2)}, u32[]{:S(2)}) collective-permute-start(bf16[8,2,64,512]{3,2,1,0:T(8,128)(2,1)S(1)} %all-to-all-done.mine_ref), channel_id=1, source_target_pairs={{0,32},{32,0},{1,33},{33,1},{2,34},{34,2},{3,35},{35,3},{4,36},{36... | collective-permute-start | bytes 3145736 | tf_op jit(solution)/shard_map/ppermute | solution.py:257
  42.3 4.4 %collective-permute-start.5 = (bf16[8,72,128]{2,1,0:T(8,128)(2,1)S(1)}, bf16[8,72,128]{2,1,0:T(8,128)(2,1)S(1)}, u32[]{:S(2)}, u32[]{:S(2)}) collective-permute-start(bf16[8,72,128]{2,1,0:T(8,128)(2,1)S(1)} %pad_maximum_fusion.refs_0_), channel_id=1, source_target_pairs={{0,3},{1,2},{2,1},{3,0},{4,7},{5,6},{6,5},{7,4},{8,11},{9,10},{10,... | collective-permute-start | bytes 442376 | tf_op jit(solution)/shard_map/ppermute | solution.py:372
  46.7 2.4 %collective-permute-start.4 = (bf16[8,72,128]{2,1,0:T(8,128)(2,1)S(1)}, bf16[8,72,128]{2,1,0:T(8,128)(2,1)S(1)}, u32[]{:S(2)}, u32[]{:S(2)}) collective-permute-start(bf16[8,72,128]{2,1,0:T(8,128)(2,1)S(1)} %pad_maximum_fusion.refs_0_), channel_id=1, source_target_pairs={{0,2},{1,3},{2,0},{3,1},{4,6},{5,7},{6,4},{7,5},{8,10},{9,11},{10,... | collective-permute-start | bytes 442376 | tf_op jit(solution)/shard_map/ppermute | solution.py:372
  49.1 2.2 %collective-permute-start.3 = (bf16[8,72,128]{2,1,0:T(8,128)(2,1)S(1)}, bf16[8,72,128]{2,1,0:T(8,128)(2,1)S(1)}, u32[]{:S(2)}, u32[]{:S(2)}) collective-permute-start(bf16[8,72,128]{2,1,0:T(8,128)(2,1)S(1)} %pad_maximum_fusion.refs_0_), channel_id=1, source_target_pairs={{0,1},{1,0},{2,3},{3,2},{4,5},{5,4},{6,7},{7,6},{8,9},{9,8},{10,11... | collective-permute-start | bytes 442376 | tf_op jit(solution)/shard_map/ppermute | solution.py:372
  52.5 5.7 %shard_map.57.refs_4_.kern_ref = bf16[512,2048]{1,0:T(8,128)(2,1)S(1)} custom-call(bf16[8,2,64,512]{3,2,1,0:T(8,128)(2,1)S(1)} %get-tuple-element.15.feats_ref, bf16[1024,2048]{1,0:T(8,128)(2,1)} %centres_ref.3, f32[1,2048]{1,0:T(1,128)S(1)} %bitcast.10), custom_call_target="tpu_custom_call" | custom-call | flops 2147483648 | bytes 4194304 | tf_op jit(solution)/shard_map/pallas_call | solution.py:231
  58.2 1.3 shard_map.58
  59.4 17.5 %all_to_all.40.arrived_ref = bf16[16,36,128]{2,1,0:T(8,128)(2,1)S(1)} all-to-all(bf16[16,36,128]{2,1,0:T(8,128)(2,1)S(1)} %shard_map.58), channel_id=1, replica_groups=mesh['y'=8,'core'=2,'z'=8,'x'=4] {'y','core'}, dimensions={0} | all-to-all | bytes 294912 | tf_op jit(solution)/shard_map/all_to_all | solution.py:26
  77.3 12.3 %all_to_all.41.resid_ref = bf16[16,36,128]{2,1,0:T(8,128)(2,1)S(1)} all-to-all(bf16[16,36,128]{2,1,0:T(8,128)(2,1)S(1)} %shard_map.59), channel_id=1, replica_groups=mesh['y'=8,'core'=2,'z'=8,'x'=4] {'y','core'}, dimensions={0} | all-to-all | bytes 294912 | tf_op jit(solution)/shard_map/all_to_all | solution.py:26
  90.3 26.3 %all_to_all.42.arrived_ref = bf16[32,72,128]{2,1,0:T(8,128)(2,1)S(1)} all-to-all(bf16[32,72,128]{2,1,0:T(8,128)(2,1)S(1)} %shard_map.60), channel_id=1, replica_groups=mesh['y'=8,'core'=2,'z'=8,'x'=4] {'z','x'}, dimensions={0} | all-to-all | bytes 1179648 | tf_op jit(solution)/shard_map/all_to_all | solution.py:26
  117.6 4.9 %all-to-all-start.4 = ((bf16[32,72,128]{2,1,0:T(8,128)(2,1)}), bf16[32,72,128]{2,1,0:T(8,128)(2,1)S(1)}, u32[]{:S(2)}, u32[]{:S(2)}) async-start(bf16[32,72,128]{2,1,0:T(8,128)(2,1)} %get-tuple-element.19), calls=%async_computation.4 | async-start | bytes 1179648 | tf_op jit(solution)/shard_map/all_to_all | solution.py:26
  122.5 1.2 copy-done.2
  123.7 5.7 %shard_map.62.refs_1_.kern_ref = bf16[512,2048]{1,0:T(8,128)(2,1)S(1)} custom-call(bf16[8,2,64,512]{3,2,1,0:T(8,128)(2,1)S(1)} %copy-done.2, bf16[1024,2048]{1,0:T(8,128)(2,1)} %centres_ref.3, f32[1,2048]{1,0:T(1,128)S(1)} %bitcast.11), custom_call_target="tpu_custom_call" | custom-call | flops 2147483648 | bytes 4194304 | tf_op jit(solution)/shard_map/pallas_call | solution.py:231
  129.4 9.5 %all-to-all-done.4.refs_0_ = bf16[32,72,128]{2,1,0:T(8,128)(2,1)S(1)} async-done(((bf16[32,72,128]{2,1,0:T(8,128)(2,1)}), bf16[32,72,128]{2,1,0:T(8,128)(2,1)S(1)}, u32[]{:S(2)}, u32[]{:S(2)}) %all-to-all-start.4) | async-done | bytes 589856 | tf_op jit(solution)/shard_map/all_to_all | solution.py:26
  138.8 1.0 shard_map.63
  139.9 15.7 %all_to_all.43.arrived_ref = bf16[16,36,128]{2,1,0:T(8,128)(2,1)S(1)} all-to-all(bf16[16,36,128]{2,1,0:T(8,128)(2,1)S(1)} %shard_map.63), channel_id=1, replica_groups=mesh['y'=8,'core'=2,'z'=8,'x'=4] {'y','core'}, dimensions={0} | all-to-all | bytes 294912 | tf_op jit(solution)/shard_map/all_to_all | solution.py:26
  156.0 12.1 %all_to_all.44.resid_ref = bf16[16,36,128]{2,1,0:T(8,128)(2,1)S(1)} all-to-all(bf16[16,36,128]{2,1,0:T(8,128)(2,1)S(1)} %shard_map.64), channel_id=1, replica_groups=mesh['y'=8,'core'=2,'z'=8,'x'=4] {'y','core'}, dimensions={0} | all-to-all | bytes 294912 | tf_op jit(solution)/shard_map/all_to_all | solution.py:26
  168.8 22.8 %all_to_all.45.arrived_ref = bf16[32,72,128]{2,1,0:T(8,128)(2,1)S(1)} all-to-all(bf16[32,72,128]{2,1,0:T(8,128)(2,1)S(1)} %shard_map.65), channel_id=1, replica_groups=mesh['y'=8,'core'=2,'z'=8,'x'=4] {'z','x'}, dimensions={0} | all-to-all | bytes 1179648 | tf_op jit(solution)/shard_map/all_to_all | solution.py:26
  (39 shorter events, 9.3 us)
Async XLA Ops:
  0.0 30.0 %copy-start = (s32[1024]{0:T(1024)S(1)}, s32[1024]{0:T(1024)}, u32[]{:S(2)}) copy-start(s32[1024]{0:T(1024)} %param.7) | copy-start | bytes 12292
  2.5 34.9 %all-to-all-start = ((bf16[8,2,64,512]{3,2,1,0:T(8,128)(2,1)}), bf16[8,2,64,512]{3,2,1,0:T(8,128)(2,1)S(1)}, u32[]{:S(2)}, u32[]{:S(2)}) async-start(bf16[8,2,64,512]{3,2,1,0:T(8,128)(2,1)} %shard_map.55), calls=%async_computation | async-start | bytes 2097152 | tf_op jit(solution)/shard_map/all_to_all | solution.py:26
  11.4 14.5 %collective-permute-start = (bf16[1,72,128]{2,1,0:T(8,128)(2,1)S(1)}, bf16[1,72,128]{2,1,0:T(8,128)(2,1)S(1)}, u32[]{:S(2)}, u32[]{:S(2)}) collective-permute-start(bf16[1,72,128]{2,1,0:T(8,128)(2,1)S(1)} %pad_maximum_fusion.4), channel_id=1, source_target_pairs={{0,16},{4,20},{8,24},{12,28},{16,0},{20,4},{24,8},{28,12},{1,17},{... | collective-permute-start | bytes 55304 | tf_op jit(solution)/shard_map/ppermute | solution.py:253
  26.0 5.9 %collective-permute-start.1 = (bf16[2,72,128]{2,1,0:T(8,128)(2,1)S(1)}, bf16[2,72,128]{2,1,0:T(8,128)(2,1)S(1)}, u32[]{:S(2)}, u32[]{:S(2)}) collective-permute-start(bf16[2,72,128]{2,1,0:T(8,128)(2,1)S(1)} %pad_maximum_fusion.2), channel_id=1, source_target_pairs={{0,8},{4,12},{8,0},{12,4},{16,24},{20,28},{24,16},{28,20},{1,9},{5... | collective-permute-start | bytes 110600 | tf_op jit(solution)/shard_map/ppermute | solution.py:253
  32.0 5.4 %collective-permute-start.2 = (bf16[4,72,128]{2,1,0:T(8,128)(2,1)S(1)}, bf16[4,72,128]{2,1,0:T(8,128)(2,1)S(1)}, u32[]{:S(2)}, u32[]{:S(2)}) collective-permute-start(bf16[4,72,128]{2,1,0:T(8,128)(2,1)S(1)} %pad_maximum_fusion.1), channel_id=1, source_target_pairs={{0,4},{4,0},{8,12},{12,8},{16,20},{20,16},{24,28},{28,24},{1,5},{5... | collective-permute-start | bytes 221192 | tf_op jit(solution)/shard_map/ppermute | solution.py:253
  37.4 13.9 %collective-permute-start.6 = (bf16[8,2,64,512]{3,2,1,0:T(8,128)(2,1)S(1)}, bf16[8,2,64,512]{3,2,1,0:T(8,128)(2,1)S(1)}, u32[]{:S(2)}, u32[]{:S(2)}) collective-permute-start(bf16[8,2,64,512]{3,2,1,0:T(8,128)(2,1)S(1)} %all-to-all-done.mine_ref), channel_id=1, source_target_pairs={{0,32},{32,0},{1,33},{33,1},{2,34},{34,2},{3,35},{35,3},{4,36},{36... | collective-permute-start | bytes 3145736 | tf_op jit(solution)/shard_map/ppermute | solution.py:257
  42.3 15.8 %collective-permute-start.5 = (bf16[8,72,128]{2,1,0:T(8,128)(2,1)S(1)}, bf16[8,72,128]{2,1,0:T(8,128)(2,1)S(1)}, u32[]{:S(2)}, u32[]{:S(2)}) collective-permute-start(bf16[8,72,128]{2,1,0:T(8,128)(2,1)S(1)} %pad_maximum_fusion.refs_0_), channel_id=1, source_target_pairs={{0,3},{1,2},{2,1},{3,0},{4,7},{5,6},{6,5},{7,4},{8,11},{9,10},{10,... | collective-permute-start | bytes 442376 | tf_op jit(solution)/shard_map/ppermute | solution.py:372
  46.7 11.5 %collective-permute-start.4 = (bf16[8,72,128]{2,1,0:T(8,128)(2,1)S(1)}, bf16[8,72,128]{2,1,0:T(8,128)(2,1)S(1)}, u32[]{:S(2)}, u32[]{:S(2)}) collective-permute-start(bf16[8,72,128]{2,1,0:T(8,128)(2,1)S(1)} %pad_maximum_fusion.refs_0_), channel_id=1, source_target_pairs={{0,2},{1,3},{2,0},{3,1},{4,6},{5,7},{6,4},{7,5},{8,10},{9,11},{10,... | collective-permute-start | bytes 442376 | tf_op jit(solution)/shard_map/ppermute | solution.py:372
  49.1 9.0 %collective-permute-start.3 = (bf16[8,72,128]{2,1,0:T(8,128)(2,1)S(1)}, bf16[8,72,128]{2,1,0:T(8,128)(2,1)S(1)}, u32[]{:S(2)}, u32[]{:S(2)}) collective-permute-start(bf16[8,72,128]{2,1,0:T(8,128)(2,1)S(1)} %pad_maximum_fusion.refs_0_), channel_id=1, source_target_pairs={{0,1},{1,0},{2,3},{3,2},{4,5},{5,4},{6,7},{7,6},{8,9},{9,8},{10,11... | collective-permute-start | bytes 442376 | tf_op jit(solution)/shard_map/ppermute | solution.py:372
  51.5 1.0 copy-start.1
  117.6 21.3 %all-to-all-start.4 = ((bf16[32,72,128]{2,1,0:T(8,128)(2,1)}), bf16[32,72,128]{2,1,0:T(8,128)(2,1)S(1)}, u32[]{:S(2)}, u32[]{:S(2)}) async-start(bf16[32,72,128]{2,1,0:T(8,128)(2,1)} %get-tuple-element.19), calls=%async_computation.4 | async-start | bytes 1179648 | tf_op jit(solution)/shard_map/all_to_all | solution.py:26
  122.5 1.2 copy-start.2

commit v13 on v12

--- a/solution.py
+++ b/solution.py
@@ -18,6 +18,7 @@
 LANES = 128
 KERN_VMEM = 48
 PICK_VMEM = 60
+JOIN_COST = 4_000_000_000
 CENTRE = ("y", "core")
 SAMPLE = ("z", "x")
 
@@ -253,6 +254,18 @@
     return jnp.concatenate([held, lax.ppermute(held, axis, pairs)])
 
 
+def joined_body(held_ref, moved_ref, out_ref):
+    near = held_ref.shape[0]
+    out_ref[:near] = held_ref[...]
+    out_ref[near:] = moved_ref[...]
+
+
+def last_doubled(held, axis, hop):
+    moved = lax.ppermute(held, axis, [(i, i ^ hop) for i in range(lax.axis_size(axis))])
+    out = jax.ShapeDtypeStruct((2 * held.shape[0], *held.shape[1:]), held.dtype)
+    return call(joined_body, out, JOIN_COST, held, moved)
+
+
 def swapped_cores(array):
     return lax.ppermute(array, "core", [(0, 1), (1, 0)])
 
@@ -366,15 +379,16 @@
 
     z_hops = [1 << i for i in reversed(range(over_z.bit_length() - 1))]
     held = packed.astype(jnp.bfloat16)[None]
-    for hop in z_hops:
+    for hop in z_hops[:-1]:
         held = doubled(held, "z", hop)
+    held = last_doubled(held, "z", z_hops[-1])
     coef_parts = [held] + [
         lax.ppermute(held, "x", [(i, i ^ k) for i in range(over_x)]) for k in range(1, over_x)
     ]
     mine = exchange(picked(pool, picks, lax.axis_size("y")), "y")
     labs = [own_labels(step) for step in range(STEPS)]
-    mine, held, centre_sq, packed, labs = lax.optimization_barrier(
-        (mine, held, centre_sq, packed, labs)
+    mine, coef_parts, centre_sq, packed, labs = lax.optimization_barrier(
+        (mine, coef_parts, centre_sq, packed, labs)
     )
     first, later = assembled(mine, swapped_cores(mine))
     kern = kernel_matrix(first, centres, centre_sq)

time: 193 us -> 199 us (1.031)
  waiting for transfers between devices: 12 us -> 19.2 us
  blocking collectives: 107 us -> 105 us
    ppermute x3, waiting for transfers between devices: 0.01 us -> 3.41 us  [on_device(): lax.ppermute(held, 'x', [(i, i ^ k) for i in range(over_x)])]
    ppermute x0 -> x1, starting transfers between devices: none -> 3.09 us  [last_doubled(): lax.ppermute(held, axis, [(i, i ^ hop) for i in range(lax.axis_size(axis))])]
    ppermute x0 -> x1, waiting for transfers between devices: none -> 2.27 us  [last_doubled(): lax.ppermute(held, axis, [(i, i ^ hop) for i in range(lax.axis_size(axis))])]
    ppermute x1, waiting for transfers between devices: 0.01 us -> 2.26 us  [swapped_cores(): return lax.ppermute(array, 'core', [(0, 1), (1, 0)])]
    ppermute x3 -> x2, starting transfers between devices: 17.7 us -> 15.5 us  [doubled(): return jnp.concatenate([held, lax.ppermute(held, axis, pairs)])]
    pallas_call x9 -> x10, Pallas kernels: 6.32 us -> 6.37 us  [call(): pl.pallas_call(body, out_shape=out, in_specs=[vmem] * len(operands), out_...]
  transfers between devices with their start and end apart: 9 -> 9, of which waited for: 3 -> 6; matrix products, arithmetic and copies ran while one was open for 4% -> 3% of each run, Pallas kernels for 6% -> 4%
where the time goes in v13:
time: 199 us
  blocking collectives  105 us (53%)
  starting transfers between devices  44.5 us (22%)
  Pallas kernels  20.2 us (10%)
  waiting for transfers between devices  19.2 us (10%)
  local copies, waits for them, and re-layouts  4.96 us (2%)
  other arithmetic  4.11 us (2%)
    all_to_all x6, blocking collectives, exchange(): return lax.all_to_all(parts, axes, 0, 0, tiled=True)  105 us
    ppermute x2, starting transfers between devices, doubled(): return jnp.concatenate([held, lax.ppermute(held, axis, pairs)])  15.5 us
    all_to_all x2, starting transfers between devices, exchange(): return lax.all_to_all(parts, axes, 0, 0, tiled=True)  11.7 us
    pallas_call x2, Pallas kernels, kernel_matrix(): pl.pallas_call(laplace_body, out_shape=jax.ShapeDtypeStruct((batch, colum...  11.3 us
    all_to_all x2, waiting for transfers between devices, exchange(): return lax.all_to_all(parts, axes, 0, 0, tiled=True)  9.46 us
    ppermute x3, starting transfers between devices, on_device(): lax.ppermute(held, 'x', [(i, i ^ k) for i in range(over_x)])  8.98 us
    pallas_call x10, Pallas kernels, call(): pl.pallas_call(body, out_shape=out, in_specs=[vmem] * len(operands), out_...  6.37 us
    ppermute x1, starting transfers between devices, swapped_cores(): return lax.ppermute(array, 'core', [(0, 1), (1, 0)])  5.21 us
  transfers between devices with their start and end apart: 9, of which 6 were waited for; matrix products, arithmetic and copies ran while one was open for 3% of the time, Pallas kernels for 4%

profile of v13, /device:TPU:1, one launch (start us, length us, event | category | flops | bytes accessed | tf_op | source)
XLA Modules:
  0.0 198.6 jit_solution(15213898117174658570)
XLA Ops:
  1.3 11.5 %collective-permute-start = (bf16[1,72,128]{2,1,0:T(8,128)(2,1)S(1)}, bf16[1,72,128]{2,1,0:T(8,128)(2,1)S(1)}, u32[]{:S(2)}, u32[]{:S(2)}) collective-permute-start(bf16[1,72,128]{2,1,0:T(8,128)(2,1)S(1)} %pad_maximum_fusion.3), channel_id=1, source_target_pairs={{0,16},{4,20},{8,24},{12,28},{16,0},{20,4},{24,8},{28,12},{1,17},{... | collective-permute-start | bytes 55304 | tf_op jit(solution)/shard_map/ppermute | solution.py:254
  12.7 2.5 %shard_map.55 = bf16[8,2,64,512]{3,2,1,0:T(8,128)(2,1)} custom-call(bf16[64,1024]{1,0:T(8,128)(2,1)} %pool_ref.1, s32[2,512]{1,0:T(2,128)} %picks_ref.1), custom_call_target="tpu_custom_call" | custom-call | flops 134217728 | bytes 131072 | tf_op jit(solution)/shard_map/pallas_call | solution.py:296
  15.2 6.8 %all-to-all-start = ((bf16[8,2,64,512]{3,2,1,0:T(8,128)(2,1)}), bf16[8,2,64,512]{3,2,1,0:T(8,128)(2,1)S(1)}, u32[]{:S(2)}, u32[]{:S(2)}) async-start(bf16[8,2,64,512]{3,2,1,0:T(8,128)(2,1)} %shard_map.55), calls=%async_computation | async-start | bytes 2097152 | tf_op jit(solution)/shard_map/all_to_all | solution.py:27
  22.7 3.1 %multiply_reduce_fusion = f32[2048]{0:T(1024)S(1)} fusion(bf16[1024,2048]{1,0:T(8,128)(2,1)} %centres_ref.3), kind=kLoop, calls=%fused_computation.2 | loop fusion | flops 6289408 | bytes 4202496 | tf_op jit(solution)/shard_map/reduce_sum | solution.py:372
  25.9 4.0 %collective-permute-start.1 = (bf16[2,72,128]{2,1,0:T(8,128)(2,1)S(1)}, bf16[2,72,128]{2,1,0:T(8,128)(2,1)S(1)}, u32[]{:S(2)}, u32[]{:S(2)}) collective-permute-start(bf16[2,72,128]{2,1,0:T(8,128)(2,1)S(1)} %pad_maximum_fusion.1), channel_id=1, source_target_pairs={{0,8},{4,12},{8,0},{12,4},{16,24},{20,28},{24,16},{28,20},{1,9},{5... | collective-permute-start | bytes 110600 | tf_op jit(solution)/shard_map/ppermute | solution.py:254
  30.0 1.8 collective-permute-done.1
  31.9 3.1 %collective-permute-start.2 = (bf16[4,72,128]{2,1,0:T(8,128)(2,1)S(1)}, bf16[4,72,128]{2,1,0:T(8,128)(2,1)S(1)}, u32[]{:S(2)}, u32[]{:S(2)}) collective-permute-start(bf16[4,72,128]{2,1,0:T(8,128)(2,1)S(1)} %pad_maximum_fusion.held_ref), channel_id=1, source_target_pairs={{0,4},{4,0},{8,12},{12,8},{16,20},{20,16},{24,28},{28,24},{1,5},{5... | collective-permute-start | bytes 221192 | tf_op jit(solution)/shard_map/ppermute | solution.py:264
  35.0 2.3 %collective-permute-done.2.moved_ref = bf16[4,72,128]{2,1,0:T(8,128)(2,1)S(1)} collective-permute-done((bf16[4,72,128]{2,1,0:T(8,128)(2,1)S(1)}, bf16[4,72,128]{2,1,0:T(8,128)(2,1)S(1)}, u32[]{:S(2)}, u32[]{:S(2)}) %collective-permute-start.2) | collective-permute-done | bytes 73760 | tf_op jit(solution)/shard_map/ppermute | solution.py:264
  37.3 4.4 %collective-permute-start.5 = (bf16[8,72,128]{2,1,0:T(8,128)(2,1)S(1)}, bf16[8,72,128]{2,1,0:T(8,128)(2,1)S(1)}, u32[]{:S(2)}, u32[]{:S(2)}) collective-permute-start(bf16[8,72,128]{2,1,0:T(8,128)(2,1)S(1)} %shard_map.56.refs_0_), channel_id=1, source_target_pairs={{0,3},{1,2},{2,1},{3,0},{4,7},{5,6},{6,5},{7,4},{8,11},{9,10},{10,... | collective-permute-start | bytes 442376 | tf_op jit(solution)/shard_map/ppermute | solution.py:386
  41.7 2.4 %collective-permute-start.4 = (bf16[8,72,128]{2,1,0:T(8,128)(2,1)S(1)}, bf16[8,72,128]{2,1,0:T(8,128)(2,1)S(1)}, u32[]{:S(2)}, u32[]{:S(2)}) collective-permute-start(bf16[8,72,128]{2,1,0:T(8,128)(2,1)S(1)} %shard_map.56.refs_0_), channel_id=1, source_target_pairs={{0,2},{1,3},{2,0},{3,1},{4,6},{5,7},{6,4},{7,5},{8,10},{9,11},{10,... | collective-permute-start | bytes 442376 | tf_op jit(solution)/shard_map/ppermute | solution.py:386
  44.1 2.2 %collective-permute-start.3 = (bf16[8,72,128]{2,1,0:T(8,128)(2,1)S(1)}, bf16[8,72,128]{2,1,0:T(8,128)(2,1)S(1)}, u32[]{:S(2)}, u32[]{:S(2)}) collective-permute-start(bf16[8,72,128]{2,1,0:T(8,128)(2,1)S(1)} %shard_map.56.refs_0_), channel_id=1, source_target_pairs={{0,1},{1,0},{2,3},{3,2},{4,5},{5,4},{6,7},{7,6},{8,9},{9,8},{10,11... | collective-permute-start | bytes 442376 | tf_op jit(solution)/shard_map/ppermute | solution.py:386
  49.4 1.9 collective-permute-done.3.refs_1_
  51.3 5.2 %collective-permute-start.6 = (bf16[8,2,64,512]{3,2,1,0:T(8,128)(2,1)S(1)}, bf16[8,2,64,512]{3,2,1,0:T(8,128)(2,1)S(1)}, u32[]{:S(2)}, u32[]{:S(2)}) collective-permute-start(bf16[8,2,64,512]{3,2,1,0:T(8,128)(2,1)S(1)} %all-to-all-done.mine_ref), channel_id=1, source_target_pairs={{0,32},{32,0},{1,33},{33,1},{2,34},{34,2},{3,35},{35,3},{4,36},{36... | collective-permute-start | bytes 3145736 | tf_op jit(solution)/shard_map/ppermute | solution.py:270
  56.6 2.3 %collective-permute-done.6.other_ref = bf16[8,2,64,512]{3,2,1,0:T(8,128)(2,1)S(1)} collective-permute-done((bf16[8,2,64,512]{3,2,1,0:T(8,128)(2,1)S(1)}, bf16[8,2,64,512]{3,2,1,0:T(8,128)(2,1)S(1)}, u32[]{:S(2)}, u32[]{:S(2)}) %collective-permute-start.6) | collective-permute-done | bytes 1048608 | tf_op jit(solution)/shard_map/ppermute | solution.py:270
  60.0 5.7 %shard_map.58.refs_4_.kern_ref = bf16[512,2048]{1,0:T(8,128)(2,1)S(1)} custom-call(bf16[8,2,64,512]{3,2,1,0:T(8,128)(2,1)S(1)} %get-tuple-element.23.feats_ref, bf16[1024,2048]{1,0:T(8,128)(2,1)} %centres_ref.3, f32[1,2048]{1,0:T(1,128)S(1)} %bitcast.10), custom_call_target="tpu_custom_call" | custom-call | flops 2147483648 | bytes 4194304 | tf_op jit(solution)/shard_map/pallas_call | solution.py:232
  66.9 17.0 %all_to_all.40.arrived_ref = bf16[16,36,128]{2,1,0:T(8,128)(2,1)S(1)} all-to-all(bf16[16,36,128]{2,1,0:T(8,128)(2,1)S(1)} %shard_map.59), channel_id=1, replica_groups=mesh['y'=8,'core'=2,'z'=8,'x'=4] {'y','core'}, dimensions={0} | all-to-all | bytes 294912 | tf_op jit(solution)/shard_map/all_to_all | solution.py:27
  84.3 12.3 %all_to_all.41.resid_ref = bf16[16,36,128]{2,1,0:T(8,128)(2,1)S(1)} all-to-all(bf16[16,36,128]{2,1,0:T(8,128)(2,1)S(1)} %shard_map.60), channel_id=1, replica_groups=mesh['y'=8,'core'=2,'z'=8,'x'=4] {'y','core'}, dimensions={0} | all-to-all | bytes 294912 | tf_op jit(solution)/shard_map/all_to_all | solution.py:27
  97.3 25.5 %all_to_all.42.arrived_ref = bf16[32,72,128]{2,1,0:T(8,128)(2,1)S(1)} all-to-all(bf16[32,72,128]{2,1,0:T(8,128)(2,1)S(1)} %shard_map.61), channel_id=1, replica_groups=mesh['y'=8,'core'=2,'z'=8,'x'=4] {'z','x'}, dimensions={0} | all-to-all | bytes 1179648 | tf_op jit(solution)/shard_map/all_to_all | solution.py:27
  123.8 4.9 %all-to-all-start.4 = ((bf16[32,72,128]{2,1,0:T(8,128)(2,1)}), bf16[32,72,128]{2,1,0:T(8,128)(2,1)S(1)}, u32[]{:S(2)}, u32[]{:S(2)}) async-start(bf16[32,72,128]{2,1,0:T(8,128)(2,1)} %get-tuple-element.27), calls=%async_computation.4 | async-start | bytes 1179648 | tf_op jit(solution)/shard_map/all_to_all | solution.py:27
  129.9 5.7 %shard_map.63.refs_1_.kern_ref = bf16[512,2048]{1,0:T(8,128)(2,1)S(1)} custom-call(bf16[8,2,64,512]{3,2,1,0:T(8,128)(2,1)S(1)} %copy-done.2, bf16[1024,2048]{1,0:T(8,128)(2,1)} %centres_ref.3, f32[1,2048]{1,0:T(1,128)S(1)} %bitcast.11), custom_call_target="tpu_custom_call" | custom-call | flops 2147483648 | bytes 4194304 | tf_op jit(solution)/shard_map/pallas_call | solution.py:232
  135.6 9.5 %all-to-all-done.4.refs_0_ = bf16[32,72,128]{2,1,0:T(8,128)(2,1)S(1)} async-done(((bf16[32,72,128]{2,1,0:T(8,128)(2,1)}), bf16[32,72,128]{2,1,0:T(8,128)(2,1)S(1)}, u32[]{:S(2)}, u32[]{:S(2)}) %all-to-all-start.4) | async-done | bytes 589856 | tf_op jit(solution)/shard_map/all_to_all | solution.py:27
  146.0 15.7 %all_to_all.43.arrived_ref = bf16[16,36,128]{2,1,0:T(8,128)(2,1)S(1)} all-to-all(bf16[16,36,128]{2,1,0:T(8,128)(2,1)S(1)} %shard_map.64), channel_id=1, replica_groups=mesh['y'=8,'core'=2,'z'=8,'x'=4] {'y','core'}, dimensions={0} | all-to-all | bytes 294912 | tf_op jit(solution)/shard_map/all_to_all | solution.py:27
  162.1 12.1 %all_to_all.44.resid_ref = bf16[16,36,128]{2,1,0:T(8,128)(2,1)S(1)} all-to-all(bf16[16,36,128]{2,1,0:T(8,128)(2,1)S(1)} %shard_map.65), channel_id=1, replica_groups=mesh['y'=8,'core'=2,'z'=8,'x'=4] {'y','core'}, dimensions={0} | all-to-all | bytes 294912 | tf_op jit(solution)/shard_map/all_to_all | solution.py:27
  175.0 22.8 %all_to_all.45.arrived_ref = bf16[32,72,128]{2,1,0:T(8,128)(2,1)S(1)} all-to-all(bf16[32,72,128]{2,1,0:T(8,128)(2,1)S(1)} %shard_map.66), channel_id=1, replica_groups=mesh['y'=8,'core'=2,'z'=8,'x'=4] {'z','x'}, dimensions={0} | all-to-all | bytes 1179648 | tf_op jit(solution)/shard_map/all_to_all | solution.py:27
  (39 shorter events, 13.9 us)
Async XLA Ops:
  0.0 46.3 %copy-start = (s32[1024]{0:T(1024)S(1)}, s32[1024]{0:T(1024)}, u32[]{:S(2)}) copy-start(s32[1024]{0:T(1024)} %param.7) | copy-start | bytes 12292
  1.3 24.6 %collective-permute-start = (bf16[1,72,128]{2,1,0:T(8,128)(2,1)S(1)}, bf16[1,72,128]{2,1,0:T(8,128)(2,1)S(1)}, u32[]{:S(2)}, u32[]{:S(2)}) collective-permute-start(bf16[1,72,128]{2,1,0:T(8,128)(2,1)S(1)} %pad_maximum_fusion.3), channel_id=1, source_target_pairs={{0,16},{4,20},{8,24},{12,28},{16,0},{20,4},{24,8},{28,12},{1,17},{... | collective-permute-start | bytes 55304 | tf_op jit(solution)/shard_map/ppermute | solution.py:254
  15.2 36.1 %all-to-all-start = ((bf16[8,2,64,512]{3,2,1,0:T(8,128)(2,1)}), bf16[8,2,64,512]{3,2,1,0:T(8,128)(2,1)S(1)}, u32[]{:S(2)}, u32[]{:S(2)}) async-start(bf16[8,2,64,512]{3,2,1,0:T(8,128)(2,1)} %shard_map.55), calls=%async_computation | async-start | bytes 2097152 | tf_op jit(solution)/shard_map/all_to_all | solution.py:27
  25.9 5.9 %collective-permute-start.1 = (bf16[2,72,128]{2,1,0:T(8,128)(2,1)S(1)}, bf16[2,72,128]{2,1,0:T(8,128)(2,1)S(1)}, u32[]{:S(2)}, u32[]{:S(2)}) collective-permute-start(bf16[2,72,128]{2,1,0:T(8,128)(2,1)S(1)} %pad_maximum_fusion.1), channel_id=1, source_target_pairs={{0,8},{4,12},{8,0},{12,4},{16,24},{20,28},{24,16},{28,20},{1,9},{5... | collective-permute-start | bytes 110600 | tf_op jit(solution)/shard_map/ppermute | solution.py:254
  31.9 5.4 %collective-permute-start.2 = (bf16[4,72,128]{2,1,0:T(8,128)(2,1)S(1)}, bf16[4,72,128]{2,1,0:T(8,128)(2,1)S(1)}, u32[]{:S(2)}, u32[]{:S(2)}) collective-permute-start(bf16[4,72,128]{2,1,0:T(8,128)(2,1)S(1)} %pad_maximum_fusion.held_ref), channel_id=1, source_target_pairs={{0,4},{4,0},{8,12},{12,8},{16,20},{20,16},{24,28},{28,24},{1,5},{5... | collective-permute-start | bytes 221192 | tf_op jit(solution)/shard_map/ppermute | solution.py:264
  37.3 10.7 %collective-permute-start.5 = (bf16[8,72,128]{2,1,0:T(8,128)(2,1)S(1)}, bf16[8,72,128]{2,1,0:T(8,128)(2,1)S(1)}, u32[]{:S(2)}, u32[]{:S(2)}) collective-permute-start(bf16[8,72,128]{2,1,0:T(8,128)(2,1)S(1)} %shard_map.56.refs_0_), channel_id=1, source_target_pairs={{0,3},{1,2},{2,1},{3,0},{4,7},{5,6},{6,5},{7,4},{8,11},{9,10},{10,... | collective-permute-start | bytes 442376 | tf_op jit(solution)/shard_map/ppermute | solution.py:386
  41.7 7.7 %collective-permute-start.4 = (bf16[8,72,128]{2,1,0:T(8,128)(2,1)S(1)}, bf16[8,72,128]{2,1,0:T(8,128)(2,1)S(1)}, u32[]{:S(2)}, u32[]{:S(2)}) collective-permute-start(bf16[8,72,128]{2,1,0:T(8,128)(2,1)S(1)} %shard_map.56.refs_0_), channel_id=1, source_target_pairs={{0,2},{1,3},{2,0},{3,1},{4,6},{5,7},{6,4},{7,5},{8,10},{9,11},{10,... | collective-permute-start | bytes 442376 | tf_op jit(solution)/shard_map/ppermute | solution.py:386
  44.1 7.2 %collective-permute-start.3 = (bf16[8,72,128]{2,1,0:T(8,128)(2,1)S(1)}, bf16[8,72,128]{2,1,0:T(8,128)(2,1)S(1)}, u32[]{:S(2)}, u32[]{:S(2)}) collective-permute-start(bf16[8,72,128]{2,1,0:T(8,128)(2,1)S(1)} %shard_map.56.refs_0_), channel_id=1, source_target_pairs={{0,1},{1,0},{2,3},{3,2},{4,5},{5,4},{6,7},{7,6},{8,9},{9,8},{10,11... | collective-permute-start | bytes 442376 | tf_op jit(solution)/shard_map/ppermute | solution.py:386
  51.3 7.5 %collective-permute-start.6 = (bf16[8,2,64,512]{3,2,1,0:T(8,128)(2,1)S(1)}, bf16[8,2,64,512]{3,2,1,0:T(8,128)(2,1)S(1)}, u32[]{:S(2)}, u32[]{:S(2)}) collective-permute-start(bf16[8,2,64,512]{3,2,1,0:T(8,128)(2,1)S(1)} %all-to-all-done.mine_ref), channel_id=1, source_target_pairs={{0,32},{32,0},{1,33},{33,1},{2,34},{34,2},{3,35},{35,3},{4,36},{36... | collective-permute-start | bytes 3145736 | tf_op jit(solution)/shard_map/ppermute | solution.py:270
  59.0 1.0 copy-start.1
  123.8 21.3 %all-to-all-start.4 = ((bf16[32,72,128]{2,1,0:T(8,128)(2,1)}), bf16[32,72,128]{2,1,0:T(8,128)(2,1)S(1)}, u32[]{:S(2)}, u32[]{:S(2)}) async-start(bf16[32,72,128]{2,1,0:T(8,128)(2,1)} %get-tuple-element.27), calls=%async_computation.4 | async-start | bytes 1179648 | tf_op jit(solution)/shard_map/all_to_all | solution.py:27
  128.7 1.2 copy-start.2

commit v14 on v11

--- a/solution.py
+++ b/solution.py
@@ -264,14 +264,21 @@
     return lax.ppermute(array, "core", [(0, 1), (1, 0)])
 
 
-def pick_body(pool_ref, picks_ref, out_ref, pool, picks, sems):
+def pick_body(pool_ref, picks_ref, coefs_ref, out_ref, packed_ref, half_ref, pool, picks, coefs, sems):
     fetches = [
         pltpu.make_async_copy(ref, into, sems.at[i])
-        for i, (ref, into) in enumerate(((picks_ref, picks), (pool_ref, pool)))
+        for i, (ref, into) in enumerate(((coefs_ref, coefs), (picks_ref, picks), (pool_ref, pool)))
     ]
     for copy in fetches:
         copy.start()
-    for copy in fetches:
+    fetches[0].wait()
+    height = packed_ref.shape[0]
+    columns = coefs.shape[1]
+    sides = [coefs[:, at : at + height] for at in range(0, columns, height)]
+    packed = jnp.transpose(jnp.concatenate(sides, axis=0))
+    packed_ref[...] = packed
+    half_ref[0] = packed.astype(half_ref.dtype)
+    for copy in fetches[1:]:
         copy.wait()
     pool_dev = pool.shape[1]
     copies, steps, _, batch = out_ref.shape
@@ -285,23 +292,29 @@
             out_ref[peer, step] = feats
 
 
-def picked(pool, picks, copies):
+def picked(pool, picks, coefs, copies):
     steps, batch = picks.shape
+    height = coefs.size // LANES
     return pl.pallas_call(
         pick_body,
-        out_shape=jax.ShapeDtypeStruct((copies, steps, pool.shape[0], batch), pool.dtype),
-        in_specs=[pl.BlockSpec(memory_space=pl.ANY)] * 2,
-        out_specs=pl.BlockSpec(memory_space=pltpu.VMEM),
+        out_shape=[
+            jax.ShapeDtypeStruct((copies, steps, pool.shape[0], batch), pool.dtype),
+            jax.ShapeDtypeStruct((height, LANES), coefs.dtype),
+            jax.ShapeDtypeStruct((1, height, LANES), jnp.bfloat16),
+        ],
+        in_specs=[pl.BlockSpec(memory_space=pl.ANY)] * 3,
+        out_specs=[pl.BlockSpec(memory_space=pltpu.VMEM)] * 3,
         scratch_shapes=[
             pltpu.VMEM(pool.shape, pool.dtype),
             pltpu.VMEM(picks.shape, picks.dtype),
-            pltpu.SemaphoreType.DMA((2,)),
+            pltpu.VMEM(coefs.shape, coefs.dtype),
+            pltpu.SemaphoreType.DMA((3,)),
         ],
         cost_estimate=pl.CostEstimate(
             flops=2 * pool.size * batch * steps, bytes_accessed=2 * pool.size, transcendentals=0
         ),
         compiler_params=pltpu.CompilerParams(vmem_limit_bytes=PICK_VMEM << 20),
-    )(pool, picks)
+    )(pool, picks, coefs)
 
 
 def update_body(rate, arrived_ref, current_ref, new_ref, half_ref):
@@ -369,13 +382,11 @@
         chosen = lax.dynamic_slice(local_picks[step], (me * own,), (own,))
         return jnp.tile(jnp.take(labels, chosen, mode="clip"), fold)[None]
 
-    packed = jnp.concatenate([coefs[: classes // 2], coefs[classes // 2 :]], axis=1)
-
     z_hops = [1 << i for i in reversed(range(over_z.bit_length() - 1))]
-    held = packed.astype(jnp.bfloat16)[None]
+    feats, packed, held = picked(pool, picks, coefs.T, lax.axis_size("y"))
     for hop in z_hops[:-1]:
         held = doubled(held, "z", hop)
-    mine = exchange(picked(pool, picks, lax.axis_size("y")), "y")
+    mine = exchange(feats, "y")
     labs = [own_labels(step) for step in range(STEPS)]
     spread_out = last_doubled(held, "z", z_hops[-1], over_x)
     mine, spread_out, centre_sq, packed, labs = lax.optimization_barrier(

time: 191 us -> 190 us (level)
  transfers between devices with their start and end apart: 7 -> 7, of which waited for: 4 -> 4; matrix products, arithmetic and copies ran while one was open for 4% -> 3% of each run, Pallas kernels for 7% -> 7%
where the time goes in v14:
time: 190 us; the launch traced here: 189 us
  blocking collectives  105 us (55%)
  starting transfers between devices  39.1 us (21%)
  Pallas kernels  21.1 us (11%)
  waiting for transfers between devices  16 us (8%)
  local copies, waits for them, and re-layouts  4.56 us (2%)
  other arithmetic  3.78 us (2%)
    all_to_all x6, blocking collectives, exchange(): return lax.all_to_all(parts, axes, 0, 0, tiled=True)  105 us
    all_to_all x3, starting transfers between devices, exchange(): return lax.all_to_all(parts, axes, 0, 0, tiled=True)  16.6 us
    ppermute x2, starting transfers between devices, doubled(): return jnp.concatenate([held, lax.ppermute(held, axis, pairs)])  14.6 us
    all_to_all x3, waiting for transfers between devices, exchange(): return lax.all_to_all(parts, axes, 0, 0, tiled=True)  12.7 us
    pallas_call x2, Pallas kernels, kernel_matrix(): pl.pallas_call(laplace_body, out_shape=jax.ShapeDtypeStruct((batch, colum...  11.3 us
    pallas_call x10, Pallas kernels, call(): pl.pallas_call(body, out_shape=out, in_specs=[vmem] * len(operands), out_...  7.22 us
    ppermute x1, starting transfers between devices, swapped_cores(): return lax.ppermute(array, 'core', [(0, 1), (1, 0)])  4.84 us
  transfers between devices with their start and end apart: 7, of which 4 were waited for; matrix products, arithmetic and copies ran while one was open for 3% of the time, Pallas kernels for 7%

profile of v14, /device:TPU:1, one launch (start us, length us, event | category | flops | bytes accessed | tf_op | source)
XLA Modules:
  0.0 189.5 jit_solution(9182899480637349022)
XLA Ops:
  0.0 2.6 %shard_map.55 = (bf16[8,2,64,512]{3,2,1,0:T(8,128)(2,1)}, f32[72,128]{1,0:T(8,128)}, bf16[1,72,128]{2,1,0:T(8,128)(2,1)}) custom-call(bf16[64,1024]{1,0:T(8,128)(2,1)} %pool_ref.1, s32[2,512]{1,0:T(2,128)} %picks_ref.1, f32[64,144]{1,0:T(8,128)} %bitcast.11), custom_call_target="tpu_custom_call" | custom-call | flops 134217728 | bytes 131072 | tf_op jit(solution)/shard_map/pallas_call | solution.py:298
  2.6 7.7 %all-to-all-start = ((bf16[8,2,64,512]{3,2,1,0:T(8,128)(2,1)}), bf16[8,2,64,512]{3,2,1,0:T(8,128)(2,1)S(1)}, u32[]{:S(2)}, u32[]{:S(2)}) async-start(bf16[8,2,64,512]{3,2,1,0:T(8,128)(2,1)} %get-tuple-element.18), calls=%async_computation | async-start | bytes 2097152 | tf_op jit(solution)/shard_map/all_to_all | solution.py:27
  10.2 10.6 %collective-permute-start = (bf16[1,72,128]{2,1,0:T(8,128)(2,1)}, bf16[1,72,128]{2,1,0:T(8,128)(2,1)S(1)}, u32[]{:S(2)}, u32[]{:S(2)}) collective-permute-start(bf16[1,72,128]{2,1,0:T(8,128)(2,1)} %get-tuple-element.19), channel_id=1, source_target_pairs={{0,16},{4,20},{8,24},{12,28},{16,0},{20,4},{24,8},{28,12},{1,17},{... | collective-permute-start | bytes 55304 | tf_op jit(solution)/shard_map/ppermute | solution.py:246
  22.4 3.1 %multiply_reduce_fusion = f32[2048]{0:T(1024)S(1)} fusion(bf16[1024,2048]{1,0:T(8,128)(2,1)} %centres_ref.3), kind=kLoop, calls=%fused_computation.2 | loop fusion | flops 6289408 | bytes 4202496 | tf_op jit(solution)/shard_map/reduce_sum | solution.py:379
  26.3 4.0 %collective-permute-start.1 = (bf16[2,72,128]{2,1,0:T(8,128)(2,1)S(1)}, bf16[2,72,128]{2,1,0:T(8,128)(2,1)S(1)}, u32[]{:S(2)}, u32[]{:S(2)}) collective-permute-start(bf16[2,72,128]{2,1,0:T(8,128)(2,1)S(1)} %pad_maximum_fusion), channel_id=1, source_target_pairs={{0,8},{4,12},{8,0},{12,4},{16,24},{20,28},{24,16},{28,20},{1,9},{5... | collective-permute-start | bytes 110600 | tf_op jit(solution)/shard_map/ppermute | solution.py:246
  30.3 1.9 collective-permute-done.1
  32.2 3.1 %collective-permute-start.2 = (bf16[4,72,128]{2,1,0:T(8,128)(2,1)S(1)}, bf16[4,72,128]{2,1,0:T(8,128)(2,1)S(1)}, u32[]{:S(2)}, u32[]{:S(2)}) collective-permute-start(bf16[4,72,128]{2,1,0:T(8,128)(2,1)S(1)} %constant_dynamic-update-slice_fusion.held_ref), channel_id=1, source_target_pairs={{0,4},{4,0},{8,12},{12,8},{16,20},{20,16},{24,28},{28,24},{1,5},{5... | collective-permute-start | bytes 221192 | tf_op jit(solution)/shard_map/ppermute | solution.py:258
  36.0 1.5 collective-permute-done.2.moved_ref
  38.5 4.8 %collective-permute-start.3 = (bf16[8,2,64,512]{3,2,1,0:T(8,128)(2,1)S(1)}, bf16[8,2,64,512]{3,2,1,0:T(8,128)(2,1)S(1)}, u32[]{:S(2)}, u32[]{:S(2)}) collective-permute-start(bf16[8,2,64,512]{3,2,1,0:T(8,128)(2,1)S(1)} %all-to-all-done.mine_ref), channel_id=1, source_target_pairs={{0,32},{32,0},{1,33},{33,1},{2,34},{34,2},{3,35},{35,3},{4,36},{36... | collective-permute-start | bytes 3145736 | tf_op jit(solution)/shard_map/ppermute | solution.py:264
  43.3 4.0 %all-to-all-start.1 = ((bf16[4,8,72,128]{3,2,1,0:T(8,128)(2,1)}), bf16[4,8,72,128]{3,2,1,0:T(8,128)(2,1)S(1)}, u32[]{:S(2)}, u32[]{:S(2)}) async-start(bf16[4,8,72,128]{3,2,1,0:T(8,128)(2,1)} %shard_map.56), calls=%async_computation.1 | async-start | bytes 1179648 | tf_op jit(solution)/shard_map/all_to_all | solution.py:27
  48.5 5.7 %shard_map.58.kern_ref = bf16[512,2048]{1,0:T(8,128)(2,1)S(1)} custom-call(bf16[8,2,64,512]{3,2,1,0:T(8,128)(2,1)S(1)} %get-tuple-element.23.feats_ref, bf16[1024,2048]{1,0:T(8,128)(2,1)} %centres_ref.3, f32[1,2048]{1,0:T(1,128)S(1)} %bitcast.9), custom_call_target="tpu_custom_call" | custom-call | flops 2147483648 | bytes 4194304 | tf_op jit(solution)/shard_map/pallas_call | solution.py:224
  54.2 3.2 %all-to-all-done.1.coef_ref = bf16[4,8,72,128]{3,2,1,0:T(8,128)(2,1)S(1)} async-done(((bf16[4,8,72,128]{3,2,1,0:T(8,128)(2,1)}), bf16[4,8,72,128]{3,2,1,0:T(8,128)(2,1)S(1)}, u32[]{:S(2)}, u32[]{:S(2)}) %all-to-all-start.1) | async-done | bytes 589856 | tf_op jit(solution)/shard_map/all_to_all | solution.py:27
  57.4 1.2 shard_map.59
  58.6 17.8 %all_to_all.45.arrived_ref = bf16[16,36,128]{2,1,0:T(8,128)(2,1)S(1)} all-to-all(bf16[16,36,128]{2,1,0:T(8,128)(2,1)S(1)} %shard_map.59), channel_id=1, replica_groups=mesh['y'=8,'core'=2,'z'=8,'x'=4] {'y','core'}, dimensions={0} | all-to-all | bytes 294912 | tf_op jit(solution)/shard_map/all_to_all | solution.py:27
  76.7 12.3 %all_to_all.46.resid_ref = bf16[16,36,128]{2,1,0:T(8,128)(2,1)S(1)} all-to-all(bf16[16,36,128]{2,1,0:T(8,128)(2,1)S(1)} %shard_map.60), channel_id=1, replica_groups=mesh['y'=8,'core'=2,'z'=8,'x'=4] {'y','core'}, dimensions={0} | all-to-all | bytes 294912 | tf_op jit(solution)/shard_map/all_to_all | solution.py:27
  89.7 24.0 %all_to_all.47.arrived_ref = bf16[32,72,128]{2,1,0:T(8,128)(2,1)S(1)} all-to-all(bf16[32,72,128]{2,1,0:T(8,128)(2,1)S(1)} %shard_map.61), channel_id=1, replica_groups=mesh['y'=8,'core'=2,'z'=8,'x'=4] {'z','x'}, dimensions={0} | all-to-all | bytes 1179648 | tf_op jit(solution)/shard_map/all_to_all | solution.py:27
  114.6 4.9 %all-to-all-start.5 = ((bf16[32,72,128]{2,1,0:T(8,128)(2,1)}), bf16[32,72,128]{2,1,0:T(8,128)(2,1)S(1)}, u32[]{:S(2)}, u32[]{:S(2)}) async-start(bf16[32,72,128]{2,1,0:T(8,128)(2,1)} %get-tuple-element.27), calls=%async_computation.5 | async-start | bytes 1179648 | tf_op jit(solution)/shard_map/all_to_all | solution.py:27
  119.5 1.2 copy-done.3
  120.8 5.7 %shard_map.63.kern_ref = bf16[512,2048]{1,0:T(8,128)(2,1)S(1)} custom-call(bf16[8,2,64,512]{3,2,1,0:T(8,128)(2,1)S(1)} %copy-done.3, bf16[1024,2048]{1,0:T(8,128)(2,1)} %centres_ref.3, f32[1,2048]{1,0:T(1,128)S(1)} %bitcast.10), custom_call_target="tpu_custom_call" | custom-call | flops 2147483648 | bytes 4194304 | tf_op jit(solution)/shard_map/pallas_call | solution.py:224
  126.4 9.5 %all-to-all-done.5 = bf16[32,72,128]{2,1,0:T(8,128)(2,1)S(1)} async-done(((bf16[32,72,128]{2,1,0:T(8,128)(2,1)}), bf16[32,72,128]{2,1,0:T(8,128)(2,1)S(1)}, u32[]{:S(2)}, u32[]{:S(2)}) %all-to-all-start.5) | async-done | bytes 589856 | tf_op jit(solution)/shard_map/all_to_all | solution.py:27
  135.9 1.0 shard_map.64
  136.9 15.7 %all_to_all.48.arrived_ref = bf16[16,36,128]{2,1,0:T(8,128)(2,1)S(1)} all-to-all(bf16[16,36,128]{2,1,0:T(8,128)(2,1)S(1)} %shard_map.64), channel_id=1, replica_groups=mesh['y'=8,'core'=2,'z'=8,'x'=4] {'y','core'}, dimensions={0} | all-to-all | bytes 294912 | tf_op jit(solution)/shard_map/all_to_all | solution.py:27
  153.0 12.1 %all_to_all.49.resid_ref = bf16[16,36,128]{2,1,0:T(8,128)(2,1)S(1)} all-to-all(bf16[16,36,128]{2,1,0:T(8,128)(2,1)S(1)} %shard_map.65), channel_id=1, replica_groups=mesh['y'=8,'core'=2,'z'=8,'x'=4] {'y','core'}, dimensions={0} | all-to-all | bytes 294912 | tf_op jit(solution)/shard_map/all_to_all | solution.py:27
  165.8 22.8 %all_to_all.50.arrived_ref = bf16[32,72,128]{2,1,0:T(8,128)(2,1)S(1)} all-to-all(bf16[32,72,128]{2,1,0:T(8,128)(2,1)S(1)} %shard_map.66), channel_id=1, replica_groups=mesh['y'=8,'core'=2,'z'=8,'x'=4] {'z','x'}, dimensions={0} | all-to-all | bytes 1179648 | tf_op jit(solution)/shard_map/all_to_all | solution.py:27
  (35 shorter events, 9.1 us)
Async XLA Ops:
  0.0 25.5 %copy-start = (s32[1024]{0:T(1024)S(1)}, s32[1024]{0:T(1024)}, u32[]{:S(2)}) copy-start(s32[1024]{0:T(1024)} %param.7) | copy-start | bytes 12292
  2.6 23.7 %copy-start.4 = (bf16[1,72,128]{2,1,0:T(8,128)(2,1)S(1)}, bf16[1,72,128]{2,1,0:T(8,128)(2,1)}, u32[]{:S(2)}) copy-start(bf16[1,72,128]{2,1,0:T(8,128)(2,1)} %get-tuple-element.19) | copy-start | bytes 55300
  2.6 35.9 %all-to-all-start = ((bf16[8,2,64,512]{3,2,1,0:T(8,128)(2,1)}), bf16[8,2,64,512]{3,2,1,0:T(8,128)(2,1)S(1)}, u32[]{:S(2)}, u32[]{:S(2)}) async-start(bf16[8,2,64,512]{3,2,1,0:T(8,128)(2,1)} %get-tuple-element.18), calls=%async_computation | async-start | bytes 2097152 | tf_op jit(solution)/shard_map/all_to_all | solution.py:27
  10.2 16.0 %collective-permute-start = (bf16[1,72,128]{2,1,0:T(8,128)(2,1)}, bf16[1,72,128]{2,1,0:T(8,128)(2,1)S(1)}, u32[]{:S(2)}, u32[]{:S(2)}) collective-permute-start(bf16[1,72,128]{2,1,0:T(8,128)(2,1)} %get-tuple-element.19), channel_id=1, source_target_pairs={{0,16},{4,20},{8,24},{12,28},{16,0},{20,4},{24,8},{28,12},{1,17},{... | collective-permute-start | bytes 55304 | tf_op jit(solution)/shard_map/ppermute | solution.py:246
  26.3 5.9 %collective-permute-start.1 = (bf16[2,72,128]{2,1,0:T(8,128)(2,1)S(1)}, bf16[2,72,128]{2,1,0:T(8,128)(2,1)S(1)}, u32[]{:S(2)}, u32[]{:S(2)}) collective-permute-start(bf16[2,72,128]{2,1,0:T(8,128)(2,1)S(1)} %pad_maximum_fusion), channel_id=1, source_target_pairs={{0,8},{4,12},{8,0},{12,4},{16,24},{20,28},{24,16},{28,20},{1,9},{5... | collective-permute-start | bytes 110600 | tf_op jit(solution)/shard_map/ppermute | solution.py:246
  32.2 5.4 %collective-permute-start.2 = (bf16[4,72,128]{2,1,0:T(8,128)(2,1)S(1)}, bf16[4,72,128]{2,1,0:T(8,128)(2,1)S(1)}, u32[]{:S(2)}, u32[]{:S(2)}) collective-permute-start(bf16[4,72,128]{2,1,0:T(8,128)(2,1)S(1)} %constant_dynamic-update-slice_fusion.held_ref), channel_id=1, source_target_pairs={{0,4},{4,0},{8,12},{12,8},{16,20},{20,16},{24,28},{28,24},{1,5},{5... | collective-permute-start | bytes 221192 | tf_op jit(solution)/shard_map/ppermute | solution.py:258
  38.5 8.9 %collective-permute-start.3 = (bf16[8,2,64,512]{3,2,1,0:T(8,128)(2,1)S(1)}, bf16[8,2,64,512]{3,2,1,0:T(8,128)(2,1)S(1)}, u32[]{:S(2)}, u32[]{:S(2)}) collective-permute-start(bf16[8,2,64,512]{3,2,1,0:T(8,128)(2,1)S(1)} %all-to-all-done.mine_ref), channel_id=1, source_target_pairs={{0,32},{32,0},{1,33},{33,1},{2,34},{34,2},{3,35},{35,3},{4,36},{36... | collective-permute-start | bytes 3145736 | tf_op jit(solution)/shard_map/ppermute | solution.py:264
  43.3 14.0 %all-to-all-start.1 = ((bf16[4,8,72,128]{3,2,1,0:T(8,128)(2,1)}), bf16[4,8,72,128]{3,2,1,0:T(8,128)(2,1)S(1)}, u32[]{:S(2)}, u32[]{:S(2)}) async-start(bf16[4,8,72,128]{3,2,1,0:T(8,128)(2,1)} %shard_map.56), calls=%async_computation.1 | async-start | bytes 1179648 | tf_op jit(solution)/shard_map/all_to_all | solution.py:27
  47.5 1.0 copy-start.2
  54.2 59.5 %copy-start.1 = (f32[72,128]{1,0:T(8,128)S(1)}, f32[72,128]{1,0:T(8,128)}, u32[]{:S(2)}) copy-start(f32[72,128]{1,0:T(8,128)} %get-tuple-element.26.current_ref) | copy-start | bytes 110596
  114.6 21.3 %all-to-all-start.5 = ((bf16[32,72,128]{2,1,0:T(8,128)(2,1)}), bf16[32,72,128]{2,1,0:T(8,128)(2,1)S(1)}, u32[]{:S(2)}, u32[]{:S(2)}) async-start(bf16[32,72,128]{2,1,0:T(8,128)(2,1)} %get-tuple-element.27), calls=%async_computation.5 | async-start | bytes 1179648 | tf_op jit(solution)/shard_map/all_to_all | solution.py:27
  119.5 1.2 copy-start.3

commit v15 on v14

--- a/solution.py
+++ b/solution.py
@@ -271,25 +271,26 @@
     ]
     for copy in fetches:
         copy.start()
-    fetches[0].wait()
-    height = packed_ref.shape[0]
-    columns = coefs.shape[1]
-    sides = [coefs[:, at : at + height] for at in range(0, columns, height)]
-    packed = jnp.transpose(jnp.concatenate(sides, axis=0))
-    packed_ref[...] = packed
-    half_ref[0] = packed.astype(half_ref.dtype)
-    for copy in fetches[1:]:
-        copy.wait()
+    fetches[1].wait()
     pool_dev = pool.shape[1]
     copies, steps, _, batch = out_ref.shape
     first = (lax.axis_index("z") * lax.axis_size("x") + lax.axis_index("x")) * pool_dev
     rows = lax.broadcasted_iota(jnp.int32, (pool_dev, batch), 0)
+    onehots = [
+        (rows == picks[step : step + 1, :] - first).astype(jnp.float32).astype(jnp.bfloat16)
+        for step in range(steps)
+    ]
+    fetches[0].wait()
+    height = packed_ref.shape[0]
+    sides = [coefs[:, at : at + height] for at in range(0, coefs.shape[1], height)]
+    packed = jnp.transpose(jnp.concatenate(sides, axis=0))
+    packed_ref[...] = packed
+    half_ref[0] = packed.astype(half_ref.dtype)
+    fetches[2].wait()
     for step in range(steps):
-        chosen = picks[step : step + 1, :] - first
-        onehot = (rows == chosen).astype(jnp.float32).astype(jnp.bfloat16)
-        feats = jnp.dot(pool[...], onehot, preferred_element_type=jnp.float32).astype(out_ref.dtype)
+        feats = jnp.dot(pool[...], onehots[step], preferred_element_type=jnp.float32)
         for peer in range(copies):
-            out_ref[peer, step] = feats
+            out_ref[peer, step] = feats.astype(out_ref.dtype)
 
 
 def picked(pool, picks, coefs, copies):

time: 190 us -> 191 us (level)
  no operation moved by 1% of the time
where the time goes in v15:
time: 191 us; the launch traced here: 190 us
  blocking collectives  105 us (55%)
  starting transfers between devices  39.1 us (20%)
  Pallas kernels  21.5 us (11%)
  waiting for transfers between devices  16 us (8%)
  local copies, waits for them, and re-layouts  4.56 us (2%)
  other arithmetic  3.78 us (2%)
    all_to_all x6, blocking collectives, exchange(): return lax.all_to_all(parts, axes, 0, 0, tiled=True)  105 us
    all_to_all x3, starting transfers between devices, exchange(): return lax.all_to_all(parts, axes, 0, 0, tiled=True)  16.6 us
    ppermute x2, starting transfers between devices, doubled(): return jnp.concatenate([held, lax.ppermute(held, axis, pairs)])  14.6 us
    all_to_all x3, waiting for transfers between devices, exchange(): return lax.all_to_all(parts, axes, 0, 0, tiled=True)  12.7 us
    pallas_call x2, Pallas kernels, kernel_matrix(): pl.pallas_call(laplace_body, out_shape=jax.ShapeDtypeStruct((batch, colum...  11.3 us
    pallas_call x10, Pallas kernels, call(): pl.pallas_call(body, out_shape=out, in_specs=[vmem] * len(operands), out_...  7.23 us
    ppermute x1, starting transfers between devices, swapped_cores(): return lax.ppermute(array, 'core', [(0, 1), (1, 0)])  4.84 us
  transfers between devices with their start and end apart: 7, of which 4 were waited for; matrix products, arithmetic and copies ran while one was open for 3% of the time, Pallas kernels for 7%

profile of v15, /device:TPU:1, one launch (start us, length us, event | category | flops | bytes accessed | tf_op | source)
XLA Modules:
  0.0 189.8 jit_solution(15537464139864782304)
XLA Ops:
  0.0 2.9 %shard_map.55 = (bf16[8,2,64,512]{3,2,1,0:T(8,128)(2,1)}, f32[72,128]{1,0:T(8,128)}, bf16[1,72,128]{2,1,0:T(8,128)(2,1)}) custom-call(bf16[64,1024]{1,0:T(8,128)(2,1)} %pool_ref.1, s32[2,512]{1,0:T(2,128)} %picks_ref.1, f32[64,144]{1,0:T(8,128)} %bitcast.11), custom_call_target="tpu_custom_call" | custom-call | flops 134217728 | bytes 131072 | tf_op jit(solution)/shard_map/pallas_call | solution.py:299
  3.0 7.7 %all-to-all-start = ((bf16[8,2,64,512]{3,2,1,0:T(8,128)(2,1)}), bf16[8,2,64,512]{3,2,1,0:T(8,128)(2,1)S(1)}, u32[]{:S(2)}, u32[]{:S(2)}) async-start(bf16[8,2,64,512]{3,2,1,0:T(8,128)(2,1)} %get-tuple-element.18), calls=%async_computation | async-start | bytes 2097152 | tf_op jit(solution)/shard_map/all_to_all | solution.py:27
  10.6 10.6 %collective-permute-start = (bf16[1,72,128]{2,1,0:T(8,128)(2,1)}, bf16[1,72,128]{2,1,0:T(8,128)(2,1)S(1)}, u32[]{:S(2)}, u32[]{:S(2)}) collective-permute-start(bf16[1,72,128]{2,1,0:T(8,128)(2,1)} %get-tuple-element.19), channel_id=1, source_target_pairs={{0,16},{4,20},{8,24},{12,28},{16,0},{20,4},{24,8},{28,12},{1,17},{... | collective-permute-start | bytes 55304 | tf_op jit(solution)/shard_map/ppermute | solution.py:246
  22.8 3.1 %multiply_reduce_fusion = f32[2048]{0:T(1024)S(1)} fusion(bf16[1024,2048]{1,0:T(8,128)(2,1)} %centres_ref.3), kind=kLoop, calls=%fused_computation.2 | loop fusion | flops 6289408 | bytes 4202496 | tf_op jit(solution)/shard_map/reduce_sum | solution.py:380
  26.6 4.0 %collective-permute-start.1 = (bf16[2,72,128]{2,1,0:T(8,128)(2,1)S(1)}, bf16[2,72,128]{2,1,0:T(8,128)(2,1)S(1)}, u32[]{:S(2)}, u32[]{:S(2)}) collective-permute-start(bf16[2,72,128]{2,1,0:T(8,128)(2,1)S(1)} %pad_maximum_fusion), channel_id=1, source_target_pairs={{0,8},{4,12},{8,0},{12,4},{16,24},{20,28},{24,16},{28,20},{1,9},{5... | collective-permute-start | bytes 110600 | tf_op jit(solution)/shard_map/ppermute | solution.py:246
  30.7 1.9 collective-permute-done.1
  32.5 3.1 %collective-permute-start.2 = (bf16[4,72,128]{2,1,0:T(8,128)(2,1)S(1)}, bf16[4,72,128]{2,1,0:T(8,128)(2,1)S(1)}, u32[]{:S(2)}, u32[]{:S(2)}) collective-permute-start(bf16[4,72,128]{2,1,0:T(8,128)(2,1)S(1)} %constant_dynamic-update-slice_fusion.held_ref), channel_id=1, source_target_pairs={{0,4},{4,0},{8,12},{12,8},{16,20},{20,16},{24,28},{28,24},{1,5},{5... | collective-permute-start | bytes 221192 | tf_op jit(solution)/shard_map/ppermute | solution.py:258
  36.4 1.5 collective-permute-done.2.moved_ref
  38.8 4.8 %collective-permute-start.3 = (bf16[8,2,64,512]{3,2,1,0:T(8,128)(2,1)S(1)}, bf16[8,2,64,512]{3,2,1,0:T(8,128)(2,1)S(1)}, u32[]{:S(2)}, u32[]{:S(2)}) collective-permute-start(bf16[8,2,64,512]{3,2,1,0:T(8,128)(2,1)S(1)} %all-to-all-done.mine_ref), channel_id=1, source_target_pairs={{0,32},{32,0},{1,33},{33,1},{2,34},{34,2},{3,35},{35,3},{4,36},{36... | collective-permute-start | bytes 3145736 | tf_op jit(solution)/shard_map/ppermute | solution.py:264
  43.7 4.0 %all-to-all-start.1 = ((bf16[4,8,72,128]{3,2,1,0:T(8,128)(2,1)}), bf16[4,8,72,128]{3,2,1,0:T(8,128)(2,1)S(1)}, u32[]{:S(2)}, u32[]{:S(2)}) async-start(bf16[4,8,72,128]{3,2,1,0:T(8,128)(2,1)} %shard_map.56), calls=%async_computation.1 | async-start | bytes 1179648 | tf_op jit(solution)/shard_map/all_to_all | solution.py:27
  48.9 5.7 %shard_map.58.kern_ref = bf16[512,2048]{1,0:T(8,128)(2,1)S(1)} custom-call(bf16[8,2,64,512]{3,2,1,0:T(8,128)(2,1)S(1)} %get-tuple-element.23.feats_ref, bf16[1024,2048]{1,0:T(8,128)(2,1)} %centres_ref.3, f32[1,2048]{1,0:T(1,128)S(1)} %bitcast.9), custom_call_target="tpu_custom_call" | custom-call | flops 2147483648 | bytes 4194304 | tf_op jit(solution)/shard_map/pallas_call | solution.py:224
  54.6 3.2 %all-to-all-done.1.coef_ref = bf16[4,8,72,128]{3,2,1,0:T(8,128)(2,1)S(1)} async-done(((bf16[4,8,72,128]{3,2,1,0:T(8,128)(2,1)}), bf16[4,8,72,128]{3,2,1,0:T(8,128)(2,1)S(1)}, u32[]{:S(2)}, u32[]{:S(2)}) %all-to-all-start.1) | async-done | bytes 589856 | tf_op jit(solution)/shard_map/all_to_all | solution.py:27
  57.7 1.2 shard_map.59
  59.0 17.8 %all_to_all.45.arrived_ref = bf16[16,36,128]{2,1,0:T(8,128)(2,1)S(1)} all-to-all(bf16[16,36,128]{2,1,0:T(8,128)(2,1)S(1)} %shard_map.59), channel_id=1, replica_groups=mesh['y'=8,'core'=2,'z'=8,'x'=4] {'y','core'}, dimensions={0} | all-to-all | bytes 294912 | tf_op jit(solution)/shard_map/all_to_all | solution.py:27
  77.1 12.3 %all_to_all.46.resid_ref = bf16[16,36,128]{2,1,0:T(8,128)(2,1)S(1)} all-to-all(bf16[16,36,128]{2,1,0:T(8,128)(2,1)S(1)} %shard_map.60), channel_id=1, replica_groups=mesh['y'=8,'core'=2,'z'=8,'x'=4] {'y','core'}, dimensions={0} | all-to-all | bytes 294912 | tf_op jit(solution)/shard_map/all_to_all | solution.py:27
  90.1 24.0 %all_to_all.47.arrived_ref = bf16[32,72,128]{2,1,0:T(8,128)(2,1)S(1)} all-to-all(bf16[32,72,128]{2,1,0:T(8,128)(2,1)S(1)} %shard_map.61), channel_id=1, replica_groups=mesh['y'=8,'core'=2,'z'=8,'x'=4] {'z','x'}, dimensions={0} | all-to-all | bytes 1179648 | tf_op jit(solution)/shard_map/all_to_all | solution.py:27
  115.0 4.9 %all-to-all-start.5 = ((bf16[32,72,128]{2,1,0:T(8,128)(2,1)}), bf16[32,72,128]{2,1,0:T(8,128)(2,1)S(1)}, u32[]{:S(2)}, u32[]{:S(2)}) async-start(bf16[32,72,128]{2,1,0:T(8,128)(2,1)} %get-tuple-element.27), calls=%async_computation.5 | async-start | bytes 1179648 | tf_op jit(solution)/shard_map/all_to_all | solution.py:27
  119.9 1.2 copy-done.3
  121.1 5.7 %shard_map.63.kern_ref = bf16[512,2048]{1,0:T(8,128)(2,1)S(1)} custom-call(bf16[8,2,64,512]{3,2,1,0:T(8,128)(2,1)S(1)} %copy-done.3, bf16[1024,2048]{1,0:T(8,128)(2,1)} %centres_ref.3, f32[1,2048]{1,0:T(1,128)S(1)} %bitcast.10), custom_call_target="tpu_custom_call" | custom-call | flops 2147483648 | bytes 4194304 | tf_op jit(solution)/shard_map/pallas_call | solution.py:224
  126.8 9.5 %all-to-all-done.5 = bf16[32,72,128]{2,1,0:T(8,128)(2,1)S(1)} async-done(((bf16[32,72,128]{2,1,0:T(8,128)(2,1)}), bf16[32,72,128]{2,1,0:T(8,128)(2,1)S(1)}, u32[]{:S(2)}, u32[]{:S(2)}) %all-to-all-start.5) | async-done | bytes 589856 | tf_op jit(solution)/shard_map/all_to_all | solution.py:27
  136.3 1.0 shard_map.64
  137.3 15.7 %all_to_all.48.arrived_ref = bf16[16,36,128]{2,1,0:T(8,128)(2,1)S(1)} all-to-all(bf16[16,36,128]{2,1,0:T(8,128)(2,1)S(1)} %shard_map.64), channel_id=1, replica_groups=mesh['y'=8,'core'=2,'z'=8,'x'=4] {'y','core'}, dimensions={0} | all-to-all | bytes 294912 | tf_op jit(solution)/shard_map/all_to_all | solution.py:27
  153.4 12.1 %all_to_all.49.resid_ref = bf16[16,36,128]{2,1,0:T(8,128)(2,1)S(1)} all-to-all(bf16[16,36,128]{2,1,0:T(8,128)(2,1)S(1)} %shard_map.65), channel_id=1, replica_groups=mesh['y'=8,'core'=2,'z'=8,'x'=4] {'y','core'}, dimensions={0} | all-to-all | bytes 294912 | tf_op jit(solution)/shard_map/all_to_all | solution.py:27
  166.2 22.8 %all_to_all.50.arrived_ref = bf16[32,72,128]{2,1,0:T(8,128)(2,1)S(1)} all-to-all(bf16[32,72,128]{2,1,0:T(8,128)(2,1)S(1)} %shard_map.66), channel_id=1, replica_groups=mesh['y'=8,'core'=2,'z'=8,'x'=4] {'z','x'}, dimensions={0} | all-to-all | bytes 1179648 | tf_op jit(solution)/shard_map/all_to_all | solution.py:27
  (35 shorter events, 9.1 us)
Async XLA Ops:
  0.0 25.8 %copy-start = (s32[1024]{0:T(1024)S(1)}, s32[1024]{0:T(1024)}, u32[]{:S(2)}) copy-start(s32[1024]{0:T(1024)} %param.7) | copy-start | bytes 12292
  2.9 23.7 %copy-start.4 = (bf16[1,72,128]{2,1,0:T(8,128)(2,1)S(1)}, bf16[1,72,128]{2,1,0:T(8,128)(2,1)}, u32[]{:S(2)}) copy-start(bf16[1,72,128]{2,1,0:T(8,128)(2,1)} %get-tuple-element.19) | copy-start | bytes 55300
  3.0 35.9 %all-to-all-start = ((bf16[8,2,64,512]{3,2,1,0:T(8,128)(2,1)}), bf16[8,2,64,512]{3,2,1,0:T(8,128)(2,1)S(1)}, u32[]{:S(2)}, u32[]{:S(2)}) async-start(bf16[8,2,64,512]{3,2,1,0:T(8,128)(2,1)} %get-tuple-element.18), calls=%async_computation | async-start | bytes 2097152 | tf_op jit(solution)/shard_map/all_to_all | solution.py:27
  10.6 16.0 %collective-permute-start = (bf16[1,72,128]{2,1,0:T(8,128)(2,1)}, bf16[1,72,128]{2,1,0:T(8,128)(2,1)S(1)}, u32[]{:S(2)}, u32[]{:S(2)}) collective-permute-start(bf16[1,72,128]{2,1,0:T(8,128)(2,1)} %get-tuple-element.19), channel_id=1, source_target_pairs={{0,16},{4,20},{8,24},{12,28},{16,0},{20,4},{24,8},{28,12},{1,17},{... | collective-permute-start | bytes 55304 | tf_op jit(solution)/shard_map/ppermute | solution.py:246
  26.6 5.9 %collective-permute-start.1 = (bf16[2,72,128]{2,1,0:T(8,128)(2,1)S(1)}, bf16[2,72,128]{2,1,0:T(8,128)(2,1)S(1)}, u32[]{:S(2)}, u32[]{:S(2)}) collective-permute-start(bf16[2,72,128]{2,1,0:T(8,128)(2,1)S(1)} %pad_maximum_fusion), channel_id=1, source_target_pairs={{0,8},{4,12},{8,0},{12,4},{16,24},{20,28},{24,16},{28,20},{1,9},{5... | collective-permute-start | bytes 110600 | tf_op jit(solution)/shard_map/ppermute | solution.py:246
  32.5 5.4 %collective-permute-start.2 = (bf16[4,72,128]{2,1,0:T(8,128)(2,1)S(1)}, bf16[4,72,128]{2,1,0:T(8,128)(2,1)S(1)}, u32[]{:S(2)}, u32[]{:S(2)}) collective-permute-start(bf16[4,72,128]{2,1,0:T(8,128)(2,1)S(1)} %constant_dynamic-update-slice_fusion.held_ref), channel_id=1, source_target_pairs={{0,4},{4,0},{8,12},{12,8},{16,20},{20,16},{24,28},{28,24},{1,5},{5... | collective-permute-start | bytes 221192 | tf_op jit(solution)/shard_map/ppermute | solution.py:258
  38.8 8.9 %collective-permute-start.3 = (bf16[8,2,64,512]{3,2,1,0:T(8,128)(2,1)S(1)}, bf16[8,2,64,512]{3,2,1,0:T(8,128)(2,1)S(1)}, u32[]{:S(2)}, u32[]{:S(2)}) collective-permute-start(bf16[8,2,64,512]{3,2,1,0:T(8,128)(2,1)S(1)} %all-to-all-done.mine_ref), channel_id=1, source_target_pairs={{0,32},{32,0},{1,33},{33,1},{2,34},{34,2},{3,35},{35,3},{4,36},{36... | collective-permute-start | bytes 3145736 | tf_op jit(solution)/shard_map/ppermute | solution.py:264
  43.7 14.0 %all-to-all-start.1 = ((bf16[4,8,72,128]{3,2,1,0:T(8,128)(2,1)}), bf16[4,8,72,128]{3,2,1,0:T(8,128)(2,1)S(1)}, u32[]{:S(2)}, u32[]{:S(2)}) async-start(bf16[4,8,72,128]{3,2,1,0:T(8,128)(2,1)} %shard_map.56), calls=%async_computation.1 | async-start | bytes 1179648 | tf_op jit(solution)/shard_map/all_to_all | solution.py:27
  47.9 1.0 copy-start.2
  54.5 59.5 %copy-start.1 = (f32[72,128]{1,0:T(8,128)S(1)}, f32[72,128]{1,0:T(8,128)}, u32[]{:S(2)}) copy-start(f32[72,128]{1,0:T(8,128)} %get-tuple-element.26.current_ref) | copy-start | bytes 110596
  115.0 21.3 %all-to-all-start.5 = ((bf16[32,72,128]{2,1,0:T(8,128)(2,1)}), bf16[32,72,128]{2,1,0:T(8,128)(2,1)S(1)}, u32[]{:S(2)}, u32[]{:S(2)}) async-start(bf16[32,72,128]{2,1,0:T(8,128)(2,1)} %get-tuple-element.27), calls=%async_computation.5 | async-start | bytes 1179648 | tf_op jit(solution)/shard_map/all_to_all | solution.py:27
  119.9 1.2 copy-start.3
